TPU v7x, 32 devices: a whole 2x2x4 slice. The times are simulated.
32 devices in a mesh: lon: 8 (over z, y), lat: 4 (over x, core).
Axes of the slice: x: 2, y: 2, z: 4, core: 2. Of those that a mesh axis runs over, the one named last changes fastest.
Arguments:
- state: float32 [32, 512, 6, 128], P('lat', 'lon'), may hold values from -4 to 4
- background: float32 [32, 512, 6, 128], P('lat', 'lon'), may hold values from -4 to 4
- diffusivity: float32 [32, 512, 128], P('lat', 'lon'), may hold values from 0.03 to 0.2
- radiances: bfloat16 [2, 32, 512, 512], P(None, 'lat', 'lon'), may hold values from -5 to 5
- owners: int32 [2, 4, 32], P(None, 'lat', 'lon'), may hold values from 0 to 7, as said below
- first_layer: bfloat16 [8, 768, 1024], P('lon'), may hold values from -0.21875 to 0.21875
- second_layer: bfloat16 [8, 1024, 1024], P('lon'), may hold values from -0.1875 to 0.1875
- third_layer: bfloat16 [8, 1024, 512], P('lon'), may hold values from -0.1875 to 0.1875
- channel_weight: float32 [8, 512], P('lon'), may hold values from 0.3 to 3
Outputs:
- gradient: float32 [32, 512, 6, 128], P('lat', 'lon')
Inputs may be any that keep to these rules, and one draw needn't show every extreme that they name: `owners`: every block is observed by one instrument in every slot. In each slot a device sends at most 1 of its blocks to one instrument, and an instrument receives at most 6 blocks from the devices of one latitude index; both bounds are reached in every slot and latitude index.
All inputs are finite; a program needn't handle non-finite values.
Results may differ from a plain program's by a relative error of at most 0.0024.
Values may be sent and summed in bfloat16 or wider, within the bound.
No kernel may reach another device: no remote copies, remote signals or barrier semaphores. Data moves between devices by JAX's collectives and lax.ppermute only.
A program may use at most 128 MiB of HBM per device.

v0:
```python
import functools
import jax
import jax.numpy as jnp
from jax import lax
from jax.experimental import pallas as pl
from jax.experimental.pallas import tpu as pltpu
from jax.sharding import PartitionSpec as P

ADVECTION = 0.25
VERTICAL = 0.1
SERVED = 4
EDGE = 16
SIDE = 8
ANY = pl.BlockSpec(memory_space=pl.ANY)
SMEM = pl.BlockSpec(memory_space=pltpu.SMEM)
VMEM = pl.BlockSpec(memory_space=pltpu.VMEM)
F32 = jnp.float32
BF16 = jnp.bfloat16


def params(mib):
    return pltpu.CompilerParams(vmem_limit_bytes=mib << 20)


def exchange(array, axis, mask):
    count = lax.axis_size(axis)
    return lax.ppermute(array, axis, [(i, i ^ mask) for i in range(count)])


def shifted(array, axis, step, periodic):
    count = lax.axis_size(axis)
    pairs = [(i, (i + step) % count) for i in range(count)]
    if not periodic:
        pairs = [(i, j) for i, j in pairs if j == i + step]
    return lax.ppermute(array, axis, pairs)


def bits_down(size):
    bit = size // 2
    while bit:
        yield bit
        bit //= 2


def pack_kernel(pos, w1, w2, w3, scale, out, tail, sems):
    lat = pos[1]
    width = out.shape[1]
    parts = width // w3.shape[1]
    n_lat = pos_lat(w1, w2, w3, out)
    r1, r2, r3 = (w.shape[0] // n_lat for w in (w1, w2, w3))
    copies = [
        pltpu.make_async_copy(w1.at[pl.ds(lat * r1, r1)], out.at[pl.ds(0, r1)], sems.at[0]),
        pltpu.make_async_copy(w2.at[pl.ds(lat * r2, r2)], out.at[pl.ds(r1, r2)], sems.at[1]),
    ]
    piece = r3 // parts
    for j in range(parts):
        copies.append(
            pltpu.make_async_copy(
                w3.at[pl.ds(lat * r3 + j * piece, piece)],
                out.at[pl.ds(r1 + r2, piece), pl.ds(j * w3.shape[1], w3.shape[1])],
                sems.at[2 + j],
            )
        )
    for copy in copies:
        copy.start()
    whole = scale[...]
    high = whole.astype(BF16).astype(F32)
    rest = whole - high
    middle = rest.astype(BF16).astype(F32)
    low = rest - middle
    tail[...] = jnp.zeros_like(tail)
    rows = lax.broadcasted_iota(jnp.int32, (tail.shape[0], scale.shape[1]), 0)
    stacked = jnp.where(rows == 0, high, jnp.where(rows == 1, middle, low))
    tail[:, 0 : scale.shape[1]] = jnp.where(rows < 3, stacked, 0.0).astype(BF16)
    last = pltpu.make_async_copy(tail, out.at[pl.ds(r1 + r2 + piece, tail.shape[0])], sems.at[2 + parts])
    last.start()
    for copy in copies:
        copy.wait()
    last.wait()


def pos_lat(w1, w2, w3, out):
    body = out.shape[0] - 16
    return (w1.shape[0] + w2.shape[0] + w3.shape[0] * w3.shape[1] // out.shape[1]) // body


def pack_weights(pos, weights, n_lat):
    w1, w2, w3, scale = weights
    width = w1.shape[1]
    parts = width // w3.shape[1]
    rows = (w1.shape[0] + w2.shape[0] + w3.shape[0] // parts) // n_lat + 16
    return pl.pallas_call(
        pack_kernel,
        out_shape=jax.ShapeDtypeStruct((rows, width), BF16),
        in_specs=[SMEM, ANY, ANY, ANY, VMEM],
        out_specs=ANY,
        scratch_shapes=[pltpu.VMEM((16, width), BF16), pltpu.SemaphoreType.DMA((3 + parts,))],
        name="pack",
    )(pos, w1, w2, w3, scale)


def spread_weights(packed, group, n_lon, n_lat):
    found = {0: packed}
    for bit in bits_down(n_lon // group):
        for near in list(found):
            found[near | bit] = exchange(found[near], "lon", bit * group)
    gathered = {}
    for served, part in found.items():
        if served == 0:
            continue
        parts = {0: part}
        for bit in bits_down(n_lat):
            for near in list(parts):
                parts[near | bit] = exchange(parts[near], "lat", bit)
        gathered[served] = parts
    return gathered


def radiance_kernel(group, pos, table, source, *refs):
    *outs, sems = refs
    slots, served, span, _ = outs[0].shape
    count = table.shape[1]
    copies = []
    for c, out in enumerate(outs, 1):
        for s in range(slots):
            for w in range(served):
                block = table[s, pos[0] ^ (w * group + c)]
                copies.append(
                    pltpu.make_async_copy(
                        source.at[s, pl.ds(pl.multiple_of(block * span, span), span)],
                        out.at[s, w],
                        sems.at[len(copies)],
                    )
                )
    for copy in copies:
        copy.start()
    for copy in copies:
        copy.wait()


def send_radiances(pos, table, radiances, group, served, span):
    slots, _, channels = radiances.shape
    shape = jax.ShapeDtypeStruct((slots, served, span, channels), BF16)
    return pl.pallas_call(
        functools.partial(radiance_kernel, group),
        out_shape=[shape] * (group - 1),
        in_specs=[SMEM, SMEM, ANY],
        out_specs=[ANY] * (group - 1),
        scratch_shapes=[pltpu.SemaphoreType.DMA(((group - 1) * slots * served,))],
        name="pick_radiances",
    )(pos, table, radiances)


def vertical_sum(values):
    lane = lax.broadcasted_iota(jnp.int32, values.shape, 1)
    size = values.shape[1]
    upper = jnp.where(lane == size - 1, 0.0, pltpu.roll(values, size - 1, 1))
    lower = jnp.where(lane == 0, 0.0, pltpu.roll(values, 1, 1))
    return upper + lower


def step_value(centre, east, west, north, south, zonal, meridional, kappa):
    transport = 0.5 * ADVECTION * (zonal * (east - west) + meridional * (north - south))
    spread = east + west + north + south - 4.0 * centre
    return centre - transport + kappa * spread + VERTICAL * (vertical_sum(centre) - 2.0 * centre)


def forward_kernel(group, pos, table, state, kappa, south, north, west, east, wide, first, columns, *sends):
    rows, fields, width, levels = state.shape
    inner = pl.ds(EDGE, width)

    def place(r, _):
        wide[r + 2, 0:fields, inner] = state[r]
        wide[r + 2, fields, inner] = kappa[r]
        return 0

    lax.fori_loop(0, rows, place, 0)
    for r in range(2):
        wide[r, :, inner] = south[r]
        wide[rows + 2 + r, :, inner] = north[r]

    def rims(r, _):
        wide[r, :, EDGE - 2 : EDGE] = west[r]
        wide[r, :, EDGE + width : EDGE + width + 2] = east[r]
        return 0

    lax.fori_loop(0, rows + 4, rims, 0)
    low = EDGE - SIDE
    span = width + 2 * SIDE

    def first_row(r, _):
        zonal = wide[r + 1, 0, pl.ds(low, span)]
        meridional = wide[r + 1, 1, pl.ds(low, span)]
        k = wide[r + 1, fields, pl.ds(low, span)]
        for f in range(fields):
            first[r, f] = step_value(
                wide[r + 1, f, pl.ds(low, span)],
                wide[r + 1, f, pl.ds(low + 1, span)],
                wide[r + 1, f, pl.ds(low - 1, span)],
                wide[r + 2, f, pl.ds(low, span)],
                wide[r, f, pl.ds(low, span)],
                zonal,
                meridional,
                k,
            )
        return 0

    lax.fori_loop(0, rows + 2, first_row, 0)

    def second_row(r, _):
        here = pl.ds(SIDE, width)
        zonal = first[r + 1, 0, here]
        meridional = first[r + 1, 1, here]
        k = wide[r + 2, fields, inner]
        lines = pl.ds(pl.multiple_of(r * width, width), width)
        for f in range(fields):
            centre = first[r + 1, f, here]
            value = step_value(
                centre,
                first[r + 1, f, pl.ds(SIDE + 1, width)],
                first[r + 1, f, pl.ds(SIDE - 1, width)],
                first[r + 2, f, here],
                first[r, f, here],
                zonal,
                meridional,
                k,
            )
            columns[0, lines, f * levels : (f + 1) * levels] = centre.astype(BF16)
            columns[1, lines, f * levels : (f + 1) * levels] = value.astype(BF16)
        return 0

    lax.fori_loop(0, rows, second_row, 0)
    slots, served, block, _ = sends[0].shape
    for c, send in enumerate(sends, 1):
        for s in range(slots):
            for w in range(served):
                b = table[s, pos[0] ^ (w * group + c)]
                send[s, w] = columns[s, pl.ds(pl.multiple_of(b * block, block), block)]


def forward(pos, table, state, kappa, rims, group, served, block):
    rows, fields, width, levels = state.shape
    slots = table.shape[0]
    outs = [
        jax.ShapeDtypeStruct((rows + 4, fields + 1, width + 2 * EDGE, levels), F32),
        jax.ShapeDtypeStruct((rows + 2, fields, width + 2 * SIDE, levels), F32),
        jax.ShapeDtypeStruct((slots, rows * width, fields * levels), BF16),
    ] + [jax.ShapeDtypeStruct((slots, served, block, fields * levels), BF16)] * (group - 1)
    return pl.pallas_call(
        functools.partial(forward_kernel, group),
        out_shape=outs,
        in_specs=[SMEM, SMEM] + [VMEM] * 6,
        out_specs=[VMEM] * len(outs),
        compiler_params=params(40),
        name="forward",
    )(pos, table, state, kappa, *rims)


def halo_of_state(state, kappa):
    width = state.shape[2]
    joined = jnp.concatenate([state, kappa[:, None]], axis=1)
    south = shifted(joined[-2:], "lat", 1, False)
    north = shifted(joined[:2], "lat", -1, False)

    def edge(cut):
        return jnp.concatenate([south[:, :, cut], joined[:, :, cut], north[:, :, cut]], axis=0)

    west = shifted(edge(slice(width - 2, width)), "lon", 1, True)
    east = shifted(edge(slice(0, 2)), "lon", -1, True)
    return south, north, west, east


def backward_kernel(first_half, *refs):
    if first_half:
        adj, south, north, west, east, base, kappa, extra, out, lo, hi, we, ea, pad = refs
        shift, row0 = SIDE, 0
    else:
        adj, south, north, west, east, base, extra, other, out, pad = refs
        shift, row0 = EDGE, 1
    rows, fields, width, levels = adj.shape
    inner = pl.ds(EDGE, width)

    def place(r, _):
        pad[r + 1, :, inner] = adj[r].astype(F32)
        pad[r + 1, :, EDGE - 1 : EDGE] = west[r][:, None]
        pad[r + 1, :, EDGE + width : EDGE + width + 1] = east[r][:, None]
        return 0

    lax.fori_loop(0, rows, place, 0)
    pad[0, :, inner] = south[...].astype(F32)
    pad[rows + 1, :, inner] = north[...].astype(F32)
    half = 0.5 * ADVECTION

    def diffusion(r, at):
        if first_half:
            return kappa[r + 1, 0, pl.ds(EDGE + at, width)]
        return base[r + 1, fields, pl.ds(EDGE + at, width)]

    def wind(r, f, at):
        return base[r + row0, f, pl.ds(shift + at, width)]

    def row(r, _):
        c_here = (1.0 - 2.0 * VERTICAL) - 4.0 * diffusion(r + 1, 0)
        c_west = diffusion(r + 1, -1) - half * wind(r + 1, 0, -1)
        c_east = diffusion(r + 1, 1) + half * wind(r + 1, 0, 1)
        c_south = diffusion(r, 0) - half * wind(r, 1, 0)
        c_north = diffusion(r + 2, 0) + half * wind(r + 2, 1, 0)
        zonal = jnp.zeros((width, levels), F32)
        meridional = jnp.zeros((width, levels), F32)
        for f in range(fields):
            here = pad[r + 1, f, inner]
            zonal += here * (wind(r + 1, f, 1) - wind(r + 1, f, -1))
            meridional += here * (wind(r + 2, f, 0) - wind(r, f, 0))
        for f in range(fields):
            here = pad[r + 1, f, inner]
            value = (
                here * c_here
                + pad[r + 1, f, pl.ds(EDGE - 1, width)] * c_west
                + pad[r + 1, f, pl.ds(EDGE + 1, width)] * c_east
                + pad[r, f, inner] * c_south
                + pad[r + 2, f, inner] * c_north
                + VERTICAL * vertical_sum(here)
            )
            if f == 0:
                value -= half * zonal
            if f == 1:
                value -= half * meridional
            if first_half:
                value += extra[r, f].astype(F32)
                we[r, f : f + 1] = value[0:1]
                ea[r, f : f + 1] = value[width - 1 : width]
            else:
                value += extra[r, f] - other[r, f]
            out[r, f] = value
        return 0

    lax.fori_loop(0, rows, row, 0)
    if first_half:
        lo[...] = out[0]
        hi[...] = out[rows - 1]


def halo_of_adjoint(edges):
    low, high, west, east = edges
    return (
        shifted(high, "lat", 1, False),
        shifted(low, "lat", -1, False),
        shifted(east, "lon", 1, True),
        shifted(west, "lon", -1, True),
    )


def backward_first(adjoint, rims, first, wide, forcing):
    rows, fields, width, levels = adjoint.shape
    line = jax.ShapeDtypeStruct((fields, width, levels), F32)
    side = jax.ShapeDtypeStruct((rows, fields, levels), F32)
    kappa_spec = pl.BlockSpec(
        (rows + 4, 1, width + 2 * EDGE, levels), lambda i: (0, fields, 0, 0)
    )

    def whole(shape):
        return pl.BlockSpec(shape, lambda i: (0,) * len(shape))

    out, *edges = pl.pallas_call(
        functools.partial(backward_kernel, True),
        grid=(1,),
        out_shape=[jax.ShapeDtypeStruct(adjoint.shape, F32), line, line, side, side],
        in_specs=[whole(a.shape) for a in (adjoint, *rims, first)]
        + [kappa_spec, whole(forcing.shape)],
        out_specs=[whole(adjoint.shape), whole(line.shape), whole(line.shape), whole(side.shape), whole(side.shape)],
        scratch_shapes=[pltpu.VMEM((rows + 2, fields, width + 2 * EDGE, levels), F32)],
        compiler_params=params(40),
        name="backward_first",
    )(adjoint, *rims, first, wide, forcing)
    return out, edges


def backward_last(adjoint, rims, wide, state, background):
    rows, fields, width, levels = adjoint.shape
    return pl.pallas_call(
        functools.partial(backward_kernel, False),
        out_shape=jax.ShapeDtypeStruct(adjoint.shape, F32),
        in_specs=[VMEM] * 8,
        out_specs=VMEM,
        scratch_shapes=[pltpu.VMEM((rows + 2, fields, width + 2 * EDGE, levels), F32)],
        compiler_params=params(40),
        name="backward_last",
    )(adjoint, *rims, wide, state, background)


def nt_dot(a, b):
    return lax.dot_general(a, b, (((1,), (1,)), ((), ())), preferred_element_type=F32)


def instrument_kernel(group, served, n_lat, pos, table, columns, radiances, *refs):
    others = group - 1
    got_columns, refs = refs[:others], refs[others:]
    got_radiances, refs = refs[:others], refs[others:]
    own_weights = served == 0
    n_weights = 4 if own_weights else n_lat
    weights, refs = refs[:n_weights], refs[n_weights:]
    outs, refs = refs[:group], refs[group:]
    x, y, w1, w2, w3, scale, a1, s1, a2, s2, mis, sem_x, sem_y, sem_w = refs
    slots, span, _ = outs[0].shape
    tile = 256
    copies_x, copies_y = [], []
    for c in range(group):
        for s in range(slots):
            j = c * slots + s
            if c == 0:
                block = table[s, pos[0] ^ (served * group)]
                lines = pl.ds(pl.multiple_of(block * span, span), span)
                from_x, from_y = columns.at[s, lines], radiances.at[s, lines]
            else:
                from_x, from_y = got_columns[c - 1].at[s, served], got_radiances[c - 1].at[s, served]
            copies_x.append(pltpu.make_async_copy(from_x, x.at[pl.ds(j * span, span)], sem_x.at[j]))
            copies_y.append(pltpu.make_async_copy(from_y, y.at[pl.ds(j * span, span)], sem_y.at[j]))
    phases = [[], [], []]
    if own_weights:
        for k, (source, target) in enumerate(zip(weights, (w1, w2, w3))):
            phases[k].append(pltpu.make_async_copy(source, target, sem_w.at[k]))
        phases[2].append(pltpu.make_async_copy(weights[3], scale, sem_w.at[3]))
    else:
        parts = w1.shape[1] // w3.shape[1]
        r1, r2, r3 = (w.shape[0] // n_lat for w in (w1, w2, w3))
        piece = r3 // parts
        count = 0
        for near in range(n_lat):
            lat = pos[1] ^ near
            source = weights[near]

            def start(phase, src, dst):
                nonlocal count
                phases[phase].append(pltpu.make_async_copy(src, dst, sem_w.at[count]))
                count += 1

            start(0, source.at[pl.ds(0, r1)], w1.at[pl.ds(pl.multiple_of(lat * r1, 16), r1)])
            start(1, source.at[pl.ds(r1, r2)], w2.at[pl.ds(pl.multiple_of(lat * r2, 16), r2)])
            for p in range(parts):
                start(
                    2,
                    source.at[pl.ds(r1 + r2, piece), pl.ds(p * w3.shape[1], w3.shape[1])],
                    w3.at[pl.ds(pl.multiple_of(lat * r3 + p * piece, 16), piece)],
                )
            if near == 0:
                start(2, source.at[pl.ds(r1 + r2 + piece, 16), pl.ds(0, w3.shape[1])], scale)
    for copy in copies_x + phases[0] + phases[1] + phases[2] + copies_y:
        copy.start()
    for copy in copies_x + phases[0]:
        copy.wait()

    def hidden(source, weight, act, slope):
        def column(n, _):
            at = pl.ds(pl.multiple_of(n * tile, tile), tile)
            z = jnp.dot(source[...], weight[:, at], preferred_element_type=F32)
            sigma = jax.nn.sigmoid(z)
            act[:, at] = (z * sigma).astype(BF16)
            slope[:, at] = sigma * (1.0 + z * (1.0 - sigma))
            return 0

        lax.fori_loop(0, weight.shape[1] // tile, column, 0)

    hidden(x, w1, a1, s1)
    for copy in phases[1]:
        copy.wait()
    hidden(a1, w2, a2, s2)
    for copy in phases[2] + copies_y:
        copy.wait()
    if not own_weights:
        triple = scale[...].astype(F32)
        factor = triple[0:1] + triple[1:2] + triple[2:3]
    else:
        factor = scale[...]
    for n in range(w3.shape[1] // tile):
        at = slice(n * tile, (n + 1) * tile)
        evolved = jnp.dot(a2[...], w3[:, at], preferred_element_type=F32)
        mis[:, at] = (factor[:, at] * (evolved - y[:, at].astype(F32))).astype(BF16)

    def back(source, weight, slope, grad):
        def column(n, _):
            at = pl.ds(pl.multiple_of(n * tile, tile), tile)
            grad[:, at] = (nt_dot(source[...], weight[at]) * slope[:, at]).astype(BF16)
            return 0

        lax.fori_loop(0, weight.shape[0] // tile, column, 0)

    back(mis, w3, s2, a2)
    back(a2, w2, s1, a1)
    for n in range(w1.shape[0] // tile):
        at = slice(n * tile, (n + 1) * tile)
        value = nt_dot(a1[...], w1[at]).astype(BF16)
        for c in range(group):
            for s in range(slots):
                j = c * slots + s
                outs[c][s, :, at] = value[j * span : (j + 1) * span]


def instrument(pos, table, columns, radiances, got_columns, got_radiances, weights, group, served, n_lat, sizes, span):
    slots, _, cin = columns.shape
    ch = radiances.shape[2]
    h1, h2 = sizes
    lines = group * slots * span
    own = served == 0
    out = jax.ShapeDtypeStruct((slots, span, cin), BF16)
    parts = h1 // ch
    return pl.pallas_call(
        functools.partial(instrument_kernel, group, served, n_lat),
        out_shape=[out] * group,
        in_specs=[SMEM, SMEM] + [ANY] * (2 + 2 * (group - 1) + len(weights)),
        out_specs=[VMEM] * group,
        scratch_shapes=[
            pltpu.VMEM((lines, cin), BF16),
            pltpu.VMEM((lines, ch), BF16),
            pltpu.VMEM((cin, h1), BF16),
            pltpu.VMEM((h1, h2), BF16),
            pltpu.VMEM((h2, ch), BF16),
            pltpu.VMEM((1, ch), F32) if own else pltpu.VMEM((16, ch), BF16),
            pltpu.VMEM((lines, h1), BF16),
            pltpu.VMEM((lines, h1), F32),
            pltpu.VMEM((lines, h2), BF16),
            pltpu.VMEM((lines, h2), F32),
            pltpu.VMEM((lines, ch), BF16),
            pltpu.SemaphoreType.DMA((group * slots,)),
            pltpu.SemaphoreType.DMA((group * slots,)),
            pltpu.SemaphoreType.DMA((4 if own else n_lat * (2 + parts) + 1,)),
        ],
        compiler_params=params(50),
        name=f"instrument_{served}",
    )(pos, table, columns, radiances, *got_columns, *got_radiances, *weights)


def collect_kernel(slot, group, edges, pos, owners, *refs):
    outs = 5 if edges else 1
    *answers, flat = refs[: len(refs) - 1 - outs] + refs[len(refs) - 1 :]
    out, *rims = refs[len(answers) : len(answers) + outs]
    rows, fields, width, levels = out.shape
    span = answers[0].shape[1]

    def block(b, _):
        apart = owners[slot, b] ^ pos[0]
        for k, answer in enumerate(answers):

            @pl.when(apart == k)
            def _():
                flat[pl.ds(pl.multiple_of(b * span, span), span)] = answer[slot]

        return 0

    lax.fori_loop(0, rows * width // span, block, 0)

    def row(r, _):
        lines = pl.ds(pl.multiple_of(r * width, width), width)
        for f in range(fields):
            value = flat[lines, f * levels : (f + 1) * levels]
            out[r, f] = value
            if edges:
                wide = value.astype(F32)
                rims[2][r, f : f + 1] = wide[0:1]
                rims[3][r, f : f + 1] = wide[width - 1 : width]
        return 0

    lax.fori_loop(0, rows, row, 0)
    if edges:
        rims[0][...] = out[0]
        rims[1][...] = out[rows - 1]


def collect(slot, pos, owners, answers, group, shape, edges):
    rows, fields, width, levels = shape
    outs = [jax.ShapeDtypeStruct(shape, BF16)]
    if edges:
        outs += [jax.ShapeDtypeStruct((fields, width, levels), BF16)] * 2
        outs += [jax.ShapeDtypeStruct((rows, fields, levels), F32)] * 2
    return pl.pallas_call(
        functools.partial(collect_kernel, slot, group, edges),
        out_shape=outs,
        in_specs=[SMEM, SMEM] + [VMEM] * len(answers),
        out_specs=[VMEM] * len(outs),
        scratch_shapes=[pltpu.VMEM((rows * width, fields * levels), BF16)],
        compiler_params=params(40),
        name=f"collect_{slot}",
    )(pos, owners, *answers)


def shards(state, background, diffusivity, radiances, owners, first_layer, second_layer, third_layer, channel_weight):
    n_lon, n_lat = lax.axis_size("lon"), lax.axis_size("lat")
    served = min(SERVED, n_lon)
    group = n_lon // served
    slots, _, blocks = owners.shape
    rows, width, fields, levels = state.shape
    span = rows * width // blocks
    cin, h1, h2 = first_layer.shape[1], first_layer.shape[2], second_layer.shape[2]
    pos = jnp.stack([lax.axis_index("lon"), lax.axis_index("lat")]).astype(jnp.int32)
    owners = owners[:, 0]
    hits = owners[:, None, :] == jnp.arange(n_lon, dtype=jnp.int32)[None, :, None]
    table = jnp.sum(jnp.where(hits, jnp.arange(blocks, dtype=jnp.int32), 0), axis=2)
    state = state.transpose(0, 2, 1, 3)
    background = background.transpose(0, 2, 1, 3)
    radiances = radiances.reshape(slots, rows * width, -1)
    own = (first_layer[0], second_layer[0], third_layer[0], channel_weight)

    rims = halo_of_state(state, diffusivity)
    gathered = spread_weights(pack_weights(pos, own, n_lat), group, n_lon, n_lat)
    sent = send_radiances(pos, table, radiances, group, served, span)
    got_radiances = [exchange(a, "lon", c) for c, a in enumerate(sent, 1)]
    wide, first, columns, *sent = forward(pos, table, state, diffusivity, rims, group, served, span)
    got_columns = [exchange(a, "lon", c) for c, a in enumerate(sent, 1)]

    answers = []
    for w in range(served):
        weights = own if w == 0 else [gathered[w][k] for k in range(n_lat)]
        mine, *theirs = instrument(
            pos, table, columns, radiances, got_columns, got_radiances, weights, group, w, n_lat, (h1, h2), span
        )
        answers.append(mine)
        answers.extend(exchange(a, "lon", c) for c, a in enumerate(theirs, 1))
    shape = state.shape
    late, *edges = collect(1, pos, owners, answers, group, shape, True)
    (early,) = collect(0, pos, owners, answers, group, shape, False)
    costate, edges = backward_first(late, halo_of_adjoint(edges), first, wide, early)
    gradient = backward_last(costate, halo_of_adjoint(edges), wide, state, background)
    return gradient.transpose(0, 2, 1, 3)


def solution(mesh):
    placed = (
        P("lat", "lon", None, None),
        P("lat", "lon", None, None),
        P("lat", "lon", None),
        P(None, "lat", "lon", None),
        P(None, "lat", "lon"),
        P("lon", None, None),
        P("lon", None, None),
        P("lon", None, None),
        P("lon", None),
    )
    return jax.shard_map(
        shards, mesh=mesh, in_specs=placed, out_specs=P("lat", "lon", None, None), check_vma=False
    )
```

profile of v0, /device:TPU:30, one launch (start us, length us, event | category | flops | bytes accessed | tf_op | source)
XLA Modules:
  0.0 308.5 jit_solution(8769345873577417295)
XLA Ops:
  0.0 0.7 pad_add_fusion.pos
  0.7 37.7 %pack.1 = bf16[592,1024]{1,0:T(8,128)(2,1)} custom-call(s32[2]{0:T(128)} %pad_add_fusion.pos, bf16[768,1024]{1,0:T(8,128)(2,1)} %bitcast.32, bf16[1024,1024]{1,0:T(8,128)(2,1)} %bitcast.30, bf16[1024,512]{1,0:T(8,128)(2,1)} %bitcast.21, f32[1,512]{1,0:T(1,128)} %scale.1), custom_call_target="tpu_custom_call" | custom-call | tf_op jit(solution)/shard_map/pack/pallas_call | solution.py:92
  38.4 0.0 copy-start.12
  38.4 0.4 collective-permute-start.12
  38.8 0.8 fusion.1
  39.7 1.9 collective-permute-start.1
  41.6 2.4 collective-permute-start
  44.0 0.5 collective-permute-start.7
  44.5 0.7 select_reduce_fusion.table
  45.2 33.6 %pick_radiances.1 = bf16[2,4,128,512]{3,2,1,0:T(8,128)(2,1)} custom-call(s32[2]{0:T(128)} %pad_add_fusion.pos, s32[2,8]{1,0:T(2,128)} %select_reduce_fusion.table, bf16[2,512,512]{2,1,0:T(8,128)(2,1)} %bitcast.16), custom_call_target="tpu_custom_call" | custom-call | tf_op jit(solution)/shard_map/pick_radiances/pallas_call | solution.py:144
  78.8 0.6 collective-permute-start.5
  79.4 14.6 %collective-permute-done.12.refs_2_ = bf16[592,1024]{1,0:T(8,128)(2,1)} collective-permute-done((bf16[592,1024]{1,0:T(8,128)(2,1)}, bf16[592,1024]{1,0:T(8,128)(2,1)}, u32[]{:S(2)}, u32[]{:S(2)}) %collective-permute-start.12) | collective-permute-done | bytes 1212448 | tf_op jit(solution)/shard_map/ppermute | solution.py:27
  94.2 0.0 copy-start.8
  94.2 0.8 copy-done.8
  95.0 0.9 collective-permute-start.2
  96.0 0.0 copy-start.1
  96.0 0.0 copy-start.3
  96.0 0.0 copy-start.13
  96.0 1.2 collective-permute-start.3
  97.2 25.2 %collective-permute-done.2.west = f32[12,7,2,128]{3,2,1,0:T(2,128)S(1)} collective-permute-done((f32[12,7,2,128]{3,2,1,0:T(2,128)S(1)}, f32[12,7,2,128]{3,2,1,0:T(2,128)S(1)}, u32[]{:S(2)}, u32[]{:S(2)}) %collective-permute-start.2) | collective-permute-done | bytes 86048 | tf_op jit(solution)/shard_map/ppermute | solution.py:35
  122.5 1.2 collective-permute-done.3.east
  123.7 4.8 %forward.1 = (f32[12,7,96,128]{3,2,1,0:T(8,128)S(1)}, f32[10,6,80,128]{3,2,1,0:T(8,128)S(1)}, bf16[2,512,768]{2,1,0:T(8,128)(2,1)S(1)}, bf16[2,4,128,768]{3,2,1,0:T(8,128)(2,1)S(1)}) custom-call(s32[2]{0:T(128)S(1)} %copy-done.11, s32[2,8]{1,0:T(2,128)S(1)} %copy-done.10, f32[8,6,64,128]{3,2,1,0:T(8,128)S(1)} %bitcast.14, f32[8,64,128]{2,1,0:T(8,128)S(1)} %copy-done.4, ...), custom_call_target="tpu_custom_call" | custom-call | tf_op jit(solution)/shard_map/forward/pallas_call | solution.py:249
  128.5 0.0 copy-start.2
  128.5 1.1 copy-done.2
  129.6 1.4 copy-done.5
  131.0 3.8 %collective-permute-start.4 = (bf16[2,4,128,768]{3,2,1,0:T(8,128)(2,1)S(1)}, bf16[2,4,128,768]{3,2,1,0:T(8,128)(2,1)S(1)}, u32[]{:S(2)}, u32[]{:S(2)}) collective-permute-start(bf16[2,4,128,768]{3,2,1,0:T(8,128)(2,1)S(1)} %get-tuple-element.28), channel_id=1, source_target_pairs={{0,4},{4,0},{8,12},{12,8},{16,20},{20,16},{24,28},{28,24},{1,5},{5... | collective-permute-start | bytes 4718600 | tf_op jit(solution)/shard_map/ppermute | solution.py:27
  134.8 2.0 collective-permute-start.9
  136.8 0.0 collective-permute-start.14
  136.8 0.0 collective-permute-done.17.refs_2_
  136.8 2.1 collective-permute-start.19
  138.9 25.7 %collective-permute-done.9.refs_4_ = bf16[592,1024]{1,0:T(8,128)(2,1)} collective-permute-done((bf16[592,1024]{1,0:T(8,128)(2,1)}, bf16[592,1024]{1,0:T(8,128)(2,1)}, u32[]{:S(2)}, u32[]{:S(2)}) %collective-permute-start.9) | collective-permute-done | bytes 1212448 | tf_op jit(solution)/shard_map/ppermute | solution.py:27
  164.7 3.2 %collective-permute-done.4.refs_0_ = bf16[2,4,128,768]{3,2,1,0:T(8,128)(2,1)S(1)} collective-permute-done((bf16[2,4,128,768]{3,2,1,0:T(8,128)(2,1)S(1)}, bf16[2,4,128,768]{3,2,1,0:T(8,128)(2,1)S(1)}, u32[]{:S(2)}, u32[]{:S(2)}) %collective-permute-start.4) | collective-permute-done | bytes 1572896 | tf_op jit(solution)/shard_map/ppermute | solution.py:27
  167.9 0.0 collective-permute-start.13
  167.9 22.8 %collective-permute-done.14.refs_4_ = bf16[592,1024]{1,0:T(8,128)(2,1)} collective-permute-done((bf16[592,1024]{1,0:T(8,128)(2,1)}, bf16[592,1024]{1,0:T(8,128)(2,1)}, u32[]{:S(2)}, u32[]{:S(2)}) %collective-permute-start.14) | collective-permute-done | bytes 1212448 | tf_op jit(solution)/shard_map/ppermute | solution.py:27
  190.6 0.5 collective-permute-start.18
  191.2 24.6 %collective-permute-done.19.refs_4_ = bf16[592,1024]{1,0:T(8,128)(2,1)} collective-permute-done((bf16[592,1024]{1,0:T(8,128)(2,1)}, bf16[592,1024]{1,0:T(8,128)(2,1)}, u32[]{:S(2)}, u32[]{:S(2)}) %collective-permute-start.19) | collective-permute-done | bytes 1212448 | tf_op jit(solution)/shard_map/ppermute | solution.py:27
  215.8 0.0 collective-permute-start.20
  215.8 11.4 %instrument_0.1 = (bf16[2,128,768]{2,1,0:T(8,128)(2,1)S(1)}, bf16[2,128,768]{2,1,0:T(8,128)(2,1)S(1)}) custom-call(s32[2]{0:T(128)S(1)} %copy-done.11, s32[2,8]{1,0:T(2,128)S(1)} %copy-done.10, bf16[2,512,768]{2,1,0:T(8,128)(2,1)} %copy-done.2, bf16[2,512,512]{2,1,0:T(8,128)(2,1)S(1)} %bitcast.17, bf16[2,4,128,768]{3,2,1,0:T(8,128)(2,1)} %copy-done.14, ...), custom_call_target="tpu_custom_call" | custom-call | tf_op jit(solution)/shard_map/instrument_0/pallas_call | solution.py:506
  227.2 0.0 collective-permute-done.10.refs_5_
  227.2 0.3 collective-permute-start.6
  227.6 11.9 %instrument_1.1 = (bf16[2,128,768]{2,1,0:T(8,128)(2,1)S(1)}, bf16[2,128,768]{2,1,0:T(8,128)(2,1)S(1)}) custom-call(s32[2]{0:T(128)S(1)} %copy-done.11, s32[2,8]{1,0:T(2,128)S(1)} %copy-done.10, bf16[2,512,768]{2,1,0:T(8,128)(2,1)} %copy-done.2, bf16[2,512,512]{2,1,0:T(8,128)(2,1)S(1)} %bitcast.18, bf16[2,4,128,768]{3,2,1,0:T(8,128)(2,1)} %copy-done.14, ...), custom_call_target="tpu_custom_call" | custom-call | tf_op jit(solution)/shard_map/instrument_1/pallas_call | solution.py:506
  239.5 1.8 collective-permute-start.11
  241.3 11.9 %instrument_2.1 = (bf16[2,128,768]{2,1,0:T(8,128)(2,1)S(1)}, bf16[2,128,768]{2,1,0:T(8,128)(2,1)S(1)}) custom-call(s32[2]{0:T(128)S(1)} %copy-done.11, s32[2,8]{1,0:T(2,128)S(1)} %copy-done.10, bf16[2,512,768]{2,1,0:T(8,128)(2,1)} %copy-done.2, bf16[2,512,512]{2,1,0:T(8,128)(2,1)S(1)} %bitcast.19, bf16[2,4,128,768]{3,2,1,0:T(8,128)(2,1)} %copy-done.14, ...), custom_call_target="tpu_custom_call" | custom-call | tf_op jit(solution)/shard_map/instrument_2/pallas_call | solution.py:506
  253.2 0.3 collective-permute-start.16
  253.6 11.9 %instrument_3.1 = (bf16[2,128,768]{2,1,0:T(8,128)(2,1)S(1)}, bf16[2,128,768]{2,1,0:T(8,128)(2,1)S(1)}) custom-call(s32[2]{0:T(128)S(1)} %copy-done.11, s32[2,8]{1,0:T(2,128)S(1)} %copy-done.10, bf16[2,512,768]{2,1,0:T(8,128)(2,1)} %copy-done.2, bf16[2,512,512]{2,1,0:T(8,128)(2,1)S(1)} %bitcast.20, bf16[2,4,128,768]{3,2,1,0:T(8,128)(2,1)} %copy-done.14, ...), custom_call_target="tpu_custom_call" | custom-call | tf_op jit(solution)/shard_map/instrument_3/pallas_call | solution.py:506
  265.5 1.8 collective-permute-start.21
  267.3 8.9 %collective-permute-done.21.refs_7_ = bf16[2,128,768]{2,1,0:T(8,128)(2,1)S(1)} collective-permute-done((bf16[2,128,768]{2,1,0:T(8,128)(2,1)S(1)}, bf16[2,128,768]{2,1,0:T(8,128)(2,1)S(1)}, u32[]{:S(2)}, u32[]{:S(2)}) %collective-permute-start.21) | collective-permute-done | bytes 393248 | tf_op jit(solution)/shard_map/ppermute | solution.py:27
  276.3 1.0 collect_1.1
  277.3 1.9 collective-permute-start.22
  279.2 3.6 %collective-permute-start.23 = (bf16[6,64,128]{2,1,0:T(8,128)(2,1)S(1)}, bf16[6,64,128]{2,1,0:T(8,128)(2,1)S(1)}, u32[]{:S(2)}, u32[]{:S(2)}) collective-permute-start(bf16[6,64,128]{2,1,0:T(8,128)(2,1)S(1)} %get-tuple-element.39), channel_id=1, source_target_pairs={{1,0},{2,1},{3,2},{5,4},{6,5},{7,6},{9,8},{10,9},{11,10},{13,12},{... | collective-permute-start | bytes 294920 | tf_op jit(solution)/shard_map/ppermute | solution.py:35
  282.9 1.4 collective-permute-start.24
  284.3 0.7 collective-permute-start.25
  285.0 1.0 collect_0.1.refs_7_
  285.9 0.9 collective-permute-done.24.refs_3_
  286.8 4.0 %collective-permute-done.25.refs_4_ = f32[8,6,128]{2,1,0:T(8,128)S(1)} collective-permute-done((f32[8,6,128]{2,1,0:T(8,128)S(1)}, f32[8,6,128]{2,1,0:T(8,128)S(1)}, u32[]{:S(2)}, u32[]{:S(2)}) %collective-permute-start.25) | collective-permute-done | bytes 24608 | tf_op jit(solution)/shard_map/ppermute | solution.py:35
  290.9 0.0 copy-start.7
  290.9 2.0 backward_first.1
  292.9 1.9 collective-permute-start.26
  294.9 3.6 %collective-permute-start.27 = (f32[6,64,128]{2,1,0:T(8,128)S(1)}, f32[6,64,128]{2,1,0:T(8,128)S(1)}, u32[]{:S(2)}, u32[]{:S(2)}) collective-permute-start(f32[6,64,128]{2,1,0:T(8,128)S(1)} %get-tuple-element.46), channel_id=1, source_target_pairs={{1,0},{2,1},{3,2},{5,4},{6,5},{7,6},{9,8},{10,9},{11,10},{13,12},{... | collective-permute-start | bytes 589832 | tf_op jit(solution)/shard_map/ppermute | solution.py:35
  298.5 0.1 collective-permute-start.28
  298.6 2.0 collective-permute-start.29
  300.6 1.9 collective-permute-done.28.refs_3_
  302.5 2.8 collective-permute-done.29.refs_4_
  305.3 3.3 %backward_last.1 = f32[8,6,64,128]{3,2,1,0:T(8,128)} custom-call(f32[8,6,64,128]{3,2,1,0:T(8,128)S(1)} %get-tuple-element.44.refs_0_, f32[6,64,128]{2,1,0:T(8,128)S(1)} %collective-permute-done.26.refs_1_, f32[6,64,128]{2,1,0:T(8,128)S(1)} %collective-permute-done.27.refs_2_, f32[8,6,128]{2,1,0:T(8,128)S(1)} %collective-permute-done.28.refs_3_, ...), custom_call_target="tpu_custom_call" | custom-call | tf_op jit(solution)/shard_map/backward_last/pallas_call | solution.py:380
  (47 shorter events, 0.2 us)
Async XLA Ops:
  0.7 38.1 %copy-start = (f32[8,64,6,128]{3,1,2,0:T(8,128)S(1)}, f32[8,64,6,128]{3,1,2,0:T(8,128)}, u32[]{:S(2)}) copy-start(f32[8,64,6,128]{3,1,2,0:T(8,128)} %param.9) | copy-start | bytes 4718596
  0.7 38.1 %copy-start.4 = (f32[8,64,128]{2,1,0:T(8,128)S(1)}, f32[8,64,128]{2,1,0:T(8,128)}, u32[]{:S(2)}) copy-start(f32[8,64,128]{2,1,0:T(8,128)} %kappa.1) | copy-start | bytes 786436
  38.4 6.1 %copy-start.12 = (s32[2,1,4]{2,1,0:T(1,128)S(1)}, s32[2,1,4]{2,1,0:T(1,128)}, u32[]{:S(2)}) copy-start(s32[2,1,4]{2,1,0:T(1,128)} %param.13) | copy-start | bytes 100
  38.4 55.7 %collective-permute-start.12 = (bf16[592,1024]{1,0:T(8,128)(2,1)}, bf16[592,1024]{1,0:T(8,128)(2,1)}, u32[]{:S(2)}, u32[]{:S(2)}) collective-permute-start(bf16[592,1024]{1,0:T(8,128)(2,1)} %pack.1), channel_id=1, source_target_pairs={{0,16},{4,20},{8,24},{12,28},{16,0},{20,4},{24,8},{28,12},{1,17},{... | collective-permute-start | bytes 3637256 | tf_op jit(solution)/shard_map/ppermute | solution.py:27
  39.7 54.5 %collective-permute-start.1 = (f32[2,7,64,128]{3,2,1,0:T(8,128)}, f32[2,7,64,128]{3,2,1,0:T(8,128)S(1)}, u32[]{:S(2)}, u32[]{:S(2)}) collective-permute-start(f32[2,7,64,128]{3,2,1,0:T(8,128)} %get-tuple-element.49), channel_id=1, source_target_pairs={{1,0},{2,1},{3,2},{5,4},{6,5},{7,6},{9,8},{10,9},{11,10},{13,12},{... | collective-permute-start | bytes 1376264 | tf_op jit(solution)/shard_map/ppermute | solution.py:35
  41.6 52.6 %collective-permute-start = (f32[2,7,64,128]{3,2,1,0:T(8,128)S(1)}, f32[2,7,64,128]{3,2,1,0:T(8,128)S(1)}, u32[]{:S(2)}, u32[]{:S(2)}) collective-permute-start(f32[2,7,64,128]{3,2,1,0:T(8,128)S(1)} %get-tuple-element.50), channel_id=1, source_target_pairs={{0,1},{1,2},{2,3},{4,5},{5,6},{6,7},{8,9},{9,10},{10,11},{12,13},{... | collective-permute-start | bytes 1376264 | tf_op jit(solution)/shard_map/ppermute | solution.py:35
  44.0 90.8 %collective-permute-start.7 = (bf16[592,1024]{1,0:T(8,128)(2,1)}, bf16[592,1024]{1,0:T(8,128)(2,1)}, u32[]{:S(2)}, u32[]{:S(2)}) collective-permute-start(bf16[592,1024]{1,0:T(8,128)(2,1)} %pack.1), channel_id=1, source_target_pairs={{0,8},{4,12},{8,0},{12,4},{16,24},{20,28},{24,16},{28,20},{1,9},{5... | collective-permute-start | bytes 3637256 | tf_op jit(solution)/shard_map/ppermute | solution.py:27
  78.8 58.0 %collective-permute-start.5 = (bf16[2,4,128,512]{3,2,1,0:T(8,128)(2,1)}, bf16[2,4,128,512]{3,2,1,0:T(8,128)(2,1)S(1)}, u32[]{:S(2)}, u32[]{:S(2)}) collective-permute-start(bf16[2,4,128,512]{3,2,1,0:T(8,128)(2,1)} %pick_radiances.1), channel_id=1, source_target_pairs={{0,4},{4,0},{8,12},{12,8},{16,20},{20,16},{24,28},{28,24},{1,5},{5... | collective-permute-start | bytes 3145736 | tf_op jit(solution)/shard_map/ppermute | solution.py:27
  94.1 42.8 %collective-permute-start.17 = (bf16[592,1024]{1,0:T(8,128)(2,1)}, bf16[592,1024]{1,0:T(8,128)(2,1)}, u32[]{:S(2)}, u32[]{:S(2)}) collective-permute-start(bf16[592,1024]{1,0:T(8,128)(2,1)} %collective-permute-done.12.refs_2_), channel_id=1, source_target_pairs={{0,8},{4,12},{8,0},{12,4},{16,24},{20,28},{24,16},{28,20},{1,9},{5... | collective-permute-start | bytes 3637256 | tf_op jit(solution)/shard_map/ppermute | solution.py:27
  94.1 29.6 %copy-start.10 = (s32[2,8]{1,0:T(2,128)S(1)}, s32[2,8]{1,0:T(2,128)}, u32[]{:S(2)}) copy-start(s32[2,8]{1,0:T(2,128)} %select_reduce_fusion.table) | copy-start | bytes 196
  94.1 29.6 %copy-start.11 = (s32[2]{0:T(128)S(1)}, s32[2]{0:T(128)}, u32[]{:S(2)}) copy-start(s32[2]{0:T(128)} %pad_add_fusion.pos) | copy-start | bytes 28
  94.2 0.8 copy-start.8
  95.0 28.7 %copy-start.9 = (f32[2,7,64,128]{3,2,1,0:T(8,128)S(1)}, f32[2,7,64,128]{3,2,1,0:T(8,128)}, u32[]{:S(2)}) copy-start(f32[2,7,64,128]{3,2,1,0:T(8,128)} %copy-done.8) | copy-start | bytes 1376260
  95.0 27.5 %collective-permute-start.2 = (f32[12,7,2,128]{3,2,1,0:T(2,128)S(1)}, f32[12,7,2,128]{3,2,1,0:T(2,128)S(1)}, u32[]{:S(2)}, u32[]{:S(2)}) collective-permute-start(f32[12,7,2,128]{3,2,1,0:T(2,128)S(1)} %pad_maximum_fusion.1), channel_id=1, source_target_pairs={{0,4},{4,8},{8,12},{12,16},{16,20},{20,24},{24,28},{28,0},{1,5},{5... | collective-permute-start | bytes 258056 | tf_op jit(solution)/shard_map/ppermute | solution.py:35
  96.0 119.8 %copy-start.1 = (bf16[2,8,64,512]{3,2,1,0:T(8,128)(2,1)S(1)}, bf16[2,8,64,512]{3,2,1,0:T(8,128)(2,1)}, u32[]{:S(2)}) copy-start(bf16[2,8,64,512]{3,2,1,0:T(8,128)(2,1)} %param.12) | copy-start | bytes 3145732
  96.0 119.8 %copy-start.3 = (bf16[1,1024,512]{2,1,0:T(8,128)(2,1)S(1)}, bf16[1,1024,512]{2,1,0:T(8,128)(2,1)}, u32[]{:S(2)}) copy-start(bf16[1,1024,512]{2,1,0:T(8,128)(2,1)} %param.16) | copy-start | bytes 3145732
  96.0 119.8 %copy-start.13 = (f32[1,512]{1,0:T(1,128)S(1)}, f32[1,512]{1,0:T(1,128)}, u32[]{:S(2)}) copy-start(f32[1,512]{1,0:T(1,128)} %scale.1) | copy-start | bytes 6148
  96.0 27.7 %collective-permute-start.3 = (f32[12,7,2,128]{3,2,1,0:T(2,128)S(1)}, f32[12,7,2,128]{3,2,1,0:T(2,128)S(1)}, u32[]{:S(2)}, u32[]{:S(2)}) collective-permute-start(f32[12,7,2,128]{3,2,1,0:T(2,128)S(1)} %fusion.3), channel_id=1, source_target_pairs={{0,28},{4,0},{8,4},{12,8},{16,12},{20,16},{24,20},{28,24},{1,29},{... | collective-permute-start | bytes 258056 | tf_op jit(solution)/shard_map/ppermute | solution.py:35
  128.5 1.1 copy-start.2
  129.6 1.4 copy-start.5
  131.0 36.8 %collective-permute-start.4 = (bf16[2,4,128,768]{3,2,1,0:T(8,128)(2,1)S(1)}, bf16[2,4,128,768]{3,2,1,0:T(8,128)(2,1)S(1)}, u32[]{:S(2)}, u32[]{:S(2)}) collective-permute-start(bf16[2,4,128,768]{3,2,1,0:T(8,128)(2,1)S(1)} %get-tuple-element.28), channel_id=1, source_target_pairs={{0,4},{4,0},{8,12},{12,8},{16,20},{20,16},{24,28},{28,24},{1,5},{5... | collective-permute-start | bytes 4718600 | tf_op jit(solution)/shard_map/ppermute | solution.py:27
  134.8 29.9 %collective-permute-start.9 = (bf16[592,1024]{1,0:T(8,128)(2,1)}, bf16[592,1024]{1,0:T(8,128)(2,1)}, u32[]{:S(2)}, u32[]{:S(2)}) collective-permute-start(bf16[592,1024]{1,0:T(8,128)(2,1)} %collective-permute-done.7.refs_2_), channel_id=1, source_target_pairs={{0,2},{1,3},{2,0},{3,1},{4,6},{5,7},{6,4},{7,5},{8,10},{9,11},{10,... | collective-permute-start | bytes 3637256 | tf_op jit(solution)/shard_map/ppermute | solution.py:27
  136.8 53.8 %collective-permute-start.14 = (bf16[592,1024]{1,0:T(8,128)(2,1)}, bf16[592,1024]{1,0:T(8,128)(2,1)}, u32[]{:S(2)}, u32[]{:S(2)}) collective-permute-start(bf16[592,1024]{1,0:T(8,128)(2,1)} %collective-permute-done.12.refs_2_), channel_id=1, source_target_pairs={{0,2},{1,3},{2,0},{3,1},{4,6},{5,7},{6,4},{7,5},{8,10},{9,11},{10,... | collective-permute-start | bytes 3637256 | tf_op jit(solution)/shard_map/ppermute | solution.py:27
  136.8 53.8 %collective-permute-start.8 = (bf16[592,1024]{1,0:T(8,128)(2,1)}, bf16[592,1024]{1,0:T(8,128)(2,1)S(1)}, u32[]{:S(2)}, u32[]{:S(2)}) collective-permute-start(bf16[592,1024]{1,0:T(8,128)(2,1)} %collective-permute-done.7.refs_2_), channel_id=1, source_target_pairs={{0,1},{1,0},{2,3},{3,2},{4,5},{5,4},{6,7},{7,6},{8,9},{9,8},{10,11... | collective-permute-start | bytes 3637256 | tf_op jit(solution)/shard_map/ppermute | solution.py:27
  136.8 78.9 %collective-permute-start.19 = (bf16[592,1024]{1,0:T(8,128)(2,1)}, bf16[592,1024]{1,0:T(8,128)(2,1)}, u32[]{:S(2)}, u32[]{:S(2)}) collective-permute-start(bf16[592,1024]{1,0:T(8,128)(2,1)} %collective-permute-done.17.refs_2_), channel_id=1, source_target_pairs={{0,2},{1,3},{2,0},{3,1},{4,6},{5,7},{6,4},{7,5},{8,10},{9,11},{10,... | collective-permute-start | bytes 3637256 | tf_op jit(solution)/shard_map/ppermute | solution.py:27
  164.7 62.6 %collective-permute-start.10 = (bf16[592,1024]{1,0:T(8,128)(2,1)}, bf16[592,1024]{1,0:T(8,128)(2,1)}, u32[]{:S(2)}, u32[]{:S(2)}) collective-permute-start(bf16[592,1024]{1,0:T(8,128)(2,1)} %collective-permute-done.9.refs_4_), channel_id=1, source_target_pairs={{0,1},{1,0},{2,3},{3,2},{4,5},{5,4},{6,7},{7,6},{8,9},{9,8},{10,11... | collective-permute-start | bytes 3637256 | tf_op jit(solution)/shard_map/ppermute | solution.py:27
  167.9 47.9 %copy-start.14 = (bf16[2,4,128,768]{3,2,1,0:T(8,128)(2,1)}, bf16[2,4,128,768]{3,2,1,0:T(8,128)(2,1)S(1)}, u32[]{:S(2)}) copy-start(bf16[2,4,128,768]{3,2,1,0:T(8,128)(2,1)S(1)} %collective-permute-done.4.refs_0_) | copy-start | bytes 4718596
  167.9 71.6 %collective-permute-start.13 = (bf16[592,1024]{1,0:T(8,128)(2,1)}, bf16[592,1024]{1,0:T(8,128)(2,1)}, u32[]{:S(2)}, u32[]{:S(2)}) collective-permute-start(bf16[592,1024]{1,0:T(8,128)(2,1)} %collective-permute-done.12.refs_2_), channel_id=1, source_target_pairs={{0,1},{1,0},{2,3},{3,2},{4,5},{5,4},{6,7},{7,6},{8,9},{9,8},{10,11... | collective-permute-start | bytes 3637256 | tf_op jit(solution)/shard_map/ppermute | solution.py:27
  190.6 50.7 %collective-permute-start.15 = (bf16[592,1024]{1,0:T(8,128)(2,1)}, bf16[592,1024]{1,0:T(8,128)(2,1)}, u32[]{:S(2)}, u32[]{:S(2)}) collective-permute-start(bf16[592,1024]{1,0:T(8,128)(2,1)} %collective-permute-done.14.refs_4_), channel_id=1, source_target_pairs={{0,1},{1,0},{2,3},{3,2},{4,5},{5,4},{6,7},{7,6},{8,9},{9,8},{10,11... | collective-permute-start | bytes 3637256 | tf_op jit(solution)/shard_map/ppermute | solution.py:27
  190.6 25.1 %copy-start.15 = (bf16[592,1024]{1,0:T(8,128)(2,1)}, bf16[592,1024]{1,0:T(8,128)(2,1)S(1)}, u32[]{:S(2)}) copy-start(bf16[592,1024]{1,0:T(8,128)(2,1)S(1)} %collective-permute-done.8.refs_3_) | copy-start | bytes 3637252
  190.6 62.9 %collective-permute-start.18 = (bf16[592,1024]{1,0:T(8,128)(2,1)}, bf16[592,1024]{1,0:T(8,128)(2,1)}, u32[]{:S(2)}, u32[]{:S(2)}) collective-permute-start(bf16[592,1024]{1,0:T(8,128)(2,1)} %collective-permute-done.17.refs_2_), channel_id=1, source_target_pairs={{0,1},{1,0},{2,3},{3,2},{4,5},{5,4},{6,7},{7,6},{8,9},{9,8},{10,11... | collective-permute-start | bytes 3637256 | tf_op jit(solution)/shard_map/ppermute | solution.py:27
  215.8 37.8 %collective-permute-start.20 = (bf16[592,1024]{1,0:T(8,128)(2,1)}, bf16[592,1024]{1,0:T(8,128)(2,1)}, u32[]{:S(2)}, u32[]{:S(2)}) collective-permute-start(bf16[592,1024]{1,0:T(8,128)(2,1)} %collective-permute-done.19.refs_4_), channel_id=1, source_target_pairs={{0,1},{1,0},{2,3},{3,2},{4,5},{5,4},{6,7},{7,6},{8,9},{9,8},{10,11... | collective-permute-start | bytes 3637256 | tf_op jit(solution)/shard_map/ppermute | solution.py:27
  227.2 40.1 %collective-permute-start.6 = (bf16[2,128,768]{2,1,0:T(8,128)(2,1)S(1)}, bf16[2,128,768]{2,1,0:T(8,128)(2,1)S(1)}, u32[]{:S(2)}, u32[]{:S(2)}) collective-permute-start(bf16[2,128,768]{2,1,0:T(8,128)(2,1)S(1)} %get-tuple-element.30), channel_id=1, source_target_pairs={{0,4},{4,0},{8,12},{12,8},{16,20},{20,16},{24,28},{28,24},{1,5},{5... | collective-permute-start | bytes 1179656 | tf_op jit(solution)/shard_map/ppermute | solution.py:27
  239.5 27.8 %collective-permute-start.11 = (bf16[2,128,768]{2,1,0:T(8,128)(2,1)S(1)}, bf16[2,128,768]{2,1,0:T(8,128)(2,1)S(1)}, u32[]{:S(2)}, u32[]{:S(2)}) collective-permute-start(bf16[2,128,768]{2,1,0:T(8,128)(2,1)S(1)} %get-tuple-element.32), channel_id=1, source_target_pairs={{0,4},{4,0},{8,12},{12,8},{16,20},{20,16},{24,28},{28,24},{1,5},{5... | collective-permute-start | bytes 1179656 | tf_op jit(solution)/shard_map/ppermute | solution.py:27
  253.2 14.1 %collective-permute-start.16 = (bf16[2,128,768]{2,1,0:T(8,128)(2,1)S(1)}, bf16[2,128,768]{2,1,0:T(8,128)(2,1)S(1)}, u32[]{:S(2)}, u32[]{:S(2)}) collective-permute-start(bf16[2,128,768]{2,1,0:T(8,128)(2,1)S(1)} %get-tuple-element.34), channel_id=1, source_target_pairs={{0,4},{4,0},{8,12},{12,8},{16,20},{20,16},{24,28},{28,24},{1,5},{5... | collective-permute-start | bytes 1179656 | tf_op jit(solution)/shard_map/ppermute | solution.py:27
  265.5 10.8 %collective-permute-start.21 = (bf16[2,128,768]{2,1,0:T(8,128)(2,1)S(1)}, bf16[2,128,768]{2,1,0:T(8,128)(2,1)S(1)}, u32[]{:S(2)}, u32[]{:S(2)}) collective-permute-start(bf16[2,128,768]{2,1,0:T(8,128)(2,1)S(1)} %get-tuple-element.36), channel_id=1, source_target_pairs={{0,4},{4,0},{8,12},{12,8},{16,20},{20,16},{24,28},{28,24},{1,5},{5... | collective-permute-start | bytes 1179656 | tf_op jit(solution)/shard_map/ppermute | solution.py:27
  277.3 13.6 %collective-permute-start.22 = (bf16[6,64,128]{2,1,0:T(8,128)(2,1)S(1)}, bf16[6,64,128]{2,1,0:T(8,128)(2,1)S(1)}, u32[]{:S(2)}, u32[]{:S(2)}) collective-permute-start(bf16[6,64,128]{2,1,0:T(8,128)(2,1)S(1)} %get-tuple-element.38), channel_id=1, source_target_pairs={{0,1},{1,2},{2,3},{4,5},{5,6},{6,7},{8,9},{9,10},{10,11},{12,13},{... | collective-permute-start | bytes 294920 | tf_op jit(solution)/shard_map/ppermute | solution.py:35
  279.2 11.7 %collective-permute-start.23 = (bf16[6,64,128]{2,1,0:T(8,128)(2,1)S(1)}, bf16[6,64,128]{2,1,0:T(8,128)(2,1)S(1)}, u32[]{:S(2)}, u32[]{:S(2)}) collective-permute-start(bf16[6,64,128]{2,1,0:T(8,128)(2,1)S(1)} %get-tuple-element.39), channel_id=1, source_target_pairs={{1,0},{2,1},{3,2},{5,4},{6,5},{7,6},{9,8},{10,9},{11,10},{13,12},{... | collective-permute-start | bytes 294920 | tf_op jit(solution)/shard_map/ppermute | solution.py:35
  282.9 4.0 %collective-permute-start.24 = (f32[8,6,128]{2,1,0:T(8,128)S(1)}, f32[8,6,128]{2,1,0:T(8,128)S(1)}, u32[]{:S(2)}, u32[]{:S(2)}) collective-permute-start(f32[8,6,128]{2,1,0:T(8,128)S(1)} %get-tuple-element.40), channel_id=1, source_target_pairs={{0,4},{4,8},{8,12},{12,16},{16,20},{20,24},{24,28},{28,0},{1,5},{5... | collective-permute-start | bytes 73736 | tf_op jit(solution)/shard_map/ppermute | solution.py:35
  284.3 6.6 %copy-start.6 = (f32[10,6,80,128]{3,2,1,0:T(8,128)S(1)}, f32[10,6,80,128]{3,2,1,0:T(8,128)}, u32[]{:S(2)}) copy-start(f32[10,6,80,128]{3,2,1,0:T(8,128)} %copy-done.5) | copy-start | bytes 7372804
  284.3 6.6 %collective-permute-start.25 = (f32[8,6,128]{2,1,0:T(8,128)S(1)}, f32[8,6,128]{2,1,0:T(8,128)S(1)}, u32[]{:S(2)}, u32[]{:S(2)}) collective-permute-start(f32[8,6,128]{2,1,0:T(8,128)S(1)} %get-tuple-element.41), channel_id=1, source_target_pairs={{0,28},{4,0},{8,4},{12,8},{16,12},{20,16},{24,20},{28,24},{1,29},{... | collective-permute-start | bytes 73736 | tf_op jit(solution)/shard_map/ppermute | solution.py:35
  290.9 14.4 %copy-start.7 = (f32[8,64,6,128]{3,1,2,0:T(8,128)S(1)}, f32[8,64,6,128]{3,1,2,0:T(8,128)}, u32[]{:S(2)}) copy-start(f32[8,64,6,128]{3,1,2,0:T(8,128)} %param.10) | copy-start | bytes 4718596
  292.9 12.3 %collective-permute-start.26 = (f32[6,64,128]{2,1,0:T(8,128)S(1)}, f32[6,64,128]{2,1,0:T(8,128)S(1)}, u32[]{:S(2)}, u32[]{:S(2)}) collective-permute-start(f32[6,64,128]{2,1,0:T(8,128)S(1)} %get-tuple-element.45), channel_id=1, source_target_pairs={{0,1},{1,2},{2,3},{4,5},{5,6},{6,7},{8,9},{9,10},{10,11},{12,13},{... | collective-permute-start | bytes 589832 | tf_op jit(solution)/shard_map/ppermute | solution.py:35
  294.9 10.4 %collective-permute-start.27 = (f32[6,64,128]{2,1,0:T(8,128)S(1)}, f32[6,64,128]{2,1,0:T(8,128)S(1)}, u32[]{:S(2)}, u32[]{:S(2)}) collective-permute-start(f32[6,64,128]{2,1,0:T(8,128)S(1)} %get-tuple-element.46), channel_id=1, source_target_pairs={{1,0},{2,1},{3,2},{5,4},{6,5},{7,6},{9,8},{10,9},{11,10},{13,12},{... | collective-permute-start | bytes 589832 | tf_op jit(solution)/shard_map/ppermute | solution.py:35
  298.5 4.0 %collective-permute-start.28 = (f32[8,6,128]{2,1,0:T(8,128)S(1)}, f32[8,6,128]{2,1,0:T(8,128)S(1)}, u32[]{:S(2)}, u32[]{:S(2)}) collective-permute-start(f32[8,6,128]{2,1,0:T(8,128)S(1)} %get-tuple-element.47), channel_id=1, source_target_pairs={{0,4},{4,8},{8,12},{12,16},{16,20},{20,24},{24,28},{28,0},{1,5},{5... | collective-permute-start | bytes 73736 | tf_op jit(solution)/shard_map/ppermute | solution.py:35
  298.6 6.7 %collective-permute-start.29 = (f32[8,6,128]{2,1,0:T(8,128)S(1)}, f32[8,6,128]{2,1,0:T(8,128)S(1)}, u32[]{:S(2)}, u32[]{:S(2)}) collective-permute-start(f32[8,6,128]{2,1,0:T(8,128)S(1)} %get-tuple-element.48), channel_id=1, source_target_pairs={{0,28},{4,0},{8,4},{12,8},{16,12},{20,16},{24,20},{28,24},{1,29},{... | collective-permute-start | bytes 73736 | tf_op jit(solution)/shard_map/ppermute | solution.py:35
where the time goes:
time: 309 us
  waiting for transfers between devices  136 us (44%)
  Pallas kernels  131 us (42%)
  starting transfers between devices  35.9 us (12%)
  local copies, waits for them, and re-layouts  3.41 us (1%)
    ppermute x18, waiting for transfers between devices, exchange(): return lax.ppermute(array, axis, [(i, i ^ mask) for i in range(count)])  99.9 us
    pallas_call x4, Pallas kernels, instrument(): pl.pallas_call(functools.partial(instrument_kernel, group, served, n_lat)...  47.1 us
    pallas_call x1, Pallas kernels, pack_weights(): pl.pallas_call(pack_kernel, out_shape=jax.ShapeDtypeStruct((rows, width),...  37.7 us
    ppermute x12, waiting for transfers between devices, shifted(): return lax.ppermute(array, axis, pairs)  36.1 us
    pallas_call x1, Pallas kernels, send_radiances(): pl.pallas_call(functools.partial(radiance_kernel, group), out_shape=[shap...  33.6 us
    ppermute x12, starting transfers between devices, shifted(): return lax.ppermute(array, axis, pairs)  21.7 us
    ppermute x18, starting transfers between devices, exchange(): return lax.ppermute(array, axis, [(i, i ^ mask) for i in range(count)])  14.2 us
  transfers between devices with their start and end apart: 30, of which 12 were waited for; matrix products, arithmetic and copies ran while one was open for 1% of the time, Pallas kernels for 28%

commit v1 on v0

--- a/solution.py
+++ b/solution.py
@@ -11,6 +11,7 @@
 SERVED = 4
 EDGE = 16
 SIDE = 8
+TAIL = 16
 ANY = pl.BlockSpec(memory_space=pl.ANY)
 SMEM = pl.BlockSpec(memory_space=pltpu.SMEM)
 VMEM = pl.BlockSpec(memory_space=pltpu.VMEM)
@@ -42,7 +43,7 @@
         bit //= 2
 
 
-def pack_kernel(pos, w1, w2, w3, scale, out, tail, sems):
+def pack_kernel(pos, w1, w2, w3, scale, out, sems):
     lat = pos[1]
     width = out.shape[1]
     parts = width // w3.shape[1]
@@ -68,19 +69,17 @@
     rest = whole - high
     middle = rest.astype(BF16).astype(F32)
     low = rest - middle
-    tail[...] = jnp.zeros_like(tail)
-    rows = lax.broadcasted_iota(jnp.int32, (tail.shape[0], scale.shape[1]), 0)
+    tail = slice(r1 + r2 + piece, out.shape[0])
+    rows = lax.broadcasted_iota(jnp.int32, (TAIL, scale.shape[1]), 0)
     stacked = jnp.where(rows == 0, high, jnp.where(rows == 1, middle, low))
-    tail[:, 0 : scale.shape[1]] = jnp.where(rows < 3, stacked, 0.0).astype(BF16)
-    last = pltpu.make_async_copy(tail, out.at[pl.ds(r1 + r2 + piece, tail.shape[0])], sems.at[2 + parts])
-    last.start()
+    out[tail] = jnp.zeros((TAIL, width), BF16)
+    out[tail, 0 : scale.shape[1]] = jnp.where(rows < 3, stacked, 0.0).astype(BF16)
     for copy in copies:
         copy.wait()
-    last.wait()
 
 
 def pos_lat(w1, w2, w3, out):
-    body = out.shape[0] - 16
+    body = out.shape[0] - TAIL
     return (w1.shape[0] + w2.shape[0] + w3.shape[0] * w3.shape[1] // out.shape[1]) // body
 
 
@@ -88,22 +87,26 @@
     w1, w2, w3, scale = weights
     width = w1.shape[1]
     parts = width // w3.shape[1]
-    rows = (w1.shape[0] + w2.shape[0] + w3.shape[0] // parts) // n_lat + 16
+    rows = (w1.shape[0] + w2.shape[0] + w3.shape[0] // parts) // n_lat + TAIL
     return pl.pallas_call(
         pack_kernel,
         out_shape=jax.ShapeDtypeStruct((rows, width), BF16),
         in_specs=[SMEM, ANY, ANY, ANY, VMEM],
-        out_specs=ANY,
-        scratch_shapes=[pltpu.VMEM((16, width), BF16), pltpu.SemaphoreType.DMA((3 + parts,))],
+        out_specs=VMEM,
+        scratch_shapes=[pltpu.SemaphoreType.DMA((2 + parts,))],
         name="pack",
     )(pos, w1, w2, w3, scale)
 
 
 def spread_weights(packed, group, n_lon, n_lat):
     found = {0: packed}
-    for bit in bits_down(n_lon // group):
-        for near in list(found):
-            found[near | bit] = exchange(found[near], "lon", bit * group)
+    bits = sorted(bits_down(n_lon // group))
+    for bit in bits:
+        found[bit] = exchange(packed, "lon", bit * group)
+    for far in range(n_lon // group):
+        if far not in found:
+            bottom = far & -far
+            found[far] = exchange(found[far ^ bottom], "lon", bottom * group)
     gathered = {}
     for served, part in found.items():
         if served == 0:
@@ -145,7 +148,7 @@
         functools.partial(radiance_kernel, group),
         out_shape=[shape] * (group - 1),
         in_specs=[SMEM, SMEM, ANY],
-        out_specs=[ANY] * (group - 1),
+        out_specs=[VMEM] * (group - 1),
         scratch_shapes=[pltpu.SemaphoreType.DMA(((group - 1) * slots * served,))],
         name="pick_radiances",
     )(pos, table, radiances)
@@ -525,6 +528,11 @@
             pltpu.SemaphoreType.DMA((4 if own else n_lat * (2 + parts) + 1,)),
         ],
         compiler_params=params(50),
+        cost_estimate=pl.CostEstimate(
+            flops=4 * lines * (cin * h1 + h1 * h2 + h2 * ch),
+            transcendentals=lines * (h1 + h2),
+            bytes_accessed=2 * (cin * h1 + h1 * h2 + h2 * ch + lines * (2 * cin + ch)),
+        ),
         name=f"instrument_{served}",
     )(pos, table, columns, radiances, *got_columns, *got_radiances, *weights)
 

time: 309 us -> 253 us (0.82)
  Pallas kernels: 131 us -> 68.6 us
  waiting for transfers between devices: 136 us -> 140 us
    pallas_call x1, Pallas kernels: 37.7 us -> 3.1 us  [pack_weights(): pl.pallas_call(pack_kernel, out_shape=jax.ShapeDtypeStruct((rows, width),...]
    pallas_call x1, Pallas kernels: 33.6 us -> 3.04 us  [send_radiances(): pl.pallas_call(functools.partial(radiance_kernel, group), out_shape=[shap...]
    ppermute x18, waiting for transfers between devices: 99.9 us -> 104 us  [exchange(): return lax.ppermute(array, axis, [(i, i ^ mask) for i in range(count)])]
  transfers between devices with their start and end apart: 30 -> 30, of which waited for: 12 -> 10; matrix products, arithmetic and copies ran while one was open for 1% -> 1% of each run, Pallas kernels for 28% -> 23%
where the time goes in v1:
time: 253 us; the launch traced here: 252 us
  waiting for transfers between devices  140 us (55%)
  Pallas kernels  68.6 us (27%)
  starting transfers between devices  35 us (14%)
  local copies, waits for them, and re-layouts  6.14 us (2%)
    ppermute x18, waiting for transfers between devices, exchange(): return lax.ppermute(array, axis, [(i, i ^ mask) for i in range(count)])  104 us
    pallas_call x4, Pallas kernels, instrument(): pl.pallas_call(functools.partial(instrument_kernel, group, served, n_lat)...  49.4 us
    ppermute x12, waiting for transfers between devices, shifted(): return lax.ppermute(array, axis, pairs)  35.9 us
    ppermute x12, starting transfers between devices, shifted(): return lax.ppermute(array, axis, pairs)  23.5 us
    ppermute x18, starting transfers between devices, exchange(): return lax.ppermute(array, axis, [(i, i ^ mask) for i in range(count)])  11.5 us
    unnamed x36, local copies, waits for them, and re-layouts  6.11 us
  transfers between devices with their start and end apart: 30, of which 10 were waited for; matrix products, arithmetic and copies ran while one was open for 1% of the time, Pallas kernels for 23%

profile of v1, /device:TPU:30, one launch (start us, length us, event | category | flops | bytes accessed | tf_op | source)
XLA Modules:
  0.0 252.2 jit_solution(15377681818783059183)
XLA Ops:
  0.0 0.6 pad_add_fusion.pos
  0.6 3.1 %pack.1 = bf16[592,1024]{1,0:T(8,128)(2,1)} custom-call(s32[2]{0:T(128)} %pad_add_fusion.pos, bf16[768,1024]{1,0:T(8,128)(2,1)} %bitcast.32, bf16[1024,1024]{1,0:T(8,128)(2,1)} %bitcast.30, bf16[1024,512]{1,0:T(8,128)(2,1)} %bitcast.25, f32[1,512]{1,0:T(1,128)} %scale.1), custom_call_target="tpu_custom_call" | custom-call | tf_op jit(solution)/shard_map/pack/pallas_call | solution.py:91
  3.7 0.0 copy-start.9
  3.7 0.4 collective-permute-start.12
  4.1 0.4 collective-permute-start.7
  4.6 0.9 fusion.1
  5.4 1.9 collective-permute-start.1
  7.3 2.4 collective-permute-start
  9.8 0.6 select_reduce_fusion.table
  10.4 3.0 %pick_radiances.1 = bf16[2,4,128,512]{3,2,1,0:T(8,128)(2,1)} custom-call(s32[2]{0:T(128)} %pad_add_fusion.pos, s32[2,8]{1,0:T(2,128)} %select_reduce_fusion.table, bf16[2,512,512]{2,1,0:T(8,128)(2,1)} %bitcast.20), custom_call_target="tpu_custom_call" | custom-call | tf_op jit(solution)/shard_map/pick_radiances/pallas_call | solution.py:147
  13.5 0.6 collective-permute-start.5
  14.1 45.2 %collective-permute-done.12.refs_2_ = bf16[592,1024]{1,0:T(8,128)(2,1)} collective-permute-done((bf16[592,1024]{1,0:T(8,128)(2,1)}, bf16[592,1024]{1,0:T(8,128)(2,1)}, u32[]{:S(2)}, u32[]{:S(2)}) %collective-permute-start.12) | collective-permute-done | bytes 1212448 | tf_op jit(solution)/shard_map/ppermute | solution.py:28
  59.3 0.8 copy-done.6
  60.1 1.0 collective-permute-start.2
  61.1 0.0 collective-permute-done.7.refs_2_
  61.1 0.5 collective-permute-start.9
  61.7 0.0 copy-start.3
  61.7 0.0 copy-start.11
  61.7 1.1 collective-permute-start.3
  62.9 24.9 %collective-permute-done.2.west = f32[12,7,2,128]{3,2,1,0:T(2,128)S(1)} collective-permute-done((f32[12,7,2,128]{3,2,1,0:T(2,128)S(1)}, f32[12,7,2,128]{3,2,1,0:T(2,128)S(1)}, u32[]{:S(2)}, u32[]{:S(2)}) %collective-permute-start.2) | collective-permute-done | bytes 86048 | tf_op jit(solution)/shard_map/ppermute | solution.py:36
  87.7 1.2 collective-permute-done.3.east
  89.0 4.9 %forward.1 = (f32[12,7,96,128]{3,2,1,0:T(8,128)S(1)}, f32[10,6,80,128]{3,2,1,0:T(8,128)S(1)}, bf16[2,512,768]{2,1,0:T(8,128)(2,1)S(1)}, bf16[2,4,128,768]{3,2,1,0:T(8,128)(2,1)S(1)}) custom-call(s32[2]{0:T(128)S(1)} %copy-done.8, s32[2,8]{1,0:T(2,128)S(1)} %copy-done.10, f32[8,6,64,128]{3,2,1,0:T(8,128)S(1)} %bitcast.14, f32[8,64,128]{2,1,0:T(8,128)S(1)} %copy-done.1, ...), custom_call_target="tpu_custom_call" | custom-call | tf_op jit(solution)/shard_map/forward/pallas_call | solution.py:252
  93.8 0.0 copy-start.12
  93.8 1.1 copy-done.12
  95.0 2.4 collective-permute-start.4
  97.4 0.5 collective-permute-start.14
  97.9 0.0 collective-permute-done.5.refs_1_
  98.0 1.0 copy-done.13
  98.9 0.0 collective-permute-done.17.refs_2_
  98.9 1.5 collective-permute-start.19
  100.4 0.2 collective-permute-start.10
  100.7 30.2 %collective-permute-done.4.refs_0_ = bf16[2,4,128,768]{3,2,1,0:T(8,128)(2,1)S(1)} collective-permute-done((bf16[2,4,128,768]{3,2,1,0:T(8,128)(2,1)S(1)}, bf16[2,4,128,768]{3,2,1,0:T(8,128)(2,1)S(1)}, u32[]{:S(2)}, u32[]{:S(2)}) %collective-permute-start.4) | collective-permute-done | bytes 1572896 | tf_op jit(solution)/shard_map/ppermute | solution.py:28
  130.8 0.5 collective-permute-start.15
  131.4 0.1 collective-permute-start.18
  131.4 19.4 %collective-permute-done.19.refs_4_ = bf16[592,1024]{1,0:T(8,128)(2,1)} collective-permute-done((bf16[592,1024]{1,0:T(8,128)(2,1)}, bf16[592,1024]{1,0:T(8,128)(2,1)}, u32[]{:S(2)}, u32[]{:S(2)}) %collective-permute-start.19) | collective-permute-done | bytes 1212448 | tf_op jit(solution)/shard_map/ppermute | solution.py:28
  150.9 0.0 copy-start.5
  150.9 1.2 copy-done.5
  152.1 1.2 copy-done.14
  153.4 12.2 %instrument_0.1 = (bf16[2,128,768]{2,1,0:T(8,128)(2,1)S(1)}, bf16[2,128,768]{2,1,0:T(8,128)(2,1)}) custom-call(s32[2]{0:T(128)S(1)} %copy-done.8, s32[2,8]{1,0:T(2,128)S(1)} %copy-done.10, bf16[2,512,768]{2,1,0:T(8,128)(2,1)} %copy-done.12, bf16[2,512,512]{2,1,0:T(8,128)(2,1)S(1)} %bitcast.21, bf16[2,4,128,768]{3,2,1,0:T(8,128)(2,1)} %copy-done.16, ...), custom_call_target="tpu_custom_call" | custom-call | flops 4831838208 | bytes 6815744 | tf_op jit(solution)/shard_map/instrument_0/pallas_call | solution.py:509
  165.6 0.3 collective-permute-start.6
  165.9 12.7 %instrument_1.1 = (bf16[2,128,768]{2,1,0:T(8,128)(2,1)S(1)}, bf16[2,128,768]{2,1,0:T(8,128)(2,1)}) custom-call(s32[2]{0:T(128)S(1)} %copy-done.8, s32[2,8]{1,0:T(2,128)S(1)} %copy-done.10, bf16[2,512,768]{2,1,0:T(8,128)(2,1)} %copy-done.12, bf16[2,512,512]{2,1,0:T(8,128)(2,1)S(1)} %bitcast.22, bf16[2,4,128,768]{3,2,1,0:T(8,128)(2,1)} %copy-done.16, ...), custom_call_target="tpu_custom_call" | custom-call | flops 4831838208 | bytes 6815744 | tf_op jit(solution)/shard_map/instrument_1/pallas_call | solution.py:509
  178.6 1.8 collective-permute-start.11
  180.4 12.7 %instrument_2.1 = (bf16[2,128,768]{2,1,0:T(8,128)(2,1)S(1)}, bf16[2,128,768]{2,1,0:T(8,128)(2,1)}) custom-call(s32[2]{0:T(128)S(1)} %copy-done.8, s32[2,8]{1,0:T(2,128)S(1)} %copy-done.10, bf16[2,512,768]{2,1,0:T(8,128)(2,1)} %copy-done.12, bf16[2,512,512]{2,1,0:T(8,128)(2,1)S(1)} %bitcast.23, bf16[2,4,128,768]{3,2,1,0:T(8,128)(2,1)} %copy-done.16, ...), custom_call_target="tpu_custom_call" | custom-call | flops 4831838208 | bytes 6815744 | tf_op jit(solution)/shard_map/instrument_2/pallas_call | solution.py:509
  193.1 0.3 collective-permute-start.16
  193.4 11.9 %instrument_3.1 = (bf16[2,128,768]{2,1,0:T(8,128)(2,1)S(1)}, bf16[2,128,768]{2,1,0:T(8,128)(2,1)S(1)}) custom-call(s32[2]{0:T(128)S(1)} %copy-done.8, s32[2,8]{1,0:T(2,128)S(1)} %copy-done.10, bf16[2,512,768]{2,1,0:T(8,128)(2,1)} %copy-done.12, bf16[2,512,512]{2,1,0:T(8,128)(2,1)S(1)} %bitcast.24, bf16[2,4,128,768]{3,2,1,0:T(8,128)(2,1)} %copy-done.16, ...), custom_call_target="tpu_custom_call" | custom-call | flops 4831838208 | bytes 6815744 | tf_op jit(solution)/shard_map/instrument_3/pallas_call | solution.py:509
  205.3 0.0 copy-start.15
  205.3 0.7 copy-done.15
  206.1 1.7 collective-permute-start.21
  207.8 9.2 %collective-permute-done.21.refs_7_ = bf16[2,128,768]{2,1,0:T(8,128)(2,1)S(1)} collective-permute-done((bf16[2,128,768]{2,1,0:T(8,128)(2,1)}, bf16[2,128,768]{2,1,0:T(8,128)(2,1)S(1)}, u32[]{:S(2)}, u32[]{:S(2)}) %collective-permute-start.21) | collective-permute-done | bytes 393248 | tf_op jit(solution)/shard_map/ppermute | solution.py:28
  217.0 1.5 collect_1.1
  218.5 1.9 collective-permute-start.22
  220.4 3.6 %collective-permute-start.23 = (bf16[6,64,128]{2,1,0:T(8,128)(2,1)S(1)}, bf16[6,64,128]{2,1,0:T(8,128)(2,1)S(1)}, u32[]{:S(2)}, u32[]{:S(2)}) collective-permute-start(bf16[6,64,128]{2,1,0:T(8,128)(2,1)S(1)} %get-tuple-element.39), channel_id=1, source_target_pairs={{1,0},{2,1},{3,2},{5,4},{6,5},{7,6},{9,8},{10,9},{11,10},{13,12},{... | collective-permute-start | bytes 294920 | tf_op jit(solution)/shard_map/ppermute | solution.py:36
  224.1 3.9 %collective-permute-start.24 = (f32[8,6,128]{2,1,0:T(8,128)S(1)}, f32[8,6,128]{2,1,0:T(8,128)S(1)}, u32[]{:S(2)}, u32[]{:S(2)}) collective-permute-start(f32[8,6,128]{2,1,0:T(8,128)S(1)} %get-tuple-element.40), channel_id=1, source_target_pairs={{0,4},{4,8},{8,12},{12,16},{16,20},{20,24},{24,28},{28,0},{1,5},{5... | collective-permute-start | bytes 73736 | tf_op jit(solution)/shard_map/ppermute | solution.py:36
  227.9 1.4 collect_0.1.refs_7_
  229.4 0.1 collective-permute-done.24.refs_3_
  229.5 5.0 %collective-permute-done.25.refs_4_ = f32[8,6,128]{2,1,0:T(8,128)S(1)} collective-permute-done((f32[8,6,128]{2,1,0:T(8,128)S(1)}, f32[8,6,128]{2,1,0:T(8,128)S(1)}, u32[]{:S(2)}, u32[]{:S(2)}) %collective-permute-start.25) | collective-permute-done | bytes 24608 | tf_op jit(solution)/shard_map/ppermute | solution.py:36
  234.5 2.0 backward_first.1
  236.6 1.9 collective-permute-start.26
  238.5 3.6 %collective-permute-start.27 = (f32[6,64,128]{2,1,0:T(8,128)S(1)}, f32[6,64,128]{2,1,0:T(8,128)S(1)}, u32[]{:S(2)}, u32[]{:S(2)}) collective-permute-start(f32[6,64,128]{2,1,0:T(8,128)S(1)} %get-tuple-element.46), channel_id=1, source_target_pairs={{1,0},{2,1},{3,2},{5,4},{6,5},{7,6},{9,8},{10,9},{11,10},{13,12},{... | collective-permute-start | bytes 589832 | tf_op jit(solution)/shard_map/ppermute | solution.py:36
  242.2 0.1 collective-permute-start.28
  242.2 2.0 collective-permute-start.29
  244.2 1.9 collective-permute-done.28.refs_3_
  246.1 2.8 %collective-permute-done.29.refs_4_ = f32[8,6,128]{2,1,0:T(8,128)S(1)} collective-permute-done((f32[8,6,128]{2,1,0:T(8,128)S(1)}, f32[8,6,128]{2,1,0:T(8,128)S(1)}, u32[]{:S(2)}, u32[]{:S(2)}) %collective-permute-start.29) | collective-permute-done | bytes 24608 | tf_op jit(solution)/shard_map/ppermute | solution.py:36
  248.9 3.3 %backward_last.1 = f32[8,6,64,128]{3,2,1,0:T(8,128)} custom-call(f32[8,6,64,128]{3,2,1,0:T(8,128)S(1)} %get-tuple-element.44.refs_0_, f32[6,64,128]{2,1,0:T(8,128)S(1)} %collective-permute-done.26.refs_1_, f32[6,64,128]{2,1,0:T(8,128)S(1)} %collective-permute-done.27.refs_2_, f32[8,6,128]{2,1,0:T(8,128)S(1)} %collective-permute-done.28.refs_3_, ...), custom_call_target="tpu_custom_call" | custom-call | tf_op jit(solution)/shard_map/backward_last/pallas_call | solution.py:383
  (51 shorter events, 0.2 us)
Async XLA Ops:
  0.6 4.0 %copy-start = (f32[8,64,6,128]{3,1,2,0:T(8,128)S(1)}, f32[8,64,6,128]{3,1,2,0:T(8,128)}, u32[]{:S(2)}) copy-start(f32[8,64,6,128]{3,1,2,0:T(8,128)} %param.9) | copy-start | bytes 4718596
  0.6 4.0 %copy-start.1 = (f32[8,64,128]{2,1,0:T(8,128)S(1)}, f32[8,64,128]{2,1,0:T(8,128)}, u32[]{:S(2)}) copy-start(f32[8,64,128]{2,1,0:T(8,128)} %kappa.1) | copy-start | bytes 786436
  3.7 6.1 %copy-start.9 = (s32[2,1,4]{2,1,0:T(1,128)S(1)}, s32[2,1,4]{2,1,0:T(1,128)}, u32[]{:S(2)}) copy-start(s32[2,1,4]{2,1,0:T(1,128)} %param.13) | copy-start | bytes 100
  3.7 55.6 %collective-permute-start.12 = (bf16[592,1024]{1,0:T(8,128)(2,1)}, bf16[592,1024]{1,0:T(8,128)(2,1)}, u32[]{:S(2)}, u32[]{:S(2)}) collective-permute-start(bf16[592,1024]{1,0:T(8,128)(2,1)} %pack.1), channel_id=1, source_target_pairs={{0,16},{4,20},{8,24},{12,28},{16,0},{20,4},{24,8},{28,12},{1,17},{... | collective-permute-start | bytes 3637256 | tf_op jit(solution)/shard_map/ppermute | solution.py:28
  4.1 57.0 %collective-permute-start.7 = (bf16[592,1024]{1,0:T(8,128)(2,1)}, bf16[592,1024]{1,0:T(8,128)(2,1)}, u32[]{:S(2)}, u32[]{:S(2)}) collective-permute-start(bf16[592,1024]{1,0:T(8,128)(2,1)} %pack.1), channel_id=1, source_target_pairs={{0,8},{4,12},{8,0},{12,4},{16,24},{20,28},{24,16},{28,20},{1,9},{5... | collective-permute-start | bytes 3637256 | tf_op jit(solution)/shard_map/ppermute | solution.py:28
  5.4 53.8 %collective-permute-start.1 = (f32[2,7,64,128]{3,2,1,0:T(8,128)}, f32[2,7,64,128]{3,2,1,0:T(8,128)S(1)}, u32[]{:S(2)}, u32[]{:S(2)}) collective-permute-start(f32[2,7,64,128]{3,2,1,0:T(8,128)} %get-tuple-element.49), channel_id=1, source_target_pairs={{1,0},{2,1},{3,2},{5,4},{6,5},{7,6},{9,8},{10,9},{11,10},{13,12},{... | collective-permute-start | bytes 1376264 | tf_op jit(solution)/shard_map/ppermute | solution.py:36
  7.3 52.0 %collective-permute-start = (f32[2,7,64,128]{3,2,1,0:T(8,128)S(1)}, f32[2,7,64,128]{3,2,1,0:T(8,128)S(1)}, u32[]{:S(2)}, u32[]{:S(2)}) collective-permute-start(f32[2,7,64,128]{3,2,1,0:T(8,128)S(1)} %get-tuple-element.50), channel_id=1, source_target_pairs={{0,1},{1,2},{2,3},{4,5},{5,6},{6,7},{8,9},{9,10},{10,11},{12,13},{... | collective-permute-start | bytes 1376264 | tf_op jit(solution)/shard_map/ppermute | solution.py:36
  13.5 84.5 %collective-permute-start.5 = (bf16[2,4,128,512]{3,2,1,0:T(8,128)(2,1)}, bf16[2,4,128,512]{3,2,1,0:T(8,128)(2,1)S(1)}, u32[]{:S(2)}, u32[]{:S(2)}) collective-permute-start(bf16[2,4,128,512]{3,2,1,0:T(8,128)(2,1)} %pick_radiances.1), channel_id=1, source_target_pairs={{0,4},{4,0},{8,12},{12,8},{16,20},{20,16},{24,28},{28,24},{1,5},{5... | collective-permute-start | bytes 3145736 | tf_op jit(solution)/shard_map/ppermute | solution.py:28
  14.1 74.9 %copy-start.8 = (s32[2]{0:T(128)S(1)}, s32[2]{0:T(128)}, u32[]{:S(2)}) copy-start(s32[2]{0:T(128)} %pad_add_fusion.pos) | copy-start | bytes 28
  14.1 74.9 %copy-start.10 = (s32[2,8]{1,0:T(2,128)S(1)}, s32[2,8]{1,0:T(2,128)}, u32[]{:S(2)}) copy-start(s32[2,8]{1,0:T(2,128)} %select_reduce_fusion.table) | copy-start | bytes 196
  59.3 39.7 %collective-permute-start.17 = (bf16[592,1024]{1,0:T(8,128)(2,1)}, bf16[592,1024]{1,0:T(8,128)(2,1)}, u32[]{:S(2)}, u32[]{:S(2)}) collective-permute-start(bf16[592,1024]{1,0:T(8,128)(2,1)} %collective-permute-done.12.refs_2_), channel_id=1, source_target_pairs={{0,8},{4,12},{8,0},{12,4},{16,24},{20,28},{24,16},{28,20},{1,9},{5... | collective-permute-start | bytes 3637256 | tf_op jit(solution)/shard_map/ppermute | solution.py:28
  59.3 0.8 copy-start.6
  60.1 28.9 %copy-start.7 = (f32[2,7,64,128]{3,2,1,0:T(8,128)S(1)}, f32[2,7,64,128]{3,2,1,0:T(8,128)}, u32[]{:S(2)}) copy-start(f32[2,7,64,128]{3,2,1,0:T(8,128)} %copy-done.6) | copy-start | bytes 1376260
  60.1 27.6 %collective-permute-start.2 = (f32[12,7,2,128]{3,2,1,0:T(2,128)S(1)}, f32[12,7,2,128]{3,2,1,0:T(2,128)S(1)}, u32[]{:S(2)}, u32[]{:S(2)}) collective-permute-start(f32[12,7,2,128]{3,2,1,0:T(2,128)S(1)} %pad_maximum_fusion.1), channel_id=1, source_target_pairs={{0,4},{4,8},{8,12},{12,16},{16,20},{20,24},{24,28},{28,0},{1,5},{5... | collective-permute-start | bytes 258056 | tf_op jit(solution)/shard_map/ppermute | solution.py:36
  61.1 39.3 %collective-permute-start.9 = (bf16[592,1024]{1,0:T(8,128)(2,1)}, bf16[592,1024]{1,0:T(8,128)(2,1)}, u32[]{:S(2)}, u32[]{:S(2)}) collective-permute-start(bf16[592,1024]{1,0:T(8,128)(2,1)} %collective-permute-done.7.refs_2_), channel_id=1, source_target_pairs={{0,2},{1,3},{2,0},{3,1},{4,6},{5,7},{6,4},{7,5},{8,10},{9,11},{10,... | collective-permute-start | bytes 3637256 | tf_op jit(solution)/shard_map/ppermute | solution.py:28
  61.7 89.2 %copy-start.3 = (bf16[2,8,64,512]{3,2,1,0:T(8,128)(2,1)S(1)}, bf16[2,8,64,512]{3,2,1,0:T(8,128)(2,1)}, u32[]{:S(2)}) copy-start(bf16[2,8,64,512]{3,2,1,0:T(8,128)(2,1)} %param.12) | copy-start | bytes 3145732
  61.7 89.2 %copy-start.11 = (f32[1,512]{1,0:T(1,128)S(1)}, f32[1,512]{1,0:T(1,128)}, u32[]{:S(2)}) copy-start(f32[1,512]{1,0:T(1,128)} %scale.1) | copy-start | bytes 6148
  61.7 27.2 %collective-permute-start.3 = (f32[12,7,2,128]{3,2,1,0:T(2,128)S(1)}, f32[12,7,2,128]{3,2,1,0:T(2,128)S(1)}, u32[]{:S(2)}, u32[]{:S(2)}) collective-permute-start(f32[12,7,2,128]{3,2,1,0:T(2,128)S(1)} %fusion.3), channel_id=1, source_target_pairs={{0,28},{4,0},{8,4},{12,8},{16,12},{20,16},{24,20},{28,24},{1,29},{... | collective-permute-start | bytes 258056 | tf_op jit(solution)/shard_map/ppermute | solution.py:36
  93.8 1.1 copy-start.12
  95.0 35.9 %collective-permute-start.4 = (bf16[2,4,128,768]{3,2,1,0:T(8,128)(2,1)S(1)}, bf16[2,4,128,768]{3,2,1,0:T(8,128)(2,1)S(1)}, u32[]{:S(2)}, u32[]{:S(2)}) collective-permute-start(bf16[2,4,128,768]{3,2,1,0:T(8,128)(2,1)S(1)} %get-tuple-element.28), channel_id=1, source_target_pairs={{0,4},{4,0},{8,12},{12,8},{16,20},{20,16},{24,28},{28,24},{1,5},{5... | collective-permute-start | bytes 4718600 | tf_op jit(solution)/shard_map/ppermute | solution.py:28
  97.4 33.4 %collective-permute-start.14 = (bf16[592,1024]{1,0:T(8,128)(2,1)}, bf16[592,1024]{1,0:T(8,128)(2,1)}, u32[]{:S(2)}, u32[]{:S(2)}) collective-permute-start(bf16[592,1024]{1,0:T(8,128)(2,1)} %collective-permute-done.12.refs_2_), channel_id=1, source_target_pairs={{0,2},{1,3},{2,0},{3,1},{4,6},{5,7},{6,4},{7,5},{8,10},{9,11},{10,... | collective-permute-start | bytes 3637256 | tf_op jit(solution)/shard_map/ppermute | solution.py:28
  98.0 1.0 copy-start.13
  98.9 32.4 %collective-permute-start.8 = (bf16[592,1024]{1,0:T(8,128)(2,1)}, bf16[592,1024]{1,0:T(8,128)(2,1)S(1)}, u32[]{:S(2)}, u32[]{:S(2)}) collective-permute-start(bf16[592,1024]{1,0:T(8,128)(2,1)} %collective-permute-done.7.refs_2_), channel_id=1, source_target_pairs={{0,1},{1,0},{2,3},{3,2},{4,5},{5,4},{6,7},{7,6},{8,9},{9,8},{10,11... | collective-permute-start | bytes 3637256 | tf_op jit(solution)/shard_map/ppermute | solution.py:28
  98.9 51.9 %collective-permute-start.19 = (bf16[592,1024]{1,0:T(8,128)(2,1)}, bf16[592,1024]{1,0:T(8,128)(2,1)}, u32[]{:S(2)}, u32[]{:S(2)}) collective-permute-start(bf16[592,1024]{1,0:T(8,128)(2,1)} %collective-permute-done.17.refs_2_), channel_id=1, source_target_pairs={{0,2},{1,3},{2,0},{3,1},{4,6},{5,7},{6,4},{7,5},{8,10},{9,11},{10,... | collective-permute-start | bytes 3637256 | tf_op jit(solution)/shard_map/ppermute | solution.py:28
  100.4 65.1 %collective-permute-start.10 = (bf16[592,1024]{1,0:T(8,128)(2,1)}, bf16[592,1024]{1,0:T(8,128)(2,1)}, u32[]{:S(2)}, u32[]{:S(2)}) collective-permute-start(bf16[592,1024]{1,0:T(8,128)(2,1)} %collective-permute-done.9.refs_4_), channel_id=1, source_target_pairs={{0,1},{1,0},{2,3},{3,2},{4,5},{5,4},{6,7},{7,6},{8,9},{9,8},{10,11... | collective-permute-start | bytes 3637256 | tf_op jit(solution)/shard_map/ppermute | solution.py:28
  130.8 20.0 %copy-start.16 = (bf16[2,4,128,768]{3,2,1,0:T(8,128)(2,1)}, bf16[2,4,128,768]{3,2,1,0:T(8,128)(2,1)S(1)}, u32[]{:S(2)}) copy-start(bf16[2,4,128,768]{3,2,1,0:T(8,128)(2,1)S(1)} %collective-permute-done.4.refs_0_) | copy-start | bytes 4718596
  130.8 47.7 %collective-permute-start.13 = (bf16[592,1024]{1,0:T(8,128)(2,1)}, bf16[592,1024]{1,0:T(8,128)(2,1)}, u32[]{:S(2)}, u32[]{:S(2)}) collective-permute-start(bf16[592,1024]{1,0:T(8,128)(2,1)} %collective-permute-done.12.refs_2_), channel_id=1, source_target_pairs={{0,1},{1,0},{2,3},{3,2},{4,5},{5,4},{6,7},{7,6},{8,9},{9,8},{10,11... | collective-permute-start | bytes 3637256 | tf_op jit(solution)/shard_map/ppermute | solution.py:28
  130.8 49.6 %collective-permute-start.15 = (bf16[592,1024]{1,0:T(8,128)(2,1)}, bf16[592,1024]{1,0:T(8,128)(2,1)}, u32[]{:S(2)}, u32[]{:S(2)}) collective-permute-start(bf16[592,1024]{1,0:T(8,128)(2,1)} %collective-permute-done.14.refs_4_), channel_id=1, source_target_pairs={{0,1},{1,0},{2,3},{3,2},{4,5},{5,4},{6,7},{7,6},{8,9},{9,8},{10,11... | collective-permute-start | bytes 3637256 | tf_op jit(solution)/shard_map/ppermute | solution.py:28
  131.4 19.5 %copy-start.17 = (bf16[592,1024]{1,0:T(8,128)(2,1)}, bf16[592,1024]{1,0:T(8,128)(2,1)S(1)}, u32[]{:S(2)}) copy-start(bf16[592,1024]{1,0:T(8,128)(2,1)S(1)} %collective-permute-done.8.refs_3_) | copy-start | bytes 3637252
  131.4 62.1 %collective-permute-start.18 = (bf16[592,1024]{1,0:T(8,128)(2,1)}, bf16[592,1024]{1,0:T(8,128)(2,1)}, u32[]{:S(2)}, u32[]{:S(2)}) collective-permute-start(bf16[592,1024]{1,0:T(8,128)(2,1)} %collective-permute-done.17.refs_2_), channel_id=1, source_target_pairs={{0,1},{1,0},{2,3},{3,2},{4,5},{5,4},{6,7},{7,6},{8,9},{9,8},{10,11... | collective-permute-start | bytes 3637256 | tf_op jit(solution)/shard_map/ppermute | solution.py:28
  150.9 42.6 %collective-permute-start.20 = (bf16[592,1024]{1,0:T(8,128)(2,1)}, bf16[592,1024]{1,0:T(8,128)(2,1)}, u32[]{:S(2)}, u32[]{:S(2)}) collective-permute-start(bf16[592,1024]{1,0:T(8,128)(2,1)} %collective-permute-done.19.refs_4_), channel_id=1, source_target_pairs={{0,1},{1,0},{2,3},{3,2},{4,5},{5,4},{6,7},{7,6},{8,9},{9,8},{10,11... | collective-permute-start | bytes 3637256 | tf_op jit(solution)/shard_map/ppermute | solution.py:28
  150.9 1.2 copy-start.5
  152.1 1.2 copy-start.14
  153.4 12.6 %copy-start.4 = (bf16[2,8,64,512]{3,2,1,0:T(8,128)(2,1)S(1)}, bf16[2,8,64,512]{3,2,1,0:T(8,128)(2,1)}, u32[]{:S(2)}) copy-start(bf16[2,8,64,512]{3,2,1,0:T(8,128)(2,1)} %param.12) | copy-start | bytes 3145732
  165.6 42.3 %collective-permute-start.6 = (bf16[2,128,768]{2,1,0:T(8,128)(2,1)}, bf16[2,128,768]{2,1,0:T(8,128)(2,1)S(1)}, u32[]{:S(2)}, u32[]{:S(2)}) collective-permute-start(bf16[2,128,768]{2,1,0:T(8,128)(2,1)} %get-tuple-element.30), channel_id=1, source_target_pairs={{0,4},{4,0},{8,12},{12,8},{16,20},{20,16},{24,28},{28,24},{1,5},{5... | collective-permute-start | bytes 1179656 | tf_op jit(solution)/shard_map/ppermute | solution.py:28
  178.6 29.2 %collective-permute-start.11 = (bf16[2,128,768]{2,1,0:T(8,128)(2,1)}, bf16[2,128,768]{2,1,0:T(8,128)(2,1)S(1)}, u32[]{:S(2)}, u32[]{:S(2)}) collective-permute-start(bf16[2,128,768]{2,1,0:T(8,128)(2,1)} %get-tuple-element.32), channel_id=1, source_target_pairs={{0,4},{4,0},{8,12},{12,8},{16,20},{20,16},{24,28},{28,24},{1,5},{5... | collective-permute-start | bytes 1179656 | tf_op jit(solution)/shard_map/ppermute | solution.py:28
  193.1 14.8 %collective-permute-start.16 = (bf16[2,128,768]{2,1,0:T(8,128)(2,1)}, bf16[2,128,768]{2,1,0:T(8,128)(2,1)}, u32[]{:S(2)}, u32[]{:S(2)}) collective-permute-start(bf16[2,128,768]{2,1,0:T(8,128)(2,1)} %get-tuple-element.34), channel_id=1, source_target_pairs={{0,4},{4,0},{8,12},{12,8},{16,20},{20,16},{24,28},{28,24},{1,5},{5... | collective-permute-start | bytes 1179656 | tf_op jit(solution)/shard_map/ppermute | solution.py:28
  205.3 0.7 copy-start.15
  206.1 10.9 %collective-permute-start.21 = (bf16[2,128,768]{2,1,0:T(8,128)(2,1)}, bf16[2,128,768]{2,1,0:T(8,128)(2,1)S(1)}, u32[]{:S(2)}, u32[]{:S(2)}) collective-permute-start(bf16[2,128,768]{2,1,0:T(8,128)(2,1)} %copy-done.15), channel_id=1, source_target_pairs={{0,4},{4,0},{8,12},{12,8},{16,20},{20,16},{24,28},{28,24},{1,5},{5... | collective-permute-start | bytes 1179656 | tf_op jit(solution)/shard_map/ppermute | solution.py:28
  218.5 16.0 %collective-permute-start.22 = (bf16[6,64,128]{2,1,0:T(8,128)(2,1)S(1)}, bf16[6,64,128]{2,1,0:T(8,128)(2,1)S(1)}, u32[]{:S(2)}, u32[]{:S(2)}) collective-permute-start(bf16[6,64,128]{2,1,0:T(8,128)(2,1)S(1)} %get-tuple-element.38), channel_id=1, source_target_pairs={{0,1},{1,2},{2,3},{4,5},{5,6},{6,7},{8,9},{9,10},{10,11},{12,13},{... | collective-permute-start | bytes 294920 | tf_op jit(solution)/shard_map/ppermute | solution.py:36
  220.4 14.1 %collective-permute-start.23 = (bf16[6,64,128]{2,1,0:T(8,128)(2,1)S(1)}, bf16[6,64,128]{2,1,0:T(8,128)(2,1)S(1)}, u32[]{:S(2)}, u32[]{:S(2)}) collective-permute-start(bf16[6,64,128]{2,1,0:T(8,128)(2,1)S(1)} %get-tuple-element.39), channel_id=1, source_target_pairs={{1,0},{2,1},{3,2},{5,4},{6,5},{7,6},{9,8},{10,9},{11,10},{13,12},{... | collective-permute-start | bytes 294920 | tf_op jit(solution)/shard_map/ppermute | solution.py:36
  224.1 5.5 %collective-permute-start.24 = (f32[8,6,128]{2,1,0:T(8,128)S(1)}, f32[8,6,128]{2,1,0:T(8,128)S(1)}, u32[]{:S(2)}, u32[]{:S(2)}) collective-permute-start(f32[8,6,128]{2,1,0:T(8,128)S(1)} %get-tuple-element.40), channel_id=1, source_target_pairs={{0,4},{4,8},{8,12},{12,16},{16,20},{20,24},{24,28},{28,0},{1,5},{5... | collective-permute-start | bytes 73736 | tf_op jit(solution)/shard_map/ppermute | solution.py:36
  227.9 6.6 %collective-permute-start.25 = (f32[8,6,128]{2,1,0:T(8,128)S(1)}, f32[8,6,128]{2,1,0:T(8,128)S(1)}, u32[]{:S(2)}, u32[]{:S(2)}) collective-permute-start(f32[8,6,128]{2,1,0:T(8,128)S(1)} %get-tuple-element.41), channel_id=1, source_target_pairs={{0,28},{4,0},{8,4},{12,8},{16,12},{20,16},{24,20},{28,24},{1,29},{... | collective-permute-start | bytes 73736 | tf_op jit(solution)/shard_map/ppermute | solution.py:36
  234.5 14.4 %copy-start.2 = (f32[8,64,6,128]{3,1,2,0:T(8,128)S(1)}, f32[8,64,6,128]{3,1,2,0:T(8,128)}, u32[]{:S(2)}) copy-start(f32[8,64,6,128]{3,1,2,0:T(8,128)} %param.10) | copy-start | bytes 4718596
  236.6 12.3 %collective-permute-start.26 = (f32[6,64,128]{2,1,0:T(8,128)S(1)}, f32[6,64,128]{2,1,0:T(8,128)S(1)}, u32[]{:S(2)}, u32[]{:S(2)}) collective-permute-start(f32[6,64,128]{2,1,0:T(8,128)S(1)} %get-tuple-element.45), channel_id=1, source_target_pairs={{0,1},{1,2},{2,3},{4,5},{5,6},{6,7},{8,9},{9,10},{10,11},{12,13},{... | collective-permute-start | bytes 589832 | tf_op jit(solution)/shard_map/ppermute | solution.py:36
  238.5 10.4 %collective-permute-start.27 = (f32[6,64,128]{2,1,0:T(8,128)S(1)}, f32[6,64,128]{2,1,0:T(8,128)S(1)}, u32[]{:S(2)}, u32[]{:S(2)}) collective-permute-start(f32[6,64,128]{2,1,0:T(8,128)S(1)} %get-tuple-element.46), channel_id=1, source_target_pairs={{1,0},{2,1},{3,2},{5,4},{6,5},{7,6},{9,8},{10,9},{11,10},{13,12},{... | collective-permute-start | bytes 589832 | tf_op jit(solution)/shard_map/ppermute | solution.py:36
  242.2 4.0 %collective-permute-start.28 = (f32[8,6,128]{2,1,0:T(8,128)S(1)}, f32[8,6,128]{2,1,0:T(8,128)S(1)}, u32[]{:S(2)}, u32[]{:S(2)}) collective-permute-start(f32[8,6,128]{2,1,0:T(8,128)S(1)} %get-tuple-element.47), channel_id=1, source_target_pairs={{0,4},{4,8},{8,12},{12,16},{16,20},{20,24},{24,28},{28,0},{1,5},{5... | collective-permute-start | bytes 73736 | tf_op jit(solution)/shard_map/ppermute | solution.py:36
  242.2 6.7 %collective-permute-start.29 = (f32[8,6,128]{2,1,0:T(8,128)S(1)}, f32[8,6,128]{2,1,0:T(8,128)S(1)}, u32[]{:S(2)}, u32[]{:S(2)}) collective-permute-start(f32[8,6,128]{2,1,0:T(8,128)S(1)} %get-tuple-element.48), channel_id=1, source_target_pairs={{0,28},{4,0},{8,4},{12,8},{16,12},{20,16},{24,20},{28,24},{1,29},{... | collective-permute-start | bytes 73736 | tf_op jit(solution)/shard_map/ppermute | solution.py:36

commit v2 on v1

--- a/solution.py
+++ b/solution.py
@@ -6,11 +6,13 @@
 from jax.experimental.pallas import tpu as pltpu
 from jax.sharding import PartitionSpec as P
 
+
 ADVECTION = 0.25
 VERTICAL = 0.1
 SERVED = 4
 EDGE = 16
 SIDE = 8
+CHUNKED = (1,)
 TAIL = 16
 ANY = pl.BlockSpec(memory_space=pl.ANY)
 SMEM = pl.BlockSpec(memory_space=pltpu.SMEM)
@@ -99,14 +101,17 @@
 
 
 def spread_weights(packed, group, n_lon, n_lat):
-    found = {0: packed}
+    rows = packed.shape[0]
+    half = rows // (2 * TAIL) * TAIL
+    found = {0: (packed,)}
     bits = sorted(bits_down(n_lon // group))
     for bit in bits:
-        found[bit] = exchange(packed, "lon", bit * group)
+        chunks = (packed[:half], packed[half:]) if bit in CHUNKED else (packed,)
+        found[bit] = tuple(exchange(a, "lon", bit * group) for a in chunks)
     for far in range(n_lon // group):
         if far not in found:
             bottom = far & -far
-            found[far] = exchange(found[far ^ bottom], "lon", bottom * group)
+            found[far] = tuple(exchange(a, "lon", bottom * group) for a in found[far ^ bottom])
     gathered = {}
     for served, part in found.items():
         if served == 0:
@@ -114,7 +119,7 @@
         parts = {0: part}
         for bit in bits_down(n_lat):
             for near in list(parts):
-                parts[near | bit] = exchange(parts[near], "lat", bit)
+                parts[near | bit] = tuple(exchange(a, "lat", bit) for a in parts[near])
         gathered[served] = parts
     return gathered
 
@@ -122,7 +127,6 @@
 def radiance_kernel(group, pos, table, source, *refs):
     *outs, sems = refs
     slots, served, span, _ = outs[0].shape
-    count = table.shape[1]
     copies = []
     for c, out in enumerate(outs, 1):
         for s in range(slots):
@@ -179,15 +183,17 @@
 
     lax.fori_loop(0, rows, place, 0)
     for r in range(2):
-        wide[r, :, inner] = south[r]
-        wide[rows + 2 + r, :, inner] = north[r]
+        for target, source in ((r, south), (rows + 2 + r, north)):
+            wide[target, :, inner] = source[r, :, 0:width]
+            wide[target, :, EDGE - 2 : EDGE] = source[r, :, width : width + 2]
+            wide[target, :, EDGE + width : EDGE + width + 2] = source[r, :, width + 2 : width + 4]
 
     def rims(r, _):
-        wide[r, :, EDGE - 2 : EDGE] = west[r]
-        wide[r, :, EDGE + width : EDGE + width + 2] = east[r]
-        return 0
-
-    lax.fori_loop(0, rows + 4, rims, 0)
+        wide[r + 2, :, EDGE - 2 : EDGE] = west[r]
+        wide[r + 2, :, EDGE + width : EDGE + width + 2] = east[r]
+        return 0
+
+    lax.fori_loop(0, rows, rims, 0)
     low = EDGE - SIDE
     span = width + 2 * SIDE
 
@@ -261,15 +267,19 @@
 
 def halo_of_state(state, kappa):
     width = state.shape[2]
-    joined = jnp.concatenate([state, kappa[:, None]], axis=1)
-    south = shifted(joined[-2:], "lat", 1, False)
-    north = shifted(joined[:2], "lat", -1, False)
-
-    def edge(cut):
-        return jnp.concatenate([south[:, :, cut], joined[:, :, cut], north[:, :, cut]], axis=0)
-
-    west = shifted(edge(slice(width - 2, width)), "lon", 1, True)
-    east = shifted(edge(slice(0, 2)), "lon", -1, True)
+
+    def cut(rows, columns):
+        return jnp.concatenate([state[rows, :, columns], kappa[rows, None, columns]], axis=1)
+
+    every = slice(None)
+    west = shifted(cut(every, slice(width - 2, width)), "lon", 1, True)
+    east = shifted(cut(every, slice(0, 2)), "lon", -1, True)
+
+    def edge(rows):
+        return jnp.concatenate([cut(rows, every), west[rows], east[rows]], axis=2)
+
+    south = shifted(edge(slice(-2, None)), "lat", 1, False)
+    north = shifted(edge(slice(0, 2)), "lat", -1, False)
     return south, north, west, east
 
 
@@ -395,12 +405,12 @@
     return lax.dot_general(a, b, (((1,), (1,)), ((), ())), preferred_element_type=F32)
 
 
-def instrument_kernel(group, served, n_lat, pos, table, columns, radiances, *refs):
+def instrument_kernel(group, served, n_lat, chosen, bounds, pos, table, columns, radiances, *refs):
     others = group - 1
     got_columns, refs = refs[:others], refs[others:]
     got_radiances, refs = refs[:others], refs[others:]
     own_weights = served == 0
-    n_weights = 4 if own_weights else n_lat
+    n_weights = 4 if own_weights else n_lat * len(bounds)
     weights, refs = refs[:n_weights], refs[n_weights:]
     outs, refs = refs[:group], refs[group:]
     x, y, w1, w2, w3, scale, a1, s1, a2, s2, mis, sem_x, sem_y, sem_w = refs
@@ -408,8 +418,8 @@
     tile = 256
     copies_x, copies_y = [], []
     for c in range(group):
-        for s in range(slots):
-            j = c * slots + s
+        for k, s in enumerate(chosen):
+            j = c * slots + k
             if c == 0:
                 block = table[s, pos[0] ^ (served * group)]
                 lines = pl.ds(pl.multiple_of(block * span, span), span)
@@ -430,23 +440,34 @@
         count = 0
         for near in range(n_lat):
             lat = pos[1] ^ near
-            source = weights[near]
-
-            def start(phase, src, dst):
+            sources = weights[near * len(bounds) : (near + 1) * len(bounds)]
+
+            def fetch(phase, first, last, lanes, target, base):
                 nonlocal count
-                phases[phase].append(pltpu.make_async_copy(src, dst, sem_w.at[count]))
-                count += 1
-
-            start(0, source.at[pl.ds(0, r1)], w1.at[pl.ds(pl.multiple_of(lat * r1, 16), r1)])
-            start(1, source.at[pl.ds(r1, r2)], w2.at[pl.ds(pl.multiple_of(lat * r2, 16), r2)])
+                for source, (low, high) in zip(sources, bounds):
+                    a, b = max(first, low), min(last, high)
+                    if a < b:
+                        begin = base + (a - first)
+                        if not isinstance(begin, int):
+                            begin = pl.multiple_of(begin, 16)
+                        phases[phase].append(
+                            pltpu.make_async_copy(
+                                source.at[pl.ds(a - low, b - a), lanes],
+                                target.at[pl.ds(begin, b - a)],
+                                sem_w.at[count],
+                            )
+                        )
+                        count += 1
+
+            everything = pl.ds(0, w1.shape[1])
+            ends = (r1, r1 + r2, r1 + r2 + piece)
+            fetch(0, 0, ends[0], everything, w1, lat * r1)
+            fetch(1, ends[0], ends[1], everything, w2, lat * r2)
             for p in range(parts):
-                start(
-                    2,
-                    source.at[pl.ds(r1 + r2, piece), pl.ds(p * w3.shape[1], w3.shape[1])],
-                    w3.at[pl.ds(pl.multiple_of(lat * r3 + p * piece, 16), piece)],
-                )
+                lanes = pl.ds(p * w3.shape[1], w3.shape[1])
+                fetch(2, ends[1], ends[2], lanes, w3, lat * r3 + p * piece)
             if near == 0:
-                start(2, source.at[pl.ds(r1 + r2 + piece, 16), pl.ds(0, w3.shape[1])], scale)
+                fetch(2, ends[2], ends[2] + TAIL, pl.ds(0, w3.shape[1]), scale, 0)
     for copy in copies_x + phases[0] + phases[1] + phases[2] + copies_y:
         copy.start()
     for copy in copies_x + phases[0]:
@@ -456,12 +477,14 @@
         def column(n, _):
             at = pl.ds(pl.multiple_of(n * tile, tile), tile)
             z = jnp.dot(source[...], weight[:, at], preferred_element_type=F32)
-            sigma = jax.nn.sigmoid(z)
-            act[:, at] = (z * sigma).astype(BF16)
-            slope[:, at] = sigma * (1.0 + z * (1.0 - sigma))
+            half = 0.5 * jnp.tanh(0.5 * z)
+            sigma = 0.5 + half
+            value = z * sigma
+            act[:, at] = value.astype(BF16)
+            slope[:, at] = sigma + value * (0.5 - half)
             return 0
 
-        lax.fori_loop(0, weight.shape[1] // tile, column, 0)
+        lax.fori_loop(0, weight.shape[1] // tile, column, 0, unroll=True)
 
     hidden(x, w1, a1, s1)
     for copy in phases[1]:
@@ -485,29 +508,33 @@
             grad[:, at] = (nt_dot(source[...], weight[at]) * slope[:, at]).astype(BF16)
             return 0
 
-        lax.fori_loop(0, weight.shape[0] // tile, column, 0)
+        lax.fori_loop(0, weight.shape[0] // tile, column, 0, unroll=True)
 
     back(mis, w3, s2, a2)
     back(a2, w2, s1, a1)
     for n in range(w1.shape[0] // tile):
         at = slice(n * tile, (n + 1) * tile)
         value = nt_dot(a1[...], w1[at]).astype(BF16)
-        for c in range(group):
-            for s in range(slots):
-                j = c * slots + s
-                outs[c][s, :, at] = value[j * span : (j + 1) * span]
-
-
-def instrument(pos, table, columns, radiances, got_columns, got_radiances, weights, group, served, n_lat, sizes, span):
-    slots, _, cin = columns.shape
-    ch = radiances.shape[2]
+        for j in range(group * slots):
+            outs[j // slots][j % slots, :, at] = value[j * span : (j + 1) * span]
+
+
+def instrument(pos, table, columns, radiances, got_columns, got_radiances, weights, group, served, n_lat, sizes, span, chosen):
+    cin, ch = columns.shape[2], radiances.shape[2]
+    slots = len(chosen)
     h1, h2 = sizes
+    own = served == 0
+    bounds = []
+    if not own:
+        for chunk in weights[0]:
+            low = bounds[-1][1] if bounds else 0
+            bounds.append((low, low + chunk.shape[0]))
+        weights = [chunk for near in range(n_lat) for chunk in weights[near]]
     lines = group * slots * span
-    own = served == 0
     out = jax.ShapeDtypeStruct((slots, span, cin), BF16)
     parts = h1 // ch
     return pl.pallas_call(
-        functools.partial(instrument_kernel, group, served, n_lat),
+        functools.partial(instrument_kernel, group, served, n_lat, chosen, tuple(bounds)),
         out_shape=[out] * group,
         in_specs=[SMEM, SMEM] + [ANY] * (2 + 2 * (group - 1) + len(weights)),
         out_specs=[VMEM] * group,
@@ -525,7 +552,7 @@
             pltpu.VMEM((lines, ch), BF16),
             pltpu.SemaphoreType.DMA((group * slots,)),
             pltpu.SemaphoreType.DMA((group * slots,)),
-            pltpu.SemaphoreType.DMA((4 if own else n_lat * (2 + parts) + 1,)),
+            pltpu.SemaphoreType.DMA((4 if own else n_lat * len(bounds) * (3 + parts),)),
         ],
         compiler_params=params(50),
         cost_estimate=pl.CostEstimate(
@@ -533,11 +560,10 @@
             transcendentals=lines * (h1 + h2),
             bytes_accessed=2 * (cin * h1 + h1 * h2 + h2 * ch + lines * (2 * cin + ch)),
         ),
-        name=f"instrument_{served}",
     )(pos, table, columns, radiances, *got_columns, *got_radiances, *weights)
 
 
-def collect_kernel(slot, group, edges, pos, owners, *refs):
+def collect_kernel(slot, places, edges, pos, owners, *refs):
     outs = 5 if edges else 1
     *answers, flat = refs[: len(refs) - 1 - outs] + refs[len(refs) - 1 :]
     out, *rims = refs[len(answers) : len(answers) + outs]
@@ -550,7 +576,7 @@
 
             @pl.when(apart == k)
             def _():
-                flat[pl.ds(pl.multiple_of(b * span, span), span)] = answer[slot]
+                flat[pl.ds(pl.multiple_of(b * span, span), span)] = answer[places[k]]
 
         return 0
 
@@ -573,20 +599,21 @@
         rims[1][...] = out[rows - 1]
 
 
-def collect(slot, pos, owners, answers, group, shape, edges):
+def collect(slot, pos, owners, answers, shape, edges):
+    places = tuple(place for _, place in answers)
+    answers = [answer for answer, _ in answers]
     rows, fields, width, levels = shape
     outs = [jax.ShapeDtypeStruct(shape, BF16)]
     if edges:
         outs += [jax.ShapeDtypeStruct((fields, width, levels), BF16)] * 2
         outs += [jax.ShapeDtypeStruct((rows, fields, levels), F32)] * 2
     return pl.pallas_call(
-        functools.partial(collect_kernel, slot, group, edges),
+        functools.partial(collect_kernel, slot, places, edges),
         out_shape=outs,
         in_specs=[SMEM, SMEM] + [VMEM] * len(answers),
         out_specs=[VMEM] * len(outs),
         scratch_shapes=[pltpu.VMEM((rows * width, fields * levels), BF16)],
         compiler_params=params(40),
-        name=f"collect_{slot}",
     )(pos, owners, *answers)
 
 
@@ -595,9 +622,9 @@
     served = min(SERVED, n_lon)
     group = n_lon // served
     slots, _, blocks = owners.shape
-    rows, width, fields, levels = state.shape
+    rows, width, _, _ = state.shape
     span = rows * width // blocks
-    cin, h1, h2 = first_layer.shape[1], first_layer.shape[2], second_layer.shape[2]
+    h1, h2 = first_layer.shape[2], second_layer.shape[2]
     pos = jnp.stack([lax.axis_index("lon"), lax.axis_index("lat")]).astype(jnp.int32)
     owners = owners[:, 0]
     hits = owners[:, None, :] == jnp.arange(n_lon, dtype=jnp.int32)[None, :, None]
@@ -614,17 +641,19 @@
     wide, first, columns, *sent = forward(pos, table, state, diffusivity, rims, group, served, span)
     got_columns = [exchange(a, "lon", c) for c, a in enumerate(sent, 1)]
 
-    answers = []
+    answers = {s: [] for s in range(slots)}
     for w in range(served):
         weights = own if w == 0 else [gathered[w][k] for k in range(n_lat)]
-        mine, *theirs = instrument(
-            pos, table, columns, radiances, got_columns, got_radiances, weights, group, w, n_lat, (h1, h2), span
-        )
-        answers.append(mine)
-        answers.extend(exchange(a, "lon", c) for c, a in enumerate(theirs, 1))
+        for chosen in [(s,) for s in reversed(range(slots))] if w == served - 1 else [tuple(range(slots))]:
+            mine, *theirs = instrument(
+                pos, table, columns, radiances, got_columns, got_radiances, weights, group, w, n_lat, (h1, h2), span, chosen
+            )
+            back = [exchange(a, "lon", c) for c, a in enumerate(theirs, 1)]
+            for place, s in enumerate(chosen):
+                answers[s] += [(mine, place)] + [(a, place) for a in back]
     shape = state.shape
-    late, *edges = collect(1, pos, owners, answers, group, shape, True)
-    (early,) = collect(0, pos, owners, answers, group, shape, False)
+    late, *edges = collect(1, pos, owners, answers[1], shape, True)
+    (early,) = collect(0, pos, owners, answers[0], shape, False)
     costate, edges = backward_first(late, halo_of_adjoint(edges), first, wide, early)
     gradient = backward_last(costate, halo_of_adjoint(edges), wide, state, background)
     return gradient.transpose(0, 2, 1, 3)
@@ -642,6 +671,4 @@
         P("lon", None, None),
         P("lon", None),
     )
-    return jax.shard_map(
-        shards, mesh=mesh, in_specs=placed, out_specs=P("lat", "lon", None, None), check_vma=False
-    )
+    return jax.shard_map(shards, mesh=mesh, in_specs=placed, out_specs=P("lat", "lon", None, None), check_vma=False)

time: 253 us -> 275 us (1.087)
  waiting for transfers between devices: 140 us -> 160 us
  local copies, waits for them, and re-layouts: 6.14 us -> 15.6 us
  Pallas kernels: 68.6 us -> 59.5 us
    ppermute x18 -> x23, waiting for transfers between devices: 104 us -> 146 us  [exchange(): return lax.ppermute(array, axis, [(i, i ^ mask) for i in range(count)])]
    ppermute x12, waiting for transfers between devices: 35.9 us -> 14.3 us  [shifted(): return lax.ppermute(array, axis, pairs)]
    pallas_call x6 -> x7, Pallas kernels: 52.3 us -> 43.1 us  [the longest x5 41.2 us: instrument(): pl.pallas_call(functools.partial(instrument_kernel, group, served, n_lat,...]
    unnamed x36 -> x58, local copies, waits for them, and re-layouts: 6.11 us -> 12.5 us
    ppermute x18 -> x23, starting transfers between devices: 11.5 us -> 12.6 us  [exchange(): return lax.ppermute(array, axis, [(i, i ^ mask) for i in range(count)])]
  transfers between devices with their start and end apart: 30 -> 35, of which waited for: 10 -> 9; matrix products, arithmetic and copies ran while one was open for 1% -> 1% of each run, Pallas kernels for 23% -> 20%
where the time goes in v2:
time: 275 us; the launch traced here: 274 us
  waiting for transfers between devices  160 us (58%)
  Pallas kernels  59.5 us (22%)
  starting transfers between devices  36.7 us (13%)
  local copies, waits for them, and re-layouts  15.6 us (6%)
    ppermute x23, waiting for transfers between devices, exchange(): return lax.ppermute(array, axis, [(i, i ^ mask) for i in range(count)])  146 us
    pallas_call x5, Pallas kernels, instrument(): pl.pallas_call(functools.partial(instrument_kernel, group, served, n_lat,...  41.2 us
    ppermute x12, starting transfers between devices, shifted(): return lax.ppermute(array, axis, pairs)  24.1 us
    ppermute x12, waiting for transfers between devices, shifted(): return lax.ppermute(array, axis, pairs)  14.3 us
    ppermute x23, starting transfers between devices, exchange(): return lax.ppermute(array, axis, [(i, i ^ mask) for i in range(count)])  12.6 us
    unnamed x58, local copies, waits for them, and re-layouts  12.5 us
  transfers between devices with their start and end apart: 35, of which 9 were waited for; matrix products, arithmetic and copies ran while one was open for 1% of the time, Pallas kernels for 20%

profile of v2, /device:TPU:30, one launch (start us, length us, event | category | flops | bytes accessed | tf_op | source)
XLA Modules:
  0.0 273.8 jit_solution(4602132267159197830)
XLA Ops:
  0.0 0.8 slice_bitcast_fusion.3
  0.8 1.1 fusion.1
  1.9 0.6 collective-permute-start.1
  2.5 4.3 %collective-permute-start = (f32[8,7,2,128]{3,2,1,0:T(2,128)S(1)}, f32[8,7,2,128]{3,2,1,0:T(2,128)S(1)}, u32[]{:S(2)}, u32[]{:S(2)}) collective-permute-start(f32[8,7,2,128]{3,2,1,0:T(2,128)S(1)} %pad_maximum_fusion.2), channel_id=1, source_target_pairs={{0,4},{4,8},{8,12},{12,16},{16,20},{20,24},{24,28},{28,0},{1,5},{5... | collective-permute-start | bytes 172040 | tf_op jit(solution)/shard_map/ppermute | solution.py:38
  6.7 0.6 pad_add_fusion.pos
  7.3 3.1 %pack.1 = bf16[592,1024]{1,0:T(8,128)(2,1)} custom-call(s32[2]{0:T(128)} %pad_add_fusion.pos, bf16[768,1024]{1,0:T(8,128)(2,1)} %bitcast.36, bf16[1024,1024]{1,0:T(8,128)(2,1)} %bitcast.34, bf16[1024,512]{1,0:T(8,128)(2,1)} %bitcast.29, f32[1,512]{1,0:T(1,128)} %scale.1), custom_call_target="tpu_custom_call" | custom-call | tf_op jit(solution)/shard_map/pack/pallas_call | solution.py:93
  10.5 0.7 select_reduce_fusion.table
  11.2 3.2 %pick_radiances.1 = bf16[2,4,128,512]{3,2,1,0:T(8,128)(2,1)} custom-call(s32[2]{0:T(128)} %pad_add_fusion.pos, s32[2,8]{1,0:T(2,128)} %select_reduce_fusion.table, bf16[2,512,512]{2,1,0:T(8,128)(2,1)} %bitcast.22), custom_call_target="tpu_custom_call" | custom-call | tf_op jit(solution)/shard_map/pick_radiances/pallas_call | solution.py:151
  14.4 1.1 slice.64
  15.5 1.2 collective-permute-start.7
  16.9 1.9 collective-permute-start.2
  18.8 44.8 %collective-permute-done.16.refs_2_ = bf16[592,1024]{1,0:T(8,128)(2,1)} collective-permute-done((bf16[592,1024]{1,0:T(8,128)(2,1)}, bf16[592,1024]{1,0:T(8,128)(2,1)}, u32[]{:S(2)}, u32[]{:S(2)}) %collective-permute-start.16) | collective-permute-done | bytes 1212448 | tf_op jit(solution)/shard_map/ppermute | solution.py:30
  63.7 2.1 collective-permute-start.8
  65.8 2.1 collective-permute-start.3
  67.9 0.6 collective-permute-start.9
  68.5 6.0 %collective-permute-done.3.north = f32[2,7,68,128]{3,2,1,0:T(8,128)S(1)} collective-permute-done((f32[2,7,68,128]{3,2,1,0:T(8,128)S(1)}, f32[2,7,68,128]{3,2,1,0:T(8,128)S(1)}, u32[]{:S(2)}, u32[]{:S(2)}) %collective-permute-start.3) | collective-permute-done | bytes 487456 | tf_op jit(solution)/shard_map/ppermute | solution.py:38
  74.5 4.8 %forward.1 = (f32[12,7,96,128]{3,2,1,0:T(8,128)S(1)}, f32[10,6,80,128]{3,2,1,0:T(8,128)S(1)}, bf16[2,512,768]{2,1,0:T(8,128)(2,1)S(1)}, bf16[2,4,128,768]{3,2,1,0:T(8,128)(2,1)S(1)}) custom-call(s32[2]{0:T(128)S(1)} %copy-done.14, s32[2,8]{1,0:T(2,128)S(1)} %copy-done.13, f32[8,6,64,128]{3,2,1,0:T(8,128)S(1)} %bitcast.20, f32[8,64,128]{2,1,0:T(8,128)S(1)} %copy-done.12, ...), custom_call_target="tpu_custom_call" | custom-call | tf_op jit(solution)/shard_map/forward/pallas_call | solution.py:258
  79.3 1.1 copy-done.3
  80.5 1.4 copy-done.6
  81.9 23.9 %collective-permute-done.8.refs_3_ = bf16[304,1024]{1,0:T(8,128)(2,1)S(1)} collective-permute-done((bf16[304,1024]{1,0:T(8,128)(2,1)S(1)}, bf16[304,1024]{1,0:T(8,128)(2,1)S(1)}, u32[]{:S(2)}, u32[]{:S(2)}) %collective-permute-start.8) | collective-permute-done | bytes 622624 | tf_op jit(solution)/shard_map/ppermute | solution.py:30
  105.8 0.5 collective-permute-start.11
  106.3 1.5 collective-permute-start.18
  107.8 0.8 copy-done.21
  108.6 0.5 collective-permute-start.23
  109.2 12.8 %collective-permute-done.11.refs_6_ = bf16[288,1024]{1,0:T(8,128)(2,1)S(1)} collective-permute-done((bf16[288,1024]{1,0:T(8,128)(2,1)S(1)}, bf16[288,1024]{1,0:T(8,128)(2,1)S(1)}, u32[]{:S(2)}, u32[]{:S(2)}) %collective-permute-start.11) | collective-permute-done | bytes 589856 | tf_op jit(solution)/shard_map/ppermute | solution.py:30
  122.0 0.5 collective-permute-start.12
  122.5 63.1 %collective-permute-done.12.refs_7_ = bf16[304,1024]{1,0:T(8,128)(2,1)} collective-permute-done((bf16[304,1024]{1,0:T(8,128)(2,1)S(1)}, bf16[304,1024]{1,0:T(8,128)(2,1)}, u32[]{:S(2)}, u32[]{:S(2)}) %collective-permute-start.12) | collective-permute-done | bytes 622624 | tf_op jit(solution)/shard_map/ppermute | solution.py:30
  185.6 0.5 collective-permute-start.19
  186.1 0.8 copy-done.25
  186.9 0.5 collective-permute-start.22
  187.4 0.1 collective-permute-start.24
  187.5 0.6 copy-done.27
  188.1 1.2 copy-done.11
  189.3 9.9 %shard_map.91 = (bf16[2,128,768]{2,1,0:T(8,128)(2,1)S(1)}, bf16[2,128,768]{2,1,0:T(8,128)(2,1)}) custom-call(s32[2]{0:T(128)S(1)} %copy-done.14, s32[2,8]{1,0:T(2,128)S(1)} %copy-done.13, bf16[2,512,768]{2,1,0:T(8,128)(2,1)} %copy-done.3, bf16[2,512,512]{2,1,0:T(8,128)(2,1)S(1)} %bitcast.24, bf16[2,4,128,768]{3,2,1,0:T(8,128)(2,1)} %copy-done.27, ...), custom_call_target="tpu_custom_call" | custom-call | flops 4831838208 | bytes 6815744 | tf_op jit(solution)/shard_map/pallas_call | solution.py:536
  199.4 1.2 copy-done.18
  200.6 1.1 copy-done.20
  201.7 1.1 copy-done.22
  202.7 1.1 copy-done.24
  203.8 1.1 copy-done.26
  204.9 10.1 %shard_map.92 = (bf16[2,128,768]{2,1,0:T(8,128)(2,1)S(1)}, bf16[2,128,768]{2,1,0:T(8,128)(2,1)}) custom-call(s32[2]{0:T(128)S(1)} %copy-done.14, s32[2,8]{1,0:T(2,128)S(1)} %copy-done.13, bf16[2,512,768]{2,1,0:T(8,128)(2,1)} %copy-done.3, bf16[2,512,512]{2,1,0:T(8,128)(2,1)} %bitcast.23, bf16[2,4,128,768]{3,2,1,0:T(8,128)(2,1)} %copy-done.27, ...), custom_call_target="tpu_custom_call" | custom-call | flops 4831838208 | bytes 6815744 | tf_op jit(solution)/shard_map/pallas_call | solution.py:536
  215.0 2.0 collective-permute-start.15
  216.9 9.6 %shard_map.93 = (bf16[2,128,768]{2,1,0:T(8,128)(2,1)S(1)}, bf16[2,128,768]{2,1,0:T(8,128)(2,1)S(1)}) custom-call(s32[2]{0:T(128)S(1)} %copy-done.14, s32[2,8]{1,0:T(2,128)S(1)} %copy-done.13, bf16[2,512,768]{2,1,0:T(8,128)(2,1)} %copy-done.3, bf16[2,512,512]{2,1,0:T(8,128)(2,1)S(1)} %bitcast.25, bf16[2,4,128,768]{3,2,1,0:T(8,128)(2,1)} %copy-done.27, ...), custom_call_target="tpu_custom_call" | custom-call | flops 4831838208 | bytes 6815744 | tf_op jit(solution)/shard_map/pallas_call | solution.py:536
  226.6 0.2 collective-permute-start.20
  226.8 5.8 %shard_map.94 = (bf16[1,128,768]{2,1,0:T(8,128)(2,1)S(1)}, bf16[1,128,768]{2,1,0:T(8,128)(2,1)S(1)}) custom-call(s32[2]{0:T(128)S(1)} %copy-done.14, s32[2,8]{1,0:T(2,128)S(1)} %copy-done.13, bf16[2,512,768]{2,1,0:T(8,128)(2,1)} %copy-done.3, bf16[2,512,512]{2,1,0:T(8,128)(2,1)S(1)} %bitcast.26, bf16[2,4,128,768]{3,2,1,0:T(8,128)(2,1)} %copy-done.27, ...), custom_call_target="tpu_custom_call" | custom-call | flops 2415919104 | bytes 5767168 | tf_op jit(solution)/shard_map/pallas_call | solution.py:536
  232.5 1.9 collective-permute-start.25
  234.5 5.8 %shard_map.96 = (bf16[1,128,768]{2,1,0:T(8,128)(2,1)S(1)}, bf16[1,128,768]{2,1,0:T(8,128)(2,1)S(1)}) custom-call(s32[2]{0:T(128)S(1)} %copy-done.14, s32[2,8]{1,0:T(2,128)S(1)} %copy-done.13, bf16[2,512,768]{2,1,0:T(8,128)(2,1)} %copy-done.3, bf16[2,512,512]{2,1,0:T(8,128)(2,1)S(1)} %bitcast.27, bf16[2,4,128,768]{3,2,1,0:T(8,128)(2,1)} %copy-done.27, ...), custom_call_target="tpu_custom_call" | custom-call | flops 2415919104 | bytes 5767168 | tf_op jit(solution)/shard_map/pallas_call | solution.py:536
  240.3 0.2 collective-permute-start.30
  240.5 1.3 collective-permute-done.25.refs_7_
  241.8 1.0 shard_map.95
  242.8 1.9 collective-permute-start.26
  244.7 3.6 %collective-permute-start.27 = (bf16[6,64,128]{2,1,0:T(8,128)(2,1)S(1)}, bf16[6,64,128]{2,1,0:T(8,128)(2,1)S(1)}, u32[]{:S(2)}, u32[]{:S(2)}) collective-permute-start(bf16[6,64,128]{2,1,0:T(8,128)(2,1)S(1)} %get-tuple-element.41), channel_id=1, source_target_pairs={{1,0},{2,1},{3,2},{5,4},{6,5},{7,6},{9,8},{10,9},{11,10},{13,12},{... | collective-permute-start | bytes 294920 | tf_op jit(solution)/shard_map/ppermute | solution.py:38
  248.4 0.4 collective-permute-start.28
  248.8 1.6 collective-permute-start.29
  250.5 1.0 copy-done.10
  251.5 1.0 shard_map.97.refs_7_
  252.5 3.0 %collective-permute-done.29.refs_4_ = f32[8,6,128]{2,1,0:T(8,128)S(1)} collective-permute-done((f32[8,6,128]{2,1,0:T(8,128)S(1)}, f32[8,6,128]{2,1,0:T(8,128)S(1)}, u32[]{:S(2)}, u32[]{:S(2)}) %collective-permute-start.29) | collective-permute-done | bytes 24608 | tf_op jit(solution)/shard_map/ppermute | solution.py:38
  255.5 2.0 backward_first.1
  257.5 1.9 collective-permute-start.31
  259.4 3.6 %collective-permute-start.32 = (f32[6,64,128]{2,1,0:T(8,128)S(1)}, f32[6,64,128]{2,1,0:T(8,128)S(1)}, u32[]{:S(2)}, u32[]{:S(2)}) collective-permute-start(f32[6,64,128]{2,1,0:T(8,128)S(1)} %get-tuple-element.50), channel_id=1, source_target_pairs={{1,0},{2,1},{3,2},{5,4},{6,5},{7,6},{9,8},{10,9},{11,10},{13,12},{... | collective-permute-start | bytes 589832 | tf_op jit(solution)/shard_map/ppermute | solution.py:38
  263.1 0.8 collective-permute-start.33
  263.9 1.3 collective-permute-start.34
  265.2 1.9 collective-permute-done.33.refs_3_
  267.1 3.5 %collective-permute-done.34.refs_4_ = f32[8,6,128]{2,1,0:T(8,128)S(1)} collective-permute-done((f32[8,6,128]{2,1,0:T(8,128)S(1)}, f32[8,6,128]{2,1,0:T(8,128)S(1)}, u32[]{:S(2)}, u32[]{:S(2)}) %collective-permute-start.34) | collective-permute-done | bytes 24608 | tf_op jit(solution)/shard_map/ppermute | solution.py:38
  270.5 3.3 %backward_last.1 = f32[8,6,64,128]{3,2,1,0:T(8,128)} custom-call(f32[8,6,64,128]{3,2,1,0:T(8,128)S(1)} %get-tuple-element.48.refs_0_, f32[6,64,128]{2,1,0:T(8,128)S(1)} %collective-permute-done.31.refs_1_, f32[6,64,128]{2,1,0:T(8,128)S(1)} %collective-permute-done.32.refs_2_, f32[8,6,128]{2,1,0:T(8,128)S(1)} %collective-permute-done.33.refs_3_, ...), custom_call_target="tpu_custom_call" | custom-call | tf_op jit(solution)/shard_map/backward_last/pallas_call | solution.py:393
  (90 shorter events, 0.7 us)
Async XLA Ops:
  1.9 14.9 %collective-permute-start.1 = (f32[8,7,2,128]{3,2,1,0:T(2,128)S(1)}, f32[8,7,2,128]{3,2,1,0:T(2,128)S(1)}, u32[]{:S(2)}, u32[]{:S(2)}) collective-permute-start(f32[8,7,2,128]{3,2,1,0:T(2,128)S(1)} %pad_maximum_fusion.3), channel_id=1, source_target_pairs={{0,28},{4,0},{8,4},{12,8},{16,12},{20,16},{24,20},{28,24},{1,29},{... | collective-permute-start | bytes 172040 | tf_op jit(solution)/shard_map/ppermute | solution.py:38
  2.5 14.3 %collective-permute-start = (f32[8,7,2,128]{3,2,1,0:T(2,128)S(1)}, f32[8,7,2,128]{3,2,1,0:T(2,128)S(1)}, u32[]{:S(2)}, u32[]{:S(2)}) collective-permute-start(f32[8,7,2,128]{3,2,1,0:T(2,128)S(1)} %pad_maximum_fusion.2), channel_id=1, source_target_pairs={{0,4},{4,8},{8,12},{12,16},{16,20},{20,24},{24,28},{28,0},{1,5},{5... | collective-permute-start | bytes 172040 | tf_op jit(solution)/shard_map/ppermute | solution.py:38
  7.3 3.2 %copy-start.15 = (s32[2,1,4]{2,1,0:T(1,128)S(1)}, s32[2,1,4]{2,1,0:T(1,128)}, u32[]{:S(2)}) copy-start(s32[2,1,4]{2,1,0:T(1,128)} %param.13) | copy-start | bytes 100
  10.4 53.2 %collective-permute-start.16 = (bf16[592,1024]{1,0:T(8,128)(2,1)}, bf16[592,1024]{1,0:T(8,128)(2,1)}, u32[]{:S(2)}, u32[]{:S(2)}) collective-permute-start(bf16[592,1024]{1,0:T(8,128)(2,1)} %pack.1), channel_id=1, source_target_pairs={{0,16},{4,20},{8,24},{12,28},{16,0},{20,4},{24,8},{28,12},{1,17},{... | collective-permute-start | bytes 3637256 | tf_op jit(solution)/shard_map/ppermute | solution.py:30
  11.2 5.6 %copy-start = (f32[8,64,6,128]{3,1,2,0:T(8,128)S(1)}, f32[8,64,6,128]{3,1,2,0:T(8,128)}, u32[]{:S(2)}) copy-start(f32[8,64,6,128]{3,1,2,0:T(8,128)} %param.9) | copy-start | bytes 4718596
  14.3 2.4 copy-start.12
  14.3 91.9 %collective-permute-start.5 = (bf16[2,4,128,512]{3,2,1,0:T(8,128)(2,1)}, bf16[2,4,128,512]{3,2,1,0:T(8,128)(2,1)S(1)}, u32[]{:S(2)}, u32[]{:S(2)}) collective-permute-start(bf16[2,4,128,512]{3,2,1,0:T(8,128)(2,1)} %pick_radiances.1), channel_id=1, source_target_pairs={{0,4},{4,0},{8,12},{12,8},{16,20},{20,16},{24,28},{28,24},{1,5},{5... | collective-permute-start | bytes 3145736 | tf_op jit(solution)/shard_map/ppermute | solution.py:30
  15.5 48.1 %copy-start.28 = (bf16[592,1024]{1,0:T(8,128)(2,1)S(1)}, bf16[592,1024]{1,0:T(8,128)(2,1)}, u32[]{:S(2)}) copy-start(bf16[592,1024]{1,0:T(8,128)(2,1)} %pack.1) | copy-start | bytes 3637252
  15.5 52.3 %collective-permute-start.7 = (bf16[288,1024]{1,0:T(8,128)(2,1)S(1)}, bf16[288,1024]{1,0:T(8,128)(2,1)S(1)}, u32[]{:S(2)}, u32[]{:S(2)}) collective-permute-start(bf16[288,1024]{1,0:T(8,128)(2,1)S(1)} %slice.64), channel_id=1, source_target_pairs={{0,8},{4,12},{8,0},{12,4},{16,24},{20,28},{24,16},{28,20},{1,9},{5... | collective-permute-start | bytes 1769480 | tf_op jit(solution)/shard_map/ppermute | solution.py:30
  16.8 57.6 %copy-start.13 = (s32[2,8]{1,0:T(2,128)S(1)}, s32[2,8]{1,0:T(2,128)}, u32[]{:S(2)}) copy-start(s32[2,8]{1,0:T(2,128)} %select_reduce_fusion.table) | copy-start | bytes 196
  16.8 57.6 %copy-start.14 = (s32[2]{0:T(128)S(1)}, s32[2]{0:T(128)}, u32[]{:S(2)}) copy-start(s32[2]{0:T(128)} %pad_add_fusion.pos) | copy-start | bytes 28
  16.9 48.9 %collective-permute-start.2 = (f32[2,7,68,128]{3,2,1,0:T(8,128)S(1)}, f32[2,7,68,128]{3,2,1,0:T(8,128)S(1)}, u32[]{:S(2)}, u32[]{:S(2)}) collective-permute-start(f32[2,7,68,128]{3,2,1,0:T(8,128)S(1)} %pad_maximum_fusion), channel_id=1, source_target_pairs={{0,1},{1,2},{2,3},{4,5},{5,6},{6,7},{8,9},{9,10},{10,11},{12,13},{... | collective-permute-start | bytes 1462280 | tf_op jit(solution)/shard_map/ppermute | solution.py:38
  63.6 45.0 %collective-permute-start.21 = (bf16[592,1024]{1,0:T(8,128)(2,1)}, bf16[592,1024]{1,0:T(8,128)(2,1)S(1)}, u32[]{:S(2)}, u32[]{:S(2)}) collective-permute-start(bf16[592,1024]{1,0:T(8,128)(2,1)} %collective-permute-done.16.refs_2_), channel_id=1, source_target_pairs={{0,8},{4,12},{8,0},{12,4},{16,24},{20,28},{24,16},{28,20},{1,9},{5... | collective-permute-start | bytes 3637256 | tf_op jit(solution)/shard_map/ppermute | solution.py:30
  63.7 42.1 %collective-permute-start.8 = (bf16[304,1024]{1,0:T(8,128)(2,1)S(1)}, bf16[304,1024]{1,0:T(8,128)(2,1)S(1)}, u32[]{:S(2)}, u32[]{:S(2)}) collective-permute-start(bf16[304,1024]{1,0:T(8,128)(2,1)S(1)} %slice.65), channel_id=1, source_target_pairs={{0,8},{4,12},{8,0},{12,4},{16,24},{20,28},{24,16},{28,20},{1,9},{5... | collective-permute-start | bytes 1867784 | tf_op jit(solution)/shard_map/ppermute | solution.py:30
  65.8 122.3 %copy-start.1 = (bf16[2,8,64,512]{3,2,1,0:T(8,128)(2,1)S(1)}, bf16[2,8,64,512]{3,2,1,0:T(8,128)(2,1)}, u32[]{:S(2)}) copy-start(bf16[2,8,64,512]{3,2,1,0:T(8,128)(2,1)} %param.12) | copy-start | bytes 3145732
  65.8 122.3 %copy-start.16 = (f32[1,512]{1,0:T(1,128)S(1)}, f32[1,512]{1,0:T(1,128)}, u32[]{:S(2)}) copy-start(f32[1,512]{1,0:T(1,128)} %scale.1) | copy-start | bytes 6148
  65.8 8.6 %collective-permute-start.3 = (f32[2,7,68,128]{3,2,1,0:T(8,128)S(1)}, f32[2,7,68,128]{3,2,1,0:T(8,128)S(1)}, u32[]{:S(2)}, u32[]{:S(2)}) collective-permute-start(f32[2,7,68,128]{3,2,1,0:T(8,128)S(1)} %pad_maximum_fusion.1), channel_id=1, source_target_pairs={{1,0},{2,1},{3,2},{5,4},{6,5},{7,6},{9,8},{10,9},{11,10},{13,12},{... | collective-permute-start | bytes 1462280 | tf_op jit(solution)/shard_map/ppermute | solution.py:38
  67.9 119.6 %copy-start.19 = (bf16[288,1024]{1,0:T(8,128)(2,1)}, bf16[288,1024]{1,0:T(8,128)(2,1)S(1)}, u32[]{:S(2)}) copy-start(bf16[288,1024]{1,0:T(8,128)(2,1)S(1)} %collective-permute-done.7.refs_2_) | copy-start | bytes 1769476
  67.9 39.9 %collective-permute-start.9 = (bf16[288,1024]{1,0:T(8,128)(2,1)S(1)}, bf16[288,1024]{1,0:T(8,128)(2,1)S(1)}, u32[]{:S(2)}, u32[]{:S(2)}) collective-permute-start(bf16[288,1024]{1,0:T(8,128)(2,1)S(1)} %collective-permute-done.7.refs_2_), channel_id=1, source_target_pairs={{0,1},{1,0},{2,3},{3,2},{4,5},{5,4},{6,7},{7,6},{8,9},{9,8},{10,11... | collective-permute-start | bytes 1769480 | tf_op jit(solution)/shard_map/ppermute | solution.py:30
  79.3 1.1 copy-start.3
  80.5 1.4 copy-start.6
  81.9 105.0 %collective-permute-start.4 = (bf16[2,4,128,768]{3,2,1,0:T(8,128)(2,1)S(1)}, bf16[2,4,128,768]{3,2,1,0:T(8,128)(2,1)S(1)}, u32[]{:S(2)}, u32[]{:S(2)}) collective-permute-start(bf16[2,4,128,768]{3,2,1,0:T(8,128)(2,1)S(1)} %get-tuple-element.30), channel_id=1, source_target_pairs={{0,4},{4,0},{8,12},{12,8},{16,20},{20,16},{24,28},{28,24},{1,5},{5... | collective-permute-start | bytes 4718600 | tf_op jit(solution)/shard_map/ppermute | solution.py:30
  105.8 93.5 %copy-start.17 = (bf16[304,1024]{1,0:T(8,128)(2,1)}, bf16[304,1024]{1,0:T(8,128)(2,1)S(1)}, u32[]{:S(2)}) copy-start(bf16[304,1024]{1,0:T(8,128)(2,1)S(1)} %collective-permute-done.8.refs_3_) | copy-start | bytes 1867780
  105.8 16.2 %collective-permute-start.11 = (bf16[288,1024]{1,0:T(8,128)(2,1)S(1)}, bf16[288,1024]{1,0:T(8,128)(2,1)S(1)}, u32[]{:S(2)}, u32[]{:S(2)}) collective-permute-start(bf16[288,1024]{1,0:T(8,128)(2,1)S(1)} %collective-permute-done.7.refs_2_), channel_id=1, source_target_pairs={{0,2},{1,3},{2,0},{3,1},{4,6},{5,7},{6,4},{7,5},{8,10},{9,11},{10,... | collective-permute-start | bytes 1769480 | tf_op jit(solution)/shard_map/ppermute | solution.py:30
  106.3 93.0 %copy-start.4 = (bf16[2,4,128,512]{3,2,1,0:T(8,128)(2,1)}, bf16[2,4,128,512]{3,2,1,0:T(8,128)(2,1)S(1)}, u32[]{:S(2)}) copy-start(bf16[2,4,128,512]{3,2,1,0:T(8,128)(2,1)S(1)} %collective-permute-done.5.refs_1_) | copy-start | bytes 3145732
  106.3 79.3 %collective-permute-start.18 = (bf16[592,1024]{1,0:T(8,128)(2,1)}, bf16[592,1024]{1,0:T(8,128)(2,1)}, u32[]{:S(2)}, u32[]{:S(2)}) collective-permute-start(bf16[592,1024]{1,0:T(8,128)(2,1)} %collective-permute-done.16.refs_2_), channel_id=1, source_target_pairs={{0,2},{1,3},{2,0},{3,1},{4,6},{5,7},{6,4},{7,5},{8,10},{9,11},{10,... | collective-permute-start | bytes 3637256 | tf_op jit(solution)/shard_map/ppermute | solution.py:30
  107.8 0.8 copy-start.21
  108.6 13.9 %collective-permute-start.10 = (bf16[304,1024]{1,0:T(8,128)(2,1)S(1)}, bf16[304,1024]{1,0:T(8,128)(2,1)}, u32[]{:S(2)}, u32[]{:S(2)}) collective-permute-start(bf16[304,1024]{1,0:T(8,128)(2,1)S(1)} %collective-permute-done.8.refs_3_), channel_id=1, source_target_pairs={{0,1},{1,0},{2,3},{3,2},{4,5},{5,4},{6,7},{7,6},{8,9},{9,8},{10,11... | collective-permute-start | bytes 1867784 | tf_op jit(solution)/shard_map/ppermute | solution.py:30
  108.6 78.8 %collective-permute-start.23 = (bf16[592,1024]{1,0:T(8,128)(2,1)S(1)}, bf16[592,1024]{1,0:T(8,128)(2,1)}, u32[]{:S(2)}, u32[]{:S(2)}) collective-permute-start(bf16[592,1024]{1,0:T(8,128)(2,1)S(1)} %collective-permute-done.21.refs_2_), channel_id=1, source_target_pairs={{0,2},{1,3},{2,0},{3,1},{4,6},{5,7},{6,4},{7,5},{8,10},{9,11},{10,... | collective-permute-start | bytes 3637256 | tf_op jit(solution)/shard_map/ppermute | solution.py:30
  122.0 77.3 %copy-start.23 = (bf16[288,1024]{1,0:T(8,128)(2,1)}, bf16[288,1024]{1,0:T(8,128)(2,1)S(1)}, u32[]{:S(2)}) copy-start(bf16[288,1024]{1,0:T(8,128)(2,1)S(1)} %collective-permute-done.11.refs_6_) | copy-start | bytes 1769476
  122.0 63.6 %collective-permute-start.12 = (bf16[304,1024]{1,0:T(8,128)(2,1)S(1)}, bf16[304,1024]{1,0:T(8,128)(2,1)}, u32[]{:S(2)}, u32[]{:S(2)}) collective-permute-start(bf16[304,1024]{1,0:T(8,128)(2,1)S(1)} %collective-permute-done.8.refs_3_), channel_id=1, source_target_pairs={{0,2},{1,3},{2,0},{3,1},{4,6},{5,7},{6,4},{7,5},{8,10},{9,11},{10,... | collective-permute-start | bytes 1867784 | tf_op jit(solution)/shard_map/ppermute | solution.py:30
  122.5 63.6 %collective-permute-start.13 = (bf16[288,1024]{1,0:T(8,128)(2,1)S(1)}, bf16[288,1024]{1,0:T(8,128)(2,1)S(1)}, u32[]{:S(2)}, u32[]{:S(2)}) collective-permute-start(bf16[288,1024]{1,0:T(8,128)(2,1)S(1)} %collective-permute-done.11.refs_6_), channel_id=1, source_target_pairs={{0,1},{1,0},{2,3},{3,2},{4,5},{5,4},{6,7},{7,6},{8,9},{9,8},{10,11... | collective-permute-start | bytes 1769480 | tf_op jit(solution)/shard_map/ppermute | solution.py:30
  185.6 29.4 %collective-permute-start.17 = (bf16[592,1024]{1,0:T(8,128)(2,1)}, bf16[592,1024]{1,0:T(8,128)(2,1)}, u32[]{:S(2)}, u32[]{:S(2)}) collective-permute-start(bf16[592,1024]{1,0:T(8,128)(2,1)} %collective-permute-done.16.refs_2_), channel_id=1, source_target_pairs={{0,1},{1,0},{2,3},{3,2},{4,5},{5,4},{6,7},{7,6},{8,9},{9,8},{10,11... | collective-permute-start | bytes 3637256 | tf_op jit(solution)/shard_map/ppermute | solution.py:30
  185.6 31.4 %collective-permute-start.19 = (bf16[592,1024]{1,0:T(8,128)(2,1)}, bf16[592,1024]{1,0:T(8,128)(2,1)}, u32[]{:S(2)}, u32[]{:S(2)}) collective-permute-start(bf16[592,1024]{1,0:T(8,128)(2,1)} %collective-permute-done.18.refs_4_), channel_id=1, source_target_pairs={{0,1},{1,0},{2,3},{3,2},{4,5},{5,4},{6,7},{7,6},{8,9},{9,8},{10,11... | collective-permute-start | bytes 3637256 | tf_op jit(solution)/shard_map/ppermute | solution.py:30
  186.1 0.8 copy-start.25
  186.9 12.4 %collective-permute-start.14 = (bf16[304,1024]{1,0:T(8,128)(2,1)}, bf16[304,1024]{1,0:T(8,128)(2,1)}, u32[]{:S(2)}, u32[]{:S(2)}) collective-permute-start(bf16[304,1024]{1,0:T(8,128)(2,1)} %collective-permute-done.12.refs_7_), channel_id=1, source_target_pairs={{0,1},{1,0},{2,3},{3,2},{4,5},{5,4},{6,7},{7,6},{8,9},{9,8},{10,11... | collective-permute-start | bytes 1867784 | tf_op jit(solution)/shard_map/ppermute | solution.py:30
  186.9 1.2 copy-start.27
  186.9 39.9 %collective-permute-start.22 = (bf16[592,1024]{1,0:T(8,128)(2,1)S(1)}, bf16[592,1024]{1,0:T(8,128)(2,1)}, u32[]{:S(2)}, u32[]{:S(2)}) collective-permute-start(bf16[592,1024]{1,0:T(8,128)(2,1)S(1)} %collective-permute-done.21.refs_2_), channel_id=1, source_target_pairs={{0,1},{1,0},{2,3},{3,2},{4,5},{5,4},{6,7},{7,6},{8,9},{9,8},{10,11... | collective-permute-start | bytes 3637256 | tf_op jit(solution)/shard_map/ppermute | solution.py:30
  187.4 39.3 %collective-permute-start.24 = (bf16[592,1024]{1,0:T(8,128)(2,1)}, bf16[592,1024]{1,0:T(8,128)(2,1)}, u32[]{:S(2)}, u32[]{:S(2)}) collective-permute-start(bf16[592,1024]{1,0:T(8,128)(2,1)} %collective-permute-done.23.refs_4_), channel_id=1, source_target_pairs={{0,1},{1,0},{2,3},{3,2},{4,5},{5,4},{6,7},{7,6},{8,9},{9,8},{10,11... | collective-permute-start | bytes 3637256 | tf_op jit(solution)/shard_map/ppermute | solution.py:30
  188.1 1.2 copy-start.11
  199.3 17.6 %copy-start.2 = (bf16[2,8,64,512]{3,2,1,0:T(8,128)(2,1)S(1)}, bf16[2,8,64,512]{3,2,1,0:T(8,128)(2,1)}, u32[]{:S(2)}) copy-start(bf16[2,8,64,512]{3,2,1,0:T(8,128)(2,1)} %param.12) | copy-start | bytes 3145732
  199.3 17.6 %copy-start.5 = (bf16[2,4,128,512]{3,2,1,0:T(8,128)(2,1)S(1)}, bf16[2,4,128,512]{3,2,1,0:T(8,128)(2,1)}, u32[]{:S(2)}) copy-start(bf16[2,4,128,512]{3,2,1,0:T(8,128)(2,1)} %copy-done.4) | copy-start | bytes 3145732
  199.3 41.2 %collective-permute-start.6 = (bf16[2,128,768]{2,1,0:T(8,128)(2,1)}, bf16[2,128,768]{2,1,0:T(8,128)(2,1)S(1)}, u32[]{:S(2)}, u32[]{:S(2)}) collective-permute-start(bf16[2,128,768]{2,1,0:T(8,128)(2,1)} %get-tuple-element.32), channel_id=1, source_target_pairs={{0,4},{4,0},{8,12},{12,8},{16,20},{20,16},{24,28},{28,24},{1,5},{5... | collective-permute-start | bytes 1179656 | tf_op jit(solution)/shard_map/ppermute | solution.py:30
  199.4 1.2 copy-start.18
  200.6 1.1 copy-start.20
  201.7 1.1 copy-start.22
  202.7 1.1 copy-start.24
  203.8 1.1 copy-start.26
  214.9 26.9 %copy-start.9 = (bf16[2,128,768]{2,1,0:T(8,128)(2,1)}, bf16[2,128,768]{2,1,0:T(8,128)(2,1)S(1)}, u32[]{:S(2)}) copy-start(bf16[2,128,768]{2,1,0:T(8,128)(2,1)S(1)} %get-tuple-element.33.refs_2_) | copy-start | bytes 1179652
  215.0 25.5 %collective-permute-start.15 = (bf16[2,128,768]{2,1,0:T(8,128)(2,1)}, bf16[2,128,768]{2,1,0:T(8,128)(2,1)S(1)}, u32[]{:S(2)}, u32[]{:S(2)}) collective-permute-start(bf16[2,128,768]{2,1,0:T(8,128)(2,1)} %get-tuple-element.34), channel_id=1, source_target_pairs={{0,4},{4,0},{8,12},{12,8},{16,20},{20,16},{24,28},{28,24},{1,5},{5... | collective-permute-start | bytes 1179656 | tf_op jit(solution)/shard_map/ppermute | solution.py:30
  226.6 13.9 %collective-permute-start.20 = (bf16[2,128,768]{2,1,0:T(8,128)(2,1)S(1)}, bf16[2,128,768]{2,1,0:T(8,128)(2,1)S(1)}, u32[]{:S(2)}, u32[]{:S(2)}) collective-permute-start(bf16[2,128,768]{2,1,0:T(8,128)(2,1)S(1)} %get-tuple-element.36), channel_id=1, source_target_pairs={{0,4},{4,0},{8,12},{12,8},{16,20},{20,16},{24,28},{28,24},{1,5},{5... | collective-permute-start | bytes 1179656 | tf_op jit(solution)/shard_map/ppermute | solution.py:30
  232.5 9.2 %collective-permute-start.25 = (bf16[1,128,768]{2,1,0:T(8,128)(2,1)S(1)}, bf16[1,128,768]{2,1,0:T(8,128)(2,1)S(1)}, u32[]{:S(2)}, u32[]{:S(2)}) collective-permute-start(bf16[1,128,768]{2,1,0:T(8,128)(2,1)S(1)} %get-tuple-element.38), channel_id=1, source_target_pairs={{0,4},{4,0},{8,12},{12,8},{16,20},{20,16},{24,28},{28,24},{1,5},{5... | collective-permute-start | bytes 589832 | tf_op jit(solution)/shard_map/ppermute | solution.py:30
  240.3 10.2 %collective-permute-start.30 = (bf16[1,128,768]{2,1,0:T(8,128)(2,1)S(1)}, bf16[1,128,768]{2,1,0:T(8,128)(2,1)S(1)}, u32[]{:S(2)}, u32[]{:S(2)}) collective-permute-start(bf16[1,128,768]{2,1,0:T(8,128)(2,1)S(1)} %get-tuple-element.47), channel_id=1, source_target_pairs={{0,4},{4,0},{8,12},{12,8},{16,20},{20,16},{24,28},{28,24},{1,5},{5... | collective-permute-start | bytes 589832 | tf_op jit(solution)/shard_map/ppermute | solution.py:30
  242.8 12.6 %collective-permute-start.26 = (bf16[6,64,128]{2,1,0:T(8,128)(2,1)S(1)}, bf16[6,64,128]{2,1,0:T(8,128)(2,1)S(1)}, u32[]{:S(2)}, u32[]{:S(2)}) collective-permute-start(bf16[6,64,128]{2,1,0:T(8,128)(2,1)S(1)} %get-tuple-element.40), channel_id=1, source_target_pairs={{0,1},{1,2},{2,3},{4,5},{5,6},{6,7},{8,9},{9,10},{10,11},{12,13},{... | collective-permute-start | bytes 294920 | tf_op jit(solution)/shard_map/ppermute | solution.py:38
  244.7 10.7 %collective-permute-start.27 = (bf16[6,64,128]{2,1,0:T(8,128)(2,1)S(1)}, bf16[6,64,128]{2,1,0:T(8,128)(2,1)S(1)}, u32[]{:S(2)}, u32[]{:S(2)}) collective-permute-start(bf16[6,64,128]{2,1,0:T(8,128)(2,1)S(1)} %get-tuple-element.41), channel_id=1, source_target_pairs={{1,0},{2,1},{3,2},{5,4},{6,5},{7,6},{9,8},{10,9},{11,10},{13,12},{... | collective-permute-start | bytes 294920 | tf_op jit(solution)/shard_map/ppermute | solution.py:38
  248.4 4.1 %collective-permute-start.28 = (f32[8,6,128]{2,1,0:T(8,128)S(1)}, f32[8,6,128]{2,1,0:T(8,128)S(1)}, u32[]{:S(2)}, u32[]{:S(2)}) collective-permute-start(f32[8,6,128]{2,1,0:T(8,128)S(1)} %get-tuple-element.42), channel_id=1, source_target_pairs={{0,4},{4,8},{8,12},{12,16},{16,20},{20,24},{24,28},{28,0},{1,5},{5... | collective-permute-start | bytes 73736 | tf_op jit(solution)/shard_map/ppermute | solution.py:38
  248.8 6.6 %collective-permute-start.29 = (f32[8,6,128]{2,1,0:T(8,128)S(1)}, f32[8,6,128]{2,1,0:T(8,128)S(1)}, u32[]{:S(2)}, u32[]{:S(2)}) collective-permute-start(f32[8,6,128]{2,1,0:T(8,128)S(1)} %get-tuple-element.43), channel_id=1, source_target_pairs={{0,28},{4,0},{8,4},{12,8},{16,12},{20,16},{24,20},{28,24},{1,29},{... | collective-permute-start | bytes 73736 | tf_op jit(solution)/shard_map/ppermute | solution.py:38
  250.5 1.0 copy-start.10
  251.5 4.0 %copy-start.7 = (f32[10,6,80,128]{3,2,1,0:T(8,128)S(1)}, f32[10,6,80,128]{3,2,1,0:T(8,128)}, u32[]{:S(2)}) copy-start(f32[10,6,80,128]{3,2,1,0:T(8,128)} %copy-done.6) | copy-start | bytes 7372804
  255.5 15.1 %copy-start.8 = (f32[8,64,6,128]{3,1,2,0:T(8,128)S(1)}, f32[8,64,6,128]{3,1,2,0:T(8,128)}, u32[]{:S(2)}) copy-start(f32[8,64,6,128]{3,1,2,0:T(8,128)} %param.10) | copy-start | bytes 4718596
  257.5 13.0 %collective-permute-start.31 = (f32[6,64,128]{2,1,0:T(8,128)S(1)}, f32[6,64,128]{2,1,0:T(8,128)S(1)}, u32[]{:S(2)}, u32[]{:S(2)}) collective-permute-start(f32[6,64,128]{2,1,0:T(8,128)S(1)} %get-tuple-element.49), channel_id=1, source_target_pairs={{0,1},{1,2},{2,3},{4,5},{5,6},{6,7},{8,9},{9,10},{10,11},{12,13},{... | collective-permute-start | bytes 589832 | tf_op jit(solution)/shard_map/ppermute | solution.py:38
  259.4 11.1 %collective-permute-start.32 = (f32[6,64,128]{2,1,0:T(8,128)S(1)}, f32[6,64,128]{2,1,0:T(8,128)S(1)}, u32[]{:S(2)}, u32[]{:S(2)}) collective-permute-start(f32[6,64,128]{2,1,0:T(8,128)S(1)} %get-tuple-element.50), channel_id=1, source_target_pairs={{1,0},{2,1},{3,2},{5,4},{6,5},{7,6},{9,8},{10,9},{11,10},{13,12},{... | collective-permute-start | bytes 589832 | tf_op jit(solution)/shard_map/ppermute | solution.py:38
  263.1 4.0 %collective-permute-start.33 = (f32[8,6,128]{2,1,0:T(8,128)S(1)}, f32[8,6,128]{2,1,0:T(8,128)S(1)}, u32[]{:S(2)}, u32[]{:S(2)}) collective-permute-start(f32[8,6,128]{2,1,0:T(8,128)S(1)} %get-tuple-element.51), channel_id=1, source_target_pairs={{0,4},{4,8},{8,12},{12,16},{16,20},{20,24},{24,28},{28,0},{1,5},{5... | collective-permute-start | bytes 73736 | tf_op jit(solution)/shard_map/ppermute | solution.py:38
  263.9 6.6 %collective-permute-start.34 = (f32[8,6,128]{2,1,0:T(8,128)S(1)}, f32[8,6,128]{2,1,0:T(8,128)S(1)}, u32[]{:S(2)}, u32[]{:S(2)}) collective-permute-start(f32[8,6,128]{2,1,0:T(8,128)S(1)} %get-tuple-element.52), channel_id=1, source_target_pairs={{0,28},{4,0},{8,4},{12,8},{16,12},{20,16},{24,20},{28,24},{1,29},{... | collective-permute-start | bytes 73736 | tf_op jit(solution)/shard_map/ppermute | solution.py:38

commit v3 on v2

--- a/solution.py
+++ b/solution.py
@@ -12,7 +12,6 @@
 SERVED = 4
 EDGE = 16
 SIDE = 8
-CHUNKED = (1,)
 TAIL = 16
 ANY = pl.BlockSpec(memory_space=pl.ANY)
 SMEM = pl.BlockSpec(memory_space=pltpu.SMEM)
@@ -45,25 +44,38 @@
         bit //= 2
 
 
-def pack_kernel(pos, w1, w2, w3, scale, out, sems):
+def packed_rows(w1, w2, w3, n_lat):
+    return (w1.shape[0] // n_lat, w2.shape[0] // n_lat, w3.shape[0] * w3.shape[1] // (w2.shape[1] * n_lat), TAIL)
+
+
+def fetches(sources, bounds, first, last, lanes, target, base):
+    for source, (low, high) in zip(sources, bounds):
+        a, b = max(first, low), min(last, high)
+        if a < b:
+            begin = base + (a - first)
+            if not isinstance(begin, int):
+                begin = pl.multiple_of(begin, 16)
+            yield source.at[pl.ds(a - low, b - a), lanes], target.at[pl.ds(begin, b - a)]
+
+
+def pack_kernel(n_lat, bounds, pos, w1, w2, w3, scale, *refs):
+    *outs, sems = refs
     lat = pos[1]
-    width = out.shape[1]
+    width = outs[0].shape[1]
+    r1, r2, piece, _ = packed_rows(w1, w2, w3, n_lat)
     parts = width // w3.shape[1]
-    n_lat = pos_lat(w1, w2, w3, out)
-    r1, r2, r3 = (w.shape[0] // n_lat for w in (w1, w2, w3))
-    copies = [
-        pltpu.make_async_copy(w1.at[pl.ds(lat * r1, r1)], out.at[pl.ds(0, r1)], sems.at[0]),
-        pltpu.make_async_copy(w2.at[pl.ds(lat * r2, r2)], out.at[pl.ds(r1, r2)], sems.at[1]),
-    ]
-    piece = r3 // parts
+    ends = (r1, r1 + r2, r1 + r2 + piece, r1 + r2 + piece + TAIL)
+    copies = []
+
+    def put(first, last, lanes, source, base):
+        for at, onto in fetches(outs, bounds, first, last, lanes, source, base):
+            copies.append(pltpu.make_async_copy(onto, at, sems.at[len(copies)]))
+
+    everything = pl.ds(0, width)
+    put(0, ends[0], everything, w1, lat * r1)
+    put(ends[0], ends[1], everything, w2, lat * r2)
     for j in range(parts):
-        copies.append(
-            pltpu.make_async_copy(
-                w3.at[pl.ds(lat * r3 + j * piece, piece)],
-                out.at[pl.ds(r1 + r2, piece), pl.ds(j * w3.shape[1], w3.shape[1])],
-                sems.at[2 + j],
-            )
-        )
+        put(ends[1], ends[2], pl.ds(j * w3.shape[1], w3.shape[1]), w3, (lat * parts + j) * piece)
     for copy in copies:
         copy.start()
     whole = scale[...]
@@ -71,43 +83,38 @@
     rest = whole - high
     middle = rest.astype(BF16).astype(F32)
     low = rest - middle
-    tail = slice(r1 + r2 + piece, out.shape[0])
     rows = lax.broadcasted_iota(jnp.int32, (TAIL, scale.shape[1]), 0)
     stacked = jnp.where(rows == 0, high, jnp.where(rows == 1, middle, low))
-    out[tail] = jnp.zeros((TAIL, width), BF16)
-    out[tail, 0 : scale.shape[1]] = jnp.where(rows < 3, stacked, 0.0).astype(BF16)
+    for out, (low_row, high_row) in zip(outs, bounds):
+        if high_row == ends[3]:
+            tail = slice(ends[2] - low_row, ends[3] - low_row)
+            out[tail] = jnp.zeros((TAIL, width), BF16)
+            out[tail, 0 : scale.shape[1]] = jnp.where(rows < 3, stacked, 0.0).astype(BF16)
     for copy in copies:
         copy.wait()
-
-
-def pos_lat(w1, w2, w3, out):
-    body = out.shape[0] - TAIL
-    return (w1.shape[0] + w2.shape[0] + w3.shape[0] * w3.shape[1] // out.shape[1]) // body
 
 
 def pack_weights(pos, weights, n_lat):
     w1, w2, w3, scale = weights
     width = w1.shape[1]
-    parts = width // w3.shape[1]
-    rows = (w1.shape[0] + w2.shape[0] + w3.shape[0] // parts) // n_lat + TAIL
+    rows = sum(packed_rows(w1, w2, w3, n_lat))
+    half = rows // (2 * TAIL) * TAIL
+    bounds = ((0, half), (half, rows))
     return pl.pallas_call(
-        pack_kernel,
-        out_shape=jax.ShapeDtypeStruct((rows, width), BF16),
+        functools.partial(pack_kernel, n_lat, bounds),
+        out_shape=[jax.ShapeDtypeStruct((b - a, width), BF16) for a, b in bounds],
         in_specs=[SMEM, ANY, ANY, ANY, VMEM],
-        out_specs=VMEM,
-        scratch_shapes=[pltpu.SemaphoreType.DMA((2 + parts,))],
+        out_specs=[VMEM] * len(bounds),
+        scratch_shapes=[pltpu.SemaphoreType.DMA((16,))],
         name="pack",
     )(pos, w1, w2, w3, scale)
 
 
 def spread_weights(packed, group, n_lon, n_lat):
-    rows = packed.shape[0]
-    half = rows // (2 * TAIL) * TAIL
-    found = {0: (packed,)}
+    found = {0: packed}
     bits = sorted(bits_down(n_lon // group))
     for bit in bits:
-        chunks = (packed[:half], packed[half:]) if bit in CHUNKED else (packed,)
-        found[bit] = tuple(exchange(a, "lon", bit * group) for a in chunks)
+        found[bit] = tuple(exchange(a, "lon", bit * group) for a in packed)
     for far in range(n_lon // group):
         if far not in found:
             bottom = far & -far
@@ -124,25 +131,13 @@
     return gathered
 
 
-def radiance_kernel(group, pos, table, source, *refs):
-    *outs, sems = refs
+def radiance_kernel(group, pos, table, source, *outs):
     slots, served, span, _ = outs[0].shape
-    copies = []
     for c, out in enumerate(outs, 1):
         for s in range(slots):
             for w in range(served):
                 block = table[s, pos[0] ^ (w * group + c)]
-                copies.append(
-                    pltpu.make_async_copy(
-                        source.at[s, pl.ds(pl.multiple_of(block * span, span), span)],
-                        out.at[s, w],
-                        sems.at[len(copies)],
-                    )
-                )
-    for copy in copies:
-        copy.start()
-    for copy in copies:
-        copy.wait()
+                out[s, w] = source[s, pl.ds(pl.multiple_of(block * span, span), span)]
 
 
 def send_radiances(pos, table, radiances, group, served, span):
@@ -151,9 +146,8 @@
     return pl.pallas_call(
         functools.partial(radiance_kernel, group),
         out_shape=[shape] * (group - 1),
-        in_specs=[SMEM, SMEM, ANY],
+        in_specs=[SMEM, SMEM, VMEM],
         out_specs=[VMEM] * (group - 1),
-        scratch_shapes=[pltpu.SemaphoreType.DMA(((group - 1) * slots * served,))],
         name="pick_radiances",
     )(pos, table, radiances)
 
@@ -260,7 +254,7 @@
         out_shape=outs,
         in_specs=[SMEM, SMEM] + [VMEM] * 6,
         out_specs=[VMEM] * len(outs),
-        compiler_params=params(40),
+        compiler_params=params(16),
         name="forward",
     )(pos, table, state, kappa, *rims)
 
@@ -382,7 +376,7 @@
         + [kappa_spec, whole(forcing.shape)],
         out_specs=[whole(adjoint.shape), whole(line.shape), whole(line.shape), whole(side.shape), whole(side.shape)],
         scratch_shapes=[pltpu.VMEM((rows + 2, fields, width + 2 * EDGE, levels), F32)],
-        compiler_params=params(40),
+        compiler_params=params(16),
         name="backward_first",
     )(adjoint, *rims, first, wide, forcing)
     return out, edges
@@ -396,7 +390,7 @@
         in_specs=[VMEM] * 8,
         out_specs=VMEM,
         scratch_shapes=[pltpu.VMEM((rows + 2, fields, width + 2 * EDGE, levels), F32)],
-        compiler_params=params(40),
+        compiler_params=params(16),
         name="backward_last",
     )(adjoint, *rims, wide, state, background)
 
@@ -413,65 +407,45 @@
     n_weights = 4 if own_weights else n_lat * len(bounds)
     weights, refs = refs[:n_weights], refs[n_weights:]
     outs, refs = refs[:group], refs[group:]
-    x, y, w1, w2, w3, scale, a1, s1, a2, s2, mis, sem_x, sem_y, sem_w = refs
+    x, y, a1, s1, a2, s2, mis, *built = refs
     slots, span, _ = outs[0].shape
     tile = 256
-    copies_x, copies_y = [], []
     for c in range(group):
         for k, s in enumerate(chosen):
             j = c * slots + k
+            lines = slice(j * span, (j + 1) * span)
             if c == 0:
                 block = table[s, pos[0] ^ (served * group)]
-                lines = pl.ds(pl.multiple_of(block * span, span), span)
-                from_x, from_y = columns.at[s, lines], radiances.at[s, lines]
+                at = pl.ds(pl.multiple_of(block * span, span), span)
+                x[lines] = columns[s, at]
+                y[lines] = radiances[s, at]
             else:
-                from_x, from_y = got_columns[c - 1].at[s, served], got_radiances[c - 1].at[s, served]
-            copies_x.append(pltpu.make_async_copy(from_x, x.at[pl.ds(j * span, span)], sem_x.at[j]))
-            copies_y.append(pltpu.make_async_copy(from_y, y.at[pl.ds(j * span, span)], sem_y.at[j]))
-    phases = [[], [], []]
+                x[lines] = got_columns[c - 1][s, served]
+                y[lines] = got_radiances[c - 1][s, served]
     if own_weights:
-        for k, (source, target) in enumerate(zip(weights, (w1, w2, w3))):
-            phases[k].append(pltpu.make_async_copy(source, target, sem_w.at[k]))
-        phases[2].append(pltpu.make_async_copy(weights[3], scale, sem_w.at[3]))
+        w1, w2, w3, scale = weights
+        factor = scale[...]
     else:
-        parts = w1.shape[1] // w3.shape[1]
-        r1, r2, r3 = (w.shape[0] // n_lat for w in (w1, w2, w3))
-        piece = r3 // parts
-        count = 0
+        w1, w2, w3 = built
+        r1, r2, piece, _ = packed_rows(w1, w2, w3, n_lat)
+        parts = w2.shape[1] // w3.shape[1]
+        ends = (r1, r1 + r2, r1 + r2 + piece)
+        everything = pl.ds(0, w1.shape[1])
+
+        def fetch(first, last, lanes, target, base):
+            for source, onto in fetches(sources, bounds, first, last, lanes, target, base):
+                onto[...] = source[...]
+
         for near in range(n_lat):
             lat = pos[1] ^ near
             sources = weights[near * len(bounds) : (near + 1) * len(bounds)]
-
-            def fetch(phase, first, last, lanes, target, base):
-                nonlocal count
-                for source, (low, high) in zip(sources, bounds):
-                    a, b = max(first, low), min(last, high)
-                    if a < b:
-                        begin = base + (a - first)
-                        if not isinstance(begin, int):
-                            begin = pl.multiple_of(begin, 16)
-                        phases[phase].append(
-                            pltpu.make_async_copy(
-                                source.at[pl.ds(a - low, b - a), lanes],
-                                target.at[pl.ds(begin, b - a)],
-                                sem_w.at[count],
-                            )
-                        )
-                        count += 1
-
-            everything = pl.ds(0, w1.shape[1])
-            ends = (r1, r1 + r2, r1 + r2 + piece)
-            fetch(0, 0, ends[0], everything, w1, lat * r1)
-            fetch(1, ends[0], ends[1], everything, w2, lat * r2)
+            fetch(0, ends[0], everything, w1, lat * r1)
+            fetch(ends[0], ends[1], everything, w2, lat * r2)
             for p in range(parts):
-                lanes = pl.ds(p * w3.shape[1], w3.shape[1])
-                fetch(2, ends[1], ends[2], lanes, w3, lat * r3 + p * piece)
-            if near == 0:
-                fetch(2, ends[2], ends[2] + TAIL, pl.ds(0, w3.shape[1]), scale, 0)
-    for copy in copies_x + phases[0] + phases[1] + phases[2] + copies_y:
-        copy.start()
-    for copy in copies_x + phases[0]:
-        copy.wait()
+                fetch(ends[1], ends[2], pl.ds(p * w3.shape[1], w3.shape[1]), w3, (lat * parts + p) * piece)
+        last, low = weights[len(bounds) - 1], bounds[-1][0]
+        triple = last[ends[2] - low : ends[2] - low + TAIL, 0 : w3.shape[1]].astype(F32)
+        factor = triple[0:1] + triple[1:2] + triple[2:3]
 
     def hidden(source, weight, act, slope):
         def column(n, _):
@@ -487,16 +461,7 @@
         lax.fori_loop(0, weight.shape[1] // tile, column, 0, unroll=True)
 
     hidden(x, w1, a1, s1)
-    for copy in phases[1]:
-        copy.wait()
     hidden(a1, w2, a2, s2)
-    for copy in phases[2] + copies_y:
-        copy.wait()
-    if not own_weights:
-        triple = scale[...].astype(F32)
-        factor = triple[0:1] + triple[1:2] + triple[2:3]
-    else:
-        factor = scale[...]
     for n in range(w3.shape[1] // tile):
         at = slice(n * tile, (n + 1) * tile)
         evolved = jnp.dot(a2[...], w3[:, at], preferred_element_type=F32)
@@ -532,29 +497,22 @@
         weights = [chunk for near in range(n_lat) for chunk in weights[near]]
     lines = group * slots * span
     out = jax.ShapeDtypeStruct((slots, span, cin), BF16)
-    parts = h1 // ch
     return pl.pallas_call(
         functools.partial(instrument_kernel, group, served, n_lat, chosen, tuple(bounds)),
         out_shape=[out] * group,
-        in_specs=[SMEM, SMEM] + [ANY] * (2 + 2 * (group - 1) + len(weights)),
+        in_specs=[SMEM, SMEM] + [VMEM] * (2 + 2 * (group - 1) + len(weights)),
         out_specs=[VMEM] * group,
         scratch_shapes=[
             pltpu.VMEM((lines, cin), BF16),
             pltpu.VMEM((lines, ch), BF16),
-            pltpu.VMEM((cin, h1), BF16),
-            pltpu.VMEM((h1, h2), BF16),
-            pltpu.VMEM((h2, ch), BF16),
-            pltpu.VMEM((1, ch), F32) if own else pltpu.VMEM((16, ch), BF16),
             pltpu.VMEM((lines, h1), BF16),
             pltpu.VMEM((lines, h1), F32),
             pltpu.VMEM((lines, h2), BF16),
             pltpu.VMEM((lines, h2), F32),
             pltpu.VMEM((lines, ch), BF16),
-            pltpu.SemaphoreType.DMA((group * slots,)),
-            pltpu.SemaphoreType.DMA((group * slots,)),
-            pltpu.SemaphoreType.DMA((4 if own else n_lat * len(bounds) * (3 + parts),)),
-        ],
-        compiler_params=params(50),
+        ]
+        + ([] if own else [pltpu.VMEM(shape, BF16) for shape in ((cin, h1), (h1, h2), (h2, ch))]),
+        compiler_params=params(32),
         cost_estimate=pl.CostEstimate(
             flops=4 * lines * (cin * h1 + h1 * h2 + h2 * ch),
             transcendentals=lines * (h1 + h2),
@@ -613,7 +571,7 @@
         in_specs=[SMEM, SMEM] + [VMEM] * len(answers),
         out_specs=[VMEM] * len(outs),
         scratch_shapes=[pltpu.VMEM((rows * width, fields * levels), BF16)],
-        compiler_params=params(40),
+        compiler_params=params(16),
     )(pos, owners, *answers)
 
 

time: 275 us -> 228 us (0.83)
  waiting for transfers between devices: 160 us -> 124 us
  Pallas kernels: 59.5 us -> 46 us
  starting transfers between devices: 36.7 us -> 48.4 us
  local copies, waits for them, and re-layouts: 15.6 us -> 5.52 us
    ppermute x23 -> x31, waiting for transfers between devices: 146 us -> 114 us  [exchange(): return lax.ppermute(array, axis, [(i, i ^ mask) for i in range(count)])]
    pallas_call x5, Pallas kernels: 41.2 us -> 27.7 us  [instrument(): pl.pallas_call(functools.partial(instrument_kernel, group, served, n_lat,...]
    ppermute x23 -> x31, starting transfers between devices: 12.6 us -> 22.8 us  [exchange(): return lax.ppermute(array, axis, [(i, i ^ mask) for i in range(count)])]
    unnamed x58 -> x26, local copies, waits for them, and re-layouts: 12.5 us -> 2.44 us
    ppermute x12, waiting for transfers between devices: 14.3 us -> 10.5 us  [shifted(): return lax.ppermute(array, axis, pairs)]
  transfers between devices with their start and end apart: 35 -> 43, of which waited for: 9 -> 16; matrix products, arithmetic and copies ran while one was open for 1% -> 1% of each run, Pallas kernels for 20% -> 18%
where the time goes in v3:
time: 228 us; the launch traced here: 227 us
  waiting for transfers between devices  124 us (54%)
  starting transfers between devices  48.4 us (21%)
  Pallas kernels  46 us (20%)
  local copies, waits for them, and re-layouts  5.52 us (2%)
  other arithmetic  3.01 us (1%)
    ppermute x31, waiting for transfers between devices, exchange(): return lax.ppermute(array, axis, [(i, i ^ mask) for i in range(count)])  114 us
    pallas_call x5, Pallas kernels, instrument(): pl.pallas_call(functools.partial(instrument_kernel, group, served, n_lat,...  27.7 us
    ppermute x12, starting transfers between devices, shifted(): return lax.ppermute(array, axis, pairs)  25.6 us
    ppermute x31, starting transfers between devices, exchange(): return lax.ppermute(array, axis, [(i, i ^ mask) for i in range(count)])  22.8 us
    ppermute x12, waiting for transfers between devices, shifted(): return lax.ppermute(array, axis, pairs)  10.5 us
    pallas_call x1, Pallas kernels, forward(): pl.pallas_call(functools.partial(forward_kernel, group), out_shape=outs,...  5.39 us
  transfers between devices with their start and end apart: 43, of which 16 were waited for; matrix products, arithmetic and copies ran while one was open for 1% of the time, Pallas kernels for 18%

profile of v3, /device:TPU:30, one launch (start us, length us, event | category | flops | bytes accessed | tf_op | source)
XLA Modules:
  0.0 227.5 jit_solution(9094712504074009157)
XLA Ops:
  0.0 0.8 slice_bitcast_fusion.3
  0.8 1.1 fusion.1
  1.9 0.6 collective-permute-start.1
  2.5 4.3 %collective-permute-start = (f32[8,7,2,128]{3,2,1,0:T(2,128)S(1)}, f32[8,7,2,128]{3,2,1,0:T(2,128)S(1)}, u32[]{:S(2)}, u32[]{:S(2)}) collective-permute-start(f32[8,7,2,128]{3,2,1,0:T(2,128)S(1)} %pad_maximum_fusion.2), channel_id=1, source_target_pairs={{0,4},{4,8},{8,12},{12,16},{16,20},{20,24},{24,28},{28,0},{1,5},{5... | collective-permute-start | bytes 172040 | tf_op jit(solution)/shard_map/ppermute | solution.py:37
  6.8 1.2 fusion
  8.0 0.9 collective-permute-done.1.east
  8.9 0.9 pad_maximum_fusion
  9.7 1.9 collective-permute-start.2
  11.7 0.8 pad_maximum_fusion.1
  12.5 3.6 %collective-permute-start.3 = (f32[2,7,68,128]{3,2,1,0:T(8,128)}, f32[2,7,68,128]{3,2,1,0:T(8,128)}, u32[]{:S(2)}, u32[]{:S(2)}) collective-permute-start(f32[2,7,68,128]{3,2,1,0:T(8,128)} %pad_maximum_fusion.1), channel_id=1, source_target_pairs={{1,0},{2,1},{3,2},{5,4},{6,5},{7,6},{9,8},{10,9},{11,10},{13,12},{... | collective-permute-start | bytes 1462280 | tf_op jit(solution)/shard_map/ppermute | solution.py:37
  16.1 0.6 pad_add_fusion.pos
  16.7 3.3 %pack.1 = (bf16[288,1024]{1,0:T(8,128)(2,1)}, bf16[304,1024]{1,0:T(8,128)(2,1)}) custom-call(s32[2]{0:T(128)} %pad_add_fusion.pos, bf16[768,1024]{1,0:T(8,128)(2,1)} %bitcast.30, bf16[1024,1024]{1,0:T(8,128)(2,1)} %bitcast.28, bf16[1024,512]{1,0:T(8,128)(2,1)} %bitcast.33, f32[1,512]{1,0:T(1,128)} %scale.1), custom_call_target="tpu_custom_call" | custom-call | tf_op jit(solution)/shard_map/pack/pallas_call | solution.py:103
  20.1 2.0 collective-permute-start.7
  22.1 0.7 select_reduce_fusion.table
  22.8 2.3 %pick_radiances.1 = bf16[2,4,128,512]{3,2,1,0:T(8,128)(2,1)} custom-call(s32[2]{0:T(128)} %pad_add_fusion.pos, s32[2,8]{1,0:T(2,128)} %select_reduce_fusion.table, bf16[2,512,512]{2,1,0:T(8,128)(2,1)} %bitcast.22), custom_call_target="tpu_custom_call" | custom-call | tf_op jit(solution)/shard_map/pick_radiances/pallas_call | solution.py:146
  25.1 4.0 %collective-permute-start.5 = (bf16[2,4,128,512]{3,2,1,0:T(8,128)(2,1)}, bf16[2,4,128,512]{3,2,1,0:T(8,128)(2,1)S(1)}, u32[]{:S(2)}, u32[]{:S(2)}) collective-permute-start(bf16[2,4,128,512]{3,2,1,0:T(8,128)(2,1)} %pick_radiances.1), channel_id=1, source_target_pairs={{0,4},{4,0},{8,12},{12,8},{16,20},{20,16},{24,28},{28,24},{1,5},{5... | collective-permute-start | bytes 3145736 | tf_op jit(solution)/shard_map/ppermute | solution.py:29
  29.1 42.0 %collective-permute-done.7.refs_2_ = bf16[288,1024]{1,0:T(8,128)(2,1)} collective-permute-done((bf16[288,1024]{1,0:T(8,128)(2,1)}, bf16[288,1024]{1,0:T(8,128)(2,1)}, u32[]{:S(2)}, u32[]{:S(2)}) %collective-permute-start.7) | collective-permute-done | bytes 589856 | tf_op jit(solution)/shard_map/ppermute | solution.py:29
  71.1 0.6 collective-permute-start.18
  71.7 5.4 %forward.1 = (f32[12,7,96,128]{3,2,1,0:T(8,128)S(1)}, f32[10,6,80,128]{3,2,1,0:T(8,128)S(1)}, bf16[2,512,768]{2,1,0:T(8,128)(2,1)S(1)}, bf16[2,4,128,768]{3,2,1,0:T(8,128)(2,1)S(1)}) custom-call(s32[2]{0:T(128)S(1)} %copy-done.8, s32[2,8]{1,0:T(2,128)S(1)} %copy-done.7, f32[8,6,64,128]{3,2,1,0:T(8,128)S(1)} %bitcast.20, f32[8,64,128]{2,1,0:T(8,128)S(1)} %copy-done.6, ...), custom_call_target="tpu_custom_call" | custom-call | tf_op jit(solution)/shard_map/forward/pallas_call | solution.py:252
  77.1 3.3 %collective-permute-start.4 = (bf16[2,4,128,768]{3,2,1,0:T(8,128)(2,1)S(1)}, bf16[2,4,128,768]{3,2,1,0:T(8,128)(2,1)S(1)}, u32[]{:S(2)}, u32[]{:S(2)}) collective-permute-start(bf16[2,4,128,768]{3,2,1,0:T(8,128)(2,1)S(1)} %get-tuple-element.32), channel_id=1, source_target_pairs={{0,4},{4,0},{8,12},{12,8},{16,20},{20,16},{24,28},{28,24},{1,5},{5... | collective-permute-start | bytes 4718600 | tf_op jit(solution)/shard_map/ppermute | solution.py:29
  80.4 1.7 collective-permute-start.20
  82.2 5.3 %collective-permute-done.11.refs_6_ = bf16[288,1024]{1,0:T(8,128)(2,1)S(1)} collective-permute-done((bf16[288,1024]{1,0:T(8,128)(2,1)}, bf16[288,1024]{1,0:T(8,128)(2,1)S(1)}, u32[]{:S(2)}, u32[]{:S(2)}) %collective-permute-start.11) | collective-permute-done | bytes 589856 | tf_op jit(solution)/shard_map/ppermute | solution.py:29
  87.5 12.6 %collective-permute-done.20.refs_6_ = bf16[288,1024]{1,0:T(8,128)(2,1)S(1)} collective-permute-done((bf16[288,1024]{1,0:T(8,128)(2,1)}, bf16[288,1024]{1,0:T(8,128)(2,1)S(1)}, u32[]{:S(2)}, u32[]{:S(2)}) %collective-permute-start.20) | collective-permute-done | bytes 589856 | tf_op jit(solution)/shard_map/ppermute | solution.py:29
  100.2 2.0 collective-permute-done.25.refs_2_
  102.2 0.3 collective-permute-start.26
  102.4 0.6 collective-permute-start.21
  103.0 10.5 %collective-permute-done.12.refs_7_ = bf16[304,1024]{1,0:T(8,128)(2,1)S(1)} collective-permute-done((bf16[304,1024]{1,0:T(8,128)(2,1)}, bf16[304,1024]{1,0:T(8,128)(2,1)S(1)}, u32[]{:S(2)}, u32[]{:S(2)}) %collective-permute-start.12) | collective-permute-done | bytes 622624 | tf_op jit(solution)/shard_map/ppermute | solution.py:29
  113.5 0.5 collective-permute-start.14
  114.0 2.6 %collective-permute-done.26.refs_3_ = bf16[304,1024]{1,0:T(8,128)(2,1)S(1)} collective-permute-done((bf16[304,1024]{1,0:T(8,128)(2,1)S(1)}, bf16[304,1024]{1,0:T(8,128)(2,1)S(1)}, u32[]{:S(2)}, u32[]{:S(2)}) %collective-permute-start.26) | collective-permute-done | bytes 622624 | tf_op jit(solution)/shard_map/ppermute | solution.py:29
  116.6 0.9 collective-permute-start.30
  117.6 9.3 %collective-permute-done.21.refs_7_ = bf16[304,1024]{1,0:T(8,128)(2,1)S(1)} collective-permute-done((bf16[304,1024]{1,0:T(8,128)(2,1)S(1)}, bf16[304,1024]{1,0:T(8,128)(2,1)S(1)}, u32[]{:S(2)}, u32[]{:S(2)}) %collective-permute-start.21) | collective-permute-done | bytes 622624 | tf_op jit(solution)/shard_map/ppermute | solution.py:29
  126.9 0.6 collective-permute-start.23
  127.5 1.6 copy-done.2
  129.0 6.1 %shard_map.91 = (bf16[2,128,768]{2,1,0:T(8,128)(2,1)S(1)}, bf16[2,128,768]{2,1,0:T(8,128)(2,1)S(1)}) custom-call(s32[2]{0:T(128)S(1)} %copy-done.8, s32[2,8]{1,0:T(2,128)S(1)} %copy-done.7, bf16[2,512,768]{2,1,0:T(8,128)(2,1)S(1)} %get-tuple-element.31.columns, bf16[2,512,512]{2,1,0:T(8,128)(2,1)S(1)} %bitcast.23, ...), custom_call_target="tpu_custom_call" | custom-call | flops 4831838208 | bytes 6815744 | tf_op jit(solution)/shard_map/pallas_call | solution.py:500
  135.2 0.8 copy-done.11
  136.1 16.3 %collective-permute-done.29.refs_6_ = bf16[288,1024]{1,0:T(8,128)(2,1)S(1)} collective-permute-done((bf16[288,1024]{1,0:T(8,128)(2,1)S(1)}, bf16[288,1024]{1,0:T(8,128)(2,1)S(1)}, u32[]{:S(2)}, u32[]{:S(2)}) %collective-permute-start.29) | collective-permute-done | bytes 589856 | tf_op jit(solution)/shard_map/ppermute | solution.py:29
  152.4 0.5 collective-permute-start.31
  153.0 7.0 %shard_map.92 = (bf16[2,128,768]{2,1,0:T(8,128)(2,1)S(1)}, bf16[2,128,768]{2,1,0:T(8,128)(2,1)S(1)}) custom-call(s32[2]{0:T(128)S(1)} %copy-done.8, s32[2,8]{1,0:T(2,128)S(1)} %copy-done.7, bf16[2,512,768]{2,1,0:T(8,128)(2,1)S(1)} %get-tuple-element.31.columns, bf16[2,512,512]{2,1,0:T(8,128)(2,1)S(1)} %bitcast.24, ...), custom_call_target="tpu_custom_call" | custom-call | flops 4831838208 | bytes 6815744 | tf_op jit(solution)/shard_map/pallas_call | solution.py:500
  160.0 3.3 %collective-permute-start.6 = (bf16[2,128,768]{2,1,0:T(8,128)(2,1)S(1)}, bf16[2,128,768]{2,1,0:T(8,128)(2,1)S(1)}, u32[]{:S(2)}, u32[]{:S(2)}) collective-permute-start(bf16[2,128,768]{2,1,0:T(8,128)(2,1)S(1)} %get-tuple-element.34), channel_id=1, source_target_pairs={{0,4},{4,0},{8,12},{12,8},{16,20},{20,16},{24,28},{28,24},{1,5},{5... | collective-permute-start | bytes 1179656 | tf_op jit(solution)/shard_map/ppermute | solution.py:29
  163.3 7.0 %shard_map.93 = (bf16[2,128,768]{2,1,0:T(8,128)(2,1)S(1)}, bf16[2,128,768]{2,1,0:T(8,128)(2,1)S(1)}) custom-call(s32[2]{0:T(128)S(1)} %copy-done.8, s32[2,8]{1,0:T(2,128)S(1)} %copy-done.7, bf16[2,512,768]{2,1,0:T(8,128)(2,1)S(1)} %get-tuple-element.31.columns, bf16[2,512,512]{2,1,0:T(8,128)(2,1)S(1)} %bitcast.25, ...), custom_call_target="tpu_custom_call" | custom-call | flops 4831838208 | bytes 6815744 | tf_op jit(solution)/shard_map/pallas_call | solution.py:500
  170.4 0.1 collective-permute-start.15
  170.5 2.0 collective-permute-start.24
  172.5 3.8 %shard_map.94 = (bf16[1,128,768]{2,1,0:T(8,128)(2,1)S(1)}, bf16[1,128,768]{2,1,0:T(8,128)(2,1)S(1)}) custom-call(s32[2]{0:T(128)S(1)} %copy-done.8, s32[2,8]{1,0:T(2,128)S(1)} %copy-done.7, bf16[2,512,768]{2,1,0:T(8,128)(2,1)S(1)} %get-tuple-element.31.columns, bf16[2,512,512]{2,1,0:T(8,128)(2,1)S(1)} %bitcast.26, ...), custom_call_target="tpu_custom_call" | custom-call | flops 2415919104 | bytes 5767168 | tf_op jit(solution)/shard_map/pallas_call | solution.py:500
  176.2 0.2 collective-permute-start.33
  176.4 3.7 %shard_map.96 = (bf16[1,128,768]{2,1,0:T(8,128)(2,1)S(1)}, bf16[1,128,768]{2,1,0:T(8,128)(2,1)S(1)}) custom-call(s32[2]{0:T(128)S(1)} %copy-done.8, s32[2,8]{1,0:T(2,128)S(1)} %copy-done.7, bf16[2,512,768]{2,1,0:T(8,128)(2,1)S(1)} %get-tuple-element.31.columns, bf16[2,512,512]{2,1,0:T(8,128)(2,1)S(1)} %bitcast.27, ...), custom_call_target="tpu_custom_call" | custom-call | flops 2415919104 | bytes 5767168 | tf_op jit(solution)/shard_map/pallas_call | solution.py:500
  180.2 2.0 collective-permute-start.38
  182.2 0.3 collective-permute-done.15.refs_3_
  182.4 8.4 %collective-permute-done.24.refs_5_ = bf16[2,128,768]{2,1,0:T(8,128)(2,1)S(1)} collective-permute-done((bf16[2,128,768]{2,1,0:T(8,128)(2,1)S(1)}, bf16[2,128,768]{2,1,0:T(8,128)(2,1)S(1)}, u32[]{:S(2)}, u32[]{:S(2)}) %collective-permute-start.24) | collective-permute-done | bytes 393248 | tf_op jit(solution)/shard_map/ppermute | solution.py:29
  190.9 4.2 %collective-permute-done.33.refs_7_ = bf16[1,128,768]{2,1,0:T(8,128)(2,1)S(1)} collective-permute-done((bf16[1,128,768]{2,1,0:T(8,128)(2,1)S(1)}, bf16[1,128,768]{2,1,0:T(8,128)(2,1)S(1)}, u32[]{:S(2)}, u32[]{:S(2)}) %collective-permute-start.33) | collective-permute-done | bytes 196640 | tf_op jit(solution)/shard_map/ppermute | solution.py:29
  195.1 1.0 shard_map.95
  196.1 1.9 collective-permute-start.34
  198.0 3.6 %collective-permute-start.35 = (bf16[6,64,128]{2,1,0:T(8,128)(2,1)S(1)}, bf16[6,64,128]{2,1,0:T(8,128)(2,1)S(1)}, u32[]{:S(2)}, u32[]{:S(2)}) collective-permute-start(bf16[6,64,128]{2,1,0:T(8,128)(2,1)S(1)} %get-tuple-element.45), channel_id=1, source_target_pairs={{1,0},{2,1},{3,2},{5,4},{6,5},{7,6},{9,8},{10,9},{11,10},{13,12},{... | collective-permute-start | bytes 294920 | tf_op jit(solution)/shard_map/ppermute | solution.py:37
  201.7 1.5 collective-permute-start.36
  203.1 0.6 collective-permute-start.37
  203.8 1.0 shard_map.97.refs_7_
  204.8 0.9 collective-permute-done.36.refs_3_
  205.6 4.1 %collective-permute-done.37.refs_4_ = f32[8,6,128]{2,1,0:T(8,128)S(1)} collective-permute-done((f32[8,6,128]{2,1,0:T(8,128)S(1)}, f32[8,6,128]{2,1,0:T(8,128)S(1)}, u32[]{:S(2)}, u32[]{:S(2)}) %collective-permute-start.37) | collective-permute-done | bytes 24608 | tf_op jit(solution)/shard_map/ppermute | solution.py:37
  209.8 2.0 backward_first.1
  211.8 1.9 collective-permute-start.39
  213.7 3.6 %collective-permute-start.40 = (f32[6,64,128]{2,1,0:T(8,128)S(1)}, f32[6,64,128]{2,1,0:T(8,128)S(1)}, u32[]{:S(2)}, u32[]{:S(2)}) collective-permute-start(f32[6,64,128]{2,1,0:T(8,128)S(1)} %get-tuple-element.54), channel_id=1, source_target_pairs={{1,0},{2,1},{3,2},{5,4},{6,5},{7,6},{9,8},{10,9},{11,10},{13,12},{... | collective-permute-start | bytes 589832 | tf_op jit(solution)/shard_map/ppermute | solution.py:37
  217.4 2.0 collective-permute-start.42
  219.5 1.9 collective-permute-done.41.refs_3_
  221.3 2.8 %collective-permute-done.42.refs_4_ = f32[8,6,128]{2,1,0:T(8,128)S(1)} collective-permute-done((f32[8,6,128]{2,1,0:T(8,128)S(1)}, f32[8,6,128]{2,1,0:T(8,128)S(1)}, u32[]{:S(2)}, u32[]{:S(2)}) %collective-permute-start.42) | collective-permute-done | bytes 24608 | tf_op jit(solution)/shard_map/ppermute | solution.py:37
  224.1 3.4 %backward_last.1 = f32[8,6,64,128]{3,2,1,0:T(8,128)} custom-call(f32[8,6,64,128]{3,2,1,0:T(8,128)S(1)} %get-tuple-element.52.refs_0_, f32[6,64,128]{2,1,0:T(8,128)S(1)} %collective-permute-done.39.refs_1_, f32[6,64,128]{2,1,0:T(8,128)S(1)} %collective-permute-done.40.refs_2_, f32[8,6,128]{2,1,0:T(8,128)S(1)} %collective-permute-done.41.refs_3_, ...), custom_call_target="tpu_custom_call" | custom-call | tf_op jit(solution)/shard_map/backward_last/pallas_call | solution.py:387
  (72 shorter events, 0.5 us)
Async XLA Ops:
  0.0 8.0 %copy-start.6 = (f32[8,64,128]{2,1,0:T(8,128)S(1)}, f32[8,64,128]{2,1,0:T(8,128)}, u32[]{:S(2)}) copy-start(f32[8,64,128]{2,1,0:T(8,128)} %kappa.1) | copy-start | bytes 786436
  1.9 6.9 %collective-permute-start.1 = (f32[8,7,2,128]{3,2,1,0:T(2,128)S(1)}, f32[8,7,2,128]{3,2,1,0:T(2,128)S(1)}, u32[]{:S(2)}, u32[]{:S(2)}) collective-permute-start(f32[8,7,2,128]{3,2,1,0:T(2,128)S(1)} %pad_maximum_fusion.3), channel_id=1, source_target_pairs={{0,28},{4,0},{8,4},{12,8},{16,12},{20,16},{24,20},{28,24},{1,29},{... | collective-permute-start | bytes 172040 | tf_op jit(solution)/shard_map/ppermute | solution.py:37
  2.5 6.3 %collective-permute-start = (f32[8,7,2,128]{3,2,1,0:T(2,128)S(1)}, f32[8,7,2,128]{3,2,1,0:T(2,128)S(1)}, u32[]{:S(2)}, u32[]{:S(2)}) collective-permute-start(f32[8,7,2,128]{3,2,1,0:T(2,128)S(1)} %pad_maximum_fusion.2), channel_id=1, source_target_pairs={{0,4},{4,8},{8,12},{12,16},{16,20},{20,24},{24,28},{28,0},{1,5},{5... | collective-permute-start | bytes 172040 | tf_op jit(solution)/shard_map/ppermute | solution.py:37
  9.7 15.3 %collective-permute-start.2 = (f32[2,7,68,128]{3,2,1,0:T(8,128)}, f32[2,7,68,128]{3,2,1,0:T(8,128)S(1)}, u32[]{:S(2)}, u32[]{:S(2)}) collective-permute-start(f32[2,7,68,128]{3,2,1,0:T(8,128)} %pad_maximum_fusion), channel_id=1, source_target_pairs={{0,1},{1,2},{2,3},{4,5},{5,6},{6,7},{8,9},{9,10},{10,11},{12,13},{... | collective-permute-start | bytes 1462280 | tf_op jit(solution)/shard_map/ppermute | solution.py:37
  12.5 16.6 %collective-permute-start.3 = (f32[2,7,68,128]{3,2,1,0:T(8,128)}, f32[2,7,68,128]{3,2,1,0:T(8,128)}, u32[]{:S(2)}, u32[]{:S(2)}) collective-permute-start(f32[2,7,68,128]{3,2,1,0:T(8,128)} %pad_maximum_fusion.1), channel_id=1, source_target_pairs={{1,0},{2,1},{3,2},{5,4},{6,5},{7,6},{9,8},{10,9},{11,10},{13,12},{... | collective-permute-start | bytes 1462280 | tf_op jit(solution)/shard_map/ppermute | solution.py:37
  16.7 5.4 %copy-start.9 = (s32[2,1,4]{2,1,0:T(1,128)S(1)}, s32[2,1,4]{2,1,0:T(1,128)}, u32[]{:S(2)}) copy-start(s32[2,1,4]{2,1,0:T(1,128)} %param.13) | copy-start | bytes 100
  16.7 110.7 %copy-start.5 = (bf16[1,1024,512]{2,1,0:T(8,128)(2,1)S(1)}, bf16[1,1024,512]{2,1,0:T(8,128)(2,1)}, u32[]{:S(2)}) copy-start(bf16[1,1024,512]{2,1,0:T(8,128)(2,1)} %param.16) | copy-start | bytes 3145732
  20.0 51.7 %copy-start = (f32[8,64,6,128]{3,1,2,0:T(8,128)S(1)}, f32[8,64,6,128]{3,1,2,0:T(8,128)}, u32[]{:S(2)}) copy-start(f32[8,64,6,128]{3,1,2,0:T(8,128)} %param.9) | copy-start | bytes 4718596
  20.0 51.7 %copy-start.8 = (s32[2]{0:T(128)S(1)}, s32[2]{0:T(128)}, u32[]{:S(2)}) copy-start(s32[2]{0:T(128)} %pad_add_fusion.pos) | copy-start | bytes 28
  20.0 51.1 %collective-permute-start.8 = (bf16[304,1024]{1,0:T(8,128)(2,1)}, bf16[304,1024]{1,0:T(8,128)(2,1)}, u32[]{:S(2)}, u32[]{:S(2)}) collective-permute-start(bf16[304,1024]{1,0:T(8,128)(2,1)} %get-tuple-element.36), channel_id=1, source_target_pairs={{0,8},{4,12},{8,0},{12,4},{16,24},{20,28},{24,16},{28,20},{1,9},{5... | collective-permute-start | bytes 1867784 | tf_op jit(solution)/shard_map/ppermute | solution.py:29
  20.1 51.0 %collective-permute-start.7 = (bf16[288,1024]{1,0:T(8,128)(2,1)}, bf16[288,1024]{1,0:T(8,128)(2,1)}, u32[]{:S(2)}, u32[]{:S(2)}) collective-permute-start(bf16[288,1024]{1,0:T(8,128)(2,1)} %get-tuple-element.35), channel_id=1, source_target_pairs={{0,8},{4,12},{8,0},{12,4},{16,24},{20,28},{24,16},{28,20},{1,9},{5... | collective-permute-start | bytes 1769480 | tf_op jit(solution)/shard_map/ppermute | solution.py:29
  22.1 49.0 %collective-permute-start.16 = (bf16[288,1024]{1,0:T(8,128)(2,1)}, bf16[288,1024]{1,0:T(8,128)(2,1)}, u32[]{:S(2)}, u32[]{:S(2)}) collective-permute-start(bf16[288,1024]{1,0:T(8,128)(2,1)} %get-tuple-element.35), channel_id=1, source_target_pairs={{0,16},{4,20},{8,24},{12,28},{16,0},{20,4},{24,8},{28,12},{1,17},{... | collective-permute-start | bytes 1769480 | tf_op jit(solution)/shard_map/ppermute | solution.py:29
  22.8 48.9 %copy-start.7 = (s32[2,8]{1,0:T(2,128)S(1)}, s32[2,8]{1,0:T(2,128)}, u32[]{:S(2)}) copy-start(s32[2,8]{1,0:T(2,128)} %select_reduce_fusion.table) | copy-start | bytes 196
  25.1 102.4 %copy-start.1 = (bf16[2,8,64,512]{3,2,1,0:T(8,128)(2,1)S(1)}, bf16[2,8,64,512]{3,2,1,0:T(8,128)(2,1)}, u32[]{:S(2)}) copy-start(bf16[2,8,64,512]{3,2,1,0:T(8,128)(2,1)} %param.12) | copy-start | bytes 3145732
  25.1 102.4 %copy-start.3 = (bf16[1,768,1024]{2,1,0:T(8,128)(2,1)S(1)}, bf16[1,768,1024]{2,1,0:T(8,128)(2,1)}, u32[]{:S(2)}) copy-start(bf16[1,768,1024]{2,1,0:T(8,128)(2,1)} %param.14) | copy-start | bytes 4718596
  25.1 102.4 %copy-start.10 = (f32[1,512]{1,0:T(1,128)S(1)}, f32[1,512]{1,0:T(1,128)}, u32[]{:S(2)}) copy-start(f32[1,512]{1,0:T(1,128)} %scale.1) | copy-start | bytes 6148
  25.1 55.3 %collective-permute-start.5 = (bf16[2,4,128,512]{3,2,1,0:T(8,128)(2,1)}, bf16[2,4,128,512]{3,2,1,0:T(8,128)(2,1)S(1)}, u32[]{:S(2)}, u32[]{:S(2)}) collective-permute-start(bf16[2,4,128,512]{3,2,1,0:T(8,128)(2,1)} %pick_radiances.1), channel_id=1, source_target_pairs={{0,4},{4,0},{8,12},{12,8},{16,20},{20,16},{24,28},{28,24},{1,5},{5... | collective-permute-start | bytes 3145736 | tf_op jit(solution)/shard_map/ppermute | solution.py:29
  29.1 48.0 %collective-permute-start.17 = (bf16[304,1024]{1,0:T(8,128)(2,1)}, bf16[304,1024]{1,0:T(8,128)(2,1)S(1)}, u32[]{:S(2)}, u32[]{:S(2)}) collective-permute-start(bf16[304,1024]{1,0:T(8,128)(2,1)} %get-tuple-element.36), channel_id=1, source_target_pairs={{0,16},{4,20},{8,24},{12,28},{16,0},{20,4},{24,8},{28,12},{1,17},{... | collective-permute-start | bytes 1867784 | tf_op jit(solution)/shard_map/ppermute | solution.py:29
  71.1 9.3 %collective-permute-start.9 = (bf16[288,1024]{1,0:T(8,128)(2,1)}, bf16[288,1024]{1,0:T(8,128)(2,1)S(1)}, u32[]{:S(2)}, u32[]{:S(2)}) collective-permute-start(bf16[288,1024]{1,0:T(8,128)(2,1)} %collective-permute-done.7.refs_2_), channel_id=1, source_target_pairs={{0,1},{1,0},{2,3},{3,2},{4,5},{5,4},{6,7},{7,6},{8,9},{9,8},{10,11... | collective-permute-start | bytes 1769480 | tf_op jit(solution)/shard_map/ppermute | solution.py:29
  71.1 16.4 %collective-permute-start.11 = (bf16[288,1024]{1,0:T(8,128)(2,1)}, bf16[288,1024]{1,0:T(8,128)(2,1)S(1)}, u32[]{:S(2)}, u32[]{:S(2)}) collective-permute-start(bf16[288,1024]{1,0:T(8,128)(2,1)} %collective-permute-done.7.refs_2_), channel_id=1, source_target_pairs={{0,2},{1,3},{2,0},{3,1},{4,6},{5,7},{6,4},{7,5},{8,10},{9,11},{10,... | collective-permute-start | bytes 1769480 | tf_op jit(solution)/shard_map/ppermute | solution.py:29
  71.1 16.4 %collective-permute-start.18 = (bf16[288,1024]{1,0:T(8,128)(2,1)}, bf16[288,1024]{1,0:T(8,128)(2,1)S(1)}, u32[]{:S(2)}, u32[]{:S(2)}) collective-permute-start(bf16[288,1024]{1,0:T(8,128)(2,1)} %collective-permute-done.16.refs_2_), channel_id=1, source_target_pairs={{0,1},{1,0},{2,3},{3,2},{4,5},{5,4},{6,7},{7,6},{8,9},{9,8},{10,11... | collective-permute-start | bytes 1769480 | tf_op jit(solution)/shard_map/ppermute | solution.py:29
  77.1 49.8 %collective-permute-start.4 = (bf16[2,4,128,768]{3,2,1,0:T(8,128)(2,1)S(1)}, bf16[2,4,128,768]{3,2,1,0:T(8,128)(2,1)S(1)}, u32[]{:S(2)}, u32[]{:S(2)}) collective-permute-start(bf16[2,4,128,768]{3,2,1,0:T(8,128)(2,1)S(1)} %get-tuple-element.32), channel_id=1, source_target_pairs={{0,4},{4,0},{8,12},{12,8},{16,20},{20,16},{24,28},{28,24},{1,5},{5... | collective-permute-start | bytes 4718600 | tf_op jit(solution)/shard_map/ppermute | solution.py:29
  80.4 22.0 %collective-permute-start.10 = (bf16[304,1024]{1,0:T(8,128)(2,1)}, bf16[304,1024]{1,0:T(8,128)(2,1)S(1)}, u32[]{:S(2)}, u32[]{:S(2)}) collective-permute-start(bf16[304,1024]{1,0:T(8,128)(2,1)} %collective-permute-done.8.refs_3_), channel_id=1, source_target_pairs={{0,1},{1,0},{2,3},{3,2},{4,5},{5,4},{6,7},{7,6},{8,9},{9,8},{10,11... | collective-permute-start | bytes 1867784 | tf_op jit(solution)/shard_map/ppermute | solution.py:29
  80.4 19.7 %collective-permute-start.20 = (bf16[288,1024]{1,0:T(8,128)(2,1)}, bf16[288,1024]{1,0:T(8,128)(2,1)S(1)}, u32[]{:S(2)}, u32[]{:S(2)}) collective-permute-start(bf16[288,1024]{1,0:T(8,128)(2,1)} %collective-permute-done.16.refs_2_), channel_id=1, source_target_pairs={{0,2},{1,3},{2,0},{3,1},{4,6},{5,7},{6,4},{7,5},{8,10},{9,11},{10,... | collective-permute-start | bytes 1769480 | tf_op jit(solution)/shard_map/ppermute | solution.py:29
  87.5 14.6 %collective-permute-start.25 = (bf16[288,1024]{1,0:T(8,128)(2,1)}, bf16[288,1024]{1,0:T(8,128)(2,1)S(1)}, u32[]{:S(2)}, u32[]{:S(2)}) collective-permute-start(bf16[288,1024]{1,0:T(8,128)(2,1)} %collective-permute-done.16.refs_2_), channel_id=1, source_target_pairs={{0,8},{4,12},{8,0},{12,4},{16,24},{20,28},{24,16},{28,20},{1,9},{5... | collective-permute-start | bytes 1769480 | tf_op jit(solution)/shard_map/ppermute | solution.py:29
  87.5 26.0 %collective-permute-start.12 = (bf16[304,1024]{1,0:T(8,128)(2,1)}, bf16[304,1024]{1,0:T(8,128)(2,1)S(1)}, u32[]{:S(2)}, u32[]{:S(2)}) collective-permute-start(bf16[304,1024]{1,0:T(8,128)(2,1)} %collective-permute-done.8.refs_3_), channel_id=1, source_target_pairs={{0,2},{1,3},{2,0},{3,1},{4,6},{5,7},{6,4},{7,5},{8,10},{9,11},{10,... | collective-permute-start | bytes 1867784 | tf_op jit(solution)/shard_map/ppermute | solution.py:29
  100.2 13.3 %collective-permute-start.19 = (bf16[304,1024]{1,0:T(8,128)(2,1)S(1)}, bf16[304,1024]{1,0:T(8,128)(2,1)S(1)}, u32[]{:S(2)}, u32[]{:S(2)}) collective-permute-start(bf16[304,1024]{1,0:T(8,128)(2,1)S(1)} %collective-permute-done.17.refs_3_), channel_id=1, source_target_pairs={{0,1},{1,0},{2,3},{3,2},{4,5},{5,4},{6,7},{7,6},{8,9},{9,8},{10,11... | collective-permute-start | bytes 1867784 | tf_op jit(solution)/shard_map/ppermute | solution.py:29
  102.2 14.5 %collective-permute-start.26 = (bf16[304,1024]{1,0:T(8,128)(2,1)S(1)}, bf16[304,1024]{1,0:T(8,128)(2,1)S(1)}, u32[]{:S(2)}, u32[]{:S(2)}) collective-permute-start(bf16[304,1024]{1,0:T(8,128)(2,1)S(1)} %collective-permute-done.17.refs_3_), channel_id=1, source_target_pairs={{0,8},{4,12},{8,0},{12,4},{16,24},{20,28},{24,16},{28,20},{1,9},{5... | collective-permute-start | bytes 1867784 | tf_op jit(solution)/shard_map/ppermute | solution.py:29
  102.4 24.4 %collective-permute-start.21 = (bf16[304,1024]{1,0:T(8,128)(2,1)S(1)}, bf16[304,1024]{1,0:T(8,128)(2,1)S(1)}, u32[]{:S(2)}, u32[]{:S(2)}) collective-permute-start(bf16[304,1024]{1,0:T(8,128)(2,1)S(1)} %collective-permute-done.17.refs_3_), channel_id=1, source_target_pairs={{0,2},{1,3},{2,0},{3,1},{4,6},{5,7},{6,4},{7,5},{8,10},{9,11},{10,... | collective-permute-start | bytes 1867784 | tf_op jit(solution)/shard_map/ppermute | solution.py:29
  113.5 13.3 %collective-permute-start.13 = (bf16[288,1024]{1,0:T(8,128)(2,1)S(1)}, bf16[288,1024]{1,0:T(8,128)(2,1)S(1)}, u32[]{:S(2)}, u32[]{:S(2)}) collective-permute-start(bf16[288,1024]{1,0:T(8,128)(2,1)S(1)} %collective-permute-done.11.refs_6_), channel_id=1, source_target_pairs={{0,1},{1,0},{2,3},{3,2},{4,5},{5,4},{6,7},{7,6},{8,9},{9,8},{10,11... | collective-permute-start | bytes 1769480 | tf_op jit(solution)/shard_map/ppermute | solution.py:29
  113.5 38.9 %collective-permute-start.14 = (bf16[304,1024]{1,0:T(8,128)(2,1)S(1)}, bf16[304,1024]{1,0:T(8,128)(2,1)S(1)}, u32[]{:S(2)}, u32[]{:S(2)}) collective-permute-start(bf16[304,1024]{1,0:T(8,128)(2,1)S(1)} %collective-permute-done.12.refs_7_), channel_id=1, source_target_pairs={{0,1},{1,0},{2,3},{3,2},{4,5},{5,4},{6,7},{7,6},{8,9},{9,8},{10,11... | collective-permute-start | bytes 1867784 | tf_op jit(solution)/shard_map/ppermute | solution.py:29
  116.6 36.3 %collective-permute-start.30 = (bf16[304,1024]{1,0:T(8,128)(2,1)S(1)}, bf16[304,1024]{1,0:T(8,128)(2,1)S(1)}, u32[]{:S(2)}, u32[]{:S(2)}) collective-permute-start(bf16[304,1024]{1,0:T(8,128)(2,1)S(1)} %collective-permute-done.26.refs_3_), channel_id=1, source_target_pairs={{0,2},{1,3},{2,0},{3,1},{4,6},{5,7},{6,4},{7,5},{8,10},{9,11},{10,... | collective-permute-start | bytes 1867784 | tf_op jit(solution)/shard_map/ppermute | solution.py:29
  126.9 8.3 %collective-permute-start.22 = (bf16[288,1024]{1,0:T(8,128)(2,1)S(1)}, bf16[288,1024]{1,0:T(8,128)(2,1)S(1)}, u32[]{:S(2)}, u32[]{:S(2)}) collective-permute-start(bf16[288,1024]{1,0:T(8,128)(2,1)S(1)} %collective-permute-done.20.refs_6_), channel_id=1, source_target_pairs={{0,1},{1,0},{2,3},{3,2},{4,5},{5,4},{6,7},{7,6},{8,9},{9,8},{10,11... | collective-permute-start | bytes 1769480 | tf_op jit(solution)/shard_map/ppermute | solution.py:29
  126.9 25.5 %collective-permute-start.29 = (bf16[288,1024]{1,0:T(8,128)(2,1)S(1)}, bf16[288,1024]{1,0:T(8,128)(2,1)S(1)}, u32[]{:S(2)}, u32[]{:S(2)}) collective-permute-start(bf16[288,1024]{1,0:T(8,128)(2,1)S(1)} %collective-permute-done.25.refs_2_), channel_id=1, source_target_pairs={{0,2},{1,3},{2,0},{3,1},{4,6},{5,7},{6,4},{7,5},{8,10},{9,11},{10,... | collective-permute-start | bytes 1769480 | tf_op jit(solution)/shard_map/ppermute | solution.py:29
  126.9 33.1 %collective-permute-start.23 = (bf16[304,1024]{1,0:T(8,128)(2,1)S(1)}, bf16[304,1024]{1,0:T(8,128)(2,1)S(1)}, u32[]{:S(2)}, u32[]{:S(2)}) collective-permute-start(bf16[304,1024]{1,0:T(8,128)(2,1)S(1)} %collective-permute-done.21.refs_7_), channel_id=1, source_target_pairs={{0,1},{1,0},{2,3},{3,2},{4,5},{5,4},{6,7},{7,6},{8,9},{9,8},{10,11... | collective-permute-start | bytes 1867784 | tf_op jit(solution)/shard_map/ppermute | solution.py:29
  127.5 1.6 copy-start.2
  135.2 0.8 copy-start.11
  136.0 34.4 %collective-permute-start.27 = (bf16[288,1024]{1,0:T(8,128)(2,1)S(1)}, bf16[288,1024]{1,0:T(8,128)(2,1)S(1)}, u32[]{:S(2)}, u32[]{:S(2)}) collective-permute-start(bf16[288,1024]{1,0:T(8,128)(2,1)S(1)} %collective-permute-done.25.refs_2_), channel_id=1, source_target_pairs={{0,1},{1,0},{2,3},{3,2},{4,5},{5,4},{6,7},{7,6},{8,9},{9,8},{10,11... | collective-permute-start | bytes 1769480 | tf_op jit(solution)/shard_map/ppermute | solution.py:29
  136.1 27.3 %copy-start.12 = (bf16[288,1024]{1,0:T(8,128)(2,1)S(1)}, bf16[288,1024]{1,0:T(8,128)(2,1)}, u32[]{:S(2)}) copy-start(bf16[288,1024]{1,0:T(8,128)(2,1)} %copy-done.11) | copy-start | bytes 1769476
  152.4 18.1 %collective-permute-start.28 = (bf16[304,1024]{1,0:T(8,128)(2,1)S(1)}, bf16[304,1024]{1,0:T(8,128)(2,1)S(1)}, u32[]{:S(2)}, u32[]{:S(2)}) collective-permute-start(bf16[304,1024]{1,0:T(8,128)(2,1)S(1)} %collective-permute-done.26.refs_3_), channel_id=1, source_target_pairs={{0,1},{1,0},{2,3},{3,2},{4,5},{5,4},{6,7},{7,6},{8,9},{9,8},{10,11... | collective-permute-start | bytes 1867784 | tf_op jit(solution)/shard_map/ppermute | solution.py:29
  152.4 20.1 %collective-permute-start.31 = (bf16[288,1024]{1,0:T(8,128)(2,1)S(1)}, bf16[288,1024]{1,0:T(8,128)(2,1)S(1)}, u32[]{:S(2)}, u32[]{:S(2)}) collective-permute-start(bf16[288,1024]{1,0:T(8,128)(2,1)S(1)} %collective-permute-done.29.refs_6_), channel_id=1, source_target_pairs={{0,1},{1,0},{2,3},{3,2},{4,5},{5,4},{6,7},{7,6},{8,9},{9,8},{10,11... | collective-permute-start | bytes 1769480 | tf_op jit(solution)/shard_map/ppermute | solution.py:29
  152.9 19.6 %collective-permute-start.32 = (bf16[304,1024]{1,0:T(8,128)(2,1)S(1)}, bf16[304,1024]{1,0:T(8,128)(2,1)S(1)}, u32[]{:S(2)}, u32[]{:S(2)}) collective-permute-start(bf16[304,1024]{1,0:T(8,128)(2,1)S(1)} %collective-permute-done.30.refs_7_), channel_id=1, source_target_pairs={{0,1},{1,0},{2,3},{3,2},{4,5},{5,4},{6,7},{7,6},{8,9},{9,8},{10,11... | collective-permute-start | bytes 1867784 | tf_op jit(solution)/shard_map/ppermute | solution.py:29
  160.0 22.2 %collective-permute-start.6 = (bf16[2,128,768]{2,1,0:T(8,128)(2,1)S(1)}, bf16[2,128,768]{2,1,0:T(8,128)(2,1)S(1)}, u32[]{:S(2)}, u32[]{:S(2)}) collective-permute-start(bf16[2,128,768]{2,1,0:T(8,128)(2,1)S(1)} %get-tuple-element.34), channel_id=1, source_target_pairs={{0,4},{4,0},{8,12},{12,8},{16,20},{20,16},{24,28},{28,24},{1,5},{5... | collective-permute-start | bytes 1179656 | tf_op jit(solution)/shard_map/ppermute | solution.py:29
  170.4 12.1 %collective-permute-start.15 = (bf16[2,128,768]{2,1,0:T(8,128)(2,1)S(1)}, bf16[2,128,768]{2,1,0:T(8,128)(2,1)S(1)}, u32[]{:S(2)}, u32[]{:S(2)}) collective-permute-start(bf16[2,128,768]{2,1,0:T(8,128)(2,1)S(1)} %get-tuple-element.38), channel_id=1, source_target_pairs={{0,4},{4,0},{8,12},{12,8},{16,20},{20,16},{24,28},{28,24},{1,5},{5... | collective-permute-start | bytes 1179656 | tf_op jit(solution)/shard_map/ppermute | solution.py:29
  170.5 20.4 %collective-permute-start.24 = (bf16[2,128,768]{2,1,0:T(8,128)(2,1)S(1)}, bf16[2,128,768]{2,1,0:T(8,128)(2,1)S(1)}, u32[]{:S(2)}, u32[]{:S(2)}) collective-permute-start(bf16[2,128,768]{2,1,0:T(8,128)(2,1)S(1)} %get-tuple-element.40), channel_id=1, source_target_pairs={{0,4},{4,0},{8,12},{12,8},{16,20},{20,16},{24,28},{28,24},{1,5},{5... | collective-permute-start | bytes 1179656 | tf_op jit(solution)/shard_map/ppermute | solution.py:29
  176.2 18.8 %collective-permute-start.33 = (bf16[1,128,768]{2,1,0:T(8,128)(2,1)S(1)}, bf16[1,128,768]{2,1,0:T(8,128)(2,1)S(1)}, u32[]{:S(2)}, u32[]{:S(2)}) collective-permute-start(bf16[1,128,768]{2,1,0:T(8,128)(2,1)S(1)} %get-tuple-element.42), channel_id=1, source_target_pairs={{0,4},{4,0},{8,12},{12,8},{16,20},{20,16},{24,28},{28,24},{1,5},{5... | collective-permute-start | bytes 589832 | tf_op jit(solution)/shard_map/ppermute | solution.py:29
  180.2 23.6 %collective-permute-start.38 = (bf16[1,128,768]{2,1,0:T(8,128)(2,1)S(1)}, bf16[1,128,768]{2,1,0:T(8,128)(2,1)S(1)}, u32[]{:S(2)}, u32[]{:S(2)}) collective-permute-start(bf16[1,128,768]{2,1,0:T(8,128)(2,1)S(1)} %get-tuple-element.51), channel_id=1, source_target_pairs={{0,4},{4,0},{8,12},{12,8},{16,20},{20,16},{24,28},{28,24},{1,5},{5... | collective-permute-start | bytes 589832 | tf_op jit(solution)/shard_map/ppermute | solution.py:29
  196.1 13.6 %collective-permute-start.34 = (bf16[6,64,128]{2,1,0:T(8,128)(2,1)S(1)}, bf16[6,64,128]{2,1,0:T(8,128)(2,1)S(1)}, u32[]{:S(2)}, u32[]{:S(2)}) collective-permute-start(bf16[6,64,128]{2,1,0:T(8,128)(2,1)S(1)} %get-tuple-element.44), channel_id=1, source_target_pairs={{0,1},{1,2},{2,3},{4,5},{5,6},{6,7},{8,9},{9,10},{10,11},{12,13},{... | collective-permute-start | bytes 294920 | tf_op jit(solution)/shard_map/ppermute | solution.py:37
  198.0 11.7 %collective-permute-start.35 = (bf16[6,64,128]{2,1,0:T(8,128)(2,1)S(1)}, bf16[6,64,128]{2,1,0:T(8,128)(2,1)S(1)}, u32[]{:S(2)}, u32[]{:S(2)}) collective-permute-start(bf16[6,64,128]{2,1,0:T(8,128)(2,1)S(1)} %get-tuple-element.45), channel_id=1, source_target_pairs={{1,0},{2,1},{3,2},{5,4},{6,5},{7,6},{9,8},{10,9},{11,10},{13,12},{... | collective-permute-start | bytes 294920 | tf_op jit(solution)/shard_map/ppermute | solution.py:37
  201.7 4.0 %collective-permute-start.36 = (f32[8,6,128]{2,1,0:T(8,128)S(1)}, f32[8,6,128]{2,1,0:T(8,128)S(1)}, u32[]{:S(2)}, u32[]{:S(2)}) collective-permute-start(f32[8,6,128]{2,1,0:T(8,128)S(1)} %get-tuple-element.46), channel_id=1, source_target_pairs={{0,4},{4,8},{8,12},{12,16},{16,20},{20,24},{24,28},{28,0},{1,5},{5... | collective-permute-start | bytes 73736 | tf_op jit(solution)/shard_map/ppermute | solution.py:37
  203.1 6.6 %collective-permute-start.37 = (f32[8,6,128]{2,1,0:T(8,128)S(1)}, f32[8,6,128]{2,1,0:T(8,128)S(1)}, u32[]{:S(2)}, u32[]{:S(2)}) collective-permute-start(f32[8,6,128]{2,1,0:T(8,128)S(1)} %get-tuple-element.47), channel_id=1, source_target_pairs={{0,28},{4,0},{8,4},{12,8},{16,12},{20,16},{24,20},{28,24},{1,29},{... | collective-permute-start | bytes 73736 | tf_op jit(solution)/shard_map/ppermute | solution.py:37
  209.8 14.4 %copy-start.4 = (f32[8,64,6,128]{3,1,2,0:T(8,128)S(1)}, f32[8,64,6,128]{3,1,2,0:T(8,128)}, u32[]{:S(2)}) copy-start(f32[8,64,6,128]{3,1,2,0:T(8,128)} %param.10) | copy-start | bytes 4718596
  211.8 12.3 %collective-permute-start.39 = (f32[6,64,128]{2,1,0:T(8,128)S(1)}, f32[6,64,128]{2,1,0:T(8,128)S(1)}, u32[]{:S(2)}, u32[]{:S(2)}) collective-permute-start(f32[6,64,128]{2,1,0:T(8,128)S(1)} %get-tuple-element.53), channel_id=1, source_target_pairs={{0,1},{1,2},{2,3},{4,5},{5,6},{6,7},{8,9},{9,10},{10,11},{12,13},{... | collective-permute-start | bytes 589832 | tf_op jit(solution)/shard_map/ppermute | solution.py:37
  213.7 10.4 %collective-permute-start.40 = (f32[6,64,128]{2,1,0:T(8,128)S(1)}, f32[6,64,128]{2,1,0:T(8,128)S(1)}, u32[]{:S(2)}, u32[]{:S(2)}) collective-permute-start(f32[6,64,128]{2,1,0:T(8,128)S(1)} %get-tuple-element.54), channel_id=1, source_target_pairs={{1,0},{2,1},{3,2},{5,4},{6,5},{7,6},{9,8},{10,9},{11,10},{13,12},{... | collective-permute-start | bytes 589832 | tf_op jit(solution)/shard_map/ppermute | solution.py:37
  217.4 4.0 %collective-permute-start.41 = (f32[8,6,128]{2,1,0:T(8,128)S(1)}, f32[8,6,128]{2,1,0:T(8,128)S(1)}, u32[]{:S(2)}, u32[]{:S(2)}) collective-permute-start(f32[8,6,128]{2,1,0:T(8,128)S(1)} %get-tuple-element.55), channel_id=1, source_target_pairs={{0,4},{4,8},{8,12},{12,16},{16,20},{20,24},{24,28},{28,0},{1,5},{5... | collective-permute-start | bytes 73736 | tf_op jit(solution)/shard_map/ppermute | solution.py:37
  217.4 6.7 %collective-permute-start.42 = (f32[8,6,128]{2,1,0:T(8,128)S(1)}, f32[8,6,128]{2,1,0:T(8,128)S(1)}, u32[]{:S(2)}, u32[]{:S(2)}) collective-permute-start(f32[8,6,128]{2,1,0:T(8,128)S(1)} %get-tuple-element.56), channel_id=1, source_target_pairs={{0,28},{4,0},{8,4},{12,8},{16,12},{20,16},{24,20},{28,24},{1,29},{... | collective-permute-start | bytes 73736 | tf_op jit(solution)/shard_map/ppermute | solution.py:37

commit v4 on v3

--- a/solution.py
+++ b/solution.py
@@ -120,13 +120,21 @@
             bottom = far & -far
             found[far] = tuple(exchange(a, "lon", bottom * group) for a in found[far ^ bottom])
     gathered = {}
-    for served, part in found.items():
+    for served in sorted(found):
         if served == 0:
             continue
-        parts = {0: part}
+        parts = {0: found[served]}
+        nearest = served & -served
         for bit in bits_down(n_lat):
             for near in list(parts):
-                parts[near | bit] = tuple(exchange(a, "lat", bit) for a in parts[near])
+                *early, last = parts[near]
+                chunks = [exchange(a, "lat", bit) for a in early]
+                if near == 0 and bit == n_lat // 2 and served != nearest:
+                    joined = gathered[served ^ nearest][bit][-1]
+                    chunks.append(exchange(joined, "lon", nearest * group))
+                else:
+                    chunks.append(exchange(last, "lat", bit))
+                parts[near | bit] = tuple(chunks)
         gathered[served] = parts
     return gathered
 
@@ -512,7 +520,7 @@
             pltpu.VMEM((lines, ch), BF16),
         ]
         + ([] if own else [pltpu.VMEM(shape, BF16) for shape in ((cin, h1), (h1, h2), (h2, ch))]),
-        compiler_params=params(32),
+        compiler_params=params(20),
         cost_estimate=pl.CostEstimate(
             flops=4 * lines * (cin * h1 + h1 * h2 + h2 * ch),
             transcendentals=lines * (h1 + h2),

time: 228 us -> 218 us (0.956)
  waiting for transfers between devices: 124 us -> 115 us
    ppermute x31, waiting for transfers between devices: 114 us -> 105 us  [exchange(): return lax.ppermute(array, axis, [(i, i ^ mask) for i in range(count)])]
  transfers between devices with their start and end apart: 43 -> 43, of which waited for: 16 -> 15; matrix products, arithmetic and copies ran while one was open for 1% -> 2% of each run, Pallas kernels for 18% -> 19%
where the time goes in v4:
time: 218 us; the launch traced here: 217 us
  waiting for transfers between devices  115 us (53%)
  starting transfers between devices  47.8 us (22%)
  Pallas kernels  46 us (21%)
  local copies, waits for them, and re-layouts  4.71 us (2%)
  other arithmetic  3 us (1%)
    ppermute x31, waiting for transfers between devices, exchange(): return lax.ppermute(array, axis, [(i, i ^ mask) for i in range(count)])  105 us
    pallas_call x5, Pallas kernels, instrument(): pl.pallas_call(functools.partial(instrument_kernel, group, served, n_lat,...  27.7 us
    ppermute x12, starting transfers between devices, shifted(): return lax.ppermute(array, axis, pairs)  25.6 us
    ppermute x31, starting transfers between devices, exchange(): return lax.ppermute(array, axis, [(i, i ^ mask) for i in range(count)])  22.2 us
    ppermute x12, waiting for transfers between devices, shifted(): return lax.ppermute(array, axis, pairs)  10.5 us
    pallas_call x1, Pallas kernels, forward(): pl.pallas_call(functools.partial(forward_kernel, group), out_shape=outs,...  5.39 us
  transfers between devices with their start and end apart: 43, of which 15 were waited for; matrix products, arithmetic and copies ran while one was open for 2% of the time, Pallas kernels for 19%

profile of v4, /device:TPU:30, one launch (start us, length us, event | category | flops | bytes accessed | tf_op | source)
XLA Modules:
  0.0 217.2 jit_solution(3196543152261423736)
XLA Ops:
  0.0 0.8 slice_bitcast_fusion.3
  0.8 1.1 fusion.1
  1.9 0.6 collective-permute-start.1
  2.5 4.3 %collective-permute-start = (f32[8,7,2,128]{3,2,1,0:T(2,128)S(1)}, f32[8,7,2,128]{3,2,1,0:T(2,128)S(1)}, u32[]{:S(2)}, u32[]{:S(2)}) collective-permute-start(f32[8,7,2,128]{3,2,1,0:T(2,128)S(1)} %pad_maximum_fusion.2), channel_id=1, source_target_pairs={{0,4},{4,8},{8,12},{12,16},{16,20},{20,24},{24,28},{28,0},{1,5},{5... | collective-permute-start | bytes 172040 | tf_op jit(solution)/shard_map/ppermute | solution.py:37
  6.8 1.2 fusion
  8.0 0.9 collective-permute-done.1.east
  8.9 0.8 pad_maximum_fusion
  9.7 1.9 collective-permute-start.2
  11.7 0.8 pad_maximum_fusion.1
  12.5 3.6 %collective-permute-start.3 = (f32[2,7,68,128]{3,2,1,0:T(8,128)}, f32[2,7,68,128]{3,2,1,0:T(8,128)}, u32[]{:S(2)}, u32[]{:S(2)}) collective-permute-start(f32[2,7,68,128]{3,2,1,0:T(8,128)} %pad_maximum_fusion.1), channel_id=1, source_target_pairs={{1,0},{2,1},{3,2},{5,4},{6,5},{7,6},{9,8},{10,9},{11,10},{13,12},{... | collective-permute-start | bytes 1462280 | tf_op jit(solution)/shard_map/ppermute | solution.py:37
  16.1 0.6 pad_add_fusion.pos
  16.7 3.3 %pack.1 = (bf16[288,1024]{1,0:T(8,128)(2,1)}, bf16[304,1024]{1,0:T(8,128)(2,1)}) custom-call(s32[2]{0:T(128)} %pad_add_fusion.pos, bf16[768,1024]{1,0:T(8,128)(2,1)} %bitcast.30, bf16[1024,1024]{1,0:T(8,128)(2,1)} %bitcast.28, bf16[1024,512]{1,0:T(8,128)(2,1)} %bitcast.33, f32[1,512]{1,0:T(1,128)} %scale.1), custom_call_target="tpu_custom_call" | custom-call | tf_op jit(solution)/shard_map/pack/pallas_call | solution.py:103
  20.0 0.1 collective-permute-start.8
  20.1 2.0 collective-permute-start.7
  22.1 0.7 select_reduce_fusion.table
  22.8 2.3 %pick_radiances.1 = bf16[2,4,128,512]{3,2,1,0:T(8,128)(2,1)} custom-call(s32[2]{0:T(128)} %pad_add_fusion.pos, s32[2,8]{1,0:T(2,128)} %select_reduce_fusion.table, bf16[2,512,512]{2,1,0:T(8,128)(2,1)} %bitcast.22), custom_call_target="tpu_custom_call" | custom-call | tf_op jit(solution)/shard_map/pick_radiances/pallas_call | solution.py:154
  25.1 4.0 %collective-permute-start.5 = (bf16[2,4,128,512]{3,2,1,0:T(8,128)(2,1)}, bf16[2,4,128,512]{3,2,1,0:T(8,128)(2,1)S(1)}, u32[]{:S(2)}, u32[]{:S(2)}) collective-permute-start(bf16[2,4,128,512]{3,2,1,0:T(8,128)(2,1)} %pick_radiances.1), channel_id=1, source_target_pairs={{0,4},{4,0},{8,12},{12,8},{16,20},{20,16},{24,28},{28,24},{1,5},{5... | collective-permute-start | bytes 3145736 | tf_op jit(solution)/shard_map/ppermute | solution.py:29
  29.1 42.0 %collective-permute-done.7.refs_2_ = bf16[288,1024]{1,0:T(8,128)(2,1)} collective-permute-done((bf16[288,1024]{1,0:T(8,128)(2,1)}, bf16[288,1024]{1,0:T(8,128)(2,1)}, u32[]{:S(2)}, u32[]{:S(2)}) %collective-permute-start.7) | collective-permute-done | bytes 589856 | tf_op jit(solution)/shard_map/ppermute | solution.py:29
  71.1 0.6 collective-permute-start.18
  71.7 5.4 %forward.1 = (f32[12,7,96,128]{3,2,1,0:T(8,128)S(1)}, f32[10,6,80,128]{3,2,1,0:T(8,128)S(1)}, bf16[2,512,768]{2,1,0:T(8,128)(2,1)S(1)}, bf16[2,4,128,768]{3,2,1,0:T(8,128)(2,1)S(1)}) custom-call(s32[2]{0:T(128)S(1)} %copy-done.8, s32[2,8]{1,0:T(2,128)S(1)} %copy-done.7, f32[8,6,64,128]{3,2,1,0:T(8,128)S(1)} %bitcast.20, f32[8,64,128]{2,1,0:T(8,128)S(1)} %copy-done.6, ...), custom_call_target="tpu_custom_call" | custom-call | tf_op jit(solution)/shard_map/forward/pallas_call | solution.py:260
  77.1 3.3 %collective-permute-start.4 = (bf16[2,4,128,768]{3,2,1,0:T(8,128)(2,1)S(1)}, bf16[2,4,128,768]{3,2,1,0:T(8,128)(2,1)S(1)}, u32[]{:S(2)}, u32[]{:S(2)}) collective-permute-start(bf16[2,4,128,768]{3,2,1,0:T(8,128)(2,1)S(1)} %get-tuple-element.32), channel_id=1, source_target_pairs={{0,4},{4,0},{8,12},{12,8},{16,20},{20,16},{24,28},{28,24},{1,5},{5... | collective-permute-start | bytes 4718600 | tf_op jit(solution)/shard_map/ppermute | solution.py:29
  80.4 1.7 collective-permute-start.20
  82.2 5.3 %collective-permute-done.11.refs_6_ = bf16[288,1024]{1,0:T(8,128)(2,1)S(1)} collective-permute-done((bf16[288,1024]{1,0:T(8,128)(2,1)}, bf16[288,1024]{1,0:T(8,128)(2,1)S(1)}, u32[]{:S(2)}, u32[]{:S(2)}) %collective-permute-start.11) | collective-permute-done | bytes 589856 | tf_op jit(solution)/shard_map/ppermute | solution.py:29
  87.5 12.6 %collective-permute-done.20.refs_6_ = bf16[288,1024]{1,0:T(8,128)(2,1)S(1)} collective-permute-done((bf16[288,1024]{1,0:T(8,128)(2,1)}, bf16[288,1024]{1,0:T(8,128)(2,1)S(1)}, u32[]{:S(2)}, u32[]{:S(2)}) %collective-permute-start.20) | collective-permute-done | bytes 589856 | tf_op jit(solution)/shard_map/ppermute | solution.py:29
  100.1 2.0 collective-permute-done.25.refs_2_
  102.1 0.6 collective-permute-start.21
  102.7 0.3 collective-permute-start.26
  103.0 10.5 %collective-permute-done.12.refs_7_ = bf16[304,1024]{1,0:T(8,128)(2,1)S(1)} collective-permute-done((bf16[304,1024]{1,0:T(8,128)(2,1)}, bf16[304,1024]{1,0:T(8,128)(2,1)S(1)}, u32[]{:S(2)}, u32[]{:S(2)}) %collective-permute-start.12) | collective-permute-done | bytes 622624 | tf_op jit(solution)/shard_map/ppermute | solution.py:29
  113.5 0.5 collective-permute-start.14
  114.0 12.4 %collective-permute-done.21.refs_7_ = bf16[304,1024]{1,0:T(8,128)(2,1)S(1)} collective-permute-done((bf16[304,1024]{1,0:T(8,128)(2,1)S(1)}, bf16[304,1024]{1,0:T(8,128)(2,1)S(1)}, u32[]{:S(2)}, u32[]{:S(2)}) %collective-permute-start.21) | collective-permute-done | bytes 622624 | tf_op jit(solution)/shard_map/ppermute | solution.py:29
  126.4 0.3 collective-permute-start.29
  126.7 0.2 collective-permute-start.23
  127.0 1.6 copy-done.2
  128.6 6.1 %shard_map.91 = (bf16[2,128,768]{2,1,0:T(8,128)(2,1)S(1)}, bf16[2,128,768]{2,1,0:T(8,128)(2,1)S(1)}) custom-call(s32[2]{0:T(128)S(1)} %copy-done.8, s32[2,8]{1,0:T(2,128)S(1)} %copy-done.7, bf16[2,512,768]{2,1,0:T(8,128)(2,1)S(1)} %get-tuple-element.31.columns, bf16[2,512,512]{2,1,0:T(8,128)(2,1)S(1)} %bitcast.23, ...), custom_call_target="tpu_custom_call" | custom-call | flops 4831838208 | bytes 6815744 | tf_op jit(solution)/shard_map/pallas_call | solution.py:508
  134.7 0.4 collective-permute-start.27
  135.1 7.0 %collective-permute-done.29.refs_6_ = bf16[288,1024]{1,0:T(8,128)(2,1)S(1)} collective-permute-done((bf16[288,1024]{1,0:T(8,128)(2,1)S(1)}, bf16[288,1024]{1,0:T(8,128)(2,1)S(1)}, u32[]{:S(2)}, u32[]{:S(2)}) %collective-permute-start.29) | collective-permute-done | bytes 589856 | tf_op jit(solution)/shard_map/ppermute | solution.py:29
  142.1 0.5 collective-permute-start.31
  142.7 7.0 %shard_map.92 = (bf16[2,128,768]{2,1,0:T(8,128)(2,1)S(1)}, bf16[2,128,768]{2,1,0:T(8,128)(2,1)S(1)}) custom-call(s32[2]{0:T(128)S(1)} %copy-done.8, s32[2,8]{1,0:T(2,128)S(1)} %copy-done.7, bf16[2,512,768]{2,1,0:T(8,128)(2,1)S(1)} %get-tuple-element.31.columns, bf16[2,512,512]{2,1,0:T(8,128)(2,1)S(1)} %bitcast.24, ...), custom_call_target="tpu_custom_call" | custom-call | flops 4831838208 | bytes 6815744 | tf_op jit(solution)/shard_map/pallas_call | solution.py:508
  149.8 3.3 %collective-permute-start.6 = (bf16[2,128,768]{2,1,0:T(8,128)(2,1)S(1)}, bf16[2,128,768]{2,1,0:T(8,128)(2,1)S(1)}, u32[]{:S(2)}, u32[]{:S(2)}) collective-permute-start(bf16[2,128,768]{2,1,0:T(8,128)(2,1)S(1)} %get-tuple-element.34), channel_id=1, source_target_pairs={{0,4},{4,0},{8,12},{12,8},{16,20},{20,16},{24,28},{28,24},{1,5},{5... | collective-permute-start | bytes 1179656 | tf_op jit(solution)/shard_map/ppermute | solution.py:29
  153.1 7.0 %shard_map.93 = (bf16[2,128,768]{2,1,0:T(8,128)(2,1)S(1)}, bf16[2,128,768]{2,1,0:T(8,128)(2,1)S(1)}) custom-call(s32[2]{0:T(128)S(1)} %copy-done.8, s32[2,8]{1,0:T(2,128)S(1)} %copy-done.7, bf16[2,512,768]{2,1,0:T(8,128)(2,1)S(1)} %get-tuple-element.31.columns, bf16[2,512,512]{2,1,0:T(8,128)(2,1)S(1)} %bitcast.25, ...), custom_call_target="tpu_custom_call" | custom-call | flops 4831838208 | bytes 6815744 | tf_op jit(solution)/shard_map/pallas_call | solution.py:508
  160.1 0.1 collective-permute-start.15
  160.2 2.0 collective-permute-start.24
  162.2 3.7 %shard_map.94 = (bf16[1,128,768]{2,1,0:T(8,128)(2,1)S(1)}, bf16[1,128,768]{2,1,0:T(8,128)(2,1)S(1)}) custom-call(s32[2]{0:T(128)S(1)} %copy-done.8, s32[2,8]{1,0:T(2,128)S(1)} %copy-done.7, bf16[2,512,768]{2,1,0:T(8,128)(2,1)S(1)} %get-tuple-element.31.columns, bf16[2,512,512]{2,1,0:T(8,128)(2,1)S(1)} %bitcast.26, ...), custom_call_target="tpu_custom_call" | custom-call | flops 2415919104 | bytes 5767168 | tf_op jit(solution)/shard_map/pallas_call | solution.py:508
  166.0 0.2 collective-permute-start.33
  166.1 3.7 %shard_map.96 = (bf16[1,128,768]{2,1,0:T(8,128)(2,1)S(1)}, bf16[1,128,768]{2,1,0:T(8,128)(2,1)S(1)}) custom-call(s32[2]{0:T(128)S(1)} %copy-done.8, s32[2,8]{1,0:T(2,128)S(1)} %copy-done.7, bf16[2,512,768]{2,1,0:T(8,128)(2,1)S(1)} %get-tuple-element.31.columns, bf16[2,512,512]{2,1,0:T(8,128)(2,1)S(1)} %bitcast.27, ...), custom_call_target="tpu_custom_call" | custom-call | flops 2415919104 | bytes 5767168 | tf_op jit(solution)/shard_map/pallas_call | solution.py:508
  169.9 2.0 collective-permute-start.38
  171.9 0.3 collective-permute-done.15.refs_3_
  172.2 8.4 %collective-permute-done.24.refs_5_ = bf16[2,128,768]{2,1,0:T(8,128)(2,1)S(1)} collective-permute-done((bf16[2,128,768]{2,1,0:T(8,128)(2,1)S(1)}, bf16[2,128,768]{2,1,0:T(8,128)(2,1)S(1)}, u32[]{:S(2)}, u32[]{:S(2)}) %collective-permute-start.24) | collective-permute-done | bytes 393248 | tf_op jit(solution)/shard_map/ppermute | solution.py:29
  180.6 4.2 %collective-permute-done.33.refs_7_ = bf16[1,128,768]{2,1,0:T(8,128)(2,1)S(1)} collective-permute-done((bf16[1,128,768]{2,1,0:T(8,128)(2,1)S(1)}, bf16[1,128,768]{2,1,0:T(8,128)(2,1)S(1)}, u32[]{:S(2)}, u32[]{:S(2)}) %collective-permute-start.33) | collective-permute-done | bytes 196640 | tf_op jit(solution)/shard_map/ppermute | solution.py:29
  184.8 1.0 shard_map.95
  185.8 1.9 collective-permute-start.34
  187.8 3.6 %collective-permute-start.35 = (bf16[6,64,128]{2,1,0:T(8,128)(2,1)S(1)}, bf16[6,64,128]{2,1,0:T(8,128)(2,1)S(1)}, u32[]{:S(2)}, u32[]{:S(2)}) collective-permute-start(bf16[6,64,128]{2,1,0:T(8,128)(2,1)S(1)} %get-tuple-element.45), channel_id=1, source_target_pairs={{1,0},{2,1},{3,2},{5,4},{6,5},{7,6},{9,8},{10,9},{11,10},{13,12},{... | collective-permute-start | bytes 294920 | tf_op jit(solution)/shard_map/ppermute | solution.py:37
  191.4 1.4 collective-permute-start.36
  192.9 0.6 collective-permute-start.37
  193.5 1.0 shard_map.97.refs_7_
  194.5 0.9 collective-permute-done.36.refs_3_
  195.4 4.1 %collective-permute-done.37.refs_4_ = f32[8,6,128]{2,1,0:T(8,128)S(1)} collective-permute-done((f32[8,6,128]{2,1,0:T(8,128)S(1)}, f32[8,6,128]{2,1,0:T(8,128)S(1)}, u32[]{:S(2)}, u32[]{:S(2)}) %collective-permute-start.37) | collective-permute-done | bytes 24608 | tf_op jit(solution)/shard_map/ppermute | solution.py:37
  199.5 2.0 backward_first.1
  201.5 1.9 collective-permute-start.39
  203.5 3.6 %collective-permute-start.40 = (f32[6,64,128]{2,1,0:T(8,128)S(1)}, f32[6,64,128]{2,1,0:T(8,128)S(1)}, u32[]{:S(2)}, u32[]{:S(2)}) collective-permute-start(f32[6,64,128]{2,1,0:T(8,128)S(1)} %get-tuple-element.54), channel_id=1, source_target_pairs={{1,0},{2,1},{3,2},{5,4},{6,5},{7,6},{9,8},{10,9},{11,10},{13,12},{... | collective-permute-start | bytes 589832 | tf_op jit(solution)/shard_map/ppermute | solution.py:37
  207.2 2.0 collective-permute-start.42
  209.2 1.9 collective-permute-done.41.refs_3_
  211.1 2.8 %collective-permute-done.42.refs_4_ = f32[8,6,128]{2,1,0:T(8,128)S(1)} collective-permute-done((f32[8,6,128]{2,1,0:T(8,128)S(1)}, f32[8,6,128]{2,1,0:T(8,128)S(1)}, u32[]{:S(2)}, u32[]{:S(2)}) %collective-permute-start.42) | collective-permute-done | bytes 24608 | tf_op jit(solution)/shard_map/ppermute | solution.py:37
  213.9 3.4 %backward_last.1 = f32[8,6,64,128]{3,2,1,0:T(8,128)} custom-call(f32[8,6,64,128]{3,2,1,0:T(8,128)S(1)} %get-tuple-element.52.refs_0_, f32[6,64,128]{2,1,0:T(8,128)S(1)} %collective-permute-done.39.refs_1_, f32[6,64,128]{2,1,0:T(8,128)S(1)} %collective-permute-done.40.refs_2_, f32[8,6,128]{2,1,0:T(8,128)S(1)} %collective-permute-done.41.refs_3_, ...), custom_call_target="tpu_custom_call" | custom-call | tf_op jit(solution)/shard_map/backward_last/pallas_call | solution.py:395
  (68 shorter events, 0.4 us)
Async XLA Ops:
  0.0 8.0 %copy-start.6 = (f32[8,64,128]{2,1,0:T(8,128)S(1)}, f32[8,64,128]{2,1,0:T(8,128)}, u32[]{:S(2)}) copy-start(f32[8,64,128]{2,1,0:T(8,128)} %kappa.1) | copy-start | bytes 786436
  1.9 6.9 %collective-permute-start.1 = (f32[8,7,2,128]{3,2,1,0:T(2,128)S(1)}, f32[8,7,2,128]{3,2,1,0:T(2,128)S(1)}, u32[]{:S(2)}, u32[]{:S(2)}) collective-permute-start(f32[8,7,2,128]{3,2,1,0:T(2,128)S(1)} %pad_maximum_fusion.3), channel_id=1, source_target_pairs={{0,28},{4,0},{8,4},{12,8},{16,12},{20,16},{24,20},{28,24},{1,29},{... | collective-permute-start | bytes 172040 | tf_op jit(solution)/shard_map/ppermute | solution.py:37
  2.5 6.3 %collective-permute-start = (f32[8,7,2,128]{3,2,1,0:T(2,128)S(1)}, f32[8,7,2,128]{3,2,1,0:T(2,128)S(1)}, u32[]{:S(2)}, u32[]{:S(2)}) collective-permute-start(f32[8,7,2,128]{3,2,1,0:T(2,128)S(1)} %pad_maximum_fusion.2), channel_id=1, source_target_pairs={{0,4},{4,8},{8,12},{12,16},{16,20},{20,24},{24,28},{28,0},{1,5},{5... | collective-permute-start | bytes 172040 | tf_op jit(solution)/shard_map/ppermute | solution.py:37
  9.7 15.3 %collective-permute-start.2 = (f32[2,7,68,128]{3,2,1,0:T(8,128)}, f32[2,7,68,128]{3,2,1,0:T(8,128)S(1)}, u32[]{:S(2)}, u32[]{:S(2)}) collective-permute-start(f32[2,7,68,128]{3,2,1,0:T(8,128)} %pad_maximum_fusion), channel_id=1, source_target_pairs={{0,1},{1,2},{2,3},{4,5},{5,6},{6,7},{8,9},{9,10},{10,11},{12,13},{... | collective-permute-start | bytes 1462280 | tf_op jit(solution)/shard_map/ppermute | solution.py:37
  12.5 16.6 %collective-permute-start.3 = (f32[2,7,68,128]{3,2,1,0:T(8,128)}, f32[2,7,68,128]{3,2,1,0:T(8,128)}, u32[]{:S(2)}, u32[]{:S(2)}) collective-permute-start(f32[2,7,68,128]{3,2,1,0:T(8,128)} %pad_maximum_fusion.1), channel_id=1, source_target_pairs={{1,0},{2,1},{3,2},{5,4},{6,5},{7,6},{9,8},{10,9},{11,10},{13,12},{... | collective-permute-start | bytes 1462280 | tf_op jit(solution)/shard_map/ppermute | solution.py:37
  16.7 5.4 %copy-start.9 = (s32[2,1,4]{2,1,0:T(1,128)S(1)}, s32[2,1,4]{2,1,0:T(1,128)}, u32[]{:S(2)}) copy-start(s32[2,1,4]{2,1,0:T(1,128)} %param.13) | copy-start | bytes 100
  16.7 110.2 %copy-start.5 = (bf16[1,1024,512]{2,1,0:T(8,128)(2,1)S(1)}, bf16[1,1024,512]{2,1,0:T(8,128)(2,1)}, u32[]{:S(2)}) copy-start(bf16[1,1024,512]{2,1,0:T(8,128)(2,1)} %param.16) | copy-start | bytes 3145732
  20.0 51.7 %copy-start = (f32[8,64,6,128]{3,1,2,0:T(8,128)S(1)}, f32[8,64,6,128]{3,1,2,0:T(8,128)}, u32[]{:S(2)}) copy-start(f32[8,64,6,128]{3,1,2,0:T(8,128)} %param.9) | copy-start | bytes 4718596
  20.0 51.7 %copy-start.8 = (s32[2]{0:T(128)S(1)}, s32[2]{0:T(128)}, u32[]{:S(2)}) copy-start(s32[2]{0:T(128)} %pad_add_fusion.pos) | copy-start | bytes 28
  20.0 51.1 %collective-permute-start.8 = (bf16[304,1024]{1,0:T(8,128)(2,1)}, bf16[304,1024]{1,0:T(8,128)(2,1)}, u32[]{:S(2)}, u32[]{:S(2)}) collective-permute-start(bf16[304,1024]{1,0:T(8,128)(2,1)} %get-tuple-element.36), channel_id=1, source_target_pairs={{0,8},{4,12},{8,0},{12,4},{16,24},{20,28},{24,16},{28,20},{1,9},{5... | collective-permute-start | bytes 1867784 | tf_op jit(solution)/shard_map/ppermute | solution.py:29
  20.1 51.0 %collective-permute-start.7 = (bf16[288,1024]{1,0:T(8,128)(2,1)}, bf16[288,1024]{1,0:T(8,128)(2,1)}, u32[]{:S(2)}, u32[]{:S(2)}) collective-permute-start(bf16[288,1024]{1,0:T(8,128)(2,1)} %get-tuple-element.35), channel_id=1, source_target_pairs={{0,8},{4,12},{8,0},{12,4},{16,24},{20,28},{24,16},{28,20},{1,9},{5... | collective-permute-start | bytes 1769480 | tf_op jit(solution)/shard_map/ppermute | solution.py:29
  22.1 49.0 %collective-permute-start.16 = (bf16[288,1024]{1,0:T(8,128)(2,1)}, bf16[288,1024]{1,0:T(8,128)(2,1)}, u32[]{:S(2)}, u32[]{:S(2)}) collective-permute-start(bf16[288,1024]{1,0:T(8,128)(2,1)} %get-tuple-element.35), channel_id=1, source_target_pairs={{0,16},{4,20},{8,24},{12,28},{16,0},{20,4},{24,8},{28,12},{1,17},{... | collective-permute-start | bytes 1769480 | tf_op jit(solution)/shard_map/ppermute | solution.py:29
  22.8 48.9 %copy-start.7 = (s32[2,8]{1,0:T(2,128)S(1)}, s32[2,8]{1,0:T(2,128)}, u32[]{:S(2)}) copy-start(s32[2,8]{1,0:T(2,128)} %select_reduce_fusion.table) | copy-start | bytes 196
  25.1 101.9 %copy-start.1 = (bf16[2,8,64,512]{3,2,1,0:T(8,128)(2,1)S(1)}, bf16[2,8,64,512]{3,2,1,0:T(8,128)(2,1)}, u32[]{:S(2)}) copy-start(bf16[2,8,64,512]{3,2,1,0:T(8,128)(2,1)} %param.12) | copy-start | bytes 3145732
  25.1 101.9 %copy-start.3 = (bf16[1,768,1024]{2,1,0:T(8,128)(2,1)S(1)}, bf16[1,768,1024]{2,1,0:T(8,128)(2,1)}, u32[]{:S(2)}) copy-start(bf16[1,768,1024]{2,1,0:T(8,128)(2,1)} %param.14) | copy-start | bytes 4718596
  25.1 101.9 %copy-start.10 = (f32[1,512]{1,0:T(1,128)S(1)}, f32[1,512]{1,0:T(1,128)}, u32[]{:S(2)}) copy-start(f32[1,512]{1,0:T(1,128)} %scale.1) | copy-start | bytes 6148
  25.1 55.3 %collective-permute-start.5 = (bf16[2,4,128,512]{3,2,1,0:T(8,128)(2,1)}, bf16[2,4,128,512]{3,2,1,0:T(8,128)(2,1)S(1)}, u32[]{:S(2)}, u32[]{:S(2)}) collective-permute-start(bf16[2,4,128,512]{3,2,1,0:T(8,128)(2,1)} %pick_radiances.1), channel_id=1, source_target_pairs={{0,4},{4,0},{8,12},{12,8},{16,20},{20,16},{24,28},{28,24},{1,5},{5... | collective-permute-start | bytes 3145736 | tf_op jit(solution)/shard_map/ppermute | solution.py:29
  29.1 48.0 %collective-permute-start.17 = (bf16[304,1024]{1,0:T(8,128)(2,1)}, bf16[304,1024]{1,0:T(8,128)(2,1)S(1)}, u32[]{:S(2)}, u32[]{:S(2)}) collective-permute-start(bf16[304,1024]{1,0:T(8,128)(2,1)} %get-tuple-element.36), channel_id=1, source_target_pairs={{0,16},{4,20},{8,24},{12,28},{16,0},{20,4},{24,8},{28,12},{1,17},{... | collective-permute-start | bytes 1867784 | tf_op jit(solution)/shard_map/ppermute | solution.py:29
  71.1 9.3 %collective-permute-start.9 = (bf16[288,1024]{1,0:T(8,128)(2,1)}, bf16[288,1024]{1,0:T(8,128)(2,1)S(1)}, u32[]{:S(2)}, u32[]{:S(2)}) collective-permute-start(bf16[288,1024]{1,0:T(8,128)(2,1)} %collective-permute-done.7.refs_2_), channel_id=1, source_target_pairs={{0,1},{1,0},{2,3},{3,2},{4,5},{5,4},{6,7},{7,6},{8,9},{9,8},{10,11... | collective-permute-start | bytes 1769480 | tf_op jit(solution)/shard_map/ppermute | solution.py:29
  71.1 16.4 %collective-permute-start.11 = (bf16[288,1024]{1,0:T(8,128)(2,1)}, bf16[288,1024]{1,0:T(8,128)(2,1)S(1)}, u32[]{:S(2)}, u32[]{:S(2)}) collective-permute-start(bf16[288,1024]{1,0:T(8,128)(2,1)} %collective-permute-done.7.refs_2_), channel_id=1, source_target_pairs={{0,2},{1,3},{2,0},{3,1},{4,6},{5,7},{6,4},{7,5},{8,10},{9,11},{10,... | collective-permute-start | bytes 1769480 | tf_op jit(solution)/shard_map/ppermute | solution.py:29
  71.1 16.4 %collective-permute-start.18 = (bf16[288,1024]{1,0:T(8,128)(2,1)}, bf16[288,1024]{1,0:T(8,128)(2,1)S(1)}, u32[]{:S(2)}, u32[]{:S(2)}) collective-permute-start(bf16[288,1024]{1,0:T(8,128)(2,1)} %collective-permute-done.16.refs_2_), channel_id=1, source_target_pairs={{0,1},{1,0},{2,3},{3,2},{4,5},{5,4},{6,7},{7,6},{8,9},{9,8},{10,11... | collective-permute-start | bytes 1769480 | tf_op jit(solution)/shard_map/ppermute | solution.py:29
  77.1 49.7 %collective-permute-start.4 = (bf16[2,4,128,768]{3,2,1,0:T(8,128)(2,1)S(1)}, bf16[2,4,128,768]{3,2,1,0:T(8,128)(2,1)S(1)}, u32[]{:S(2)}, u32[]{:S(2)}) collective-permute-start(bf16[2,4,128,768]{3,2,1,0:T(8,128)(2,1)S(1)} %get-tuple-element.32), channel_id=1, source_target_pairs={{0,4},{4,0},{8,12},{12,8},{16,20},{20,16},{24,28},{28,24},{1,5},{5... | collective-permute-start | bytes 4718600 | tf_op jit(solution)/shard_map/ppermute | solution.py:29
  80.4 22.3 %collective-permute-start.10 = (bf16[304,1024]{1,0:T(8,128)(2,1)}, bf16[304,1024]{1,0:T(8,128)(2,1)S(1)}, u32[]{:S(2)}, u32[]{:S(2)}) collective-permute-start(bf16[304,1024]{1,0:T(8,128)(2,1)} %collective-permute-done.8.refs_3_), channel_id=1, source_target_pairs={{0,1},{1,0},{2,3},{3,2},{4,5},{5,4},{6,7},{7,6},{8,9},{9,8},{10,11... | collective-permute-start | bytes 1867784 | tf_op jit(solution)/shard_map/ppermute | solution.py:29
  80.4 19.7 %collective-permute-start.20 = (bf16[288,1024]{1,0:T(8,128)(2,1)}, bf16[288,1024]{1,0:T(8,128)(2,1)S(1)}, u32[]{:S(2)}, u32[]{:S(2)}) collective-permute-start(bf16[288,1024]{1,0:T(8,128)(2,1)} %collective-permute-done.16.refs_2_), channel_id=1, source_target_pairs={{0,2},{1,3},{2,0},{3,1},{4,6},{5,7},{6,4},{7,5},{8,10},{9,11},{10,... | collective-permute-start | bytes 1769480 | tf_op jit(solution)/shard_map/ppermute | solution.py:29
  87.5 14.6 %collective-permute-start.25 = (bf16[288,1024]{1,0:T(8,128)(2,1)}, bf16[288,1024]{1,0:T(8,128)(2,1)S(1)}, u32[]{:S(2)}, u32[]{:S(2)}) collective-permute-start(bf16[288,1024]{1,0:T(8,128)(2,1)} %collective-permute-done.16.refs_2_), channel_id=1, source_target_pairs={{0,8},{4,12},{8,0},{12,4},{16,24},{20,28},{24,16},{28,20},{1,9},{5... | collective-permute-start | bytes 1769480 | tf_op jit(solution)/shard_map/ppermute | solution.py:29
  87.5 26.0 %collective-permute-start.12 = (bf16[304,1024]{1,0:T(8,128)(2,1)}, bf16[304,1024]{1,0:T(8,128)(2,1)S(1)}, u32[]{:S(2)}, u32[]{:S(2)}) collective-permute-start(bf16[304,1024]{1,0:T(8,128)(2,1)} %collective-permute-done.8.refs_3_), channel_id=1, source_target_pairs={{0,2},{1,3},{2,0},{3,1},{4,6},{5,7},{6,4},{7,5},{8,10},{9,11},{10,... | collective-permute-start | bytes 1867784 | tf_op jit(solution)/shard_map/ppermute | solution.py:29
  100.1 13.3 %collective-permute-start.19 = (bf16[304,1024]{1,0:T(8,128)(2,1)S(1)}, bf16[304,1024]{1,0:T(8,128)(2,1)S(1)}, u32[]{:S(2)}, u32[]{:S(2)}) collective-permute-start(bf16[304,1024]{1,0:T(8,128)(2,1)S(1)} %collective-permute-done.17.refs_3_), channel_id=1, source_target_pairs={{0,1},{1,0},{2,3},{3,2},{4,5},{5,4},{6,7},{7,6},{8,9},{9,8},{10,11... | collective-permute-start | bytes 1867784 | tf_op jit(solution)/shard_map/ppermute | solution.py:29
  102.1 24.2 %collective-permute-start.21 = (bf16[304,1024]{1,0:T(8,128)(2,1)S(1)}, bf16[304,1024]{1,0:T(8,128)(2,1)S(1)}, u32[]{:S(2)}, u32[]{:S(2)}) collective-permute-start(bf16[304,1024]{1,0:T(8,128)(2,1)S(1)} %collective-permute-done.17.refs_3_), channel_id=1, source_target_pairs={{0,2},{1,3},{2,0},{3,1},{4,6},{5,7},{6,4},{7,5},{8,10},{9,11},{10,... | collective-permute-start | bytes 1867784 | tf_op jit(solution)/shard_map/ppermute | solution.py:29
  102.7 23.7 %collective-permute-start.26 = (bf16[304,1024]{1,0:T(8,128)(2,1)S(1)}, bf16[304,1024]{1,0:T(8,128)(2,1)S(1)}, u32[]{:S(2)}, u32[]{:S(2)}) collective-permute-start(bf16[304,1024]{1,0:T(8,128)(2,1)S(1)} %collective-permute-done.17.refs_3_), channel_id=1, source_target_pairs={{0,8},{4,12},{8,0},{12,4},{16,24},{20,28},{24,16},{28,20},{1,9},{5... | collective-permute-start | bytes 1867784 | tf_op jit(solution)/shard_map/ppermute | solution.py:29
  113.5 12.9 %collective-permute-start.13 = (bf16[288,1024]{1,0:T(8,128)(2,1)S(1)}, bf16[288,1024]{1,0:T(8,128)(2,1)S(1)}, u32[]{:S(2)}, u32[]{:S(2)}) collective-permute-start(bf16[288,1024]{1,0:T(8,128)(2,1)S(1)} %collective-permute-done.11.refs_6_), channel_id=1, source_target_pairs={{0,1},{1,0},{2,3},{3,2},{4,5},{5,4},{6,7},{7,6},{8,9},{9,8},{10,11... | collective-permute-start | bytes 1769480 | tf_op jit(solution)/shard_map/ppermute | solution.py:29
  113.5 28.6 %collective-permute-start.14 = (bf16[304,1024]{1,0:T(8,128)(2,1)S(1)}, bf16[304,1024]{1,0:T(8,128)(2,1)S(1)}, u32[]{:S(2)}, u32[]{:S(2)}) collective-permute-start(bf16[304,1024]{1,0:T(8,128)(2,1)S(1)} %collective-permute-done.12.refs_7_), channel_id=1, source_target_pairs={{0,1},{1,0},{2,3},{3,2},{4,5},{5,4},{6,7},{7,6},{8,9},{9,8},{10,11... | collective-permute-start | bytes 1867784 | tf_op jit(solution)/shard_map/ppermute | solution.py:29
  126.4 16.3 %collective-permute-start.30 = (bf16[304,1024]{1,0:T(8,128)(2,1)S(1)}, bf16[304,1024]{1,0:T(8,128)(2,1)S(1)}, u32[]{:S(2)}, u32[]{:S(2)}) collective-permute-start(bf16[304,1024]{1,0:T(8,128)(2,1)S(1)} %collective-permute-done.21.refs_7_), channel_id=1, source_target_pairs={{0,8},{4,12},{8,0},{12,4},{16,24},{20,28},{24,16},{28,20},{1,9},{5... | collective-permute-start | bytes 1867784 | tf_op jit(solution)/shard_map/ppermute | solution.py:29
  126.4 8.4 %collective-permute-start.22 = (bf16[288,1024]{1,0:T(8,128)(2,1)S(1)}, bf16[288,1024]{1,0:T(8,128)(2,1)S(1)}, u32[]{:S(2)}, u32[]{:S(2)}) collective-permute-start(bf16[288,1024]{1,0:T(8,128)(2,1)S(1)} %collective-permute-done.20.refs_6_), channel_id=1, source_target_pairs={{0,1},{1,0},{2,3},{3,2},{4,5},{5,4},{6,7},{7,6},{8,9},{9,8},{10,11... | collective-permute-start | bytes 1769480 | tf_op jit(solution)/shard_map/ppermute | solution.py:29
  126.4 15.7 %collective-permute-start.29 = (bf16[288,1024]{1,0:T(8,128)(2,1)S(1)}, bf16[288,1024]{1,0:T(8,128)(2,1)S(1)}, u32[]{:S(2)}, u32[]{:S(2)}) collective-permute-start(bf16[288,1024]{1,0:T(8,128)(2,1)S(1)} %collective-permute-done.25.refs_2_), channel_id=1, source_target_pairs={{0,2},{1,3},{2,0},{3,1},{4,6},{5,7},{6,4},{7,5},{8,10},{9,11},{10,... | collective-permute-start | bytes 1769480 | tf_op jit(solution)/shard_map/ppermute | solution.py:29
  126.7 23.0 %collective-permute-start.23 = (bf16[304,1024]{1,0:T(8,128)(2,1)S(1)}, bf16[304,1024]{1,0:T(8,128)(2,1)S(1)}, u32[]{:S(2)}, u32[]{:S(2)}) collective-permute-start(bf16[304,1024]{1,0:T(8,128)(2,1)S(1)} %collective-permute-done.21.refs_7_), channel_id=1, source_target_pairs={{0,1},{1,0},{2,3},{3,2},{4,5},{5,4},{6,7},{7,6},{8,9},{9,8},{10,11... | collective-permute-start | bytes 1867784 | tf_op jit(solution)/shard_map/ppermute | solution.py:29
  127.0 1.6 copy-start.2
  134.7 25.4 %collective-permute-start.27 = (bf16[288,1024]{1,0:T(8,128)(2,1)S(1)}, bf16[288,1024]{1,0:T(8,128)(2,1)S(1)}, u32[]{:S(2)}, u32[]{:S(2)}) collective-permute-start(bf16[288,1024]{1,0:T(8,128)(2,1)S(1)} %collective-permute-done.25.refs_2_), channel_id=1, source_target_pairs={{0,1},{1,0},{2,3},{3,2},{4,5},{5,4},{6,7},{7,6},{8,9},{9,8},{10,11... | collective-permute-start | bytes 1769480 | tf_op jit(solution)/shard_map/ppermute | solution.py:29
  142.1 18.1 %collective-permute-start.28 = (bf16[304,1024]{1,0:T(8,128)(2,1)S(1)}, bf16[304,1024]{1,0:T(8,128)(2,1)S(1)}, u32[]{:S(2)}, u32[]{:S(2)}) collective-permute-start(bf16[304,1024]{1,0:T(8,128)(2,1)S(1)} %collective-permute-done.26.refs_3_), channel_id=1, source_target_pairs={{0,1},{1,0},{2,3},{3,2},{4,5},{5,4},{6,7},{7,6},{8,9},{9,8},{10,11... | collective-permute-start | bytes 1867784 | tf_op jit(solution)/shard_map/ppermute | solution.py:29
  142.1 20.1 %collective-permute-start.31 = (bf16[288,1024]{1,0:T(8,128)(2,1)S(1)}, bf16[288,1024]{1,0:T(8,128)(2,1)S(1)}, u32[]{:S(2)}, u32[]{:S(2)}) collective-permute-start(bf16[288,1024]{1,0:T(8,128)(2,1)S(1)} %collective-permute-done.29.refs_6_), channel_id=1, source_target_pairs={{0,1},{1,0},{2,3},{3,2},{4,5},{5,4},{6,7},{7,6},{8,9},{9,8},{10,11... | collective-permute-start | bytes 1769480 | tf_op jit(solution)/shard_map/ppermute | solution.py:29
  142.6 19.6 %collective-permute-start.32 = (bf16[304,1024]{1,0:T(8,128)(2,1)S(1)}, bf16[304,1024]{1,0:T(8,128)(2,1)S(1)}, u32[]{:S(2)}, u32[]{:S(2)}) collective-permute-start(bf16[304,1024]{1,0:T(8,128)(2,1)S(1)} %collective-permute-done.30.refs_7_), channel_id=1, source_target_pairs={{0,1},{1,0},{2,3},{3,2},{4,5},{5,4},{6,7},{7,6},{8,9},{9,8},{10,11... | collective-permute-start | bytes 1867784 | tf_op jit(solution)/shard_map/ppermute | solution.py:29
  149.8 22.1 %collective-permute-start.6 = (bf16[2,128,768]{2,1,0:T(8,128)(2,1)S(1)}, bf16[2,128,768]{2,1,0:T(8,128)(2,1)S(1)}, u32[]{:S(2)}, u32[]{:S(2)}) collective-permute-start(bf16[2,128,768]{2,1,0:T(8,128)(2,1)S(1)} %get-tuple-element.34), channel_id=1, source_target_pairs={{0,4},{4,0},{8,12},{12,8},{16,20},{20,16},{24,28},{28,24},{1,5},{5... | collective-permute-start | bytes 1179656 | tf_op jit(solution)/shard_map/ppermute | solution.py:29
  160.1 12.1 %collective-permute-start.15 = (bf16[2,128,768]{2,1,0:T(8,128)(2,1)S(1)}, bf16[2,128,768]{2,1,0:T(8,128)(2,1)S(1)}, u32[]{:S(2)}, u32[]{:S(2)}) collective-permute-start(bf16[2,128,768]{2,1,0:T(8,128)(2,1)S(1)} %get-tuple-element.38), channel_id=1, source_target_pairs={{0,4},{4,0},{8,12},{12,8},{16,20},{20,16},{24,28},{28,24},{1,5},{5... | collective-permute-start | bytes 1179656 | tf_op jit(solution)/shard_map/ppermute | solution.py:29
  160.2 20.4 %collective-permute-start.24 = (bf16[2,128,768]{2,1,0:T(8,128)(2,1)S(1)}, bf16[2,128,768]{2,1,0:T(8,128)(2,1)S(1)}, u32[]{:S(2)}, u32[]{:S(2)}) collective-permute-start(bf16[2,128,768]{2,1,0:T(8,128)(2,1)S(1)} %get-tuple-element.40), channel_id=1, source_target_pairs={{0,4},{4,0},{8,12},{12,8},{16,20},{20,16},{24,28},{28,24},{1,5},{5... | collective-permute-start | bytes 1179656 | tf_op jit(solution)/shard_map/ppermute | solution.py:29
  166.0 18.8 %collective-permute-start.33 = (bf16[1,128,768]{2,1,0:T(8,128)(2,1)S(1)}, bf16[1,128,768]{2,1,0:T(8,128)(2,1)S(1)}, u32[]{:S(2)}, u32[]{:S(2)}) collective-permute-start(bf16[1,128,768]{2,1,0:T(8,128)(2,1)S(1)} %get-tuple-element.42), channel_id=1, source_target_pairs={{0,4},{4,0},{8,12},{12,8},{16,20},{20,16},{24,28},{28,24},{1,5},{5... | collective-permute-start | bytes 589832 | tf_op jit(solution)/shard_map/ppermute | solution.py:29
  169.9 23.6 %collective-permute-start.38 = (bf16[1,128,768]{2,1,0:T(8,128)(2,1)S(1)}, bf16[1,128,768]{2,1,0:T(8,128)(2,1)S(1)}, u32[]{:S(2)}, u32[]{:S(2)}) collective-permute-start(bf16[1,128,768]{2,1,0:T(8,128)(2,1)S(1)} %get-tuple-element.51), channel_id=1, source_target_pairs={{0,4},{4,0},{8,12},{12,8},{16,20},{20,16},{24,28},{28,24},{1,5},{5... | collective-permute-start | bytes 589832 | tf_op jit(solution)/shard_map/ppermute | solution.py:29
  185.8 13.6 %collective-permute-start.34 = (bf16[6,64,128]{2,1,0:T(8,128)(2,1)S(1)}, bf16[6,64,128]{2,1,0:T(8,128)(2,1)S(1)}, u32[]{:S(2)}, u32[]{:S(2)}) collective-permute-start(bf16[6,64,128]{2,1,0:T(8,128)(2,1)S(1)} %get-tuple-element.44), channel_id=1, source_target_pairs={{0,1},{1,2},{2,3},{4,5},{5,6},{6,7},{8,9},{9,10},{10,11},{12,13},{... | collective-permute-start | bytes 294920 | tf_op jit(solution)/shard_map/ppermute | solution.py:37
  187.8 11.7 %collective-permute-start.35 = (bf16[6,64,128]{2,1,0:T(8,128)(2,1)S(1)}, bf16[6,64,128]{2,1,0:T(8,128)(2,1)S(1)}, u32[]{:S(2)}, u32[]{:S(2)}) collective-permute-start(bf16[6,64,128]{2,1,0:T(8,128)(2,1)S(1)} %get-tuple-element.45), channel_id=1, source_target_pairs={{1,0},{2,1},{3,2},{5,4},{6,5},{7,6},{9,8},{10,9},{11,10},{13,12},{... | collective-permute-start | bytes 294920 | tf_op jit(solution)/shard_map/ppermute | solution.py:37
  191.4 4.0 %collective-permute-start.36 = (f32[8,6,128]{2,1,0:T(8,128)S(1)}, f32[8,6,128]{2,1,0:T(8,128)S(1)}, u32[]{:S(2)}, u32[]{:S(2)}) collective-permute-start(f32[8,6,128]{2,1,0:T(8,128)S(1)} %get-tuple-element.46), channel_id=1, source_target_pairs={{0,4},{4,8},{8,12},{12,16},{16,20},{20,24},{24,28},{28,0},{1,5},{5... | collective-permute-start | bytes 73736 | tf_op jit(solution)/shard_map/ppermute | solution.py:37
  192.9 6.6 %collective-permute-start.37 = (f32[8,6,128]{2,1,0:T(8,128)S(1)}, f32[8,6,128]{2,1,0:T(8,128)S(1)}, u32[]{:S(2)}, u32[]{:S(2)}) collective-permute-start(f32[8,6,128]{2,1,0:T(8,128)S(1)} %get-tuple-element.47), channel_id=1, source_target_pairs={{0,28},{4,0},{8,4},{12,8},{16,12},{20,16},{24,20},{28,24},{1,29},{... | collective-permute-start | bytes 73736 | tf_op jit(solution)/shard_map/ppermute | solution.py:37
  199.5 14.4 %copy-start.4 = (f32[8,64,6,128]{3,1,2,0:T(8,128)S(1)}, f32[8,64,6,128]{3,1,2,0:T(8,128)}, u32[]{:S(2)}) copy-start(f32[8,64,6,128]{3,1,2,0:T(8,128)} %param.10) | copy-start | bytes 4718596
  201.5 12.3 %collective-permute-start.39 = (f32[6,64,128]{2,1,0:T(8,128)S(1)}, f32[6,64,128]{2,1,0:T(8,128)S(1)}, u32[]{:S(2)}, u32[]{:S(2)}) collective-permute-start(f32[6,64,128]{2,1,0:T(8,128)S(1)} %get-tuple-element.53), channel_id=1, source_target_pairs={{0,1},{1,2},{2,3},{4,5},{5,6},{6,7},{8,9},{9,10},{10,11},{12,13},{... | collective-permute-start | bytes 589832 | tf_op jit(solution)/shard_map/ppermute | solution.py:37
  203.5 10.4 %collective-permute-start.40 = (f32[6,64,128]{2,1,0:T(8,128)S(1)}, f32[6,64,128]{2,1,0:T(8,128)S(1)}, u32[]{:S(2)}, u32[]{:S(2)}) collective-permute-start(f32[6,64,128]{2,1,0:T(8,128)S(1)} %get-tuple-element.54), channel_id=1, source_target_pairs={{1,0},{2,1},{3,2},{5,4},{6,5},{7,6},{9,8},{10,9},{11,10},{13,12},{... | collective-permute-start | bytes 589832 | tf_op jit(solution)/shard_map/ppermute | solution.py:37
  207.1 4.0 %collective-permute-start.41 = (f32[8,6,128]{2,1,0:T(8,128)S(1)}, f32[8,6,128]{2,1,0:T(8,128)S(1)}, u32[]{:S(2)}, u32[]{:S(2)}) collective-permute-start(f32[8,6,128]{2,1,0:T(8,128)S(1)} %get-tuple-element.55), channel_id=1, source_target_pairs={{0,4},{4,8},{8,12},{12,16},{16,20},{20,24},{24,28},{28,0},{1,5},{5... | collective-permute-start | bytes 73736 | tf_op jit(solution)/shard_map/ppermute | solution.py:37
  207.2 6.7 %collective-permute-start.42 = (f32[8,6,128]{2,1,0:T(8,128)S(1)}, f32[8,6,128]{2,1,0:T(8,128)S(1)}, u32[]{:S(2)}, u32[]{:S(2)}) collective-permute-start(f32[8,6,128]{2,1,0:T(8,128)S(1)} %get-tuple-element.56), channel_id=1, source_target_pairs={{0,28},{4,0},{8,4},{12,8},{16,12},{20,16},{24,20},{28,24},{1,29},{... | collective-permute-start | bytes 73736 | tf_op jit(solution)/shard_map/ppermute | solution.py:37

commit v5 on v4

--- a/solution.py
+++ b/solution.py
@@ -34,6 +34,14 @@
     pairs = [(i, (i + step) % count) for i in range(count)]
     if not periodic:
         pairs = [(i, j) for i, j in pairs if j == i + step]
+    return lax.ppermute(array, axis, pairs)
+
+
+def paired(array, axis, start, periodic):
+    count = lax.axis_size(axis)
+    pairs = []
+    for i in range(start, count if periodic else count - 1, 2):
+        pairs += [(i, (i + 1) % count), ((i + 1) % count, i)]
     return lax.ppermute(array, axis, pairs)
 
 
@@ -287,23 +295,26 @@
 
 def backward_kernel(first_half, *refs):
     if first_half:
-        adj, south, north, west, east, base, kappa, extra, out, lo, hi, we, ea, pad = refs
+        pos, adj, inner_row, outer_row, close, distant, base, kappa, extra, out, lo, hi, we, ea, pad = refs
         shift, row0 = SIDE, 0
     else:
-        adj, south, north, west, east, base, extra, other, out, pad = refs
+        pos, adj, inner_row, outer_row, close, distant, base, extra, other, out, pad = refs
         shift, row0 = EDGE, 1
     rows, fields, width, levels = adj.shape
     inner = pl.ds(EDGE, width)
+    even_lon = pos[0] % 2 == 0
 
     def place(r, _):
         pad[r + 1, :, inner] = adj[r].astype(F32)
-        pad[r + 1, :, EDGE - 1 : EDGE] = west[r][:, None]
-        pad[r + 1, :, EDGE + width : EDGE + width + 1] = east[r][:, None]
+        one, two = close[r], distant[r]
+        pad[r + 1, :, EDGE - 1 : EDGE] = jnp.where(even_lon, two, one)[:, None]
+        pad[r + 1, :, EDGE + width : EDGE + width + 1] = jnp.where(even_lon, one, two)[:, None]
         return 0
 
     lax.fori_loop(0, rows, place, 0)
-    pad[0, :, inner] = south[...].astype(F32)
-    pad[rows + 1, :, inner] = north[...].astype(F32)
+    even = pos[1] % 2 == 0
+    pad[jnp.where(even, rows + 1, 0), :, inner] = inner_row[...].astype(F32)
+    pad[jnp.where(even, 0, rows + 1), :, inner] = outer_row[...].astype(F32)
     half = 0.5 * ADVECTION
 
     def diffusion(r, at):
@@ -342,8 +353,9 @@
                 value -= half * meridional
             if first_half:
                 value += extra[r, f].astype(F32)
-                we[r, f : f + 1] = value[0:1]
-                ea[r, f : f + 1] = value[width - 1 : width]
+                begin, end = value[0:1], value[width - 1 : width]
+                we[r, f : f + 1] = jnp.where(even_lon, end, begin)
+                ea[r, f : f + 1] = jnp.where(even_lon, begin, end)
             else:
                 value += extra[r, f] - other[r, f]
             out[r, f] = value
@@ -351,21 +363,21 @@
 
     lax.fori_loop(0, rows, row, 0)
     if first_half:
-        lo[...] = out[0]
-        hi[...] = out[rows - 1]
+        lo[...] = out[jnp.where(even, rows - 1, 0)]
+        hi[...] = out[jnp.where(even, 0, rows - 1)]
 
 
 def halo_of_adjoint(edges):
-    low, high, west, east = edges
+    inner, outer, close, distant = edges
     return (
-        shifted(high, "lat", 1, False),
-        shifted(low, "lat", -1, False),
-        shifted(east, "lon", 1, True),
-        shifted(west, "lon", -1, True),
+        paired(inner, "lat", 0, False),
+        paired(outer, "lat", 1, False),
+        paired(close, "lon", 0, True),
+        paired(distant, "lon", 1, True),
     )
 
 
-def backward_first(adjoint, rims, first, wide, forcing):
+def backward_first(pos, adjoint, rims, first, wide, forcing):
     rows, fields, width, levels = adjoint.shape
     line = jax.ShapeDtypeStruct((fields, width, levels), F32)
     side = jax.ShapeDtypeStruct((rows, fields, levels), F32)
@@ -380,27 +392,28 @@
         functools.partial(backward_kernel, True),
         grid=(1,),
         out_shape=[jax.ShapeDtypeStruct(adjoint.shape, F32), line, line, side, side],
-        in_specs=[whole(a.shape) for a in (adjoint, *rims, first)]
+        in_specs=[SMEM]
+        + [whole(a.shape) for a in (adjoint, *rims, first)]
         + [kappa_spec, whole(forcing.shape)],
         out_specs=[whole(adjoint.shape), whole(line.shape), whole(line.shape), whole(side.shape), whole(side.shape)],
         scratch_shapes=[pltpu.VMEM((rows + 2, fields, width + 2 * EDGE, levels), F32)],
         compiler_params=params(16),
         name="backward_first",
-    )(adjoint, *rims, first, wide, forcing)
+    )(pos, adjoint, *rims, first, wide, forcing)
     return out, edges
 
 
-def backward_last(adjoint, rims, wide, state, background):
+def backward_last(pos, adjoint, rims, wide, state, background):
     rows, fields, width, levels = adjoint.shape
     return pl.pallas_call(
         functools.partial(backward_kernel, False),
         out_shape=jax.ShapeDtypeStruct(adjoint.shape, F32),
-        in_specs=[VMEM] * 8,
+        in_specs=[SMEM] + [VMEM] * 8,
         out_specs=VMEM,
         scratch_shapes=[pltpu.VMEM((rows + 2, fields, width + 2 * EDGE, levels), F32)],
         compiler_params=params(16),
         name="backward_last",
-    )(adjoint, *rims, wide, state, background)
+    )(pos, adjoint, *rims, wide, state, background)
 
 
 def nt_dot(a, b):
@@ -520,7 +533,7 @@
             pltpu.VMEM((lines, ch), BF16),
         ]
         + ([] if own else [pltpu.VMEM(shape, BF16) for shape in ((cin, h1), (h1, h2), (h2, ch))]),
-        compiler_params=params(20),
+        compiler_params=params(14 + 2 * (group - 1)),
         cost_estimate=pl.CostEstimate(
             flops=4 * lines * (cin * h1 + h1 * h2 + h2 * ch),
             transcendentals=lines * (h1 + h2),
@@ -547,6 +560,7 @@
         return 0
 
     lax.fori_loop(0, rows * width // span, block, 0)
+    even_lon = pos[0] % 2 == 0
 
     def row(r, _):
         lines = pl.ds(pl.multiple_of(r * width, width), width)
@@ -555,14 +569,16 @@
             out[r, f] = value
             if edges:
                 wide = value.astype(F32)
-                rims[2][r, f : f + 1] = wide[0:1]
-                rims[3][r, f : f + 1] = wide[width - 1 : width]
+                begin, end = wide[0:1], wide[width - 1 : width]
+                rims[2][r, f : f + 1] = jnp.where(even_lon, end, begin)
+                rims[3][r, f : f + 1] = jnp.where(even_lon, begin, end)
         return 0
 
     lax.fori_loop(0, rows, row, 0)
     if edges:
-        rims[0][...] = out[0]
-        rims[1][...] = out[rows - 1]
+        even = pos[1] % 2 == 0
+        rims[0][...] = out[jnp.where(even, rows - 1, 0)]
+        rims[1][...] = out[jnp.where(even, 0, rows - 1)]
 
 
 def collect(slot, pos, owners, answers, shape, edges):
@@ -620,8 +636,8 @@
     shape = state.shape
     late, *edges = collect(1, pos, owners, answers[1], shape, True)
     (early,) = collect(0, pos, owners, answers[0], shape, False)
-    costate, edges = backward_first(late, halo_of_adjoint(edges), first, wide, early)
-    gradient = backward_last(costate, halo_of_adjoint(edges), wide, state, background)
+    costate, edges = backward_first(pos, late, halo_of_adjoint(edges), first, wide, early)
+    gradient = backward_last(pos, costate, halo_of_adjoint(edges), wide, state, background)
     return gradient.transpose(0, 2, 1, 3)
 
 

time: 218 us -> 215 us (0.986); the launches traced: 217 us -> 212 us
  starting transfers between devices: 47.8 us -> 41.2 us
    ppermute x12 -> x4, starting transfers between devices: 25.6 us -> 10.4 us  [shifted(): return lax.ppermute(array, axis, pairs)]
    ppermute x12 -> x4, waiting for transfers between devices: 10.5 us -> 0.88 us  [shifted(): return lax.ppermute(array, axis, pairs)]
    ppermute x0 -> x8, waiting for transfers between devices: none -> 9.43 us  [paired(): return lax.ppermute(array, axis, pairs)]
    ppermute x0 -> x8, starting transfers between devices: none -> 8.65 us  [paired(): return lax.ppermute(array, axis, pairs)]
where the time goes in v5:
time: 215 us; the launch traced here: 212 us
  waiting for transfers between devices  115 us (53%)
  Pallas kernels  47.2 us (22%)
  starting transfers between devices  41.2 us (19%)
  local copies, waits for them, and re-layouts  4.71 us (2%)
  other arithmetic  3 us (1%)
    ppermute x31, waiting for transfers between devices, exchange(): return lax.ppermute(array, axis, [(i, i ^ mask) for i in range(count)])  105 us
    pallas_call x5, Pallas kernels, instrument(): pl.pallas_call(functools.partial(instrument_kernel, group, served, n_lat,...  27.7 us
    ppermute x31, starting transfers between devices, exchange(): return lax.ppermute(array, axis, [(i, i ^ mask) for i in range(count)])  22.2 us
    ppermute x4, starting transfers between devices, shifted(): return lax.ppermute(array, axis, pairs)  10.4 us
    ppermute x8, waiting for transfers between devices, paired(): return lax.ppermute(array, axis, pairs)  9.43 us
    ppermute x8, starting transfers between devices, paired(): return lax.ppermute(array, axis, pairs)  8.65 us
    pallas_call x1, Pallas kernels, forward(): pl.pallas_call(functools.partial(forward_kernel, group), out_shape=outs,...  5.39 us
  transfers between devices with their start and end apart: 43, of which 15 were waited for; matrix products, arithmetic and copies ran while one was open for 2% of the time, Pallas kernels for 19%

profile of v5, /device:TPU:30, one launch (start us, length us, event | category | flops | bytes accessed | tf_op | source)
XLA Modules:
  0.0 211.6 jit_solution(1538061375826738047)
XLA Ops:
  0.0 0.8 slice_bitcast_fusion.3
  0.8 1.1 fusion.1
  1.9 0.6 collective-permute-start.1
  2.5 4.3 %collective-permute-start = (f32[8,7,2,128]{3,2,1,0:T(2,128)S(1)}, f32[8,7,2,128]{3,2,1,0:T(2,128)S(1)}, u32[]{:S(2)}, u32[]{:S(2)}) collective-permute-start(f32[8,7,2,128]{3,2,1,0:T(2,128)S(1)} %pad_maximum_fusion.2), channel_id=1, source_target_pairs={{0,4},{4,8},{8,12},{12,16},{16,20},{20,24},{24,28},{28,0},{1,5},{5... | collective-permute-start | bytes 172040 | tf_op jit(solution)/shard_map/ppermute | solution.py:37
  6.8 1.2 fusion
  8.0 0.9 collective-permute-done.1.east
  8.9 0.8 pad_maximum_fusion
  9.7 1.9 collective-permute-start.2
  11.7 0.8 pad_maximum_fusion.1
  12.5 3.6 %collective-permute-start.3 = (f32[2,7,68,128]{3,2,1,0:T(8,128)}, f32[2,7,68,128]{3,2,1,0:T(8,128)}, u32[]{:S(2)}, u32[]{:S(2)}) collective-permute-start(f32[2,7,68,128]{3,2,1,0:T(8,128)} %pad_maximum_fusion.1), channel_id=1, source_target_pairs={{1,0},{2,1},{3,2},{5,4},{6,5},{7,6},{9,8},{10,9},{11,10},{13,12},{... | collective-permute-start | bytes 1462280 | tf_op jit(solution)/shard_map/ppermute | solution.py:37
  16.1 0.6 pad_add_fusion.pos.refs_0_
  16.7 3.3 %pack.1 = (bf16[288,1024]{1,0:T(8,128)(2,1)}, bf16[304,1024]{1,0:T(8,128)(2,1)}) custom-call(s32[2]{0:T(128)} %pad_add_fusion.pos.refs_0_, bf16[768,1024]{1,0:T(8,128)(2,1)} %bitcast.30, bf16[1024,1024]{1,0:T(8,128)(2,1)} %bitcast.28, bf16[1024,512]{1,0:T(8,128)(2,1)} %bitcast.33, f32[1,512]{1,0:T(1,128)} %scale.1), custom_call_target="tpu_custom_call" | custom-call | tf_op jit(solution)/shard_map/pack/pallas_call | solution.py:111
  20.0 0.1 collective-permute-start.8
  20.1 2.0 collective-permute-start.7
  22.1 0.7 select_reduce_fusion.table
  22.8 2.3 %pick_radiances.1 = bf16[2,4,128,512]{3,2,1,0:T(8,128)(2,1)} custom-call(s32[2]{0:T(128)} %pad_add_fusion.pos.refs_0_, s32[2,8]{1,0:T(2,128)} %select_reduce_fusion.table, bf16[2,512,512]{2,1,0:T(8,128)(2,1)} %bitcast.22), custom_call_target="tpu_custom_call" | custom-call | tf_op jit(solution)/shard_map/pick_radiances/pallas_call | solution.py:162
  25.1 4.0 %collective-permute-start.5 = (bf16[2,4,128,512]{3,2,1,0:T(8,128)(2,1)}, bf16[2,4,128,512]{3,2,1,0:T(8,128)(2,1)S(1)}, u32[]{:S(2)}, u32[]{:S(2)}) collective-permute-start(bf16[2,4,128,512]{3,2,1,0:T(8,128)(2,1)} %pick_radiances.1), channel_id=1, source_target_pairs={{0,4},{4,0},{8,12},{12,8},{16,20},{20,16},{24,28},{28,24},{1,5},{5... | collective-permute-start | bytes 3145736 | tf_op jit(solution)/shard_map/ppermute | solution.py:29
  29.1 42.0 %collective-permute-done.7.refs_2_ = bf16[288,1024]{1,0:T(8,128)(2,1)} collective-permute-done((bf16[288,1024]{1,0:T(8,128)(2,1)}, bf16[288,1024]{1,0:T(8,128)(2,1)}, u32[]{:S(2)}, u32[]{:S(2)}) %collective-permute-start.7) | collective-permute-done | bytes 589856 | tf_op jit(solution)/shard_map/ppermute | solution.py:29
  71.1 0.6 collective-permute-start.18
  71.7 5.4 %forward.1 = (f32[12,7,96,128]{3,2,1,0:T(8,128)S(1)}, f32[10,6,80,128]{3,2,1,0:T(8,128)S(1)}, bf16[2,512,768]{2,1,0:T(8,128)(2,1)S(1)}, bf16[2,4,128,768]{3,2,1,0:T(8,128)(2,1)S(1)}) custom-call(s32[2]{0:T(128)S(1)} %copy-done.7, s32[2,8]{1,0:T(2,128)S(1)} %copy-done.8, f32[8,6,64,128]{3,2,1,0:T(8,128)S(1)} %bitcast.20, f32[8,64,128]{2,1,0:T(8,128)S(1)} %copy-done.6, ...), custom_call_target="tpu_custom_call" | custom-call | tf_op jit(solution)/shard_map/forward/pallas_call | solution.py:268
  77.1 3.3 %collective-permute-start.4 = (bf16[2,4,128,768]{3,2,1,0:T(8,128)(2,1)S(1)}, bf16[2,4,128,768]{3,2,1,0:T(8,128)(2,1)S(1)}, u32[]{:S(2)}, u32[]{:S(2)}) collective-permute-start(bf16[2,4,128,768]{3,2,1,0:T(8,128)(2,1)S(1)} %get-tuple-element.32), channel_id=1, source_target_pairs={{0,4},{4,0},{8,12},{12,8},{16,20},{20,16},{24,28},{28,24},{1,5},{5... | collective-permute-start | bytes 4718600 | tf_op jit(solution)/shard_map/ppermute | solution.py:29
  80.4 1.7 collective-permute-start.20
  82.2 5.3 %collective-permute-done.11.refs_6_ = bf16[288,1024]{1,0:T(8,128)(2,1)S(1)} collective-permute-done((bf16[288,1024]{1,0:T(8,128)(2,1)}, bf16[288,1024]{1,0:T(8,128)(2,1)S(1)}, u32[]{:S(2)}, u32[]{:S(2)}) %collective-permute-start.11) | collective-permute-done | bytes 589856 | tf_op jit(solution)/shard_map/ppermute | solution.py:29
  87.5 12.6 %collective-permute-done.20.refs_6_ = bf16[288,1024]{1,0:T(8,128)(2,1)S(1)} collective-permute-done((bf16[288,1024]{1,0:T(8,128)(2,1)}, bf16[288,1024]{1,0:T(8,128)(2,1)S(1)}, u32[]{:S(2)}, u32[]{:S(2)}) %collective-permute-start.20) | collective-permute-done | bytes 589856 | tf_op jit(solution)/shard_map/ppermute | solution.py:29
  100.1 2.0 collective-permute-done.25.refs_2_
  102.1 0.6 collective-permute-start.21
  102.7 0.3 collective-permute-start.26
  103.0 10.5 %collective-permute-done.12.refs_7_ = bf16[304,1024]{1,0:T(8,128)(2,1)S(1)} collective-permute-done((bf16[304,1024]{1,0:T(8,128)(2,1)}, bf16[304,1024]{1,0:T(8,128)(2,1)S(1)}, u32[]{:S(2)}, u32[]{:S(2)}) %collective-permute-start.12) | collective-permute-done | bytes 622624 | tf_op jit(solution)/shard_map/ppermute | solution.py:29
  113.5 0.5 collective-permute-start.14
  114.0 12.4 %collective-permute-done.21.refs_7_ = bf16[304,1024]{1,0:T(8,128)(2,1)S(1)} collective-permute-done((bf16[304,1024]{1,0:T(8,128)(2,1)S(1)}, bf16[304,1024]{1,0:T(8,128)(2,1)S(1)}, u32[]{:S(2)}, u32[]{:S(2)}) %collective-permute-start.21) | collective-permute-done | bytes 622624 | tf_op jit(solution)/shard_map/ppermute | solution.py:29
  126.4 0.3 collective-permute-start.29
  126.7 0.2 collective-permute-start.23
  127.0 1.6 copy-done.2
  128.6 6.1 %shard_map.91 = (bf16[2,128,768]{2,1,0:T(8,128)(2,1)S(1)}, bf16[2,128,768]{2,1,0:T(8,128)(2,1)S(1)}) custom-call(s32[2]{0:T(128)S(1)} %copy-done.7, s32[2,8]{1,0:T(2,128)S(1)} %copy-done.8, bf16[2,512,768]{2,1,0:T(8,128)(2,1)S(1)} %get-tuple-element.31.columns, bf16[2,512,512]{2,1,0:T(8,128)(2,1)S(1)} %bitcast.23, ...), custom_call_target="tpu_custom_call" | custom-call | flops 4831838208 | bytes 6815744 | tf_op jit(solution)/shard_map/pallas_call | solution.py:521
  134.7 0.4 collective-permute-start.27
  135.1 7.0 %collective-permute-done.29.refs_6_ = bf16[288,1024]{1,0:T(8,128)(2,1)S(1)} collective-permute-done((bf16[288,1024]{1,0:T(8,128)(2,1)S(1)}, bf16[288,1024]{1,0:T(8,128)(2,1)S(1)}, u32[]{:S(2)}, u32[]{:S(2)}) %collective-permute-start.29) | collective-permute-done | bytes 589856 | tf_op jit(solution)/shard_map/ppermute | solution.py:29
  142.1 0.5 collective-permute-start.31
  142.7 7.0 %shard_map.92 = (bf16[2,128,768]{2,1,0:T(8,128)(2,1)S(1)}, bf16[2,128,768]{2,1,0:T(8,128)(2,1)S(1)}) custom-call(s32[2]{0:T(128)S(1)} %copy-done.7, s32[2,8]{1,0:T(2,128)S(1)} %copy-done.8, bf16[2,512,768]{2,1,0:T(8,128)(2,1)S(1)} %get-tuple-element.31.columns, bf16[2,512,512]{2,1,0:T(8,128)(2,1)S(1)} %bitcast.24, ...), custom_call_target="tpu_custom_call" | custom-call | flops 4831838208 | bytes 6815744 | tf_op jit(solution)/shard_map/pallas_call | solution.py:521
  149.8 3.3 %collective-permute-start.6 = (bf16[2,128,768]{2,1,0:T(8,128)(2,1)S(1)}, bf16[2,128,768]{2,1,0:T(8,128)(2,1)S(1)}, u32[]{:S(2)}, u32[]{:S(2)}) collective-permute-start(bf16[2,128,768]{2,1,0:T(8,128)(2,1)S(1)} %get-tuple-element.34), channel_id=1, source_target_pairs={{0,4},{4,0},{8,12},{12,8},{16,20},{20,16},{24,28},{28,24},{1,5},{5... | collective-permute-start | bytes 1179656 | tf_op jit(solution)/shard_map/ppermute | solution.py:29
  153.1 7.0 %shard_map.93 = (bf16[2,128,768]{2,1,0:T(8,128)(2,1)S(1)}, bf16[2,128,768]{2,1,0:T(8,128)(2,1)S(1)}) custom-call(s32[2]{0:T(128)S(1)} %copy-done.7, s32[2,8]{1,0:T(2,128)S(1)} %copy-done.8, bf16[2,512,768]{2,1,0:T(8,128)(2,1)S(1)} %get-tuple-element.31.columns, bf16[2,512,512]{2,1,0:T(8,128)(2,1)S(1)} %bitcast.25, ...), custom_call_target="tpu_custom_call" | custom-call | flops 4831838208 | bytes 6815744 | tf_op jit(solution)/shard_map/pallas_call | solution.py:521
  160.1 0.1 collective-permute-start.15
  160.2 2.0 collective-permute-start.24
  162.2 3.7 %shard_map.94 = (bf16[1,128,768]{2,1,0:T(8,128)(2,1)S(1)}, bf16[1,128,768]{2,1,0:T(8,128)(2,1)S(1)}) custom-call(s32[2]{0:T(128)S(1)} %copy-done.7, s32[2,8]{1,0:T(2,128)S(1)} %copy-done.8, bf16[2,512,768]{2,1,0:T(8,128)(2,1)S(1)} %get-tuple-element.31.columns, bf16[2,512,512]{2,1,0:T(8,128)(2,1)S(1)} %bitcast.26, ...), custom_call_target="tpu_custom_call" | custom-call | flops 2415919104 | bytes 5767168 | tf_op jit(solution)/shard_map/pallas_call | solution.py:521
  166.0 0.2 collective-permute-start.33
  166.1 3.7 %shard_map.96 = (bf16[1,128,768]{2,1,0:T(8,128)(2,1)S(1)}, bf16[1,128,768]{2,1,0:T(8,128)(2,1)S(1)}) custom-call(s32[2]{0:T(128)S(1)} %copy-done.7, s32[2,8]{1,0:T(2,128)S(1)} %copy-done.8, bf16[2,512,768]{2,1,0:T(8,128)(2,1)S(1)} %get-tuple-element.31.columns, bf16[2,512,512]{2,1,0:T(8,128)(2,1)S(1)} %bitcast.27, ...), custom_call_target="tpu_custom_call" | custom-call | flops 2415919104 | bytes 5767168 | tf_op jit(solution)/shard_map/pallas_call | solution.py:521
  169.9 2.0 collective-permute-start.38
  171.9 0.3 collective-permute-done.15.refs_3_
  172.2 8.4 %collective-permute-done.24.refs_5_ = bf16[2,128,768]{2,1,0:T(8,128)(2,1)S(1)} collective-permute-done((bf16[2,128,768]{2,1,0:T(8,128)(2,1)S(1)}, bf16[2,128,768]{2,1,0:T(8,128)(2,1)S(1)}, u32[]{:S(2)}, u32[]{:S(2)}) %collective-permute-start.24) | collective-permute-done | bytes 393248 | tf_op jit(solution)/shard_map/ppermute | solution.py:29
  180.6 4.2 %collective-permute-done.33.refs_7_ = bf16[1,128,768]{2,1,0:T(8,128)(2,1)S(1)} collective-permute-done((bf16[1,128,768]{2,1,0:T(8,128)(2,1)S(1)}, bf16[1,128,768]{2,1,0:T(8,128)(2,1)S(1)}, u32[]{:S(2)}, u32[]{:S(2)}) %collective-permute-start.33) | collective-permute-done | bytes 196640 | tf_op jit(solution)/shard_map/ppermute | solution.py:29
  184.8 1.0 shard_map.95
  185.9 0.1 collective-permute-start.34
  185.9 2.3 %collective-permute-start.35 = (bf16[6,64,128]{2,1,0:T(8,128)(2,1)S(1)}, bf16[6,64,128]{2,1,0:T(8,128)(2,1)S(1)}, u32[]{:S(2)}, u32[]{:S(2)}) collective-permute-start(bf16[6,64,128]{2,1,0:T(8,128)(2,1)S(1)} %get-tuple-element.45), channel_id=1, source_target_pairs={{1,2},{2,1},{5,6},{6,5},{9,10},{10,9},{13,14},{14,13},{17,18},{18,... | collective-permute-start | bytes 294920 | tf_op jit(solution)/shard_map/ppermute | solution.py:45
  188.2 1.4 collective-permute-start.36
  189.6 1.4 collective-permute-start.37
  191.0 1.0 shard_map.97.refs_8_
  192.0 0.2 collective-permute-done.36.refs_4_
  192.2 4.0 %collective-permute-done.37.refs_5_ = f32[8,6,128]{2,1,0:T(8,128)S(1)} collective-permute-done((f32[8,6,128]{2,1,0:T(8,128)S(1)}, f32[8,6,128]{2,1,0:T(8,128)S(1)}, u32[]{:S(2)}, u32[]{:S(2)}) %collective-permute-start.37) | collective-permute-done | bytes 24608 | tf_op jit(solution)/shard_map/ppermute | solution.py:45
  196.2 2.7 %backward_first.1 = (f32[8,6,64,128]{3,2,1,0:T(8,128)S(1)}, f32[6,64,128]{2,1,0:T(8,128)S(1)}, f32[6,64,128]{2,1,0:T(8,128)S(1)}, f32[8,6,128]{2,1,0:T(8,128)S(1)}, f32[8,6,128]{2,1,0:T(8,128)S(1)}) custom-call(s32[2]{0:T(128)S(1)} %copy-done.7, bf16[8,6,64,128]{3,2,1,0:T(8,128)(2,1)S(1)} %get-tuple-element.43.refs_1_, ...), custom_call_target="tpu_custom_call" | custom-call | tf_op jit(solution)/shard_map/backward_first/pallas_call | solution.py:391
  198.9 0.1 collective-permute-start.39
  199.0 1.9 collective-permute-start.40
  201.0 1.5 collective-permute-start.42
  202.5 2.4 %collective-permute-done.41.refs_4_ = f32[8,6,128]{2,1,0:T(8,128)S(1)} collective-permute-done((f32[8,6,128]{2,1,0:T(8,128)S(1)}, f32[8,6,128]{2,1,0:T(8,128)S(1)}, u32[]{:S(2)}, u32[]{:S(2)}) %collective-permute-start.41) | collective-permute-done | bytes 24608 | tf_op jit(solution)/shard_map/ppermute | solution.py:45
  204.9 2.8 %collective-permute-done.42.refs_5_ = f32[8,6,128]{2,1,0:T(8,128)S(1)} collective-permute-done((f32[8,6,128]{2,1,0:T(8,128)S(1)}, f32[8,6,128]{2,1,0:T(8,128)S(1)}, u32[]{:S(2)}, u32[]{:S(2)}) %collective-permute-start.42) | collective-permute-done | bytes 24608 | tf_op jit(solution)/shard_map/ppermute | solution.py:45
  207.7 3.9 %backward_last.1 = f32[8,6,64,128]{3,2,1,0:T(8,128)} custom-call(s32[2]{0:T(128)S(1)} %copy-done.7, f32[8,6,64,128]{3,2,1,0:T(8,128)S(1)} %get-tuple-element.52.refs_1_, f32[6,64,128]{2,1,0:T(8,128)S(1)} %collective-permute-done.39.refs_2_, f32[6,64,128]{2,1,0:T(8,128)S(1)} %collective-permute-done.40.refs_3_, ...), custom_call_target="tpu_custom_call" | custom-call | tf_op jit(solution)/shard_map/backward_last/pallas_call | solution.py:408
  (68 shorter events, 0.4 us)
Async XLA Ops:
  0.0 8.0 %copy-start.6 = (f32[8,64,128]{2,1,0:T(8,128)S(1)}, f32[8,64,128]{2,1,0:T(8,128)}, u32[]{:S(2)}) copy-start(f32[8,64,128]{2,1,0:T(8,128)} %kappa.1) | copy-start | bytes 786436
  1.9 6.9 %collective-permute-start.1 = (f32[8,7,2,128]{3,2,1,0:T(2,128)S(1)}, f32[8,7,2,128]{3,2,1,0:T(2,128)S(1)}, u32[]{:S(2)}, u32[]{:S(2)}) collective-permute-start(f32[8,7,2,128]{3,2,1,0:T(2,128)S(1)} %pad_maximum_fusion.3), channel_id=1, source_target_pairs={{0,28},{4,0},{8,4},{12,8},{16,12},{20,16},{24,20},{28,24},{1,29},{... | collective-permute-start | bytes 172040 | tf_op jit(solution)/shard_map/ppermute | solution.py:37
  2.5 6.3 %collective-permute-start = (f32[8,7,2,128]{3,2,1,0:T(2,128)S(1)}, f32[8,7,2,128]{3,2,1,0:T(2,128)S(1)}, u32[]{:S(2)}, u32[]{:S(2)}) collective-permute-start(f32[8,7,2,128]{3,2,1,0:T(2,128)S(1)} %pad_maximum_fusion.2), channel_id=1, source_target_pairs={{0,4},{4,8},{8,12},{12,16},{16,20},{20,24},{24,28},{28,0},{1,5},{5... | collective-permute-start | bytes 172040 | tf_op jit(solution)/shard_map/ppermute | solution.py:37
  9.7 15.3 %collective-permute-start.2 = (f32[2,7,68,128]{3,2,1,0:T(8,128)}, f32[2,7,68,128]{3,2,1,0:T(8,128)S(1)}, u32[]{:S(2)}, u32[]{:S(2)}) collective-permute-start(f32[2,7,68,128]{3,2,1,0:T(8,128)} %pad_maximum_fusion), channel_id=1, source_target_pairs={{0,1},{1,2},{2,3},{4,5},{5,6},{6,7},{8,9},{9,10},{10,11},{12,13},{... | collective-permute-start | bytes 1462280 | tf_op jit(solution)/shard_map/ppermute | solution.py:37
  12.5 16.6 %collective-permute-start.3 = (f32[2,7,68,128]{3,2,1,0:T(8,128)}, f32[2,7,68,128]{3,2,1,0:T(8,128)}, u32[]{:S(2)}, u32[]{:S(2)}) collective-permute-start(f32[2,7,68,128]{3,2,1,0:T(8,128)} %pad_maximum_fusion.1), channel_id=1, source_target_pairs={{1,0},{2,1},{3,2},{5,4},{6,5},{7,6},{9,8},{10,9},{11,10},{13,12},{... | collective-permute-start | bytes 1462280 | tf_op jit(solution)/shard_map/ppermute | solution.py:37
  16.7 5.4 %copy-start.9 = (s32[2,1,4]{2,1,0:T(1,128)S(1)}, s32[2,1,4]{2,1,0:T(1,128)}, u32[]{:S(2)}) copy-start(s32[2,1,4]{2,1,0:T(1,128)} %param.13) | copy-start | bytes 100
  16.7 110.2 %copy-start.5 = (bf16[1,1024,512]{2,1,0:T(8,128)(2,1)S(1)}, bf16[1,1024,512]{2,1,0:T(8,128)(2,1)}, u32[]{:S(2)}) copy-start(bf16[1,1024,512]{2,1,0:T(8,128)(2,1)} %param.16) | copy-start | bytes 3145732
  20.0 51.7 %copy-start = (f32[8,64,6,128]{3,1,2,0:T(8,128)S(1)}, f32[8,64,6,128]{3,1,2,0:T(8,128)}, u32[]{:S(2)}) copy-start(f32[8,64,6,128]{3,1,2,0:T(8,128)} %param.9) | copy-start | bytes 4718596
  20.0 51.7 %copy-start.7 = (s32[2]{0:T(128)S(1)}, s32[2]{0:T(128)}, u32[]{:S(2)}) copy-start(s32[2]{0:T(128)} %pad_add_fusion.pos.refs_0_) | copy-start | bytes 28
  20.0 51.1 %collective-permute-start.8 = (bf16[304,1024]{1,0:T(8,128)(2,1)}, bf16[304,1024]{1,0:T(8,128)(2,1)}, u32[]{:S(2)}, u32[]{:S(2)}) collective-permute-start(bf16[304,1024]{1,0:T(8,128)(2,1)} %get-tuple-element.36), channel_id=1, source_target_pairs={{0,8},{4,12},{8,0},{12,4},{16,24},{20,28},{24,16},{28,20},{1,9},{5... | collective-permute-start | bytes 1867784 | tf_op jit(solution)/shard_map/ppermute | solution.py:29
  20.1 51.0 %collective-permute-start.7 = (bf16[288,1024]{1,0:T(8,128)(2,1)}, bf16[288,1024]{1,0:T(8,128)(2,1)}, u32[]{:S(2)}, u32[]{:S(2)}) collective-permute-start(bf16[288,1024]{1,0:T(8,128)(2,1)} %get-tuple-element.35), channel_id=1, source_target_pairs={{0,8},{4,12},{8,0},{12,4},{16,24},{20,28},{24,16},{28,20},{1,9},{5... | collective-permute-start | bytes 1769480 | tf_op jit(solution)/shard_map/ppermute | solution.py:29
  22.1 49.0 %collective-permute-start.16 = (bf16[288,1024]{1,0:T(8,128)(2,1)}, bf16[288,1024]{1,0:T(8,128)(2,1)}, u32[]{:S(2)}, u32[]{:S(2)}) collective-permute-start(bf16[288,1024]{1,0:T(8,128)(2,1)} %get-tuple-element.35), channel_id=1, source_target_pairs={{0,16},{4,20},{8,24},{12,28},{16,0},{20,4},{24,8},{28,12},{1,17},{... | collective-permute-start | bytes 1769480 | tf_op jit(solution)/shard_map/ppermute | solution.py:29
  22.8 48.9 %copy-start.8 = (s32[2,8]{1,0:T(2,128)S(1)}, s32[2,8]{1,0:T(2,128)}, u32[]{:S(2)}) copy-start(s32[2,8]{1,0:T(2,128)} %select_reduce_fusion.table) | copy-start | bytes 196
  25.1 101.9 %copy-start.1 = (bf16[2,8,64,512]{3,2,1,0:T(8,128)(2,1)S(1)}, bf16[2,8,64,512]{3,2,1,0:T(8,128)(2,1)}, u32[]{:S(2)}) copy-start(bf16[2,8,64,512]{3,2,1,0:T(8,128)(2,1)} %param.12) | copy-start | bytes 3145732
  25.1 101.9 %copy-start.3 = (bf16[1,768,1024]{2,1,0:T(8,128)(2,1)S(1)}, bf16[1,768,1024]{2,1,0:T(8,128)(2,1)}, u32[]{:S(2)}) copy-start(bf16[1,768,1024]{2,1,0:T(8,128)(2,1)} %param.14) | copy-start | bytes 4718596
  25.1 101.9 %copy-start.10 = (f32[1,512]{1,0:T(1,128)S(1)}, f32[1,512]{1,0:T(1,128)}, u32[]{:S(2)}) copy-start(f32[1,512]{1,0:T(1,128)} %scale.1) | copy-start | bytes 6148
  25.1 55.3 %collective-permute-start.5 = (bf16[2,4,128,512]{3,2,1,0:T(8,128)(2,1)}, bf16[2,4,128,512]{3,2,1,0:T(8,128)(2,1)S(1)}, u32[]{:S(2)}, u32[]{:S(2)}) collective-permute-start(bf16[2,4,128,512]{3,2,1,0:T(8,128)(2,1)} %pick_radiances.1), channel_id=1, source_target_pairs={{0,4},{4,0},{8,12},{12,8},{16,20},{20,16},{24,28},{28,24},{1,5},{5... | collective-permute-start | bytes 3145736 | tf_op jit(solution)/shard_map/ppermute | solution.py:29
  29.1 48.0 %collective-permute-start.17 = (bf16[304,1024]{1,0:T(8,128)(2,1)}, bf16[304,1024]{1,0:T(8,128)(2,1)S(1)}, u32[]{:S(2)}, u32[]{:S(2)}) collective-permute-start(bf16[304,1024]{1,0:T(8,128)(2,1)} %get-tuple-element.36), channel_id=1, source_target_pairs={{0,16},{4,20},{8,24},{12,28},{16,0},{20,4},{24,8},{28,12},{1,17},{... | collective-permute-start | bytes 1867784 | tf_op jit(solution)/shard_map/ppermute | solution.py:29
  71.1 9.3 %collective-permute-start.9 = (bf16[288,1024]{1,0:T(8,128)(2,1)}, bf16[288,1024]{1,0:T(8,128)(2,1)S(1)}, u32[]{:S(2)}, u32[]{:S(2)}) collective-permute-start(bf16[288,1024]{1,0:T(8,128)(2,1)} %collective-permute-done.7.refs_2_), channel_id=1, source_target_pairs={{0,1},{1,0},{2,3},{3,2},{4,5},{5,4},{6,7},{7,6},{8,9},{9,8},{10,11... | collective-permute-start | bytes 1769480 | tf_op jit(solution)/shard_map/ppermute | solution.py:29
  71.1 16.4 %collective-permute-start.11 = (bf16[288,1024]{1,0:T(8,128)(2,1)}, bf16[288,1024]{1,0:T(8,128)(2,1)S(1)}, u32[]{:S(2)}, u32[]{:S(2)}) collective-permute-start(bf16[288,1024]{1,0:T(8,128)(2,1)} %collective-permute-done.7.refs_2_), channel_id=1, source_target_pairs={{0,2},{1,3},{2,0},{3,1},{4,6},{5,7},{6,4},{7,5},{8,10},{9,11},{10,... | collective-permute-start | bytes 1769480 | tf_op jit(solution)/shard_map/ppermute | solution.py:29
  71.1 16.4 %collective-permute-start.18 = (bf16[288,1024]{1,0:T(8,128)(2,1)}, bf16[288,1024]{1,0:T(8,128)(2,1)S(1)}, u32[]{:S(2)}, u32[]{:S(2)}) collective-permute-start(bf16[288,1024]{1,0:T(8,128)(2,1)} %collective-permute-done.16.refs_2_), channel_id=1, source_target_pairs={{0,1},{1,0},{2,3},{3,2},{4,5},{5,4},{6,7},{7,6},{8,9},{9,8},{10,11... | collective-permute-start | bytes 1769480 | tf_op jit(solution)/shard_map/ppermute | solution.py:29
  77.1 49.7 %collective-permute-start.4 = (bf16[2,4,128,768]{3,2,1,0:T(8,128)(2,1)S(1)}, bf16[2,4,128,768]{3,2,1,0:T(8,128)(2,1)S(1)}, u32[]{:S(2)}, u32[]{:S(2)}) collective-permute-start(bf16[2,4,128,768]{3,2,1,0:T(8,128)(2,1)S(1)} %get-tuple-element.32), channel_id=1, source_target_pairs={{0,4},{4,0},{8,12},{12,8},{16,20},{20,16},{24,28},{28,24},{1,5},{5... | collective-permute-start | bytes 4718600 | tf_op jit(solution)/shard_map/ppermute | solution.py:29
  80.4 22.3 %collective-permute-start.10 = (bf16[304,1024]{1,0:T(8,128)(2,1)}, bf16[304,1024]{1,0:T(8,128)(2,1)S(1)}, u32[]{:S(2)}, u32[]{:S(2)}) collective-permute-start(bf16[304,1024]{1,0:T(8,128)(2,1)} %collective-permute-done.8.refs_3_), channel_id=1, source_target_pairs={{0,1},{1,0},{2,3},{3,2},{4,5},{5,4},{6,7},{7,6},{8,9},{9,8},{10,11... | collective-permute-start | bytes 1867784 | tf_op jit(solution)/shard_map/ppermute | solution.py:29
  80.4 19.7 %collective-permute-start.20 = (bf16[288,1024]{1,0:T(8,128)(2,1)}, bf16[288,1024]{1,0:T(8,128)(2,1)S(1)}, u32[]{:S(2)}, u32[]{:S(2)}) collective-permute-start(bf16[288,1024]{1,0:T(8,128)(2,1)} %collective-permute-done.16.refs_2_), channel_id=1, source_target_pairs={{0,2},{1,3},{2,0},{3,1},{4,6},{5,7},{6,4},{7,5},{8,10},{9,11},{10,... | collective-permute-start | bytes 1769480 | tf_op jit(solution)/shard_map/ppermute | solution.py:29
  87.5 14.6 %collective-permute-start.25 = (bf16[288,1024]{1,0:T(8,128)(2,1)}, bf16[288,1024]{1,0:T(8,128)(2,1)S(1)}, u32[]{:S(2)}, u32[]{:S(2)}) collective-permute-start(bf16[288,1024]{1,0:T(8,128)(2,1)} %collective-permute-done.16.refs_2_), channel_id=1, source_target_pairs={{0,8},{4,12},{8,0},{12,4},{16,24},{20,28},{24,16},{28,20},{1,9},{5... | collective-permute-start | bytes 1769480 | tf_op jit(solution)/shard_map/ppermute | solution.py:29
  87.5 26.0 %collective-permute-start.12 = (bf16[304,1024]{1,0:T(8,128)(2,1)}, bf16[304,1024]{1,0:T(8,128)(2,1)S(1)}, u32[]{:S(2)}, u32[]{:S(2)}) collective-permute-start(bf16[304,1024]{1,0:T(8,128)(2,1)} %collective-permute-done.8.refs_3_), channel_id=1, source_target_pairs={{0,2},{1,3},{2,0},{3,1},{4,6},{5,7},{6,4},{7,5},{8,10},{9,11},{10,... | collective-permute-start | bytes 1867784 | tf_op jit(solution)/shard_map/ppermute | solution.py:29
  100.1 13.3 %collective-permute-start.19 = (bf16[304,1024]{1,0:T(8,128)(2,1)S(1)}, bf16[304,1024]{1,0:T(8,128)(2,1)S(1)}, u32[]{:S(2)}, u32[]{:S(2)}) collective-permute-start(bf16[304,1024]{1,0:T(8,128)(2,1)S(1)} %collective-permute-done.17.refs_3_), channel_id=1, source_target_pairs={{0,1},{1,0},{2,3},{3,2},{4,5},{5,4},{6,7},{7,6},{8,9},{9,8},{10,11... | collective-permute-start | bytes 1867784 | tf_op jit(solution)/shard_map/ppermute | solution.py:29
  102.1 24.2 %collective-permute-start.21 = (bf16[304,1024]{1,0:T(8,128)(2,1)S(1)}, bf16[304,1024]{1,0:T(8,128)(2,1)S(1)}, u32[]{:S(2)}, u32[]{:S(2)}) collective-permute-start(bf16[304,1024]{1,0:T(8,128)(2,1)S(1)} %collective-permute-done.17.refs_3_), channel_id=1, source_target_pairs={{0,2},{1,3},{2,0},{3,1},{4,6},{5,7},{6,4},{7,5},{8,10},{9,11},{10,... | collective-permute-start | bytes 1867784 | tf_op jit(solution)/shard_map/ppermute | solution.py:29
  102.7 23.7 %collective-permute-start.26 = (bf16[304,1024]{1,0:T(8,128)(2,1)S(1)}, bf16[304,1024]{1,0:T(8,128)(2,1)S(1)}, u32[]{:S(2)}, u32[]{:S(2)}) collective-permute-start(bf16[304,1024]{1,0:T(8,128)(2,1)S(1)} %collective-permute-done.17.refs_3_), channel_id=1, source_target_pairs={{0,8},{4,12},{8,0},{12,4},{16,24},{20,28},{24,16},{28,20},{1,9},{5... | collective-permute-start | bytes 1867784 | tf_op jit(solution)/shard_map/ppermute | solution.py:29
  113.5 12.9 %collective-permute-start.13 = (bf16[288,1024]{1,0:T(8,128)(2,1)S(1)}, bf16[288,1024]{1,0:T(8,128)(2,1)S(1)}, u32[]{:S(2)}, u32[]{:S(2)}) collective-permute-start(bf16[288,1024]{1,0:T(8,128)(2,1)S(1)} %collective-permute-done.11.refs_6_), channel_id=1, source_target_pairs={{0,1},{1,0},{2,3},{3,2},{4,5},{5,4},{6,7},{7,6},{8,9},{9,8},{10,11... | collective-permute-start | bytes 1769480 | tf_op jit(solution)/shard_map/ppermute | solution.py:29
  113.5 28.6 %collective-permute-start.14 = (bf16[304,1024]{1,0:T(8,128)(2,1)S(1)}, bf16[304,1024]{1,0:T(8,128)(2,1)S(1)}, u32[]{:S(2)}, u32[]{:S(2)}) collective-permute-start(bf16[304,1024]{1,0:T(8,128)(2,1)S(1)} %collective-permute-done.12.refs_7_), channel_id=1, source_target_pairs={{0,1},{1,0},{2,3},{3,2},{4,5},{5,4},{6,7},{7,6},{8,9},{9,8},{10,11... | collective-permute-start | bytes 1867784 | tf_op jit(solution)/shard_map/ppermute | solution.py:29
  126.4 16.3 %collective-permute-start.30 = (bf16[304,1024]{1,0:T(8,128)(2,1)S(1)}, bf16[304,1024]{1,0:T(8,128)(2,1)S(1)}, u32[]{:S(2)}, u32[]{:S(2)}) collective-permute-start(bf16[304,1024]{1,0:T(8,128)(2,1)S(1)} %collective-permute-done.21.refs_7_), channel_id=1, source_target_pairs={{0,8},{4,12},{8,0},{12,4},{16,24},{20,28},{24,16},{28,20},{1,9},{5... | collective-permute-start | bytes 1867784 | tf_op jit(solution)/shard_map/ppermute | solution.py:29
  126.4 8.4 %collective-permute-start.22 = (bf16[288,1024]{1,0:T(8,128)(2,1)S(1)}, bf16[288,1024]{1,0:T(8,128)(2,1)S(1)}, u32[]{:S(2)}, u32[]{:S(2)}) collective-permute-start(bf16[288,1024]{1,0:T(8,128)(2,1)S(1)} %collective-permute-done.20.refs_6_), channel_id=1, source_target_pairs={{0,1},{1,0},{2,3},{3,2},{4,5},{5,4},{6,7},{7,6},{8,9},{9,8},{10,11... | collective-permute-start | bytes 1769480 | tf_op jit(solution)/shard_map/ppermute | solution.py:29
  126.4 15.7 %collective-permute-start.29 = (bf16[288,1024]{1,0:T(8,128)(2,1)S(1)}, bf16[288,1024]{1,0:T(8,128)(2,1)S(1)}, u32[]{:S(2)}, u32[]{:S(2)}) collective-permute-start(bf16[288,1024]{1,0:T(8,128)(2,1)S(1)} %collective-permute-done.25.refs_2_), channel_id=1, source_target_pairs={{0,2},{1,3},{2,0},{3,1},{4,6},{5,7},{6,4},{7,5},{8,10},{9,11},{10,... | collective-permute-start | bytes 1769480 | tf_op jit(solution)/shard_map/ppermute | solution.py:29
  126.7 23.0 %collective-permute-start.23 = (bf16[304,1024]{1,0:T(8,128)(2,1)S(1)}, bf16[304,1024]{1,0:T(8,128)(2,1)S(1)}, u32[]{:S(2)}, u32[]{:S(2)}) collective-permute-start(bf16[304,1024]{1,0:T(8,128)(2,1)S(1)} %collective-permute-done.21.refs_7_), channel_id=1, source_target_pairs={{0,1},{1,0},{2,3},{3,2},{4,5},{5,4},{6,7},{7,6},{8,9},{9,8},{10,11... | collective-permute-start | bytes 1867784 | tf_op jit(solution)/shard_map/ppermute | solution.py:29
  127.0 1.6 copy-start.2
  134.7 25.4 %collective-permute-start.27 = (bf16[288,1024]{1,0:T(8,128)(2,1)S(1)}, bf16[288,1024]{1,0:T(8,128)(2,1)S(1)}, u32[]{:S(2)}, u32[]{:S(2)}) collective-permute-start(bf16[288,1024]{1,0:T(8,128)(2,1)S(1)} %collective-permute-done.25.refs_2_), channel_id=1, source_target_pairs={{0,1},{1,0},{2,3},{3,2},{4,5},{5,4},{6,7},{7,6},{8,9},{9,8},{10,11... | collective-permute-start | bytes 1769480 | tf_op jit(solution)/shard_map/ppermute | solution.py:29
  142.1 18.1 %collective-permute-start.28 = (bf16[304,1024]{1,0:T(8,128)(2,1)S(1)}, bf16[304,1024]{1,0:T(8,128)(2,1)S(1)}, u32[]{:S(2)}, u32[]{:S(2)}) collective-permute-start(bf16[304,1024]{1,0:T(8,128)(2,1)S(1)} %collective-permute-done.26.refs_3_), channel_id=1, source_target_pairs={{0,1},{1,0},{2,3},{3,2},{4,5},{5,4},{6,7},{7,6},{8,9},{9,8},{10,11... | collective-permute-start | bytes 1867784 | tf_op jit(solution)/shard_map/ppermute | solution.py:29
  142.1 20.1 %collective-permute-start.31 = (bf16[288,1024]{1,0:T(8,128)(2,1)S(1)}, bf16[288,1024]{1,0:T(8,128)(2,1)S(1)}, u32[]{:S(2)}, u32[]{:S(2)}) collective-permute-start(bf16[288,1024]{1,0:T(8,128)(2,1)S(1)} %collective-permute-done.29.refs_6_), channel_id=1, source_target_pairs={{0,1},{1,0},{2,3},{3,2},{4,5},{5,4},{6,7},{7,6},{8,9},{9,8},{10,11... | collective-permute-start | bytes 1769480 | tf_op jit(solution)/shard_map/ppermute | solution.py:29
  142.6 19.6 %collective-permute-start.32 = (bf16[304,1024]{1,0:T(8,128)(2,1)S(1)}, bf16[304,1024]{1,0:T(8,128)(2,1)S(1)}, u32[]{:S(2)}, u32[]{:S(2)}) collective-permute-start(bf16[304,1024]{1,0:T(8,128)(2,1)S(1)} %collective-permute-done.30.refs_7_), channel_id=1, source_target_pairs={{0,1},{1,0},{2,3},{3,2},{4,5},{5,4},{6,7},{7,6},{8,9},{9,8},{10,11... | collective-permute-start | bytes 1867784 | tf_op jit(solution)/shard_map/ppermute | solution.py:29
  149.8 22.1 %collective-permute-start.6 = (bf16[2,128,768]{2,1,0:T(8,128)(2,1)S(1)}, bf16[2,128,768]{2,1,0:T(8,128)(2,1)S(1)}, u32[]{:S(2)}, u32[]{:S(2)}) collective-permute-start(bf16[2,128,768]{2,1,0:T(8,128)(2,1)S(1)} %get-tuple-element.34), channel_id=1, source_target_pairs={{0,4},{4,0},{8,12},{12,8},{16,20},{20,16},{24,28},{28,24},{1,5},{5... | collective-permute-start | bytes 1179656 | tf_op jit(solution)/shard_map/ppermute | solution.py:29
  160.1 12.1 %collective-permute-start.15 = (bf16[2,128,768]{2,1,0:T(8,128)(2,1)S(1)}, bf16[2,128,768]{2,1,0:T(8,128)(2,1)S(1)}, u32[]{:S(2)}, u32[]{:S(2)}) collective-permute-start(bf16[2,128,768]{2,1,0:T(8,128)(2,1)S(1)} %get-tuple-element.38), channel_id=1, source_target_pairs={{0,4},{4,0},{8,12},{12,8},{16,20},{20,16},{24,28},{28,24},{1,5},{5... | collective-permute-start | bytes 1179656 | tf_op jit(solution)/shard_map/ppermute | solution.py:29
  160.2 20.4 %collective-permute-start.24 = (bf16[2,128,768]{2,1,0:T(8,128)(2,1)S(1)}, bf16[2,128,768]{2,1,0:T(8,128)(2,1)S(1)}, u32[]{:S(2)}, u32[]{:S(2)}) collective-permute-start(bf16[2,128,768]{2,1,0:T(8,128)(2,1)S(1)} %get-tuple-element.40), channel_id=1, source_target_pairs={{0,4},{4,0},{8,12},{12,8},{16,20},{20,16},{24,28},{28,24},{1,5},{5... | collective-permute-start | bytes 1179656 | tf_op jit(solution)/shard_map/ppermute | solution.py:29
  166.0 18.8 %collective-permute-start.33 = (bf16[1,128,768]{2,1,0:T(8,128)(2,1)S(1)}, bf16[1,128,768]{2,1,0:T(8,128)(2,1)S(1)}, u32[]{:S(2)}, u32[]{:S(2)}) collective-permute-start(bf16[1,128,768]{2,1,0:T(8,128)(2,1)S(1)} %get-tuple-element.42), channel_id=1, source_target_pairs={{0,4},{4,0},{8,12},{12,8},{16,20},{20,16},{24,28},{28,24},{1,5},{5... | collective-permute-start | bytes 589832 | tf_op jit(solution)/shard_map/ppermute | solution.py:29
  169.9 21.1 %collective-permute-start.38 = (bf16[1,128,768]{2,1,0:T(8,128)(2,1)S(1)}, bf16[1,128,768]{2,1,0:T(8,128)(2,1)S(1)}, u32[]{:S(2)}, u32[]{:S(2)}) collective-permute-start(bf16[1,128,768]{2,1,0:T(8,128)(2,1)S(1)} %get-tuple-element.51), channel_id=1, source_target_pairs={{0,4},{4,0},{8,12},{12,8},{16,20},{20,16},{24,28},{28,24},{1,5},{5... | collective-permute-start | bytes 589832 | tf_op jit(solution)/shard_map/ppermute | solution.py:29
  185.9 10.4 %collective-permute-start.34 = (bf16[6,64,128]{2,1,0:T(8,128)(2,1)S(1)}, bf16[6,64,128]{2,1,0:T(8,128)(2,1)S(1)}, u32[]{:S(2)}, u32[]{:S(2)}) collective-permute-start(bf16[6,64,128]{2,1,0:T(8,128)(2,1)S(1)} %get-tuple-element.44), channel_id=1, source_target_pairs={{0,1},{1,0},{2,3},{3,2},{4,5},{5,4},{6,7},{7,6},{8,9},{9,8},{10,11... | collective-permute-start | bytes 294920 | tf_op jit(solution)/shard_map/ppermute | solution.py:45
  185.9 10.3 %collective-permute-start.35 = (bf16[6,64,128]{2,1,0:T(8,128)(2,1)S(1)}, bf16[6,64,128]{2,1,0:T(8,128)(2,1)S(1)}, u32[]{:S(2)}, u32[]{:S(2)}) collective-permute-start(bf16[6,64,128]{2,1,0:T(8,128)(2,1)S(1)} %get-tuple-element.45), channel_id=1, source_target_pairs={{1,2},{2,1},{5,6},{6,5},{9,10},{10,9},{13,14},{14,13},{17,18},{18,... | collective-permute-start | bytes 294920 | tf_op jit(solution)/shard_map/ppermute | solution.py:45
  188.2 4.0 %collective-permute-start.36 = (f32[8,6,128]{2,1,0:T(8,128)S(1)}, f32[8,6,128]{2,1,0:T(8,128)S(1)}, u32[]{:S(2)}, u32[]{:S(2)}) collective-permute-start(f32[8,6,128]{2,1,0:T(8,128)S(1)} %get-tuple-element.46), channel_id=1, source_target_pairs={{0,4},{4,0},{8,12},{12,8},{16,20},{20,16},{24,28},{28,24},{1,5},{5... | collective-permute-start | bytes 73736 | tf_op jit(solution)/shard_map/ppermute | solution.py:45
  189.6 6.6 %collective-permute-start.37 = (f32[8,6,128]{2,1,0:T(8,128)S(1)}, f32[8,6,128]{2,1,0:T(8,128)S(1)}, u32[]{:S(2)}, u32[]{:S(2)}) collective-permute-start(f32[8,6,128]{2,1,0:T(8,128)S(1)} %get-tuple-element.47), channel_id=1, source_target_pairs={{4,8},{8,4},{12,16},{16,12},{20,24},{24,20},{28,0},{0,28},{5,9},{9... | collective-permute-start | bytes 73736 | tf_op jit(solution)/shard_map/ppermute | solution.py:45
  196.2 11.5 %copy-start.4 = (f32[8,64,6,128]{3,1,2,0:T(8,128)S(1)}, f32[8,64,6,128]{3,1,2,0:T(8,128)}, u32[]{:S(2)}) copy-start(f32[8,64,6,128]{3,1,2,0:T(8,128)} %param.10) | copy-start | bytes 4718596
  198.9 8.8 %collective-permute-start.39 = (f32[6,64,128]{2,1,0:T(8,128)S(1)}, f32[6,64,128]{2,1,0:T(8,128)S(1)}, u32[]{:S(2)}, u32[]{:S(2)}) collective-permute-start(f32[6,64,128]{2,1,0:T(8,128)S(1)} %get-tuple-element.53), channel_id=1, source_target_pairs={{0,1},{1,0},{2,3},{3,2},{4,5},{5,4},{6,7},{7,6},{8,9},{9,8},{10,11... | collective-permute-start | bytes 589832 | tf_op jit(solution)/shard_map/ppermute | solution.py:45
  199.0 8.7 %collective-permute-start.40 = (f32[6,64,128]{2,1,0:T(8,128)S(1)}, f32[6,64,128]{2,1,0:T(8,128)S(1)}, u32[]{:S(2)}, u32[]{:S(2)}) collective-permute-start(f32[6,64,128]{2,1,0:T(8,128)S(1)} %get-tuple-element.54), channel_id=1, source_target_pairs={{1,2},{2,1},{5,6},{6,5},{9,10},{10,9},{13,14},{14,13},{17,18},{18,... | collective-permute-start | bytes 589832 | tf_op jit(solution)/shard_map/ppermute | solution.py:45
  200.9 4.0 %collective-permute-start.41 = (f32[8,6,128]{2,1,0:T(8,128)S(1)}, f32[8,6,128]{2,1,0:T(8,128)S(1)}, u32[]{:S(2)}, u32[]{:S(2)}) collective-permute-start(f32[8,6,128]{2,1,0:T(8,128)S(1)} %get-tuple-element.55), channel_id=1, source_target_pairs={{0,4},{4,0},{8,12},{12,8},{16,20},{20,16},{24,28},{28,24},{1,5},{5... | collective-permute-start | bytes 73736 | tf_op jit(solution)/shard_map/ppermute | solution.py:45
  201.0 6.7 %collective-permute-start.42 = (f32[8,6,128]{2,1,0:T(8,128)S(1)}, f32[8,6,128]{2,1,0:T(8,128)S(1)}, u32[]{:S(2)}, u32[]{:S(2)}) collective-permute-start(f32[8,6,128]{2,1,0:T(8,128)S(1)} %get-tuple-element.56), channel_id=1, source_target_pairs={{4,8},{8,4},{12,16},{16,12},{20,24},{24,20},{28,0},{0,28},{5,9},{9... | collective-permute-start | bytes 73736 | tf_op jit(solution)/shard_map/ppermute | solution.py:45

commit v6 on v5

--- a/solution.py
+++ b/solution.py
@@ -298,7 +298,7 @@
         pos, adj, inner_row, outer_row, close, distant, base, kappa, extra, out, lo, hi, we, ea, pad = refs
         shift, row0 = SIDE, 0
     else:
-        pos, adj, inner_row, outer_row, close, distant, base, extra, other, out, pad = refs
+        pos, adj, inner_row, outer_row, close, distant, base, extra, other, result, out, pad, sems = refs
         shift, row0 = EDGE, 1
     rows, fields, width, levels = adj.shape
     inner = pl.ds(EDGE, width)
@@ -359,9 +359,14 @@
             else:
                 value += extra[r, f] - other[r, f]
             out[r, f] = value
+        if not first_half:
+            pltpu.make_async_copy(out.at[r], result.at[r], sems.at[r]).start()
         return 0
 
     lax.fori_loop(0, rows, row, 0)
+    if not first_half:
+        for r in range(rows):
+            pltpu.make_async_copy(out.at[r], result.at[r], sems.at[r]).wait()
     if first_half:
         lo[...] = out[jnp.where(even, rows - 1, 0)]
         hi[...] = out[jnp.where(even, 0, rows - 1)]
@@ -409,8 +414,12 @@
         functools.partial(backward_kernel, False),
         out_shape=jax.ShapeDtypeStruct(adjoint.shape, F32),
         in_specs=[SMEM] + [VMEM] * 8,
-        out_specs=VMEM,
-        scratch_shapes=[pltpu.VMEM((rows + 2, fields, width + 2 * EDGE, levels), F32)],
+        out_specs=ANY,
+        scratch_shapes=[
+            pltpu.VMEM((rows, fields, width, levels), F32),
+            pltpu.VMEM((rows + 2, fields, width + 2 * EDGE, levels), F32),
+            pltpu.SemaphoreType.DMA((rows,)),
+        ],
         compiler_params=params(16),
         name="backward_last",
     )(pos, adjoint, *rims, wide, state, background)

time: 215 us -> 214 us (level)
  no operation moved by 1% of the time
where the time goes in v6:
time: 214 us; the launch traced here: 211 us
  waiting for transfers between devices  115 us (54%)
  Pallas kernels  46.8 us (22%)
  starting transfers between devices  41.2 us (19%)
  local copies, waits for them, and re-layouts  4.71 us (2%)
  other arithmetic  3 us (1%)
    ppermute x31, waiting for transfers between devices, exchange(): return lax.ppermute(array, axis, [(i, i ^ mask) for i in range(count)])  105 us
    pallas_call x5, Pallas kernels, instrument(): pl.pallas_call(functools.partial(instrument_kernel, group, served, n_lat,...  27.7 us
    ppermute x31, starting transfers between devices, exchange(): return lax.ppermute(array, axis, [(i, i ^ mask) for i in range(count)])  22.2 us
    ppermute x4, starting transfers between devices, shifted(): return lax.ppermute(array, axis, pairs)  10.4 us
    ppermute x8, waiting for transfers between devices, paired(): return lax.ppermute(array, axis, pairs)  9.43 us
    ppermute x8, starting transfers between devices, paired(): return lax.ppermute(array, axis, pairs)  8.65 us
    pallas_call x1, Pallas kernels, forward(): pl.pallas_call(functools.partial(forward_kernel, group), out_shape=outs,...  5.39 us
  transfers between devices with their start and end apart: 43, of which 15 were waited for; matrix products, arithmetic and copies ran while one was open for 2% of the time, Pallas kernels for 19%

profile of v6, /device:TPU:30, one launch (start us, length us, event | category | flops | bytes accessed | tf_op | source)
XLA Modules:
  0.0 211.3 jit_solution(7205017164758205763)
XLA Ops:
  0.0 0.8 slice_bitcast_fusion.3
  0.8 1.1 fusion.1
  1.9 0.6 collective-permute-start.1
  2.5 4.3 %collective-permute-start = (f32[8,7,2,128]{3,2,1,0:T(2,128)S(1)}, f32[8,7,2,128]{3,2,1,0:T(2,128)S(1)}, u32[]{:S(2)}, u32[]{:S(2)}) collective-permute-start(f32[8,7,2,128]{3,2,1,0:T(2,128)S(1)} %pad_maximum_fusion.2), channel_id=1, source_target_pairs={{0,4},{4,8},{8,12},{12,16},{16,20},{20,24},{24,28},{28,0},{1,5},{5... | collective-permute-start | bytes 172040 | tf_op jit(solution)/shard_map/ppermute | solution.py:37
  6.8 1.2 fusion
  8.0 0.9 collective-permute-done.1.east
  8.9 0.8 pad_maximum_fusion
  9.7 1.9 collective-permute-start.2
  11.7 0.8 pad_maximum_fusion.1
  12.5 3.6 %collective-permute-start.3 = (f32[2,7,68,128]{3,2,1,0:T(8,128)}, f32[2,7,68,128]{3,2,1,0:T(8,128)}, u32[]{:S(2)}, u32[]{:S(2)}) collective-permute-start(f32[2,7,68,128]{3,2,1,0:T(8,128)} %pad_maximum_fusion.1), channel_id=1, source_target_pairs={{1,0},{2,1},{3,2},{5,4},{6,5},{7,6},{9,8},{10,9},{11,10},{13,12},{... | collective-permute-start | bytes 1462280 | tf_op jit(solution)/shard_map/ppermute | solution.py:37
  16.1 0.6 pad_add_fusion.pos.refs_0_
  16.7 3.3 %pack.1 = (bf16[288,1024]{1,0:T(8,128)(2,1)}, bf16[304,1024]{1,0:T(8,128)(2,1)}) custom-call(s32[2]{0:T(128)} %pad_add_fusion.pos.refs_0_, bf16[768,1024]{1,0:T(8,128)(2,1)} %bitcast.30, bf16[1024,1024]{1,0:T(8,128)(2,1)} %bitcast.28, bf16[1024,512]{1,0:T(8,128)(2,1)} %bitcast.33, f32[1,512]{1,0:T(1,128)} %scale.1), custom_call_target="tpu_custom_call" | custom-call | tf_op jit(solution)/shard_map/pack/pallas_call | solution.py:111
  20.0 0.1 collective-permute-start.8
  20.1 2.0 collective-permute-start.7
  22.1 0.7 select_reduce_fusion.table
  22.8 2.3 %pick_radiances.1 = bf16[2,4,128,512]{3,2,1,0:T(8,128)(2,1)} custom-call(s32[2]{0:T(128)} %pad_add_fusion.pos.refs_0_, s32[2,8]{1,0:T(2,128)} %select_reduce_fusion.table, bf16[2,512,512]{2,1,0:T(8,128)(2,1)} %bitcast.22), custom_call_target="tpu_custom_call" | custom-call | tf_op jit(solution)/shard_map/pick_radiances/pallas_call | solution.py:162
  25.1 4.0 %collective-permute-start.5 = (bf16[2,4,128,512]{3,2,1,0:T(8,128)(2,1)}, bf16[2,4,128,512]{3,2,1,0:T(8,128)(2,1)S(1)}, u32[]{:S(2)}, u32[]{:S(2)}) collective-permute-start(bf16[2,4,128,512]{3,2,1,0:T(8,128)(2,1)} %pick_radiances.1), channel_id=1, source_target_pairs={{0,4},{4,0},{8,12},{12,8},{16,20},{20,16},{24,28},{28,24},{1,5},{5... | collective-permute-start | bytes 3145736 | tf_op jit(solution)/shard_map/ppermute | solution.py:29
  29.1 42.0 %collective-permute-done.7.refs_2_ = bf16[288,1024]{1,0:T(8,128)(2,1)} collective-permute-done((bf16[288,1024]{1,0:T(8,128)(2,1)}, bf16[288,1024]{1,0:T(8,128)(2,1)}, u32[]{:S(2)}, u32[]{:S(2)}) %collective-permute-start.7) | collective-permute-done | bytes 589856 | tf_op jit(solution)/shard_map/ppermute | solution.py:29
  71.1 0.6 collective-permute-start.18
  71.7 5.4 %forward.1 = (f32[12,7,96,128]{3,2,1,0:T(8,128)S(1)}, f32[10,6,80,128]{3,2,1,0:T(8,128)S(1)}, bf16[2,512,768]{2,1,0:T(8,128)(2,1)S(1)}, bf16[2,4,128,768]{3,2,1,0:T(8,128)(2,1)S(1)}) custom-call(s32[2]{0:T(128)S(1)} %copy-done.7, s32[2,8]{1,0:T(2,128)S(1)} %copy-done.8, f32[8,6,64,128]{3,2,1,0:T(8,128)S(1)} %bitcast.20, f32[8,64,128]{2,1,0:T(8,128)S(1)} %copy-done.6, ...), custom_call_target="tpu_custom_call" | custom-call | tf_op jit(solution)/shard_map/forward/pallas_call | solution.py:268
  77.1 3.3 %collective-permute-start.4 = (bf16[2,4,128,768]{3,2,1,0:T(8,128)(2,1)S(1)}, bf16[2,4,128,768]{3,2,1,0:T(8,128)(2,1)S(1)}, u32[]{:S(2)}, u32[]{:S(2)}) collective-permute-start(bf16[2,4,128,768]{3,2,1,0:T(8,128)(2,1)S(1)} %get-tuple-element.32), channel_id=1, source_target_pairs={{0,4},{4,0},{8,12},{12,8},{16,20},{20,16},{24,28},{28,24},{1,5},{5... | collective-permute-start | bytes 4718600 | tf_op jit(solution)/shard_map/ppermute | solution.py:29
  80.4 1.7 collective-permute-start.20
  82.2 5.3 %collective-permute-done.11.refs_6_ = bf16[288,1024]{1,0:T(8,128)(2,1)S(1)} collective-permute-done((bf16[288,1024]{1,0:T(8,128)(2,1)}, bf16[288,1024]{1,0:T(8,128)(2,1)S(1)}, u32[]{:S(2)}, u32[]{:S(2)}) %collective-permute-start.11) | collective-permute-done | bytes 589856 | tf_op jit(solution)/shard_map/ppermute | solution.py:29
  87.5 12.6 %collective-permute-done.20.refs_6_ = bf16[288,1024]{1,0:T(8,128)(2,1)S(1)} collective-permute-done((bf16[288,1024]{1,0:T(8,128)(2,1)}, bf16[288,1024]{1,0:T(8,128)(2,1)S(1)}, u32[]{:S(2)}, u32[]{:S(2)}) %collective-permute-start.20) | collective-permute-done | bytes 589856 | tf_op jit(solution)/shard_map/ppermute | solution.py:29
  100.1 2.0 collective-permute-done.25.refs_2_
  102.1 0.6 collective-permute-start.21
  102.7 0.3 collective-permute-start.26
  103.0 10.5 %collective-permute-done.12.refs_7_ = bf16[304,1024]{1,0:T(8,128)(2,1)S(1)} collective-permute-done((bf16[304,1024]{1,0:T(8,128)(2,1)}, bf16[304,1024]{1,0:T(8,128)(2,1)S(1)}, u32[]{:S(2)}, u32[]{:S(2)}) %collective-permute-start.12) | collective-permute-done | bytes 622624 | tf_op jit(solution)/shard_map/ppermute | solution.py:29
  113.5 0.5 collective-permute-start.14
  114.0 12.4 %collective-permute-done.21.refs_7_ = bf16[304,1024]{1,0:T(8,128)(2,1)S(1)} collective-permute-done((bf16[304,1024]{1,0:T(8,128)(2,1)S(1)}, bf16[304,1024]{1,0:T(8,128)(2,1)S(1)}, u32[]{:S(2)}, u32[]{:S(2)}) %collective-permute-start.21) | collective-permute-done | bytes 622624 | tf_op jit(solution)/shard_map/ppermute | solution.py:29
  126.4 0.3 collective-permute-start.29
  126.7 0.2 collective-permute-start.23
  127.0 1.6 copy-done.2
  128.6 6.1 %shard_map.91 = (bf16[2,128,768]{2,1,0:T(8,128)(2,1)S(1)}, bf16[2,128,768]{2,1,0:T(8,128)(2,1)S(1)}) custom-call(s32[2]{0:T(128)S(1)} %copy-done.7, s32[2,8]{1,0:T(2,128)S(1)} %copy-done.8, bf16[2,512,768]{2,1,0:T(8,128)(2,1)S(1)} %get-tuple-element.31.columns, bf16[2,512,512]{2,1,0:T(8,128)(2,1)S(1)} %bitcast.23, ...), custom_call_target="tpu_custom_call" | custom-call | flops 4831838208 | bytes 6815744 | tf_op jit(solution)/shard_map/pallas_call | solution.py:530
  134.7 0.4 collective-permute-start.27
  135.1 7.0 %collective-permute-done.29.refs_6_ = bf16[288,1024]{1,0:T(8,128)(2,1)S(1)} collective-permute-done((bf16[288,1024]{1,0:T(8,128)(2,1)S(1)}, bf16[288,1024]{1,0:T(8,128)(2,1)S(1)}, u32[]{:S(2)}, u32[]{:S(2)}) %collective-permute-start.29) | collective-permute-done | bytes 589856 | tf_op jit(solution)/shard_map/ppermute | solution.py:29
  142.1 0.5 collective-permute-start.31
  142.7 7.0 %shard_map.92 = (bf16[2,128,768]{2,1,0:T(8,128)(2,1)S(1)}, bf16[2,128,768]{2,1,0:T(8,128)(2,1)S(1)}) custom-call(s32[2]{0:T(128)S(1)} %copy-done.7, s32[2,8]{1,0:T(2,128)S(1)} %copy-done.8, bf16[2,512,768]{2,1,0:T(8,128)(2,1)S(1)} %get-tuple-element.31.columns, bf16[2,512,512]{2,1,0:T(8,128)(2,1)S(1)} %bitcast.24, ...), custom_call_target="tpu_custom_call" | custom-call | flops 4831838208 | bytes 6815744 | tf_op jit(solution)/shard_map/pallas_call | solution.py:530
  149.8 3.3 %collective-permute-start.6 = (bf16[2,128,768]{2,1,0:T(8,128)(2,1)S(1)}, bf16[2,128,768]{2,1,0:T(8,128)(2,1)S(1)}, u32[]{:S(2)}, u32[]{:S(2)}) collective-permute-start(bf16[2,128,768]{2,1,0:T(8,128)(2,1)S(1)} %get-tuple-element.34), channel_id=1, source_target_pairs={{0,4},{4,0},{8,12},{12,8},{16,20},{20,16},{24,28},{28,24},{1,5},{5... | collective-permute-start | bytes 1179656 | tf_op jit(solution)/shard_map/ppermute | solution.py:29
  153.1 7.0 %shard_map.93 = (bf16[2,128,768]{2,1,0:T(8,128)(2,1)S(1)}, bf16[2,128,768]{2,1,0:T(8,128)(2,1)S(1)}) custom-call(s32[2]{0:T(128)S(1)} %copy-done.7, s32[2,8]{1,0:T(2,128)S(1)} %copy-done.8, bf16[2,512,768]{2,1,0:T(8,128)(2,1)S(1)} %get-tuple-element.31.columns, bf16[2,512,512]{2,1,0:T(8,128)(2,1)S(1)} %bitcast.25, ...), custom_call_target="tpu_custom_call" | custom-call | flops 4831838208 | bytes 6815744 | tf_op jit(solution)/shard_map/pallas_call | solution.py:530
  160.1 0.1 collective-permute-start.15
  160.2 2.0 collective-permute-start.24
  162.2 3.7 %shard_map.94 = (bf16[1,128,768]{2,1,0:T(8,128)(2,1)S(1)}, bf16[1,128,768]{2,1,0:T(8,128)(2,1)S(1)}) custom-call(s32[2]{0:T(128)S(1)} %copy-done.7, s32[2,8]{1,0:T(2,128)S(1)} %copy-done.8, bf16[2,512,768]{2,1,0:T(8,128)(2,1)S(1)} %get-tuple-element.31.columns, bf16[2,512,512]{2,1,0:T(8,128)(2,1)S(1)} %bitcast.26, ...), custom_call_target="tpu_custom_call" | custom-call | flops 2415919104 | bytes 5767168 | tf_op jit(solution)/shard_map/pallas_call | solution.py:530
  166.0 0.2 collective-permute-start.33
  166.1 3.7 %shard_map.96 = (bf16[1,128,768]{2,1,0:T(8,128)(2,1)S(1)}, bf16[1,128,768]{2,1,0:T(8,128)(2,1)S(1)}) custom-call(s32[2]{0:T(128)S(1)} %copy-done.7, s32[2,8]{1,0:T(2,128)S(1)} %copy-done.8, bf16[2,512,768]{2,1,0:T(8,128)(2,1)S(1)} %get-tuple-element.31.columns, bf16[2,512,512]{2,1,0:T(8,128)(2,1)S(1)} %bitcast.27, ...), custom_call_target="tpu_custom_call" | custom-call | flops 2415919104 | bytes 5767168 | tf_op jit(solution)/shard_map/pallas_call | solution.py:530
  169.9 2.0 collective-permute-start.38
  171.9 0.3 collective-permute-done.15.refs_3_
  172.2 8.4 %collective-permute-done.24.refs_5_ = bf16[2,128,768]{2,1,0:T(8,128)(2,1)S(1)} collective-permute-done((bf16[2,128,768]{2,1,0:T(8,128)(2,1)S(1)}, bf16[2,128,768]{2,1,0:T(8,128)(2,1)S(1)}, u32[]{:S(2)}, u32[]{:S(2)}) %collective-permute-start.24) | collective-permute-done | bytes 393248 | tf_op jit(solution)/shard_map/ppermute | solution.py:29
  180.6 4.2 %collective-permute-done.33.refs_7_ = bf16[1,128,768]{2,1,0:T(8,128)(2,1)S(1)} collective-permute-done((bf16[1,128,768]{2,1,0:T(8,128)(2,1)S(1)}, bf16[1,128,768]{2,1,0:T(8,128)(2,1)S(1)}, u32[]{:S(2)}, u32[]{:S(2)}) %collective-permute-start.33) | collective-permute-done | bytes 196640 | tf_op jit(solution)/shard_map/ppermute | solution.py:29
  184.8 1.0 shard_map.95
  185.9 0.1 collective-permute-start.34
  185.9 2.3 %collective-permute-start.35 = (bf16[6,64,128]{2,1,0:T(8,128)(2,1)S(1)}, bf16[6,64,128]{2,1,0:T(8,128)(2,1)S(1)}, u32[]{:S(2)}, u32[]{:S(2)}) collective-permute-start(bf16[6,64,128]{2,1,0:T(8,128)(2,1)S(1)} %get-tuple-element.45), channel_id=1, source_target_pairs={{1,2},{2,1},{5,6},{6,5},{9,10},{10,9},{13,14},{14,13},{17,18},{18,... | collective-permute-start | bytes 294920 | tf_op jit(solution)/shard_map/ppermute | solution.py:45
  188.2 1.4 collective-permute-start.36
  189.6 1.4 collective-permute-start.37
  191.0 1.0 shard_map.97.refs_8_
  192.0 0.2 collective-permute-done.36.refs_4_
  192.2 4.0 %collective-permute-done.37.refs_5_ = f32[8,6,128]{2,1,0:T(8,128)S(1)} collective-permute-done((f32[8,6,128]{2,1,0:T(8,128)S(1)}, f32[8,6,128]{2,1,0:T(8,128)S(1)}, u32[]{:S(2)}, u32[]{:S(2)}) %collective-permute-start.37) | collective-permute-done | bytes 24608 | tf_op jit(solution)/shard_map/ppermute | solution.py:45
  196.2 2.7 %backward_first.1 = (f32[8,6,64,128]{3,2,1,0:T(8,128)S(1)}, f32[6,64,128]{2,1,0:T(8,128)S(1)}, f32[6,64,128]{2,1,0:T(8,128)S(1)}, f32[8,6,128]{2,1,0:T(8,128)S(1)}, f32[8,6,128]{2,1,0:T(8,128)S(1)}) custom-call(s32[2]{0:T(128)S(1)} %copy-done.7, bf16[8,6,64,128]{3,2,1,0:T(8,128)(2,1)S(1)} %get-tuple-element.43.refs_1_, ...), custom_call_target="tpu_custom_call" | custom-call | tf_op jit(solution)/shard_map/backward_first/pallas_call | solution.py:396
  198.9 0.1 collective-permute-start.39
  199.0 1.9 collective-permute-start.40
  201.0 1.5 collective-permute-start.42
  202.5 2.4 %collective-permute-done.41.refs_4_ = f32[8,6,128]{2,1,0:T(8,128)S(1)} collective-permute-done((f32[8,6,128]{2,1,0:T(8,128)S(1)}, f32[8,6,128]{2,1,0:T(8,128)S(1)}, u32[]{:S(2)}, u32[]{:S(2)}) %collective-permute-start.41) | collective-permute-done | bytes 24608 | tf_op jit(solution)/shard_map/ppermute | solution.py:45
  204.9 2.8 %collective-permute-done.42.refs_5_ = f32[8,6,128]{2,1,0:T(8,128)S(1)} collective-permute-done((f32[8,6,128]{2,1,0:T(8,128)S(1)}, f32[8,6,128]{2,1,0:T(8,128)S(1)}, u32[]{:S(2)}, u32[]{:S(2)}) %collective-permute-start.42) | collective-permute-done | bytes 24608 | tf_op jit(solution)/shard_map/ppermute | solution.py:45
  207.7 3.4 %backward_last.1 = f32[8,6,64,128]{3,2,1,0:T(8,128)} custom-call(s32[2]{0:T(128)S(1)} %copy-done.7, f32[8,6,64,128]{3,2,1,0:T(8,128)S(1)} %get-tuple-element.52.refs_1_, f32[6,64,128]{2,1,0:T(8,128)S(1)} %collective-permute-done.39.refs_2_, f32[6,64,128]{2,1,0:T(8,128)S(1)} %collective-permute-done.40.refs_3_, ...), custom_call_target="tpu_custom_call" | custom-call | tf_op jit(solution)/shard_map/backward_last/pallas_call | solution.py:413
  (68 shorter events, 0.4 us)
Async XLA Ops:
  0.0 8.0 %copy-start.6 = (f32[8,64,128]{2,1,0:T(8,128)S(1)}, f32[8,64,128]{2,1,0:T(8,128)}, u32[]{:S(2)}) copy-start(f32[8,64,128]{2,1,0:T(8,128)} %kappa.1) | copy-start | bytes 786436
  1.9 6.9 %collective-permute-start.1 = (f32[8,7,2,128]{3,2,1,0:T(2,128)S(1)}, f32[8,7,2,128]{3,2,1,0:T(2,128)S(1)}, u32[]{:S(2)}, u32[]{:S(2)}) collective-permute-start(f32[8,7,2,128]{3,2,1,0:T(2,128)S(1)} %pad_maximum_fusion.3), channel_id=1, source_target_pairs={{0,28},{4,0},{8,4},{12,8},{16,12},{20,16},{24,20},{28,24},{1,29},{... | collective-permute-start | bytes 172040 | tf_op jit(solution)/shard_map/ppermute | solution.py:37
  2.5 6.3 %collective-permute-start = (f32[8,7,2,128]{3,2,1,0:T(2,128)S(1)}, f32[8,7,2,128]{3,2,1,0:T(2,128)S(1)}, u32[]{:S(2)}, u32[]{:S(2)}) collective-permute-start(f32[8,7,2,128]{3,2,1,0:T(2,128)S(1)} %pad_maximum_fusion.2), channel_id=1, source_target_pairs={{0,4},{4,8},{8,12},{12,16},{16,20},{20,24},{24,28},{28,0},{1,5},{5... | collective-permute-start | bytes 172040 | tf_op jit(solution)/shard_map/ppermute | solution.py:37
  9.7 15.3 %collective-permute-start.2 = (f32[2,7,68,128]{3,2,1,0:T(8,128)}, f32[2,7,68,128]{3,2,1,0:T(8,128)S(1)}, u32[]{:S(2)}, u32[]{:S(2)}) collective-permute-start(f32[2,7,68,128]{3,2,1,0:T(8,128)} %pad_maximum_fusion), channel_id=1, source_target_pairs={{0,1},{1,2},{2,3},{4,5},{5,6},{6,7},{8,9},{9,10},{10,11},{12,13},{... | collective-permute-start | bytes 1462280 | tf_op jit(solution)/shard_map/ppermute | solution.py:37
  12.5 16.6 %collective-permute-start.3 = (f32[2,7,68,128]{3,2,1,0:T(8,128)}, f32[2,7,68,128]{3,2,1,0:T(8,128)}, u32[]{:S(2)}, u32[]{:S(2)}) collective-permute-start(f32[2,7,68,128]{3,2,1,0:T(8,128)} %pad_maximum_fusion.1), channel_id=1, source_target_pairs={{1,0},{2,1},{3,2},{5,4},{6,5},{7,6},{9,8},{10,9},{11,10},{13,12},{... | collective-permute-start | bytes 1462280 | tf_op jit(solution)/shard_map/ppermute | solution.py:37
  16.7 5.4 %copy-start.9 = (s32[2,1,4]{2,1,0:T(1,128)S(1)}, s32[2,1,4]{2,1,0:T(1,128)}, u32[]{:S(2)}) copy-start(s32[2,1,4]{2,1,0:T(1,128)} %param.13) | copy-start | bytes 100
  16.7 110.2 %copy-start.5 = (bf16[1,1024,512]{2,1,0:T(8,128)(2,1)S(1)}, bf16[1,1024,512]{2,1,0:T(8,128)(2,1)}, u32[]{:S(2)}) copy-start(bf16[1,1024,512]{2,1,0:T(8,128)(2,1)} %param.16) | copy-start | bytes 3145732
  20.0 51.7 %copy-start = (f32[8,64,6,128]{3,1,2,0:T(8,128)S(1)}, f32[8,64,6,128]{3,1,2,0:T(8,128)}, u32[]{:S(2)}) copy-start(f32[8,64,6,128]{3,1,2,0:T(8,128)} %param.9) | copy-start | bytes 4718596
  20.0 51.7 %copy-start.7 = (s32[2]{0:T(128)S(1)}, s32[2]{0:T(128)}, u32[]{:S(2)}) copy-start(s32[2]{0:T(128)} %pad_add_fusion.pos.refs_0_) | copy-start | bytes 28
  20.0 51.1 %collective-permute-start.8 = (bf16[304,1024]{1,0:T(8,128)(2,1)}, bf16[304,1024]{1,0:T(8,128)(2,1)}, u32[]{:S(2)}, u32[]{:S(2)}) collective-permute-start(bf16[304,1024]{1,0:T(8,128)(2,1)} %get-tuple-element.36), channel_id=1, source_target_pairs={{0,8},{4,12},{8,0},{12,4},{16,24},{20,28},{24,16},{28,20},{1,9},{5... | collective-permute-start | bytes 1867784 | tf_op jit(solution)/shard_map/ppermute | solution.py:29
  20.1 51.0 %collective-permute-start.7 = (bf16[288,1024]{1,0:T(8,128)(2,1)}, bf16[288,1024]{1,0:T(8,128)(2,1)}, u32[]{:S(2)}, u32[]{:S(2)}) collective-permute-start(bf16[288,1024]{1,0:T(8,128)(2,1)} %get-tuple-element.35), channel_id=1, source_target_pairs={{0,8},{4,12},{8,0},{12,4},{16,24},{20,28},{24,16},{28,20},{1,9},{5... | collective-permute-start | bytes 1769480 | tf_op jit(solution)/shard_map/ppermute | solution.py:29
  22.1 49.0 %collective-permute-start.16 = (bf16[288,1024]{1,0:T(8,128)(2,1)}, bf16[288,1024]{1,0:T(8,128)(2,1)}, u32[]{:S(2)}, u32[]{:S(2)}) collective-permute-start(bf16[288,1024]{1,0:T(8,128)(2,1)} %get-tuple-element.35), channel_id=1, source_target_pairs={{0,16},{4,20},{8,24},{12,28},{16,0},{20,4},{24,8},{28,12},{1,17},{... | collective-permute-start | bytes 1769480 | tf_op jit(solution)/shard_map/ppermute | solution.py:29
  22.8 48.9 %copy-start.8 = (s32[2,8]{1,0:T(2,128)S(1)}, s32[2,8]{1,0:T(2,128)}, u32[]{:S(2)}) copy-start(s32[2,8]{1,0:T(2,128)} %select_reduce_fusion.table) | copy-start | bytes 196
  25.1 101.9 %copy-start.1 = (bf16[2,8,64,512]{3,2,1,0:T(8,128)(2,1)S(1)}, bf16[2,8,64,512]{3,2,1,0:T(8,128)(2,1)}, u32[]{:S(2)}) copy-start(bf16[2,8,64,512]{3,2,1,0:T(8,128)(2,1)} %param.12) | copy-start | bytes 3145732
  25.1 101.9 %copy-start.3 = (bf16[1,768,1024]{2,1,0:T(8,128)(2,1)S(1)}, bf16[1,768,1024]{2,1,0:T(8,128)(2,1)}, u32[]{:S(2)}) copy-start(bf16[1,768,1024]{2,1,0:T(8,128)(2,1)} %param.14) | copy-start | bytes 4718596
  25.1 101.9 %copy-start.10 = (f32[1,512]{1,0:T(1,128)S(1)}, f32[1,512]{1,0:T(1,128)}, u32[]{:S(2)}) copy-start(f32[1,512]{1,0:T(1,128)} %scale.1) | copy-start | bytes 6148
  25.1 55.3 %collective-permute-start.5 = (bf16[2,4,128,512]{3,2,1,0:T(8,128)(2,1)}, bf16[2,4,128,512]{3,2,1,0:T(8,128)(2,1)S(1)}, u32[]{:S(2)}, u32[]{:S(2)}) collective-permute-start(bf16[2,4,128,512]{3,2,1,0:T(8,128)(2,1)} %pick_radiances.1), channel_id=1, source_target_pairs={{0,4},{4,0},{8,12},{12,8},{16,20},{20,16},{24,28},{28,24},{1,5},{5... | collective-permute-start | bytes 3145736 | tf_op jit(solution)/shard_map/ppermute | solution.py:29
  29.1 48.0 %collective-permute-start.17 = (bf16[304,1024]{1,0:T(8,128)(2,1)}, bf16[304,1024]{1,0:T(8,128)(2,1)S(1)}, u32[]{:S(2)}, u32[]{:S(2)}) collective-permute-start(bf16[304,1024]{1,0:T(8,128)(2,1)} %get-tuple-element.36), channel_id=1, source_target_pairs={{0,16},{4,20},{8,24},{12,28},{16,0},{20,4},{24,8},{28,12},{1,17},{... | collective-permute-start | bytes 1867784 | tf_op jit(solution)/shard_map/ppermute | solution.py:29
  71.1 9.3 %collective-permute-start.9 = (bf16[288,1024]{1,0:T(8,128)(2,1)}, bf16[288,1024]{1,0:T(8,128)(2,1)S(1)}, u32[]{:S(2)}, u32[]{:S(2)}) collective-permute-start(bf16[288,1024]{1,0:T(8,128)(2,1)} %collective-permute-done.7.refs_2_), channel_id=1, source_target_pairs={{0,1},{1,0},{2,3},{3,2},{4,5},{5,4},{6,7},{7,6},{8,9},{9,8},{10,11... | collective-permute-start | bytes 1769480 | tf_op jit(solution)/shard_map/ppermute | solution.py:29
  71.1 16.4 %collective-permute-start.11 = (bf16[288,1024]{1,0:T(8,128)(2,1)}, bf16[288,1024]{1,0:T(8,128)(2,1)S(1)}, u32[]{:S(2)}, u32[]{:S(2)}) collective-permute-start(bf16[288,1024]{1,0:T(8,128)(2,1)} %collective-permute-done.7.refs_2_), channel_id=1, source_target_pairs={{0,2},{1,3},{2,0},{3,1},{4,6},{5,7},{6,4},{7,5},{8,10},{9,11},{10,... | collective-permute-start | bytes 1769480 | tf_op jit(solution)/shard_map/ppermute | solution.py:29
  71.1 16.4 %collective-permute-start.18 = (bf16[288,1024]{1,0:T(8,128)(2,1)}, bf16[288,1024]{1,0:T(8,128)(2,1)S(1)}, u32[]{:S(2)}, u32[]{:S(2)}) collective-permute-start(bf16[288,1024]{1,0:T(8,128)(2,1)} %collective-permute-done.16.refs_2_), channel_id=1, source_target_pairs={{0,1},{1,0},{2,3},{3,2},{4,5},{5,4},{6,7},{7,6},{8,9},{9,8},{10,11... | collective-permute-start | bytes 1769480 | tf_op jit(solution)/shard_map/ppermute | solution.py:29
  77.1 49.7 %collective-permute-start.4 = (bf16[2,4,128,768]{3,2,1,0:T(8,128)(2,1)S(1)}, bf16[2,4,128,768]{3,2,1,0:T(8,128)(2,1)S(1)}, u32[]{:S(2)}, u32[]{:S(2)}) collective-permute-start(bf16[2,4,128,768]{3,2,1,0:T(8,128)(2,1)S(1)} %get-tuple-element.32), channel_id=1, source_target_pairs={{0,4},{4,0},{8,12},{12,8},{16,20},{20,16},{24,28},{28,24},{1,5},{5... | collective-permute-start | bytes 4718600 | tf_op jit(solution)/shard_map/ppermute | solution.py:29
  80.4 22.3 %collective-permute-start.10 = (bf16[304,1024]{1,0:T(8,128)(2,1)}, bf16[304,1024]{1,0:T(8,128)(2,1)S(1)}, u32[]{:S(2)}, u32[]{:S(2)}) collective-permute-start(bf16[304,1024]{1,0:T(8,128)(2,1)} %collective-permute-done.8.refs_3_), channel_id=1, source_target_pairs={{0,1},{1,0},{2,3},{3,2},{4,5},{5,4},{6,7},{7,6},{8,9},{9,8},{10,11... | collective-permute-start | bytes 1867784 | tf_op jit(solution)/shard_map/ppermute | solution.py:29
  80.4 19.7 %collective-permute-start.20 = (bf16[288,1024]{1,0:T(8,128)(2,1)}, bf16[288,1024]{1,0:T(8,128)(2,1)S(1)}, u32[]{:S(2)}, u32[]{:S(2)}) collective-permute-start(bf16[288,1024]{1,0:T(8,128)(2,1)} %collective-permute-done.16.refs_2_), channel_id=1, source_target_pairs={{0,2},{1,3},{2,0},{3,1},{4,6},{5,7},{6,4},{7,5},{8,10},{9,11},{10,... | collective-permute-start | bytes 1769480 | tf_op jit(solution)/shard_map/ppermute | solution.py:29
  87.5 14.6 %collective-permute-start.25 = (bf16[288,1024]{1,0:T(8,128)(2,1)}, bf16[288,1024]{1,0:T(8,128)(2,1)S(1)}, u32[]{:S(2)}, u32[]{:S(2)}) collective-permute-start(bf16[288,1024]{1,0:T(8,128)(2,1)} %collective-permute-done.16.refs_2_), channel_id=1, source_target_pairs={{0,8},{4,12},{8,0},{12,4},{16,24},{20,28},{24,16},{28,20},{1,9},{5... | collective-permute-start | bytes 1769480 | tf_op jit(solution)/shard_map/ppermute | solution.py:29
  87.5 26.0 %collective-permute-start.12 = (bf16[304,1024]{1,0:T(8,128)(2,1)}, bf16[304,1024]{1,0:T(8,128)(2,1)S(1)}, u32[]{:S(2)}, u32[]{:S(2)}) collective-permute-start(bf16[304,1024]{1,0:T(8,128)(2,1)} %collective-permute-done.8.refs_3_), channel_id=1, source_target_pairs={{0,2},{1,3},{2,0},{3,1},{4,6},{5,7},{6,4},{7,5},{8,10},{9,11},{10,... | collective-permute-start | bytes 1867784 | tf_op jit(solution)/shard_map/ppermute | solution.py:29
  100.1 13.3 %collective-permute-start.19 = (bf16[304,1024]{1,0:T(8,128)(2,1)S(1)}, bf16[304,1024]{1,0:T(8,128)(2,1)S(1)}, u32[]{:S(2)}, u32[]{:S(2)}) collective-permute-start(bf16[304,1024]{1,0:T(8,128)(2,1)S(1)} %collective-permute-done.17.refs_3_), channel_id=1, source_target_pairs={{0,1},{1,0},{2,3},{3,2},{4,5},{5,4},{6,7},{7,6},{8,9},{9,8},{10,11... | collective-permute-start | bytes 1867784 | tf_op jit(solution)/shard_map/ppermute | solution.py:29
  102.1 24.2 %collective-permute-start.21 = (bf16[304,1024]{1,0:T(8,128)(2,1)S(1)}, bf16[304,1024]{1,0:T(8,128)(2,1)S(1)}, u32[]{:S(2)}, u32[]{:S(2)}) collective-permute-start(bf16[304,1024]{1,0:T(8,128)(2,1)S(1)} %collective-permute-done.17.refs_3_), channel_id=1, source_target_pairs={{0,2},{1,3},{2,0},{3,1},{4,6},{5,7},{6,4},{7,5},{8,10},{9,11},{10,... | collective-permute-start | bytes 1867784 | tf_op jit(solution)/shard_map/ppermute | solution.py:29
  102.7 23.7 %collective-permute-start.26 = (bf16[304,1024]{1,0:T(8,128)(2,1)S(1)}, bf16[304,1024]{1,0:T(8,128)(2,1)S(1)}, u32[]{:S(2)}, u32[]{:S(2)}) collective-permute-start(bf16[304,1024]{1,0:T(8,128)(2,1)S(1)} %collective-permute-done.17.refs_3_), channel_id=1, source_target_pairs={{0,8},{4,12},{8,0},{12,4},{16,24},{20,28},{24,16},{28,20},{1,9},{5... | collective-permute-start | bytes 1867784 | tf_op jit(solution)/shard_map/ppermute | solution.py:29
  113.5 12.9 %collective-permute-start.13 = (bf16[288,1024]{1,0:T(8,128)(2,1)S(1)}, bf16[288,1024]{1,0:T(8,128)(2,1)S(1)}, u32[]{:S(2)}, u32[]{:S(2)}) collective-permute-start(bf16[288,1024]{1,0:T(8,128)(2,1)S(1)} %collective-permute-done.11.refs_6_), channel_id=1, source_target_pairs={{0,1},{1,0},{2,3},{3,2},{4,5},{5,4},{6,7},{7,6},{8,9},{9,8},{10,11... | collective-permute-start | bytes 1769480 | tf_op jit(solution)/shard_map/ppermute | solution.py:29
  113.5 28.6 %collective-permute-start.14 = (bf16[304,1024]{1,0:T(8,128)(2,1)S(1)}, bf16[304,1024]{1,0:T(8,128)(2,1)S(1)}, u32[]{:S(2)}, u32[]{:S(2)}) collective-permute-start(bf16[304,1024]{1,0:T(8,128)(2,1)S(1)} %collective-permute-done.12.refs_7_), channel_id=1, source_target_pairs={{0,1},{1,0},{2,3},{3,2},{4,5},{5,4},{6,7},{7,6},{8,9},{9,8},{10,11... | collective-permute-start | bytes 1867784 | tf_op jit(solution)/shard_map/ppermute | solution.py:29
  126.4 16.3 %collective-permute-start.30 = (bf16[304,1024]{1,0:T(8,128)(2,1)S(1)}, bf16[304,1024]{1,0:T(8,128)(2,1)S(1)}, u32[]{:S(2)}, u32[]{:S(2)}) collective-permute-start(bf16[304,1024]{1,0:T(8,128)(2,1)S(1)} %collective-permute-done.21.refs_7_), channel_id=1, source_target_pairs={{0,8},{4,12},{8,0},{12,4},{16,24},{20,28},{24,16},{28,20},{1,9},{5... | collective-permute-start | bytes 1867784 | tf_op jit(solution)/shard_map/ppermute | solution.py:29
  126.4 8.4 %collective-permute-start.22 = (bf16[288,1024]{1,0:T(8,128)(2,1)S(1)}, bf16[288,1024]{1,0:T(8,128)(2,1)S(1)}, u32[]{:S(2)}, u32[]{:S(2)}) collective-permute-start(bf16[288,1024]{1,0:T(8,128)(2,1)S(1)} %collective-permute-done.20.refs_6_), channel_id=1, source_target_pairs={{0,1},{1,0},{2,3},{3,2},{4,5},{5,4},{6,7},{7,6},{8,9},{9,8},{10,11... | collective-permute-start | bytes 1769480 | tf_op jit(solution)/shard_map/ppermute | solution.py:29
  126.4 15.7 %collective-permute-start.29 = (bf16[288,1024]{1,0:T(8,128)(2,1)S(1)}, bf16[288,1024]{1,0:T(8,128)(2,1)S(1)}, u32[]{:S(2)}, u32[]{:S(2)}) collective-permute-start(bf16[288,1024]{1,0:T(8,128)(2,1)S(1)} %collective-permute-done.25.refs_2_), channel_id=1, source_target_pairs={{0,2},{1,3},{2,0},{3,1},{4,6},{5,7},{6,4},{7,5},{8,10},{9,11},{10,... | collective-permute-start | bytes 1769480 | tf_op jit(solution)/shard_map/ppermute | solution.py:29
  126.7 23.0 %collective-permute-start.23 = (bf16[304,1024]{1,0:T(8,128)(2,1)S(1)}, bf16[304,1024]{1,0:T(8,128)(2,1)S(1)}, u32[]{:S(2)}, u32[]{:S(2)}) collective-permute-start(bf16[304,1024]{1,0:T(8,128)(2,1)S(1)} %collective-permute-done.21.refs_7_), channel_id=1, source_target_pairs={{0,1},{1,0},{2,3},{3,2},{4,5},{5,4},{6,7},{7,6},{8,9},{9,8},{10,11... | collective-permute-start | bytes 1867784 | tf_op jit(solution)/shard_map/ppermute | solution.py:29
  127.0 1.6 copy-start.2
  134.7 25.4 %collective-permute-start.27 = (bf16[288,1024]{1,0:T(8,128)(2,1)S(1)}, bf16[288,1024]{1,0:T(8,128)(2,1)S(1)}, u32[]{:S(2)}, u32[]{:S(2)}) collective-permute-start(bf16[288,1024]{1,0:T(8,128)(2,1)S(1)} %collective-permute-done.25.refs_2_), channel_id=1, source_target_pairs={{0,1},{1,0},{2,3},{3,2},{4,5},{5,4},{6,7},{7,6},{8,9},{9,8},{10,11... | collective-permute-start | bytes 1769480 | tf_op jit(solution)/shard_map/ppermute | solution.py:29
  142.1 18.1 %collective-permute-start.28 = (bf16[304,1024]{1,0:T(8,128)(2,1)S(1)}, bf16[304,1024]{1,0:T(8,128)(2,1)S(1)}, u32[]{:S(2)}, u32[]{:S(2)}) collective-permute-start(bf16[304,1024]{1,0:T(8,128)(2,1)S(1)} %collective-permute-done.26.refs_3_), channel_id=1, source_target_pairs={{0,1},{1,0},{2,3},{3,2},{4,5},{5,4},{6,7},{7,6},{8,9},{9,8},{10,11... | collective-permute-start | bytes 1867784 | tf_op jit(solution)/shard_map/ppermute | solution.py:29
  142.1 20.1 %collective-permute-start.31 = (bf16[288,1024]{1,0:T(8,128)(2,1)S(1)}, bf16[288,1024]{1,0:T(8,128)(2,1)S(1)}, u32[]{:S(2)}, u32[]{:S(2)}) collective-permute-start(bf16[288,1024]{1,0:T(8,128)(2,1)S(1)} %collective-permute-done.29.refs_6_), channel_id=1, source_target_pairs={{0,1},{1,0},{2,3},{3,2},{4,5},{5,4},{6,7},{7,6},{8,9},{9,8},{10,11... | collective-permute-start | bytes 1769480 | tf_op jit(solution)/shard_map/ppermute | solution.py:29
  142.6 19.6 %collective-permute-start.32 = (bf16[304,1024]{1,0:T(8,128)(2,1)S(1)}, bf16[304,1024]{1,0:T(8,128)(2,1)S(1)}, u32[]{:S(2)}, u32[]{:S(2)}) collective-permute-start(bf16[304,1024]{1,0:T(8,128)(2,1)S(1)} %collective-permute-done.30.refs_7_), channel_id=1, source_target_pairs={{0,1},{1,0},{2,3},{3,2},{4,5},{5,4},{6,7},{7,6},{8,9},{9,8},{10,11... | collective-permute-start | bytes 1867784 | tf_op jit(solution)/shard_map/ppermute | solution.py:29
  149.8 22.1 %collective-permute-start.6 = (bf16[2,128,768]{2,1,0:T(8,128)(2,1)S(1)}, bf16[2,128,768]{2,1,0:T(8,128)(2,1)S(1)}, u32[]{:S(2)}, u32[]{:S(2)}) collective-permute-start(bf16[2,128,768]{2,1,0:T(8,128)(2,1)S(1)} %get-tuple-element.34), channel_id=1, source_target_pairs={{0,4},{4,0},{8,12},{12,8},{16,20},{20,16},{24,28},{28,24},{1,5},{5... | collective-permute-start | bytes 1179656 | tf_op jit(solution)/shard_map/ppermute | solution.py:29
  160.1 12.1 %collective-permute-start.15 = (bf16[2,128,768]{2,1,0:T(8,128)(2,1)S(1)}, bf16[2,128,768]{2,1,0:T(8,128)(2,1)S(1)}, u32[]{:S(2)}, u32[]{:S(2)}) collective-permute-start(bf16[2,128,768]{2,1,0:T(8,128)(2,1)S(1)} %get-tuple-element.38), channel_id=1, source_target_pairs={{0,4},{4,0},{8,12},{12,8},{16,20},{20,16},{24,28},{28,24},{1,5},{5... | collective-permute-start | bytes 1179656 | tf_op jit(solution)/shard_map/ppermute | solution.py:29
  160.2 20.4 %collective-permute-start.24 = (bf16[2,128,768]{2,1,0:T(8,128)(2,1)S(1)}, bf16[2,128,768]{2,1,0:T(8,128)(2,1)S(1)}, u32[]{:S(2)}, u32[]{:S(2)}) collective-permute-start(bf16[2,128,768]{2,1,0:T(8,128)(2,1)S(1)} %get-tuple-element.40), channel_id=1, source_target_pairs={{0,4},{4,0},{8,12},{12,8},{16,20},{20,16},{24,28},{28,24},{1,5},{5... | collective-permute-start | bytes 1179656 | tf_op jit(solution)/shard_map/ppermute | solution.py:29
  166.0 18.8 %collective-permute-start.33 = (bf16[1,128,768]{2,1,0:T(8,128)(2,1)S(1)}, bf16[1,128,768]{2,1,0:T(8,128)(2,1)S(1)}, u32[]{:S(2)}, u32[]{:S(2)}) collective-permute-start(bf16[1,128,768]{2,1,0:T(8,128)(2,1)S(1)} %get-tuple-element.42), channel_id=1, source_target_pairs={{0,4},{4,0},{8,12},{12,8},{16,20},{20,16},{24,28},{28,24},{1,5},{5... | collective-permute-start | bytes 589832 | tf_op jit(solution)/shard_map/ppermute | solution.py:29
  169.9 21.1 %collective-permute-start.38 = (bf16[1,128,768]{2,1,0:T(8,128)(2,1)S(1)}, bf16[1,128,768]{2,1,0:T(8,128)(2,1)S(1)}, u32[]{:S(2)}, u32[]{:S(2)}) collective-permute-start(bf16[1,128,768]{2,1,0:T(8,128)(2,1)S(1)} %get-tuple-element.51), channel_id=1, source_target_pairs={{0,4},{4,0},{8,12},{12,8},{16,20},{20,16},{24,28},{28,24},{1,5},{5... | collective-permute-start | bytes 589832 | tf_op jit(solution)/shard_map/ppermute | solution.py:29
  185.9 10.4 %collective-permute-start.34 = (bf16[6,64,128]{2,1,0:T(8,128)(2,1)S(1)}, bf16[6,64,128]{2,1,0:T(8,128)(2,1)S(1)}, u32[]{:S(2)}, u32[]{:S(2)}) collective-permute-start(bf16[6,64,128]{2,1,0:T(8,128)(2,1)S(1)} %get-tuple-element.44), channel_id=1, source_target_pairs={{0,1},{1,0},{2,3},{3,2},{4,5},{5,4},{6,7},{7,6},{8,9},{9,8},{10,11... | collective-permute-start | bytes 294920 | tf_op jit(solution)/shard_map/ppermute | solution.py:45
  185.9 10.3 %collective-permute-start.35 = (bf16[6,64,128]{2,1,0:T(8,128)(2,1)S(1)}, bf16[6,64,128]{2,1,0:T(8,128)(2,1)S(1)}, u32[]{:S(2)}, u32[]{:S(2)}) collective-permute-start(bf16[6,64,128]{2,1,0:T(8,128)(2,1)S(1)} %get-tuple-element.45), channel_id=1, source_target_pairs={{1,2},{2,1},{5,6},{6,5},{9,10},{10,9},{13,14},{14,13},{17,18},{18,... | collective-permute-start | bytes 294920 | tf_op jit(solution)/shard_map/ppermute | solution.py:45
  188.2 4.0 %collective-permute-start.36 = (f32[8,6,128]{2,1,0:T(8,128)S(1)}, f32[8,6,128]{2,1,0:T(8,128)S(1)}, u32[]{:S(2)}, u32[]{:S(2)}) collective-permute-start(f32[8,6,128]{2,1,0:T(8,128)S(1)} %get-tuple-element.46), channel_id=1, source_target_pairs={{0,4},{4,0},{8,12},{12,8},{16,20},{20,16},{24,28},{28,24},{1,5},{5... | collective-permute-start | bytes 73736 | tf_op jit(solution)/shard_map/ppermute | solution.py:45
  189.6 6.6 %collective-permute-start.37 = (f32[8,6,128]{2,1,0:T(8,128)S(1)}, f32[8,6,128]{2,1,0:T(8,128)S(1)}, u32[]{:S(2)}, u32[]{:S(2)}) collective-permute-start(f32[8,6,128]{2,1,0:T(8,128)S(1)} %get-tuple-element.47), channel_id=1, source_target_pairs={{4,8},{8,4},{12,16},{16,12},{20,24},{24,20},{28,0},{0,28},{5,9},{9... | collective-permute-start | bytes 73736 | tf_op jit(solution)/shard_map/ppermute | solution.py:45
  196.2 11.5 %copy-start.4 = (f32[8,64,6,128]{3,1,2,0:T(8,128)S(1)}, f32[8,64,6,128]{3,1,2,0:T(8,128)}, u32[]{:S(2)}) copy-start(f32[8,64,6,128]{3,1,2,0:T(8,128)} %param.10) | copy-start | bytes 4718596
  198.9 8.8 %collective-permute-start.39 = (f32[6,64,128]{2,1,0:T(8,128)S(1)}, f32[6,64,128]{2,1,0:T(8,128)S(1)}, u32[]{:S(2)}, u32[]{:S(2)}) collective-permute-start(f32[6,64,128]{2,1,0:T(8,128)S(1)} %get-tuple-element.53), channel_id=1, source_target_pairs={{0,1},{1,0},{2,3},{3,2},{4,5},{5,4},{6,7},{7,6},{8,9},{9,8},{10,11... | collective-permute-start | bytes 589832 | tf_op jit(solution)/shard_map/ppermute | solution.py:45
  199.0 8.7 %collective-permute-start.40 = (f32[6,64,128]{2,1,0:T(8,128)S(1)}, f32[6,64,128]{2,1,0:T(8,128)S(1)}, u32[]{:S(2)}, u32[]{:S(2)}) collective-permute-start(f32[6,64,128]{2,1,0:T(8,128)S(1)} %get-tuple-element.54), channel_id=1, source_target_pairs={{1,2},{2,1},{5,6},{6,5},{9,10},{10,9},{13,14},{14,13},{17,18},{18,... | collective-permute-start | bytes 589832 | tf_op jit(solution)/shard_map/ppermute | solution.py:45
  200.9 4.0 %collective-permute-start.41 = (f32[8,6,128]{2,1,0:T(8,128)S(1)}, f32[8,6,128]{2,1,0:T(8,128)S(1)}, u32[]{:S(2)}, u32[]{:S(2)}) collective-permute-start(f32[8,6,128]{2,1,0:T(8,128)S(1)} %get-tuple-element.55), channel_id=1, source_target_pairs={{0,4},{4,0},{8,12},{12,8},{16,20},{20,16},{24,28},{28,24},{1,5},{5... | collective-permute-start | bytes 73736 | tf_op jit(solution)/shard_map/ppermute | solution.py:45
  201.0 6.7 %collective-permute-start.42 = (f32[8,6,128]{2,1,0:T(8,128)S(1)}, f32[8,6,128]{2,1,0:T(8,128)S(1)}, u32[]{:S(2)}, u32[]{:S(2)}) collective-permute-start(f32[8,6,128]{2,1,0:T(8,128)S(1)} %get-tuple-element.56), channel_id=1, source_target_pairs={{4,8},{8,4},{12,16},{16,12},{20,24},{24,20},{28,0},{0,28},{5,9},{9... | collective-permute-start | bytes 73736 | tf_op jit(solution)/shard_map/ppermute | solution.py:45
